TPU v7x, 32 devices: a whole 2x2x4 slice. The times are simulated.
32 devices in a mesh: shard: 4 (over z), ctx: 4 (over x, core), tp: 2 (over y).
Axes of the slice: x: 2, y: 2, z: 4, core: 2. Of those that a mesh axis runs over, the one named last changes fastest.
Arguments:
- hidden_in: bfloat16 [8, 2048, 768], P('shard', ('ctx', 'tp')), may hold values from -6 to 6
- doc_lengths: int32 [8, 4], P('shard'), may hold values from 1 to 1024, 2048 in all within a row
- ln1_gain: bfloat16 [2, 768], P(None, 'shard'), may hold values from 0.25 to 1.75
- ln1_bias: bfloat16 [2, 768], P(None, 'shard'), may hold values from -1.1953125 to 1.1953125
- qkv_weight: bfloat16 [2, 768, 2304], P(None, 'shard'), may hold values from -0.21875 to 0.21875
- qv_bias: bfloat16 [2, 1536], P(None, 'shard'), may hold values from -0.29882812 to 0.29882812
- out_weight: bfloat16 [2, 768, 768], P(None, 'shard'), may hold values from -2.5 to 2.5
- out_bias: bfloat16 [2, 768], P(None, 'shard'), may hold values from -1.1953125 to 1.1953125
- ln2_gain: bfloat16 [2, 768], P(None, 'shard'), may hold values from 0.25 to 1.75
- ln2_bias: bfloat16 [2, 768], P(None, 'shard'), may hold values from -1.1953125 to 1.1953125
- up_weight: bfloat16 [2, 768, 3072], P(None, None, ('shard', 'tp')), may hold values from -0.21875 to 0.21875
- up_bias: bfloat16 [2, 3072], P(None, ('shard', 'tp')), may hold values from -3 to 3
- down_weight: bfloat16 [2, 3072, 768], P(None, ('shard', 'tp')), may hold values from -0.109375 to 0.109375
- down_bias: bfloat16 [2, 768], P(None, 'shard'), may hold values from -1.1953125 to 1.1953125
- output_grad: bfloat16 [8, 2048, 768], P('shard', ('ctx', 'tp')), may hold values from -6 to 6
Outputs:
- hidden_out: bfloat16 [8, 2048, 768], P('shard', ('ctx', 'tp'))
- hidden_grad: float32 [8, 2048, 768], P('shard', ('ctx', 'tp'))
- ln1_gain_grad: float32 [2, 768], P(None, 'shard')
- ln1_bias_grad: float32 [2, 768], P(None, 'shard')
- qkv_weight_grad: float32 [2, 768, 2304], P(None, 'shard')
- qv_bias_grad: float32 [2, 1536], P(None, 'shard')
- out_weight_grad: float32 [2, 768, 768], P(None, 'shard')
- out_bias_grad: float32 [2, 768], P(None, 'shard')
- ln2_gain_grad: float32 [2, 768], P(None, 'shard')
- ln2_bias_grad: float32 [2, 768], P(None, 'shard')
- up_weight_grad: float32 [2, 768, 3072], P(None, None, ('shard', 'tp'))
- up_bias_grad: float32 [2, 3072], P(None, ('shard', 'tp'))
- down_weight_grad: float32 [2, 3072, 768], P(None, ('shard', 'tp'))
- down_bias_grad: float32 [2, 768], P(None, 'shard')
Inputs may be any that keep to these rules, and one draw needn't show every extreme that they name: `doc_lengths`: row s holds the lengths of sequence s's 3 documents in order, then the number of padding tokens at its end; each row sums to 2048.
All inputs are finite; a program needn't handle non-finite values.
Results may differ from a plain program's by a relative error of at most 0.017.
Values may be sent and summed in bfloat16 or wider, within the bound.
No kernel may reach another device: no remote copies, remote signals or barrier semaphores. Data moves between devices by JAX's collectives and lax.ppermute only.
A program may use at most 192 MiB of HBM per device.

v0:
```python
from functools import partial

import jax
import jax.numpy as jnp
from jax import lax
from jax.sharding import PartitionSpec as P

HEADS = 12
HEAD = 64
LAYERS = 2


ln_epsilon = 1e-06
masked_score = -1e30


def norm_forward(values_in, gain, bias):
    row_mean = jnp.mean(values_in, axis=-1, keepdims=True)
    centred = values_in - row_mean
    inv_std = lax.rsqrt(jnp.mean(centred * centred, axis=-1, keepdims=True) + ln_epsilon)
    normed = centred * inv_std
    return (normed * gain + bias, normed, inv_std)


def norm_backward(grad_out, normed, inv_std, gain):
    grad_normed = grad_out * gain
    grad_in = inv_std * (
        grad_normed
        - jnp.mean(grad_normed, axis=-1, keepdims=True)
        - normed * jnp.mean(grad_normed * normed, axis=-1, keepdims=True)
    )
    return (grad_in, jnp.sum(grad_out * normed, axis=(0, 1)), jnp.sum(grad_out, axis=(0, 1)))


def segment_ids(doc_lengths, places):
    doc_ends = jnp.cumsum(doc_lengths[:, :-1], axis=1)
    return jnp.sum((places[None, :, None] >= doc_ends[:, None, :]).astype(jnp.int32), axis=2)


def gather_layer(params, layer_index):
    return (
        lax.all_gather(params[0][layer_index], "shard", axis=0, tiled=True),
        lax.all_gather(params[1][layer_index], "shard", axis=0, tiled=True),
        lax.all_gather(params[2][layer_index], "shard", axis=0, tiled=True),
        lax.all_gather(params[3][layer_index], "shard", axis=0, tiled=True),
        lax.all_gather(params[4][layer_index], "shard", axis=0, tiled=True),
        lax.all_gather(params[5][layer_index], "shard", axis=0, tiled=True),
        lax.all_gather(params[6][layer_index], "shard", axis=0, tiled=True),
        lax.all_gather(params[7][layer_index], "shard", axis=0, tiled=True),
        lax.all_gather(params[8][layer_index], "shard", axis=1, tiled=True),
        lax.all_gather(params[9][layer_index], "shard", axis=0, tiled=True),
        lax.all_gather(params[10][layer_index], "shard", axis=0, tiled=True),
        lax.all_gather(params[11][layer_index], "shard", axis=0, tiled=True),
    )


def to_items(tensor, per_dev):
    seqs_here, row_count, feat_width = tensor.shape
    split_view = tensor.reshape(seqs_here, row_count, per_dev, feat_width // per_dev)
    return jnp.transpose(split_view, (0, 2, 1, 3)).reshape(
        seqs_here * per_dev, row_count, feat_width // per_dev
    )


def from_items(tensor, per_dev):
    item_count, row_count, head_size = tensor.shape
    split_view = tensor.reshape(item_count // per_dev, per_dev, row_count, head_size)
    return jnp.transpose(split_view, (0, 2, 1, 3)).reshape(
        item_count // per_dev, row_count, per_dev * head_size
    )


def item_forward(inputs, block_rows, score_scale):
    query_rows, key_rows, value_rows, query_segs, key_segs = inputs
    row_count, head_size = query_rows.shape

    def one_block(block_inputs):
        query_block, segs_block = block_inputs
        scores = (
            jnp.einsum("qd,kd->qk", query_block, key_rows, preferred_element_type=jnp.float32)
            * score_scale
        )
        allowed = segs_block[:, None] == key_segs[None, :]
        row_top = jnp.max(jnp.where(allowed, scores, masked_score), axis=1, keepdims=True)
        exp_scores = jnp.where(allowed, jnp.exp(scores - row_top), 0.0)
        row_total = jnp.sum(exp_scores, axis=1, keepdims=True)
        attn_probs = (exp_scores / row_total).astype(jnp.bfloat16)
        out_block = jnp.dot(attn_probs, value_rows, preferred_element_type=jnp.float32).astype(
            jnp.bfloat16
        )
        return (out_block, (row_top + jnp.log(row_total))[:, 0])

    outputs, log_totals = lax.map(
        one_block,
        (
            query_rows.reshape(row_count // block_rows, block_rows, head_size),
            query_segs.reshape(row_count // block_rows, block_rows),
        ),
    )
    return (outputs.reshape(row_count, head_size), log_totals.reshape(row_count))


def item_backward(inputs, block_rows, score_scale):
    query_rows, key_rows, value_rows, query_segs, key_segs, log_totals, grad_rows = inputs
    row_count, head_size = query_rows.shape

    def one_block(carried, block_inputs):
        key_grad, value_grad = carried
        query_block, segs_block, lse_block, grad_block = block_inputs
        scores = (
            jnp.einsum("qd,kd->qk", query_block, key_rows, preferred_element_type=jnp.float32)
            * score_scale
        )
        allowed = segs_block[:, None] == key_segs[None, :]
        attn_probs = jnp.where(allowed, jnp.exp(scores - lse_block[:, None]), 0.0)
        grad_probs = jnp.einsum(
            "qd,kd->qk", grad_block, value_rows, preferred_element_type=jnp.float32
        )
        delta_rows = jnp.sum(attn_probs * grad_probs, axis=1, keepdims=True)
        grad_scores = (attn_probs * (grad_probs - delta_rows)).astype(jnp.bfloat16)
        query_grad = (
            jnp.dot(grad_scores, key_rows, preferred_element_type=jnp.float32) * score_scale
        )
        key_grad = (
            key_grad
            + jnp.einsum("qk,qd->kd", grad_scores, query_block, preferred_element_type=jnp.float32)
            * score_scale
        )
        value_grad = value_grad + jnp.einsum(
            "qk,qd->kd",
            attn_probs.astype(jnp.bfloat16),
            grad_block,
            preferred_element_type=jnp.float32,
        )
        return ((key_grad, value_grad), query_grad)

    zero_grads = jnp.zeros(key_rows.shape, jnp.float32)
    block_count = row_count // block_rows
    (key_grad, value_grad), query_grads = lax.scan(
        one_block,
        (zero_grads, zero_grads),
        (
            query_rows.reshape(block_count, block_rows, head_size),
            query_segs.reshape(block_count, block_rows),
            log_totals.reshape(block_count, block_rows),
            grad_rows.reshape(block_count, block_rows, head_size),
        ),
    )
    return (query_grads.reshape(row_count, head_size), key_grad, value_grad)


def local(
    hidden_in,
    doc_lengths,
    ln1_gain,
    ln1_bias,
    qkv_weight,
    qv_bias,
    out_weight,
    out_bias,
    ln2_gain,
    ln2_bias,
    up_weight,
    up_bias,
    down_weight,
    down_bias,
    output_grad,
):
    params = (
        ln1_gain,
        ln1_bias,
        qkv_weight,
        qv_bias,
        out_weight,
        out_bias,
        ln2_gain,
        ln2_bias,
        up_weight,
        up_bias,
        down_weight,
        down_bias,
    )
    ctx_count = lax.axis_size("ctx")
    tp_count = lax.axis_size("tp")
    ctx_index = lax.axis_index("ctx")
    tp_index = lax.axis_index("tp")
    seqs_here, tok_count, model_width = hidden_in.shape
    row_count = ctx_count * tok_count
    key_count = tp_count * row_count
    per_dev = HEADS // ctx_count
    block_rows = min(512, row_count)
    score_scale = HEAD ** (-0.5)
    local_places = (ctx_index * tp_count + tp_index) * tok_count + jnp.arange(
        tok_count, dtype=jnp.int32
    )
    row_ids = jnp.arange(row_count, dtype=jnp.int32)
    query_places = (row_ids // tok_count * tp_count + tp_index) * tok_count + row_ids % tok_count
    key_ids = jnp.arange(key_count, dtype=jnp.int32)
    key_rest = key_ids % row_count
    key_places = (
        key_rest // tok_count * tp_count + key_ids // row_count
    ) * tok_count + key_rest % tok_count
    local_segs = segment_ids(doc_lengths, local_places)
    query_segs = jnp.repeat(segment_ids(doc_lengths, query_places), per_dev, axis=0)
    key_segs = jnp.repeat(segment_ids(doc_lengths, key_places), per_dev, axis=0)
    keep_mask = (local_segs < doc_lengths.shape[1] - 1).astype(jnp.float32)[:, :, None]
    forward_item = partial(item_forward, block_rows=block_rows, score_scale=score_scale)
    backward_item = partial(item_backward, block_rows=block_rows, score_scale=score_scale)
    kept_state = []
    current = hidden_in.astype(jnp.float32)
    for layer_index in range(LAYERS):
        layer_params = gather_layer(params, layer_index)
        (
            gain_one,
            bias_one,
            w_qkv,
            b_qv,
            w_out,
            b_out,
            gain_two,
            bias_two,
            w_up,
            b_up,
            w_down,
            b_down,
        ) = layer_params
        normed_in, normed_one, inv_one = norm_forward(
            current, gain_one.astype(jnp.float32), bias_one.astype(jnp.float32)
        )
        attn_in = normed_in.astype(jnp.bfloat16)
        projected = jnp.dot(attn_in, w_qkv, preferred_element_type=jnp.float32)
        bias_wide = b_qv.astype(jnp.float32)
        bias_full = jnp.stack(
            (
                bias_wide[:model_width],
                jnp.zeros((model_width,), jnp.float32),
                bias_wide[model_width:],
            )
        )
        heads_all = (projected.reshape(seqs_here, tok_count, 3, model_width) + bias_full).astype(
            jnp.bfloat16
        )
        exchanged = lax.all_to_all(heads_all, "ctx", split_axis=3, concat_axis=1, tiled=True)
        key_value = lax.all_gather(exchanged[:, :, 1:], "tp", axis=1, tiled=True)
        query_items = to_items(exchanged[:, :, 0], per_dev)
        key_items = to_items(key_value[:, :, 0], per_dev)
        value_items = to_items(key_value[:, :, 1], per_dev)
        attended, log_totals = lax.map(
            forward_item, (query_items, key_items, value_items, query_segs, key_segs)
        )
        context = lax.all_to_all(
            from_items(attended, per_dev), "ctx", split_axis=1, concat_axis=2, tiled=True
        )
        middle = (
            current
            + jnp.dot(context, w_out, preferred_element_type=jnp.float32)
            + b_out.astype(jnp.float32)
        )
        mlp_normed, normed_two, inv_two = norm_forward(
            middle, gain_two.astype(jnp.float32), bias_two.astype(jnp.float32)
        )
        mlp_rows = lax.all_gather(mlp_normed.astype(jnp.bfloat16), "tp", axis=1, tiled=True)
        pre_act = jnp.dot(mlp_rows, w_up, preferred_element_type=jnp.float32) + b_up.astype(
            jnp.float32
        )
        activated = jax.nn.gelu(pre_act, approximate=True).astype(jnp.bfloat16)
        down_terms = jnp.dot(activated, w_down, preferred_element_type=jnp.float32)
        mlp_out = lax.psum_scatter(
            down_terms.astype(jnp.bfloat16), "tp", scatter_dimension=1, tiled=True
        ).astype(jnp.float32) + b_down.astype(jnp.float32)
        stored_weights = None
        kept_state.append(
            (
                stored_weights,
                normed_one,
                inv_one,
                attn_in,
                exchanged,
                key_value,
                log_totals,
                context,
                normed_two,
                inv_two,
                mlp_rows,
                pre_act,
                activated,
            )
        )
        current = middle + mlp_out
    hidden_out = (current * keep_mask).astype(jnp.bfloat16)
    carry_grad = output_grad.astype(jnp.float32) * keep_mask
    layer_grads = [None] * LAYERS
    for layer_index in reversed(range(LAYERS)):
        (
            stored_weights,
            normed_one,
            inv_one,
            attn_in,
            exchanged,
            key_value,
            log_totals,
            context,
            normed_two,
            inv_two,
            mlp_rows,
            pre_act,
            activated,
        ) = kept_state[layer_index]
        layer_params = gather_layer(params, layer_index)
        (
            gain_one,
            bias_one,
            w_qkv,
            b_qv,
            w_out,
            b_out,
            gain_two,
            bias_two,
            w_up,
            b_up,
            w_down,
            b_down,
        ) = layer_params
        mlp_grad = carry_grad.astype(jnp.bfloat16)
        b_down_grad = jnp.sum(mlp_grad.astype(jnp.float32), axis=(0, 1))
        mlp_grad_rows = lax.all_gather(mlp_grad, "tp", axis=1, tiled=True)
        act_grad = jnp.einsum(
            "stm,fm->stf", mlp_grad_rows, w_down, preferred_element_type=jnp.float32
        )
        w_down_grad = jnp.einsum(
            "stf,stm->fm", activated, mlp_grad_rows, preferred_element_type=jnp.float32
        )
        gelu_pull = jax.vjp(partial(jax.nn.gelu, approximate=True), pre_act)[1]
        pre_grad = gelu_pull(act_grad)[0].astype(jnp.bfloat16)
        b_up_grad = jnp.sum(pre_grad.astype(jnp.float32), axis=(0, 1))
        w_up_grad = jnp.einsum(
            "std,stf->df", mlp_rows, pre_grad, preferred_element_type=jnp.float32
        )
        rows_grad = jnp.einsum("stf,df->std", pre_grad, w_up, preferred_element_type=jnp.float32)
        mlp_in_grad = lax.psum_scatter(
            rows_grad.astype(jnp.bfloat16), "tp", scatter_dimension=1, tiled=True
        ).astype(jnp.float32)
        middle_norm_grad, gain_two_grad, bias_two_grad = norm_backward(
            mlp_in_grad, normed_two, inv_two, gain_two.astype(jnp.float32)
        )
        middle_grad = carry_grad + middle_norm_grad
        branch_grad = middle_grad.astype(jnp.bfloat16)
        b_out_grad = jnp.sum(branch_grad.astype(jnp.float32), axis=(0, 1))
        w_out_grad = jnp.einsum(
            "std,ste->de", context, branch_grad, preferred_element_type=jnp.float32
        )
        context_grad = jnp.einsum(
            "ste,de->std", branch_grad, w_out, preferred_element_type=jnp.float32
        ).astype(jnp.bfloat16)
        context_rows_grad = lax.all_to_all(
            context_grad, "ctx", split_axis=2, concat_axis=1, tiled=True
        )
        query_items = to_items(exchanged[:, :, 0], per_dev)
        key_items = to_items(key_value[:, :, 0], per_dev)
        value_items = to_items(key_value[:, :, 1], per_dev)
        query_grads, key_grads, value_grads = lax.map(
            backward_item,
            (
                query_items,
                key_items,
                value_items,
                query_segs,
                key_segs,
                log_totals,
                to_items(context_rows_grad, per_dev),
            ),
        )
        query_grad = from_items(query_grads, per_dev).astype(jnp.bfloat16)
        pair_grad = jnp.stack(
            (from_items(key_grads, per_dev), from_items(value_grads, per_dev)), axis=2
        )
        own_pair = lax.psum_scatter(
            pair_grad.astype(jnp.bfloat16), "tp", scatter_dimension=1, tiled=True
        )
        heads_grad = jnp.concatenate((query_grad[:, :, None], own_pair), axis=2)
        qkv_grad = lax.all_to_all(
            heads_grad, "ctx", split_axis=1, concat_axis=3, tiled=True
        ).reshape(seqs_here, tok_count, 3 * model_width)
        b_qv_grad = jnp.concatenate(
            (
                jnp.sum(qkv_grad[..., :model_width].astype(jnp.float32), axis=(0, 1)),
                jnp.sum(qkv_grad[..., 2 * model_width :].astype(jnp.float32), axis=(0, 1)),
            )
        )
        w_qkv_grad = jnp.einsum(
            "std,ste->de", attn_in, qkv_grad, preferred_element_type=jnp.float32
        )
        attn_in_grad = jnp.einsum(
            "ste,de->std", qkv_grad, w_qkv, preferred_element_type=jnp.float32
        )
        input_norm_grad, gain_one_grad, bias_one_grad = norm_backward(
            attn_in_grad, normed_one, inv_one, gain_one.astype(jnp.float32)
        )
        carry_grad = middle_grad + input_norm_grad
        reduced = (
            lax.psum_scatter(
                gain_one_grad.astype(jnp.bfloat16), "shard", scatter_dimension=0, tiled=True
            ).astype(jnp.float32),
            lax.psum_scatter(
                bias_one_grad.astype(jnp.bfloat16), "shard", scatter_dimension=0, tiled=True
            ).astype(jnp.float32),
            lax.psum_scatter(
                w_qkv_grad.astype(jnp.bfloat16), "shard", scatter_dimension=0, tiled=True
            ).astype(jnp.float32),
            lax.psum_scatter(
                b_qv_grad.astype(jnp.bfloat16), "shard", scatter_dimension=0, tiled=True
            ).astype(jnp.float32),
            lax.psum_scatter(
                w_out_grad.astype(jnp.bfloat16), "shard", scatter_dimension=0, tiled=True
            ).astype(jnp.float32),
            lax.psum_scatter(
                b_out_grad.astype(jnp.bfloat16), "shard", scatter_dimension=0, tiled=True
            ).astype(jnp.float32),
            lax.psum_scatter(
                gain_two_grad.astype(jnp.bfloat16), "shard", scatter_dimension=0, tiled=True
            ).astype(jnp.float32),
            lax.psum_scatter(
                bias_two_grad.astype(jnp.bfloat16), "shard", scatter_dimension=0, tiled=True
            ).astype(jnp.float32),
            lax.psum_scatter(
                w_up_grad.astype(jnp.bfloat16), "shard", scatter_dimension=1, tiled=True
            ).astype(jnp.float32),
            lax.psum_scatter(
                b_up_grad.astype(jnp.bfloat16), "shard", scatter_dimension=0, tiled=True
            ).astype(jnp.float32),
            lax.psum_scatter(
                w_down_grad.astype(jnp.bfloat16), "shard", scatter_dimension=0, tiled=True
            ).astype(jnp.float32),
            lax.psum_scatter(
                b_down_grad.astype(jnp.bfloat16), "shard", scatter_dimension=0, tiled=True
            ).astype(jnp.float32),
        )
        attn_totals = (
            lax.psum(reduced[0].astype(jnp.bfloat16), ("ctx", "tp")).astype(jnp.float32),
            lax.psum(reduced[1].astype(jnp.bfloat16), ("ctx", "tp")).astype(jnp.float32),
            lax.psum(reduced[2].astype(jnp.bfloat16), ("ctx", "tp")).astype(jnp.float32),
            lax.psum(reduced[3].astype(jnp.bfloat16), ("ctx", "tp")).astype(jnp.float32),
            lax.psum(reduced[4].astype(jnp.bfloat16), ("ctx", "tp")).astype(jnp.float32),
            lax.psum(reduced[5].astype(jnp.bfloat16), ("ctx", "tp")).astype(jnp.float32),
            lax.psum(reduced[6].astype(jnp.bfloat16), ("ctx", "tp")).astype(jnp.float32),
            lax.psum(reduced[7].astype(jnp.bfloat16), ("ctx", "tp")).astype(jnp.float32),
            lax.psum(reduced[11].astype(jnp.bfloat16), ("ctx", "tp")).astype(jnp.float32),
        )
        mlp_totals = (
            lax.psum(reduced[8].astype(jnp.bfloat16), "ctx").astype(jnp.float32),
            lax.psum(reduced[9].astype(jnp.bfloat16), "ctx").astype(jnp.float32),
            lax.psum(reduced[10].astype(jnp.bfloat16), "ctx").astype(jnp.float32),
        )
        layer_grads[layer_index] = tuple(attn_totals[:8]) + tuple(mlp_totals) + (attn_totals[8],)
    stacked_grads = [
        jnp.stack([layer_grads[which][position] for which in range(LAYERS)])
        for position in range(12)
    ]
    return (
        hidden_out,
        carry_grad,
        stacked_grads[0],
        stacked_grads[1],
        stacked_grads[2],
        stacked_grads[3],
        stacked_grads[4],
        stacked_grads[5],
        stacked_grads[6],
        stacked_grads[7],
        stacked_grads[8],
        stacked_grads[9],
        stacked_grads[10],
        stacked_grads[11],
    )


def solution(mesh):
    placed = (
        P("shard", ("ctx", "tp"), None),
        P("shard", None),
        P(None, "shard"),
        P(None, "shard"),
        P(None, "shard", None),
        P(None, "shard"),
        P(None, "shard", None),
        P(None, "shard"),
        P(None, "shard"),
        P(None, "shard"),
        P(None, None, ("shard", "tp")),
        P(None, ("shard", "tp")),
        P(None, ("shard", "tp"), None),
        P(None, "shard"),
        P("shard", ("ctx", "tp"), None),
    )
    return jax.shard_map(
        local,
        mesh=mesh,
        in_specs=placed,
        out_specs=(
            P("shard", ("ctx", "tp"), None),
            P("shard", ("ctx", "tp"), None),
            P(None, "shard"),
            P(None, "shard"),
            P(None, "shard", None),
            P(None, "shard"),
            P(None, "shard", None),
            P(None, "shard"),
            P(None, "shard"),
            P(None, "shard"),
            P(None, None, ("shard", "tp")),
            P(None, ("shard", "tp")),
            P(None, ("shard", "tp"), None),
            P(None, "shard"),
        ),
        check_vma=False,
    )
```

profile of v0, /device:TPU:9, one launch (start us, length us, event | category | flops | bytes accessed | tf_op | source)
XLA Modules:
  0.0 1857.5 jit_solution(4526294994582346275)
XLA Ops:
  14.6 13.8 all-reduce.33
  28.4 10.6 all-gather.15
  39.0 9.9 all-gather.3
  50.2 29.9 %all-gather.51.cloned.1.call-done = bf16[1,768,2304]{2,1,0:T(8,128)(2,1)} async-done(((bf16[1,192,2304]{2,1,0:T(8,128)(2,1)}), bf16[1,768,2304]{2,1,0:T(8,128)(2,1)}) %all-gather.51.cloned.1.call-update) | async-done | bytes 3538960 | tf_op jit(solution)/shard_map/all_gather | solution.py:44
  87.2 30.8 %all_to_all.132 = bf16[2,256,3,768]{1,0,2,3:T(2,128)(2,1)S(1)} all-to-all(bf16[2,256,3,768]{1,0,2,3:T(2,128)(2,1)S(1)} %copy.278), channel_id=1, replica_groups=mesh['shard'=4,'ctx'=4,'tp'=2] {'ctx'}, dimensions={3} | all-to-all | bytes 4718592 | tf_op jit(solution)/shard_map/all_to_all | solution.py:243
  127.1 38.2 %all-gather.39.cloned.1.call-done = bf16[2,2048,2,192]{1,3,2,0:T(8,128)(2,1)} async-done(((bf16[2,1024,2,192]{1,3,2,0:T(8,128)(2,1)}), bf16[2,2048,2,192]{1,3,2,0:T(8,128)(2,1)}) %all-gather.39.cloned.1.call-update) | async-done | bytes 3145744 | tf_op jit(solution)/shard_map/all_gather | solution.py:244
  178.1 120.2 %while.107 = (s32[]{:T(128)}, bf16[6,1024,64]{1,2,0:T(8,128)(2,1)}, f32[6,1024]{1,0:T(8,128)}, bf16[6,1024,64]{2,1,0:T(8,128)(2,1)}, s32[6,1024]{1,0:T(8,128)}, ...) while((s32[]{:T(128)}, bf16[6,1024,64]{1,2,0:T(8,128)(2,1)}, ...), condition=%wide.region_10.11_spmd, body=%wide.region_5.10_spmd.sunk | while | flops 284196352 | bytes 16816516 | solution.py:248
  182.8 12.3 while.114
  202.9 12.3 while.114
  222.9 12.3 while.114
  242.9 12.3 while.114
  263.0 12.3 while.114
  283.0 12.3 while.114
  307.2 13.6 all-to-all-done.1
  332.5 10.0 all-gather.9
  342.6 14.3 all-gather.41.cloned.1.call-done
  364.2 43.3 %all-gather.57.cloned.1.call-done = bf16[1,1536,768]{2,1,0:T(8,128)(2,1)} async-done(((bf16[1,384,768]{2,1,0:T(8,128)(2,1)}), bf16[1,1536,768]{2,1,0:T(8,128)(2,1)}) %all-gather.57.cloned.1.call-update) | async-done | bytes 2359312 | tf_op jit(solution)/shard_map/all_gather | solution.py:52
  417.1 26.0 %reduce-scatter.19.cloned.1.call-done = bf16[2,256,768]{2,1,0:T(8,128)(2,1)} async-done(((bf16[2,512,768]{2,1,0:T(8,128)(2,1)}), bf16[2,256,768]{2,1,0:T(8,128)(2,1)}) %reduce-scatter.19.cloned.1.call-update) | async-done | bytes 786448 | tf_op jit(solution)/shard_map/reduce_scatter | solution.py:268
  444.8 67.4 %all-gather.59.cloned.1.call-done = bf16[1,768,2304]{2,1,0:T(8,128)(2,1)} async-done(((bf16[1,192,2304]{2,1,0:T(8,128)(2,1)}), bf16[1,768,2304]{2,1,0:T(8,128)(2,1)}) %all-gather.59.cloned.1.call-update) | async-done | bytes 3538960 | tf_op jit(solution)/shard_map/all_gather | solution.py:44
  519.3 30.8 %all_to_all.133 = bf16[2,256,3,768]{1,0,2,3:T(2,128)(2,1)S(1)} all-to-all(bf16[2,256,3,768]{1,0,2,3:T(2,128)(2,1)S(1)} %copy.292), channel_id=1, replica_groups=mesh['shard'=4,'ctx'=4,'tp'=2] {'ctx'}, dimensions={3} | all-to-all | bytes 4718592 | tf_op jit(solution)/shard_map/all_to_all | solution.py:243
  554.9 42.6 %all-gather.43.cloned.1.call-done = bf16[2,2048,2,192]{1,3,2,0:T(8,128)(2,1)} async-done(((bf16[2,1024,2,192]{1,3,2,0:T(8,128)(2,1)}), bf16[2,2048,2,192]{1,3,2,0:T(8,128)(2,1)}) %all-gather.43.cloned.1.call-update) | async-done | bytes 3145744 | tf_op jit(solution)/shard_map/all_gather | solution.py:244
  610.4 120.1 %while.109 = (s32[]{:T(128)}, bf16[6,1024,64]{1,2,0:T(8,128)(2,1)}, f32[6,1024]{1,0:T(8,128)}, bf16[6,1024,64]{2,1,0:T(8,128)(2,1)}, s32[6,1024]{1,0:T(8,128)}, ...) while((s32[]{:T(128)}, bf16[6,1024,64]{1,2,0:T(8,128)(2,1)}, ...), condition=%wide.region_21.22_spmd, body=%wide.region_16.21_spmd.sunk | while | flops 284196352 | bytes 16816516 | solution.py:248
  615.1 12.3 while.115
  635.1 12.3 while.115
  655.1 12.3 while.115
  675.2 12.3 while.115
  695.2 12.3 while.115
  715.2 12.2 while.115
  739.4 13.7 all-to-all-done.3
  765.2 9.8 all-gather.21
  775.0 14.2 all-gather.45.cloned.1.call-done
  796.7 22.0 %all-gather.47.cloned.1.call-done = bf16[2,512,768]{2,1,0:T(8,128)(2,1)} async-done(((bf16[2,256,768]{2,1,0:T(8,128)(2,1)}), bf16[2,512,768]{2,1,0:T(8,128)(2,1)}) %all-gather.47.cloned.1.call-update) | async-done | bytes 1572880 | tf_op jit(solution)/shard_map/all_gather | solution.py:326
  818.7 50.2 %all-gather.65.cloned.1.call-done = bf16[1,1536,768]{2,1,0:T(8,128)(2,1)} async-done(((bf16[1,384,768]{2,1,0:T(8,128)(2,1)}), bf16[1,1536,768]{2,1,0:T(8,128)(2,1)}) %all-gather.65.cloned.1.call-update) | async-done | bytes 2359312 | tf_op jit(solution)/shard_map/all_gather | solution.py:52
  868.9 9.6 fusion.199
  883.8 26.9 %reduce-scatter.23.cloned.1.call-done = bf16[2,256,768]{2,1,0:T(8,128)(2,1)} async-done(((bf16[2,512,768]{2,1,0:T(8,128)(2,1)}), bf16[2,256,768]{2,1,0:T(8,128)(2,1)}) %reduce-scatter.23.cloned.1.call-update) | async-done | bytes 786448 | tf_op jit(solution)/shard_map/reduce_scatter | solution.py:340
  922.9 10.5 all-to-all-done.4
  938.8 101.0 %while.111 = (s32[]{:T(128)}, bf16[6,1024,64]{2,1,0:T(8,128)(2,1)}, bf16[6,2048,64]{1,2,0:T(8,128)(2,1)}, bf16[6,2048,64]{1,2,0:T(8,128)(2,1)}, bf16[6,1024,64]{...) while((s32[]{:T(128)}, bf16[6,1024,64]{2,1,0:T(8,128)(2,1)}, ...), condition=%wide.region_33.34_spmd, body=%wide.region_29.33_spmd.sunk | while | flops 682262016 | bytes 40444368 | solution.py:361
  944.6 9.3 while.116
  961.4 9.3 while.116
  978.3 9.2 while.116
  995.1 9.3 while.116
  1012.0 9.3 while.116
  1028.8 9.2 while.116
  1045.8 40.7 %reduce-scatter.25.cloned.1.call-done = bf16[2,1024,2,192]{1,3,0,2:T(8,128)(2,1)} async-done(((bf16[2,2048,2,192]{1,3,0,2:T(8,128)(2,1)}), bf16[2,1024,2,192]{1,3,0,2:T(8,128)(2,1)}) %reduce-scatter.25.cloned.1.call-update) | async-done | bytes 1572880 | tf_op jit(solution)/shard_map/reduce_scatter | solution.py:377
  1096.9 39.9 %all_to_all.134 = bf16[2,1024,3,192]{3,0,2,1:T(2,128)(2,1)} all-to-all(bf16[2,1024,3,192]{3,0,2,1:T(2,128)(2,1)S(1)} %copy.312), channel_id=1, replica_groups=mesh['shard'=4,'ctx'=4,'tp'=2] {'ctx'}, dimensions={1} | all-to-all | bytes 4718592 | tf_op jit(solution)/shard_map/all_to_all | solution.py:381
  1154.4 26.3 %all-gather.49.cloned.1.call-done = bf16[2,512,768]{2,1,0:T(8,128)(2,1)} async-done(((bf16[2,256,768]{2,1,0:T(8,128)(2,1)}), bf16[2,512,768]{2,1,0:T(8,128)(2,1)}) %all-gather.49.cloned.1.call-update) | async-done | bytes 1572880 | tf_op jit(solution)/shard_map/all_gather | solution.py:326
  1180.8 9.6 fusion.200
  1256.8 101.1 %while.113 = (s32[]{:T(128)}, bf16[6,1024,64]{2,1,0:T(8,128)(2,1)}, bf16[6,2048,64]{1,2,0:T(8,128)(2,1)}, bf16[6,2048,64]{1,2,0:T(8,128)(2,1)}, bf16[6,1024,64]{...) while((s32[]{:T(128)}, bf16[6,1024,64]{2,1,0:T(8,128)(2,1)}, ...), condition=%wide.region_44.45_spmd, body=%wide.region_40.44_spmd.sunk | while | flops 682262016 | bytes 40444368 | solution.py:361
  1262.7 9.3 while.117
  1279.5 9.2 while.117
  1296.3 9.2 while.117
  1313.2 9.2 while.117
  1330.0 9.2 while.117
  1346.8 9.3 while.117
  1370.2 49.9 %reduce-scatter.39.cloned.1.call-done = bf16[384,768]{1,0:T(8,128)(2,1)} async-done(((bf16[1536,768]{1,0:T(8,128)(2,1)}), bf16[384,768]{1,0:T(8,128)(2,1)}) %reduce-scatter.39.cloned.1.call-update) | async-done | bytes 589840 | tf_op jit(solution)/shard_map/reduce_scatter | solution.py:431
  1435.2 32.4 %reduce-scatter.29.cloned.1.call-done = bf16[2,1024,2,192]{1,3,0,2:T(8,128)(2,1)} async-done(((bf16[2,2048,2,192]{1,3,0,2:T(8,128)(2,1)}), bf16[2,1024,2,192]{1,3,0,2:T(8,128)(2,1)}) %reduce-scatter.29.cloned.1.call-update) | async-done | bytes 1572880 | tf_op jit(solution)/shard_map/reduce_scatter | solution.py:377
  1479.5 64.9 %all_to_all.135 = bf16[2,1024,3,192]{3,0,2,1:T(2,128)(2,1)} all-to-all(bf16[2,1024,3,192]{3,0,2,1:T(2,128)(2,1)} %copy.324), channel_id=1, replica_groups=mesh['shard'=4,'ctx'=4,'tp'=2] {'ctx'}, dimensions={1} | all-to-all | bytes 4718592 | tf_op jit(solution)/shard_map/all_to_all | solution.py:381
  1583.4 15.7 all-reduce.32
  1600.5 25.9 %all-reduce.28 = (bf16[1,192]{1,0:T(2,128)(2,1)S(1)}, bf16[1,192]{1,0:T(2,128)(2,1)S(1)}, bf16[1,192]{1,0:T(2,128)(2,1)S(1)}, bf16[1,192]{1,0:T(2,128)(2,1)S(1)}...) all-reduce(bf16[1,192]{1,0:T(2,128)(2,1)S(1)} %stack.203, ...), channel_id=1, replica_groups=mesh['shard'=4,'ctx'=4,'tp'=2] {'ctx','tp'}, use_global_device_ids=true, to_apply=%region_53.54 | all-reduce | flops 3072 | bytes 12288 | tf_op jit(solution)/shard_map/psum | solution.py:439
  1636.0 15.1 reduce-scatter.33.cloned.1.call-done
  1651.1 29.6 %reduce-scatter.35.cloned.1.call-done = bf16[192,768]{1,0:T(8,128)(2,1)} async-done(((bf16[768,768]{1,0:T(8,128)(2,1)}), bf16[192,768]{1,0:T(8,128)(2,1)}) %reduce-scatter.35.cloned.1.call-update) | async-done | bytes 294928 | tf_op jit(solution)/shard_map/reduce_scatter | solution.py:413
  1680.7 69.4 %reduce-scatter.31.cloned.1.call-done = bf16[192,2304]{1,0:T(8,128)(2,1)} async-done(((bf16[768,2304]{1,0:T(8,128)(2,1)}), bf16[192,2304]{1,0:T(8,128)(2,1)}) %reduce-scatter.31.cloned.1.call-update) | async-done | bytes 884752 | tf_op jit(solution)/shard_map/reduce_scatter | solution.py:407
  1750.7 28.9 %reduce-scatter.21.cloned.1.call-done = bf16[2,256,768]{2,1,0:T(8,128)(2,1)} async-done(((bf16[2,512,768]{2,1,0:T(8,128)(2,1)}), bf16[2,256,768]{2,1,0:T(8,128)(2,1)}) %reduce-scatter.21.cloned.1.call-update) | async-done | bytes 786448 | tf_op jit(solution)/shard_map/reduce_scatter | solution.py:268
  1783.7 62.2 %all-reduce.37.cloned.1.call-done = (bf16[1,192,2304]{2,1,0:T(8,128)(2,1)}, bf16[1,192,2304]{2,1,0:T(8,128)(2,1)}, bf16[1,192,768]{2,1,0:T(8,128)(2,1)}, bf16[1,192,768]{2,1,0:T(8,128)(2,1)}) async-done(((bf16[1,192,2304]{2,1,0:T(8,128)(2,1)}, bf16[1,192,2304]{2,1,0:T(8,128)(2,1)}, bf16[1,192,768]{2,1,0:T(8,128)(2,1)}, bf16[1,192,768]{2,1,0:T(8,128)(2,1)}), (bf16[1,192,2304]{2,1,0:T(8,128)(2,1)}, ...) | async-done | bytes 2359312 | tf_op jit(solution)/shard_map/psum | solution.py:441
  (1251 shorter events, 787.2 us)
Async XLA Ops:
  7.3 21.2 %copy-start.75 = (bf16[2,384]{1,0:T(2,128)(2,1)S(1)}, bf16[2,384]{1,0:T(2,128)(2,1)}, u32[]{:S(2)}) copy-start(bf16[2,384]{1,0:T(2,128)(2,1)} %param.36) | copy-start | bytes 4612
  7.3 41.6 %copy-start.16 = (bf16[2,256,768]{2,1,0:T(8,128)(2,1)S(1)}, bf16[2,256,768]{2,1,0:T(8,128)(2,1)}, u32[]{:S(2)}) copy-start(bf16[2,256,768]{2,1,0:T(8,128)(2,1)} %param.31) | copy-start | bytes 2359300
  7.3 72.8 %all-gather.51.cloned.1.call-start = ((), (), s32[]{:S(2)}) async-start(), calls=%async_computation.40 | async-start | bytes 4423680 | tf_op jit(solution)/shard_map/all_gather | solution.py:44
  10.2 155.2 %all-gather.39.cloned.1.call-start = ((), (), s32[]{:S(2)}) async-start(), calls=%async_computation.22 | async-start | bytes 4718592 | tf_op jit(solution)/shard_map/all_gather | solution.py:244
  28.3 56.0 %copy-start.78 = (f32[768]{0:T(1024)}, f32[768]{0:T(1024)S(1)}, u32[]{:S(2)}) copy-start(f32[768]{0:T(1024)S(1)} %convert_element_type.445) | copy-start | bytes 9220
  28.3 56.0 %copy-start.52 = (f32[768]{0:T(1024)}, f32[768]{0:T(1024)S(1)}, u32[]{:S(2)}) copy-start(f32[768]{0:T(1024)S(1)} %convert_element_type.444) | copy-start | bytes 9220
  49.1 35.3 %copy-start.47 = (f32[2,256]{1,0:T(2,128)}, f32[2,256]{1,0:T(2,128)S(1)}, u32[]{:S(2)}) copy-start(f32[2,256]{1,0:T(2,128)S(1)} %broadcast_multiply_fusion.11) | copy-start | bytes 6148
  49.5 34.9 %copy-start.57 = (f32[2,256]{1,0:T(2,128)}, f32[2,256]{1,0:T(2,128)S(1)}, u32[]{:S(2)}) copy-start(f32[2,256]{1,0:T(2,128)S(1)} %add_rsqrt_fusion.3) | copy-start | bytes 6148
  119.9 206.0 %all-gather.53.cloned.1.call-start = ((), (), s32[]{:S(2)}) async-start(), calls=%async_computation.41 | async-start | bytes 1474560 | tf_op jit(solution)/shard_map/all_gather | solution.py:46
  121.9 220.7 %all-gather.55.cloned.1.call-start = ((), (), s32[]{:S(2)}) async-start(), calls=%async_computation.42 | async-start | bytes 2949120 | tf_op jit(solution)/shard_map/all_gather | solution.py:50
  298.3 26.3 %copy-start.4 = (bf16[6,2048,64]{2,1,0:T(8,128)(2,1)}, bf16[6,2048,64]{2,1,0:T(8,128)(2,1)S(1)}, u32[]{:S(2)}) copy-start(bf16[6,2048,64]{2,1,0:T(8,128)(2,1)S(1)} %get-tuple-element.1933) | copy-start | bytes 4718596
  298.3 8.9 copy-start.98
  298.3 8.9 copy-start.97
  298.3 8.9 copy-start.96
  302.3 18.6 all-to-all-start.1
  307.2 49.7 %all-gather.41.cloned.1.call-start = ((), (), s32[]{:S(2)}) async-start(), calls=%async_computation.23 | async-start | bytes 2359296 | tf_op jit(solution)/shard_map/all_gather | solution.py:262
  307.2 21.8 %copy-start.36 = (f32[768]{0:T(1024)}, f32[768]{0:T(1024)S(1)}, u32[]{:S(2)}) copy-start(f32[768]{0:T(1024)S(1)} %convert_element_type.447) | copy-start | bytes 9220
  328.6 114.4 %copy-start = (f32[2,256,768]{2,1,0:T(8,128)}, f32[2,256,768]{2,1,0:T(8,128)S(1)}, u32[]{:S(2)}) copy-start(f32[2,256,768]{2,1,0:T(8,128)S(1)} %get-tuple-element.982) | copy-start | bytes 4718596
  330.2 77.3 %all-gather.57.cloned.1.call-start = ((), (), s32[]{:S(2)}) async-start(), calls=%async_computation.43 | async-start | bytes 2949120 | tf_op jit(solution)/shard_map/all_gather | solution.py:52
  331.9 111.2 %reduce-scatter.19.cloned.1.call-start = ((), (), s32[]{:S(2)}) async-start(), calls=%async_computation.24 | async-start | bytes 2359296 | tf_op jit(solution)/shard_map/reduce_scatter | solution.py:268
  342.6 65.0 %copy-start.68 = (f32[1536]{0:T(1024)}, f32[1536]{0:T(1024)S(1)}, u32[]{:S(2)}) copy-start(f32[1536]{0:T(1024)S(1)} %convert_reduce_fusion.2) | copy-start | bytes 18436
  416.2 96.0 %all-gather.59.cloned.1.call-start = ((), (), s32[]{:S(2)}) async-start(), calls=%async_computation.44 | async-start | bytes 4423680 | tf_op jit(solution)/shard_map/all_gather | solution.py:44
  416.9 180.6 %all-gather.43.cloned.1.call-start = ((), (), s32[]{:S(2)}) async-start(), calls=%async_computation.25 | async-start | bytes 4718592 | tf_op jit(solution)/shard_map/all_gather | solution.py:244
  417.0 95.2 %copy-start.54 = (f32[768]{0:T(1024)}, f32[768]{0:T(1024)S(1)}, u32[]{:S(2)}) copy-start(f32[768]{0:T(1024)S(1)} %convert_element_type.450) | copy-start | bytes 9220
  417.0 95.2 %copy-start.80 = (f32[768]{0:T(1024)}, f32[768]{0:T(1024)S(1)}, u32[]{:S(2)}) copy-start(f32[768]{0:T(1024)S(1)} %convert_element_type.451) | copy-start | bytes 9220
  444.5 72.0 %copy-start.6 = (f32[2,256,768]{2,1,0:T(8,128)}, f32[2,256,768]{2,1,0:T(8,128)S(1)}, u32[]{:S(2)}) copy-start(f32[2,256,768]{2,1,0:T(8,128)S(1)} %get-tuple-element.938) | copy-start | bytes 4718596
  444.5 72.0 %copy-start.49 = (f32[2,256]{1,0:T(2,128)}, f32[2,256]{1,0:T(2,128)S(1)}, u32[]{:S(2)}) copy-start(f32[2,256]{1,0:T(2,128)S(1)} %broadcast_multiply_fusion.9) | copy-start | bytes 6148
  444.8 71.6 %copy-start.59 = (f32[2,256]{1,0:T(2,128)}, f32[2,256]{1,0:T(2,128)S(1)}, u32[]{:S(2)}) copy-start(f32[2,256]{1,0:T(2,128)S(1)} %add_rsqrt_fusion.1) | copy-start | bytes 6148
  444.8 71.6 %copy-start.40 = (f32[3,768]{1,0:T(4,128)S(1)}, f32[3,768]{1,0:T(4,128)}, u32[]{:S(2)}) copy-start(f32[3,768]{1,0:T(4,128)} %get-tuple-element.979) | copy-start | bytes 27652
  552.0 206.0 %all-gather.61.cloned.1.call-start = ((), (), s32[]{:S(2)}) async-start(), calls=%async_computation.45 | async-start | bytes 1474560 | tf_op jit(solution)/shard_map/all_gather | solution.py:46
  552.6 222.4 %all-gather.63.cloned.1.call-start = ((), (), s32[]{:S(2)}) async-start(), calls=%async_computation.46 | async-start | bytes 2949120 | tf_op jit(solution)/shard_map/all_gather | solution.py:50
  730.5 26.3 %copy-start.5 = (bf16[6,2048,64]{2,1,0:T(8,128)(2,1)}, bf16[6,2048,64]{2,1,0:T(8,128)(2,1)S(1)}, u32[]{:S(2)}) copy-start(bf16[6,2048,64]{2,1,0:T(8,128)(2,1)S(1)} %get-tuple-element.1935) | copy-start | bytes 4718596
  734.4 18.6 %all-to-all-start.3 = ((bf16[2,1024,192]{2,0,1:T(2,128)(2,1)}), bf16[2,1024,192]{2,0,1:T(2,128)(2,1)}, u32[]{:S(2)}, u32[]{:S(2)}) async-start(bf16[2,1024,192]{2,0,1:T(2,128)(2,1)} %copy.299), calls=%async_computation.4 | async-start | bytes 2097152 | tf_op jit(solution)/shard_map/all_to_all | solution.py:251
  739.3 49.9 %all-gather.45.cloned.1.call-start = ((), (), s32[]{:S(2)}) async-start(), calls=%async_computation.26 | async-start | bytes 2359296 | tf_op jit(solution)/shard_map/all_gather | solution.py:262
  761.0 152.3 %copy-start.2 = (f32[2,256,768]{2,1,0:T(8,128)}, f32[2,256,768]{2,1,0:T(8,128)S(1)}, u32[]{:S(2)}) copy-start(f32[2,256,768]{2,1,0:T(8,128)S(1)} %get-tuple-element.984) | copy-start | bytes 4718596
  762.6 56.1 %all-gather.47.cloned.1.call-start = ((), (), s32[]{:S(2)}) async-start(), calls=%async_computation.28 | async-start | bytes 2359296 | tf_op jit(solution)/shard_map/all_gather | solution.py:326
  762.8 150.5 %copy-start.43 = (f32[2,256]{1,0:T(2,128)}, f32[2,256]{1,0:T(2,128)S(1)}, u32[]{:S(2)}) copy-start(f32[2,256]{1,0:T(2,128)S(1)} %compare_convert_fusion.3) | copy-start | bytes 6148
  764.5 104.4 %all-gather.65.cloned.1.call-start = ((), (), s32[]{:S(2)}) async-start(), calls=%async_computation.47 | async-start | bytes 2949120 | tf_op jit(solution)/shard_map/all_gather | solution.py:52
  765.1 145.6 %reduce-scatter.23.cloned.1.call-start = ((), (), s32[]{:S(2)}) async-start(), calls=%async_computation.29 | async-start | bytes 2359296 | tf_op jit(solution)/shard_map/reduce_scatter | solution.py:340
  775.0 93.9 %copy-start.70 = (f32[1536]{0:T(1024)}, f32[1536]{0:T(1024)S(1)}, u32[]{:S(2)}) copy-start(f32[1536]{0:T(1024)S(1)} %convert_reduce_fusion.1) | copy-start | bytes 18436
  868.9 11.2 copy-start.106
  918.5 14.9 all-to-all-start.4
  922.7 163.8 %reduce-scatter.25.cloned.1.call-start = ((), (), s32[]{:S(2)}) async-start(), calls=%async_computation.30 | async-start | bytes 4718592 | tf_op jit(solution)/shard_map/reduce_scatter | solution.py:377
  1043.7 137.0 %all-gather.49.cloned.1.call-start = ((), (), s32[]{:S(2)}) async-start(), calls=%async_computation.31 | async-start | bytes 2359296 | tf_op jit(solution)/shard_map/all_gather | solution.py:326
  1151.8 28.9 %copy-start.69 = (f32[1536]{0:T(1024)S(1)}, f32[1536]{0:T(1024)}, u32[]{:S(2)}) copy-start(f32[1536]{0:T(1024)} %copy-done.68) | copy-start | bytes 18436
  1153.9 73.2 %reduce-scatter.27.cloned.1.call-start = ((), (), s32[]{:S(2)}) async-start(), calls=%async_computation.32 | async-start | bytes 2359296 | tf_op jit(solution)/shard_map/reduce_scatter | solution.py:340
  1180.7 11.3 copy-start.105
  1195.8 166.1 %reduce-scatter.45.cloned.1.call-start = ((), (), s32[]{:S(2)}) async-start(), calls=%async_computation.49 | async-start | bytes 2949120
  1206.0 158.2 %reduce-scatter.43.cloned.1.call-start = ((), (), s32[]{:S(2)}) async-start(), calls=%async_computation.48 | async-start | bytes 2949120
  1217.5 152.7 %reduce-scatter.41.cloned.1.call-start = ((), (), s32[]{:S(2)}) async-start(), calls=%async_computation.39 | async-start | bytes 2949120 | tf_op jit(solution)/shard_map/reduce_scatter | solution.py:431
  1236.2 15.3 all-to-all-start.6
  1240.6 179.5 %reduce-scatter.39.cloned.1.call-start = ((), (), s32[]{:S(2)}) async-start(), calls=%async_computation.38 | async-start | bytes 2949120 | tf_op jit(solution)/shard_map/reduce_scatter | solution.py:431
  1248.8 218.7 %reduce-scatter.29.cloned.1.call-start = ((), (), s32[]{:S(2)}) async-start(), calls=%async_computation.33 | async-start | bytes 4718592 | tf_op jit(solution)/shard_map/reduce_scatter | solution.py:377
  1361.8 211.9 %all-reduce.39.cloned.1.call-start = ((), (), s32[]{:S(2)}) async-start(), calls=%async_computation.51 | async-start | bytes 4718592 | tf_op jit(solution)/shard_map/psum | solution.py:450
  1361.9 58.3 %copy-start.13 = (f32[2,256,768]{2,1,0:T(8,128)S(1)}, f32[2,256,768]{2,1,0:T(8,128)}, u32[]{:S(2)}) copy-start(f32[2,256,768]{2,1,0:T(8,128)} %copy-done.11) | copy-start | bytes 4718596
  1420.1 215.9 %reduce-scatter.37.cloned.1.call-start = ((), (), s32[]{:S(2)}) async-start(), calls=%async_computation.37 | async-start | bytes 1474560 | tf_op jit(solution)/shard_map/reduce_scatter | solution.py:413
  1423.2 227.9 %reduce-scatter.33.cloned.1.call-start = ((), (), s32[]{:S(2)}) async-start(), calls=%async_computation.35 | async-start | bytes 4423680 | tf_op jit(solution)/shard_map/reduce_scatter | solution.py:407
  1429.1 251.6 %reduce-scatter.35.cloned.1.call-start = ((), (), s32[]{:S(2)}) async-start(), calls=%async_computation.36 | async-start | bytes 1474560 | tf_op jit(solution)/shard_map/reduce_scatter | solution.py:413
  1433.7 316.4 %reduce-scatter.31.cloned.1.call-start = ((), (), s32[]{:S(2)}) async-start(), calls=%async_computation.34 | async-start | bytes 4423680 | tf_op jit(solution)/shard_map/reduce_scatter | solution.py:407
  1561.2 10.6 copy-start.103
  1561.2 218.4 %reduce-scatter.21.cloned.1.call-start = ((), (), s32[]{:S(2)}) async-start(), calls=%async_computation.27 | async-start | bytes 2359296 | tf_op jit(solution)/shard_map/reduce_scatter | solution.py:268
  1570.5 275.4 %all-reduce.37.cloned.1.call-start = ((), (), s32[]{:S(2)}) async-start(), calls=%async_computation.50 | async-start | bytes 4718592 | tf_op jit(solution)/shard_map/psum | solution.py:441
  1583.3 196.3 %copy-start.3 = (f32[2,256,768]{2,1,0:T(8,128)S(1)}, f32[2,256,768]{2,1,0:T(8,128)}, u32[]{:S(2)}) copy-start(f32[2,256,768]{2,1,0:T(8,128)} %copy-done.2) | copy-start | bytes 4718596
  1583.3 196.3 %copy-start.44 = (f32[2,256]{1,0:T(2,128)S(1)}, f32[2,256]{1,0:T(2,128)}, u32[]{:S(2)}) copy-start(f32[2,256]{1,0:T(2,128)} %copy-done.43) | copy-start | bytes 6148
  (107 other events, 279.8 us)
Sparse Core Ops, SparseCore 0:
  10.3 69.7 all-gather.50
  120.0 45.2 all-gather.38
  166.9 29.7 all-gather.52
  198.1 48.7 all-gather.54
  330.3 26.4 all-gather.40
  358.9 48.6 all-gather.56
  416.3 26.6 reduce-scatter.18
  444.7 67.4 all-gather.58
  552.1 45.3 all-gather.42
  599.0 29.7 all-gather.60
  630.5 48.7 all-gather.62
  762.7 26.4 all-gather.44
  791.4 27.1 all-gather.46
  820.2 48.6 all-gather.64
  883.9 26.7 reduce-scatter.22
  1043.9 42.6 reduce-scatter.24
  1154.0 26.6 all-gather.48
  1195.9 26.0 reduce-scatter.26
  1224.3 45.6 reduce-scatter.44
  1272.2 47.5 reduce-scatter.42
  1322.6 47.5 reduce-scatter.40
  1372.5 47.5 reduce-scatter.38
  1422.3 45.2 reduce-scatter.28
  1470.2 80.0 all-reduce.38
  1553.2 26.9 reduce-scatter.36
  1583.1 67.9 reduce-scatter.32
  1653.4 27.2 reduce-scatter.34
  1683.2 66.9 reduce-scatter.30
  1753.0 26.5 reduce-scatter.20
  1783.0 62.8 all-reduce.36
where the time goes:
time: 1880 us; the launch traced here: 1860 us
  waiting for transfers between devices  777 us (41%)
  local copies, waits for them, and re-layouts  367 us (20%)
  matrix products  314 us (17%)
  blocking collectives  268 us (14%)
  other arithmetic  89.7 us (5%)
  starting transfers between devices  20.8 us (1%)
    all_to_all x2, blocking collectives, local(): lax.all_to_all(heads_grad, 'ctx', split_axis=1, concat_axis=3, tiled=True)  105 us
    all_gather x2, waiting for transfers between devices, gather_layer(): lax.all_gather(params[2][layer_index], 'shard', axis=0, tiled=True)  97.3 us
    all_gather x2, waiting for transfers between devices, gather_layer(): lax.all_gather(params[10][layer_index], 'shard', axis=0, tiled=True)  93.5 us
    reduce_scatter x2, waiting for transfers between devices, local(): lax.psum_scatter(w_qkv_grad.astype(jnp.bfloat16), 'shard', scatter_dimens...  84.5 us
    dot_general x48, matrix products, one_block(): jnp.einsum('qd,kd->qk', query_block, key_rows, preferred_element_type=jnp...  81 us
    all_gather x2, waiting for transfers between devices, local(): key_value = lax.all_gather(exchanged[:, :, 1:], 'tp', axis=1, tiled=True)  80.9 us
    reduce_scatter x2, waiting for transfers between devices, local(): lax.psum_scatter(pair_grad.astype(jnp.bfloat16), 'tp', scatter_dimension=...  73.1 us
    dynamic_slice x96, local copies, waits for them, and re-layouts, local(): lax.map(forward_item, (query_items, key_items, value_items, query_segs, k...  64.7 us
  transfers between devices with their start and end apart: 34, of which 25 were waited for; matrix products, arithmetic and copies ran while one was open for 30% of the time, Pallas kernels for 0%

commit v1 on v0

v1 whole, which is shorter than its diff:
```python
import jax
import jax.numpy as jnp
from jax import lax
from jax.experimental import pallas as pl
from jax.experimental.pallas import tpu as pltpu
from jax.sharding import Mesh
from jax.sharding import PartitionSpec as P

HEADS = 12
HEAD = 64
LAYERS = 2
BLK = 256
NEG = -1e30
EPS = 1e-06
F32 = jnp.float32
BF16 = jnp.bfloat16


def dot(left, right, dims=((1,), (0,))):
    return lax.dot_general(left, right, (dims, ((), ())), preferred_element_type=F32)


def swap(value, axis):
    return lax.ppermute(value, axis, ((0, 1), (1, 0)))


def block_place(block, dev, half):
    return (((block // 2) ^ dev) * 2) + ((block % 2) ^ half)


def doc_range(first, ends, length):
    last = first + BLK - 1
    start, stop = jnp.int32(0), jnp.int32(length)
    for end in ends:
        start = jnp.maximum(start, jnp.where(first >= end, end, 0))
        stop = jnp.minimum(stop, jnp.where(last < end, end, length))
    return start // BLK, (stop + BLK - 1) // BLK


def seg_of(places, ends):
    seg = (places >= ends[0]).astype(jnp.int32)
    for end in ends[1:]:
        seg = seg + (places >= end).astype(jnp.int32)
    return seg


def three_heads(pair, single):
    blank = jnp.zeros_like(single)
    return (
        jnp.concatenate((pair[:HEAD], blank), axis=0),
        jnp.concatenate((blank, pair[HEAD:]), axis=0),
        jnp.concatenate((single, blank), axis=0),
    )


def attention_forward_kernel(info, qkv_ref, out_ref, lse_ref, v01_t, v2_t):
    step = pl.program_id(0)
    length = qkv_ref.shape[0]
    ends = (info[0], info[1], info[2])
    dev, half = info[3], info[4]

    @pl.when(step == 0)
    def _():
        v01_t[...] = qkv_ref[:, 256:384].T
        v2_t[...] = qkv_ref[:, 128:256].T

    mine = pl.ds(pl.multiple_of(step * BLK, BLK), BLK)
    first = block_place(step, dev, half) * BLK
    seg_q = seg_of(first + lax.broadcasted_iota(jnp.int32, (1, BLK), 1), ends)
    queries = three_heads(qkv_ref[mine, 384:512].T, qkv_ref[mine, 512:576].T)
    low, high = doc_range(first, ends, length)

    def body(block, carry):
        rows = pl.ds(pl.multiple_of(block_place(block, dev, half) * BLK, BLK), BLK)
        places = block * BLK + lax.broadcasted_iota(jnp.int32, (BLK, 1), 0)
        allowed = seg_of(places, ends) == seg_q
        k01 = qkv_ref[rows, 0:128]
        k2 = qkv_ref[rows, 128:256]
        values = (v01_t[0:HEAD, rows], v01_t[HEAD:128, rows], v2_t[HEAD:128, rows])
        result = []
        for head in range(3):
            top, total, acc = carry[head]
            scores = dot(k2 if head == 2 else k01, queries[head])
            scores = jnp.where(allowed, scores, NEG)
            new_top = jnp.maximum(top, jnp.max(scores, axis=0, keepdims=True))
            exps = jnp.exp(scores - new_top)
            shrink = jnp.exp(top - new_top)
            total = total * shrink + jnp.sum(exps, axis=0, keepdims=True)
            acc = acc * shrink + dot(values[head], exps.astype(BF16))
            result.append((new_top, total, acc))
        return tuple(result)

    start = tuple(
        (
            jnp.full((1, BLK), NEG, F32),
            jnp.zeros((1, BLK), F32),
            jnp.zeros((HEAD, BLK), F32),
        )
        for _ in range(3)
    )
    final = lax.fori_loop(low, high, body, start)
    for head in range(3):
        top, total, acc = final[head]
        out_ref[0, head * HEAD : (head + 1) * HEAD, :] = (acc / total).astype(BF16)
        lse_ref[head : head + 1, :] = top + jnp.log(total)
    lse_ref[3:8, :] = jnp.zeros((5, BLK), F32)


def attention_forward(info, qkv):
    length = qkv.shape[0]
    return pl.pallas_call(
        attention_forward_kernel,
        name="attention_forward",
        grid_spec=pltpu.PrefetchScalarGridSpec(
            num_scalar_prefetch=1,
            grid=(length // BLK,),
            in_specs=[pl.BlockSpec(qkv.shape, lambda i, info: (0, 0))],
            out_specs=[
                pl.BlockSpec((1, 192, BLK), lambda i, info: (i // 2, 0, i % 2)),
                pl.BlockSpec((8, BLK), lambda i, info: (0, i)),
            ],
            scratch_shapes=[
                pltpu.VMEM((128, length), BF16),
                pltpu.VMEM((128, length), BF16),
            ],
        ),
        out_shape=(
            jax.ShapeDtypeStruct((length // 512, 192, 512), BF16),
            jax.ShapeDtypeStruct((8, length), F32),
        ),
        compiler_params=pltpu.CompilerParams(vmem_limit_bytes=48 << 20),
        cost_estimate=pl.CostEstimate(
            flops=4 * 3 * HEAD * length * 1024, transcendentals=3 * length * 1024, bytes_accessed=6 << 20
        ),
    )(info, qkv)


def attention_backward_kernel(info, qkv_ref, out_ref, grad_ref, lse_ref, du_ref, q01_t, q2_t, delta, dq_t):
    step = pl.program_id(0)
    length = qkv_ref.shape[0]
    ends = (info[0], info[1], info[2])
    dev, half = info[3], info[4]

    @pl.when(step == 0)
    def _():
        q01_t[...] = qkv_ref[:, 384:512].T
        q2_t[...] = qkv_ref[:, 512:576].T
        dq_t[...] = jnp.zeros_like(dq_t)
        for part in range(length // 512):
            both = out_ref[part].astype(F32) * grad_ref[part].astype(F32)
            for head in range(3):
                delta[head : head + 1, part * 512 : (part + 1) * 512] = jnp.sum(
                    both[head * HEAD : (head + 1) * HEAD], axis=0, keepdims=True
                )

    mine = pl.ds(pl.multiple_of(step * BLK, BLK), BLK)
    first = block_place(step, dev, half) * BLK
    seg_k = seg_of(first + lax.broadcasted_iota(jnp.int32, (BLK, 1), 0), ends)
    k01 = qkv_ref[mine, 0:128]
    k2v2 = qkv_ref[mine, 128:256]
    v01 = qkv_ref[mine, 256:384]
    k01_t = k01.T
    k2_t = k2v2.T[:HEAD]
    keys_t = (k01_t[:HEAD], k01_t[HEAD:], k2_t)
    low, high = doc_range(first, ends, length)

    def body(block, carry):
        dk01, dk2v2, dv01 = carry
        place = block_place(block, dev, half)
        cols = pl.ds(pl.multiple_of(place * BLK, BLK), BLK)
        part_cols = pl.ds(pl.multiple_of((place % 2) * BLK, BLK), BLK)
        places = block * BLK + lax.broadcasted_iota(jnp.int32, (1, BLK), 1)
        allowed = seg_k == seg_of(places, ends)
        queries = three_heads(q01_t[:, cols], q2_t[:, cols])
        grads = grad_ref[place // 2, :, part_cols]
        blank = jnp.zeros((HEAD, BLK), BF16)
        dos = (
            jnp.concatenate((grads[:HEAD], blank), axis=0),
            jnp.concatenate((blank, grads[HEAD:128]), axis=0),
            jnp.concatenate((blank, grads[128:192]), axis=0),
        )
        for head in range(3):
            scores = dot(k2v2 if head == 2 else k01, queries[head])
            probs = jnp.where(allowed, jnp.exp(scores - lse_ref[head : head + 1, cols]), 0.0)
            grad_probs = dot(k2v2 if head == 2 else v01, dos[head])
            grad_scores = (probs * (grad_probs - delta[head : head + 1, cols])).astype(BF16)
            probs = probs.astype(BF16)
            more_k = dot(grad_scores, queries[head], ((1,), (1,)))
            more_v = dot(probs, dos[head], ((1,), (1,)))
            if head == 2:
                dk2v2 = dk2v2 + more_k + more_v
            else:
                dk01 = dk01 + more_k
                dv01 = dv01 + more_v
            rows = slice(head * HEAD, (head + 1) * HEAD)
            dq_t[rows, cols] = dq_t[rows, cols] + dot(keys_t[head], grad_scores)
        return dk01, dk2v2, dv01

    zero = jnp.zeros((BLK, 128), F32)
    dk01, dk2v2, dv01 = lax.fori_loop(low, high, body, (zero, zero, zero))
    du_ref[mine, 0:128] = dk01.astype(BF16)
    du_ref[mine, 128:256] = dk2v2.astype(BF16)
    du_ref[mine, 256:384] = dv01.astype(BF16)

    @pl.when(step == pl.num_programs(0) - 1)
    def _():
        scale = HEAD**-0.5
        du_ref[:, 384:512] = (dq_t[0:128, :] * scale).T.astype(BF16)
        du_ref[:, 512:576] = (dq_t[128:192, :] * scale).T.astype(BF16)


def attention_backward(info, qkv, out, grad, lse):
    length = qkv.shape[0]

    def whole(shape):
        return pl.BlockSpec(shape, lambda i, info: (0,) * len(shape))

    return pl.pallas_call(
        attention_backward_kernel,
        name="attention_backward",
        grid_spec=pltpu.PrefetchScalarGridSpec(
            num_scalar_prefetch=1,
            grid=(length // BLK,),
            in_specs=[whole(qkv.shape), whole(out.shape), whole(grad.shape), whole(lse.shape)],
            out_specs=whole(qkv.shape),
            scratch_shapes=[
                pltpu.VMEM((128, length), BF16),
                pltpu.VMEM((64, length), BF16),
                pltpu.VMEM((8, length), F32),
                pltpu.VMEM((192, length), F32),
            ],
        ),
        out_shape=jax.ShapeDtypeStruct(qkv.shape, BF16),
        compiler_params=pltpu.CompilerParams(vmem_limit_bytes=48 << 20),
        cost_estimate=pl.CostEstimate(
            flops=10 * 3 * HEAD * length * 1024, transcendentals=3 * length * 1024, bytes_accessed=10 << 20
        ),
    )(info, qkv, out, grad, lse)


def norm_forward(values, gain, bias):
    centred = values - jnp.mean(values, axis=-1, keepdims=True)
    inv_std = lax.rsqrt(jnp.mean(centred * centred, axis=-1, keepdims=True) + EPS)
    normed = centred * inv_std
    return normed * gain + bias, normed, inv_std


def norm_backward(grad_out, normed, inv_std, gain):
    grad_normed = grad_out * gain
    grad_in = inv_std * (
        grad_normed
        - jnp.mean(grad_normed, axis=-1, keepdims=True)
        - normed * jnp.mean(grad_normed * normed, axis=-1, keepdims=True)
    )
    return grad_in, jnp.sum(grad_out * normed, axis=0), jnp.sum(grad_out, axis=0)


GELU_A = (2.0 / 3.141592653589793) ** 0.5
GELU_B = 0.044715


def gelu(t):
    return 0.5 * t * (1.0 + jnp.tanh(GELU_A * (t + GELU_B * t * t * t)))


def gelu_slope(t):
    tanh = jnp.tanh(GELU_A * (t + GELU_B * t * t * t))
    return 0.5 * (1.0 + tanh) + 0.5 * t * (1.0 - tanh * tanh) * GELU_A * (1.0 + 3.0 * GELU_B * t * t)


def local(
    hidden_in,
    doc_lengths,
    ln1_gain,
    ln1_bias,
    qkv_weight,
    qv_bias,
    out_weight,
    out_bias,
    ln2_gain,
    ln2_bias,
    up_weight,
    up_bias,
    down_weight,
    down_bias,
    output_grad,
):
    shards = lax.axis_size("shard")
    ix, ic, iy = lax.axis_index("cx"), lax.axis_index("core"), lax.axis_index("tp")
    dev = ix * 2 + ic
    seqs, toks, width = hidden_in.shape
    rows = ln1_gain.shape[1]
    hid = up_bias.shape[1] // 2
    loc = width // 4
    hidden_all = up_bias.shape[1] * shards * 2

    def to_sequence(tokens):
        own = lax.dynamic_index_in_dim(tokens, iy, 0, keepdims=False)
        other = lax.dynamic_index_in_dim(tokens, 1 - iy, 0, keepdims=False)
        return jnp.concatenate((own, swap(other, "tp")), axis=0).astype(F32)

    def from_sequence(tokens):
        own, other = tokens[:toks], swap(tokens[toks:], "tp")
        return jnp.where(iy == 0, jnp.stack((own, other)), jnp.stack((other, own)))

    lengths = lax.dynamic_index_in_dim(doc_lengths, iy, 0, keepdims=False)
    end0 = lengths[0]
    end1 = end0 + lengths[1]
    end2 = end1 + lengths[2]
    info = jnp.stack((end0, end1, end2, dev, iy, dev, dev, dev)).astype(jnp.int32)
    row_ids = jnp.arange(2 * toks, dtype=jnp.int32)
    places = dev * (2 * toks) + ((row_ids // toks) ^ iy) * toks + row_ids % toks
    keep = (places < end2).astype(F32)[:, None]

    small = jnp.concatenate(
        [p.reshape(-1) for p in (ln1_gain, ln1_bias, out_bias, ln2_gain, ln2_bias, down_bias, qv_bias, up_bias)]
    ).reshape(1, -1)
    small_all = lax.all_gather(small, ("shard", "tp"), axis=0, tiled=True).astype(F32)
    small_all = small_all.reshape(shards, 2, -1)
    at = 0
    smalls = []
    for _ in range(6):
        piece = small_all[:, 0, at : at + LAYERS * rows].reshape(shards, LAYERS, rows)
        smalls.append(jnp.transpose(piece, (1, 0, 2)).reshape(LAYERS, width))
        at += LAYERS * rows
    piece = small_all[:, 0, at : at + LAYERS * 2 * rows].reshape(shards, LAYERS, 2 * rows)
    qv_full = jnp.transpose(piece, (1, 0, 2)).reshape(LAYERS, 2 * width)
    at += LAYERS * 2 * rows
    up_bias_all = small_all[:, :, at:].reshape(shards, 2, LAYERS, 2, hid)

    def columns(array, start):
        return lax.dynamic_slice_in_dim(array, start, loc, 1)

    def gather_attention(layer):
        weight = qkv_weight[layer]
        q, k, v = (columns(weight, which * width + loc * dev) for which in range(3))
        out = columns(out_weight[layer], loc * dev)
        piece = jnp.concatenate((k[:, :128], k[:, 128:], v[:, 128:], v[:, :128], q, out), axis=1)
        gathered = lax.all_gather(piece, "shard", axis=0, tiled=True)
        qkv_w = gathered[:, : 3 * loc]
        own = gathered[:, 3 * loc :]
        core = swap(own, "core")
        far = swap(own, "cx")
        diag = swap(far, "core")
        full = jnp.zeros((width, width), BF16)
        for rel, part in enumerate((own, core, far, diag)):
            full = lax.dynamic_update_slice_in_dim(full, part, loc * (dev ^ rel), 1)
        return qkv_w, full

    def gather_hidden(piece):
        own = lax.all_gather(piece, "shard", axis=0, tiled=True)
        other = swap(own, "tp")
        return (own, other, swap(own, "core"), swap(other, "core"))

    def bias_parts(layer):
        parts = []
        for rc in range(2):
            for ry in range(2):
                part = lax.dynamic_index_in_dim(up_bias_all[:, :, layer], iy ^ ry, 1, keepdims=False)
                part = lax.dynamic_index_in_dim(part, ic ^ rc, 1, keepdims=False)
                parts.append(part.reshape(-1))
        return parts

    weights = []
    for layer in range(LAYERS):
        w_qkv, w_out = gather_attention(layer)
        up_piece = lax.dynamic_slice_in_dim(up_weight[layer], ic * hid, hid, 1).T
        down_piece = lax.dynamic_slice_in_dim(down_weight[layer], ic * hid, hid, 0)
        weights.append((w_qkv, w_out, gather_hidden(up_piece), gather_hidden(down_piece)))

    qkv_scale = jnp.concatenate((jnp.ones((2 * loc,), F32), jnp.full((loc,), HEAD**-0.5, F32)))

    current = to_sequence(hidden_in)
    grad = to_sequence(output_grad) * keep
    saved = []
    for layer in range(LAYERS):
        gain_one, bias_one, bias_out, gain_two, bias_two, bias_down = (s[layer] for s in smalls)
        w_qkv, w_out, w_up, w_down = weights[layer]
        normed, normed_one, inv_one = norm_forward(current, gain_one, bias_one)
        own = normed.astype(BF16)
        far = swap(own, "cx")
        attn_in = jnp.concatenate((own, swap(own, "core"), far, swap(far, "core")), axis=0)
        q_bias = lax.dynamic_slice_in_dim(qv_full[layer], loc * dev, loc, 0)
        v_bias = lax.dynamic_slice_in_dim(qv_full[layer], width + loc * dev, loc, 0)
        zeros = jnp.zeros((128,), F32)
        bias = jnp.concatenate((zeros, zeros[:64], v_bias[128:], v_bias[:128], q_bias))
        qkv = ((dot(attn_in, w_qkv) + bias) * qkv_scale).astype(BF16)
        attended, lse = attention_forward(info, qkv)
        from_core = swap(attended[1], "core")
        from_far = lax.ppermute(attended[2], "cx", ((0, 1), (1, 0)))
        from_diag = lax.ppermute(attended[3], ("cx", "core"), ((0, 3), (1, 2), (2, 1), (3, 0)))
        context = jnp.zeros((width, 2 * toks), BF16)
        for rel, part in enumerate((attended[0], from_core, from_far, from_diag)):
            context = lax.dynamic_update_slice_in_dim(context, part, loc * (dev ^ rel), 0)
        middle = current + dot(context, w_out, ((0,), (0,))) + bias_out
        mlp_in, normed_two, inv_two = norm_forward(middle, gain_two, bias_two)
        mlp_in = mlp_in.astype(BF16)
        pre, act = [], []
        result = middle + bias_down
        for part, part_bias in enumerate(bias_parts(layer)):
            pre_act = dot(mlp_in, w_up[part], ((1,), (1,))) + part_bias
            pre.append(pre_act.astype(BF16))
            act.append(gelu(pre_act).astype(BF16))
        for part in range(4):
            result = result + dot(act[part], w_down[part])
        saved.append((normed_one, inv_one, attn_in, qkv, attended, lse, context, normed_two, inv_two, mlp_in, pre, act))
        current = result
    hidden_out = from_sequence((current * keep).astype(BF16))

    def reduce_hidden(parts):
        send = swap(jnp.concatenate((parts[2], parts[3]), axis=0).astype(BF16), "core").astype(F32)
        own = parts[0] + send[: parts[0].shape[0]]
        other = parts[1] + send[parts[0].shape[0] :]
        own = own + swap(other.astype(BF16), "tp").astype(F32)
        return lax.psum_scatter(own.astype(BF16), "shard", scatter_dimension=0, tiled=True)

    small_grads = [None] * LAYERS
    qkv_grads = [None] * LAYERS
    out_grads = [None] * LAYERS
    up_grads = [None] * LAYERS
    down_grads = [None] * LAYERS
    quarter = rows // 4
    for layer in reversed(range(LAYERS)):
        normed_one, inv_one, attn_in, qkv, attended, lse, context, normed_two, inv_two, mlp_in, pre, act = saved[layer]
        gain_one, _, _, gain_two, _, _ = (s[layer] for s in smalls)
        w_qkv, w_out, w_up, w_down = weights[layer]
        mlp_grad = grad.astype(BF16)
        b_down_grad = jnp.sum(mlp_grad.astype(F32), axis=0)
        pre_grads = []
        mlp_in_grad = None
        for part in range(4):
            act_grad = dot(mlp_grad, w_down[part], ((1,), (1,)))
            pre_grad = (act_grad * gelu_slope(pre[part].astype(F32))).astype(BF16)
            pre_grads.append(pre_grad)
            term = dot(pre_grad, w_up[part])
            mlp_in_grad = term if mlp_in_grad is None else mlp_in_grad + term
        norm_grad, gain_two_grad, bias_two_grad = norm_backward(mlp_in_grad, normed_two, inv_two, gain_two)
        middle_grad = grad + norm_grad
        branch_grad = middle_grad.astype(BF16)
        b_out_grad = jnp.sum(branch_grad.astype(F32), axis=0)
        context_grad = dot(w_out, branch_grad, ((1,), (1,))).astype(BF16)
        pieces = [lax.dynamic_slice_in_dim(context_grad, loc * (dev ^ rel), loc, 0) for rel in range(4)]
        attn_grad = jnp.stack(
            (
                pieces[0],
                swap(pieces[1], "core"),
                swap(pieces[2], "cx"),
                lax.ppermute(pieces[3], ("cx", "core"), ((0, 3), (1, 2), (2, 1), (3, 0))),
            )
        )
        down_parts = [dot(act[part], mlp_grad, ((0,), (0,))) for part in range(4)]
        up_parts = [dot(pre_grads[part], mlp_in, ((0,), (0,))) for part in range(4)]
        b_up_parts = [jnp.sum(pre_grads[part].astype(F32), axis=0).reshape(shards, hid) for part in range(4)]
        w_out_grad = dot(context, branch_grad).reshape(shards, 2, 2, quarter, width)
        bundle = []
        for rc in range(2):
            for ry in range(2):
                piece = lax.dynamic_index_in_dim(w_out_grad, ic ^ rc, 1, keepdims=False)
                piece = lax.dynamic_index_in_dim(piece, iy ^ ry, 1, keepdims=False)
                up_part = up_parts[rc * 2 + ry].reshape(shards, hid, width)
                bundle.append(jnp.concatenate((up_part, piece), axis=1).reshape(-1, width))
        down_grads[layer] = reduce_hidden(down_parts)
        up_grads[layer] = reduce_hidden(bundle)
        du = attention_backward(info, qkv, attended, attn_grad, lse)
        w_qkv_grad = dot(attn_in, du, ((0,), (0,))).astype(BF16)
        qkv_grads[layer] = lax.psum_scatter(w_qkv_grad, "shard", scatter_dimension=0, tiled=True)
        attn_in_grad = dot(du, w_qkv, ((1,), (1,)))
        n = 2 * toks
        send = swap(jnp.concatenate((attn_in_grad[n : 2 * n], attn_in_grad[3 * n :]), axis=0).astype(BF16), "core")
        far = (attn_in_grad[2 * n : 3 * n] + send[n:].astype(F32)).astype(BF16)
        normed_grad = attn_in_grad[:n] + send[:n].astype(F32) + swap(far, "cx").astype(F32)
        du_sum = jnp.sum(du.astype(F32), axis=0)
        norm_grad, gain_one_grad, bias_one_grad = norm_backward(normed_grad, normed_one, inv_one, gain_one)
        grad = middle_grad + norm_grad
        v_sum = jnp.concatenate((du_sum[256:384], du_sum[192:256]))
        qv_grad = jnp.zeros((2 * width,), F32)
        qv_grad = lax.dynamic_update_slice_in_dim(qv_grad, du_sum[384:], loc * dev, 0)
        qv_grad = lax.dynamic_update_slice_in_dim(qv_grad, v_sum, width + loc * dev, 0)
        b_up_grad = jnp.zeros((shards, 2, 2, hid), F32)
        for rc in range(2):
            for ry in range(2):
                piece = b_up_parts[rc * 2 + ry][:, None, None]
                b_up_grad = lax.dynamic_update_slice(b_up_grad, piece, (0, iy ^ ry, ic ^ rc, 0))
        small_grads[layer] = jnp.concatenate(
            (
                gain_one_grad,
                bias_one_grad,
                b_out_grad,
                gain_two_grad,
                bias_two_grad,
                b_down_grad,
                qv_grad,
                b_up_grad.reshape(-1),
            )
        )

    hidden_grad = from_sequence(grad.astype(BF16)).astype(F32)

    total = jnp.stack(small_grads).reshape(-1, 128)
    for axis in ("core", "cx", "tp"):
        total = total + swap(total, axis)
    if shards <= 4:
        shifted = [
            lax.ppermute(total, "shard", [(i, (i + by) % shards) for i in range(shards)]) for by in range(1, shards)
        ]
        for term in shifted:
            total = total + term
    else:
        total = lax.psum(total, "shard")
    total = total.reshape(LAYERS, -1)
    shard = lax.axis_index("shard")
    outs_small = [
        lax.dynamic_slice_in_dim(total[:, which * width : (which + 1) * width], shard * rows, rows, 1)
        for which in range(6)
    ]
    qv_out = lax.dynamic_slice_in_dim(total[:, 6 * width : 8 * width], shard * 2 * rows, 2 * rows, 1)
    up_bias_out = lax.dynamic_slice_in_dim(
        total[:, 8 * width : 8 * width + hidden_all], (shard * 2 + iy) * 2 * hid, 2 * hid, 1
    )

    def both_cores(value):
        other = swap(value, "core")
        return jnp.where(ic == 0, jnp.stack((value, other)), jnp.stack((other, value)))

    w_qkv_out, w_out_out, w_up_out, w_down_out = [], [], [], []
    for layer in range(LAYERS):
        own = qkv_grads[layer]
        own = (own.astype(F32) + swap(own, "tp").astype(F32)).astype(BF16)
        core = swap(own, "core")
        far = swap(own, "cx")
        diag = swap(far, "core")
        full = jnp.zeros((rows, 3, 4, loc), F32)
        for rel, part in enumerate((own, core, far, diag)):
            part = part.astype(F32)
            k = part[:, :192]
            v = jnp.concatenate((part[:, 256:384], part[:, 192:256]), axis=1)
            q = part[:, 384:]
            full = lax.dynamic_update_slice(full, jnp.stack((q, k, v), axis=1)[:, :, None], (0, 0, dev ^ rel, 0))
        w_qkv_out.append(full.reshape(rows, 3 * width))
        own = down_grads[layer]
        own = (own.astype(F32) + swap(own, "cx").astype(F32)).astype(BF16)
        w_down_out.append(both_cores(own).reshape(2 * hid, width).astype(F32))
        own = up_grads[layer]
        own = (own.astype(F32) + swap(own, "cx").astype(F32)).astype(BF16)
        both = both_cores(own)
        w_up_out.append(both[:, :hid].reshape(2 * hid, width).astype(F32).T)
        mine = both[:, hid:]
        other = swap(mine, "tp")
        out_rows = jnp.where(iy == 0, jnp.stack((mine, other), axis=1), jnp.stack((other, mine), axis=1))
        w_out_out.append(out_rows.reshape(rows, width).astype(F32))

    return (
        hidden_out,
        hidden_grad,
        outs_small[0],
        outs_small[1],
        jnp.stack(w_qkv_out),
        qv_out,
        jnp.stack(w_out_out),
        outs_small[2],
        outs_small[3],
        outs_small[4],
        jnp.stack(w_up_out),
        up_bias_out,
        jnp.stack(w_down_out),
        outs_small[5],
    )


def solution(mesh):
    names = tuple(mesh.axis_names)
    shape = dict(mesh.shape)
    split = Mesh(
        mesh.devices.reshape(shape[names[0]], 2, shape[names[1]] // 2, shape[names[2]]),
        ("shard", "cx", "core", "tp"),
    )
    tokens = P("shard", ("cx", "core", "tp"), None)
    vector = P(None, "shard")
    attn = P(None, "shard", None)
    placed = (
        tokens,
        P("shard", None),
        vector,
        vector,
        attn,
        vector,
        attn,
        vector,
        vector,
        vector,
        P(None, None, ("shard", "tp")),
        P(None, ("shard", "tp")),
        P(None, ("shard", "tp"), None),
        vector,
        tokens,
    )
    return jax.shard_map(
        local,
        mesh=split,
        in_specs=placed,
        out_specs=(
            tokens,
            tokens,
            vector,
            vector,
            attn,
            vector,
            attn,
            vector,
            vector,
            vector,
            P(None, None, ("shard", "tp")),
            P(None, ("shard", "tp")),
            P(None, ("shard", "tp"), None),
            vector,
        ),
        check_vma=False,
    )
```

time: 1880 us -> 794 us (0.42)
  waiting for transfers between devices: 777 us -> 193 us
  blocking collectives: 268 us -> 23.4 us
  local copies, waits for them, and re-layouts: 367 us -> 130 us
  matrix products: 314 us -> 126 us
  Pallas kernels: 0 us -> 116 us
  starting transfers between devices: 20.8 us -> 85.8 us
    all_gather x14 -> x6, waiting for transfers between devices: 349 us -> 1.15 us  [the longest x4 1.15 us: gather_hidden(): own = lax.all_gather(piece, 'shard', axis=0, tiled=True)]
    reduce_scatter x12 -> x6, waiting for transfers between devices: 323 us -> 41.6 us  [the longest x2 41.6 us: local(): lax.psum_scatter(w_qkv_grad, 'shard', scatter_dimension=0, tiled=True)]
    dot_general x192 -> x60, matrix products: 314 us -> 126 us  [dot(): lax.dot_general(left, right, (dims, ((), ())), preferred_element_type=F32)]
    all_to_all x4 -> x0, blocking collectives: 166 us -> none  [the longest x2 105 us: local(): lax.all_to_all(heads_grad, 'ctx', split_axis=1, concat_axis=3, tiled=True)]
    ppermute x0 -> x76, waiting for transfers between devices: none -> 150 us  [the longest x67 133 us: swap(): return lax.ppermute(value, axis, ((0, 1), (1, 0)))]
    pallas_call x0 -> x4, Pallas kernels: none -> 116 us  [the longest x2 60.4 us: attention_backward(): pl.pallas_call(attention_backward_kernel, name='attention_backward', grid...]
    ppermute x0 -> x76, starting transfers between devices: none -> 84.4 us  [the longest x67 60.4 us: swap(): return lax.ppermute(value, axis, ((0, 1), (1, 0)))]
    dynamic_slice x180 -> x19, local copies, waits for them, and re-layouts: 74.7 us -> 11 us  [the longest x6 3.91 us: local(): lax.dynamic_slice_in_dim(total[:, which * width:(which + 1) * width], sha...]
  transfers between devices with their start and end apart: 34 -> 88, of which waited for: 25 -> 25; matrix products, arithmetic and copies ran while one was open for 30% -> 39% of each run, Pallas kernels for 0% -> 15%
where the time goes in v1:
time: 794 us; the launch traced here: 785 us
  waiting for transfers between devices  193 us (24%)
  local copies, waits for them, and re-layouts  130 us (16%)
  matrix products  126 us (16%)
  Pallas kernels  116 us (15%)
  other arithmetic  90.6 us (11%)
  starting transfers between devices  85.8 us (11%)
  blocking collectives  23.4 us (3%)
  between operations  19.4 us (2%)
    ppermute x67, waiting for transfers between devices, swap(): return lax.ppermute(value, axis, ((0, 1), (1, 0)))  133 us
    dot_general x60, matrix products, dot(): lax.dot_general(left, right, (dims, ((), ())), preferred_element_type=F32)  126 us
    pallas_call x2, Pallas kernels, attention_backward(): pl.pallas_call(attention_backward_kernel, name='attention_backward', grid...  60.4 us
    ppermute x67, starting transfers between devices, swap(): return lax.ppermute(value, axis, ((0, 1), (1, 0)))  60.4 us
    pallas_call x2, Pallas kernels, attention_forward(): pl.pallas_call(attention_forward_kernel, name='attention_forward', grid_s...  55.6 us
    reduce_scatter x2, waiting for transfers between devices, local(): lax.psum_scatter(w_qkv_grad, 'shard', scatter_dimension=0, tiled=True)  41.6 us
    dynamic_update_slice x8, local copies, waits for them, and re-layouts, gather_attention(): full = lax.dynamic_update_slice_in_dim(full, part, loc * (dev ^ rel), 1)  37.6 us
    all_gather x1, blocking collectives, local(): lax.all_gather(small, ('shard', 'tp'), axis=0, tiled=True).astype(F32)  23.4 us
  transfers between devices with their start and end apart: 88, of which 25 were waited for; matrix products, arithmetic and copies ran while one was open for 39% of the time, Pallas kernels for 15%

profile of v1, /device:TPU:9, one launch (start us, length us, event | category | flops | bytes accessed | tf_op | source)
XLA Modules:
  0.0 784.6 jit_solution(2689615335490962586)
XLA Ops:
  21.7 23.4 %all-gather.3 = bf16[8,1,3840]{2,1,0:T(2,128)(2,1)S(1)} all-gather(bf16[1,1,3840]{2,1,0:T(2,128)(2,1)S(1)} %reshape.515), channel_id=2, replica_groups=mesh['shard'=4,'cx'=2,'core'=2,'tp'=2] {'shard','tp'}, dimensions={0}, use_global_device_ids=true | all-gather | bytes 69120 | tf_op jit(solution)/shard_map/all_gather | solution.py:318
  49.9 6.2 collective-permute-start.1
  56.1 4.0 collective-permute-done.2
  60.2 7.0 collective-permute-start.3
  77.7 5.0 dynamic_update_slice.112
  82.7 4.2 multiply_convert_fusion.1.qkv_ref
  86.9 27.6 %attention_forward.2 = (bf16[4,192,512]{2,1,0:T(8,128)(2,1)S(1)}, f32[8,2048]{1,0:T(8,128)S(1)}) custom-call(s32[8]{0:T(128)S(1)} %stack.302.info, bf16[2048,576]{1,0:T(8,128)(2,1)S(1)} %multiply_convert_fusion.1.qkv_ref), custom_call_target="tpu_custom_call" | custom-call | flops 1610612736 | bytes 6291456 | tf_op jit(solution)/shard_map/attention_forward/pallas_call | solution.py:111
  117.1 4.6 dynamic_update_slice.113
  122.1 4.6 dynamic_update_slice.114
  130.4 4.5 dynamic_update_slice.115
  140.1 2.9 fusion.192
  143.4 11.4 %collective-permute-done.10 = bf16[768,768]{1,0:T(8,128)(2,1)} collective-permute-done((bf16[768,768]{1,0:T(8,128)(2,1)}, bf16[768,768]{1,0:T(8,128)(2,1)}, u32[]{:S(2)}, u32[]{:S(2)}) %collective-permute-start.10) | collective-permute-done | bytes 1179680 | tf_op jit(solution)/shard_map/ppermute | solution.py:24
  160.6 2.9 fusion.223
  172.1 18.0 %collective-permute-done.17 = bf16[512,768]{1,0:T(8,128)(2,1)} collective-permute-done((bf16[512,768]{1,0:T(8,128)(2,1)}, bf16[512,768]{1,0:T(8,128)(2,1)}, u32[]{:S(2)}, u32[]{:S(2)}) %collective-permute-start.17) | collective-permute-done | bytes 786464 | tf_op jit(solution)/shard_map/ppermute | solution.py:24
  193.7 9.1 %collective-permute-done.23 = bf16[768,192]{1,0:T(8,128)(2,1)} collective-permute-done((bf16[768,192]{1,0:T(8,128)(2,1)S(1)}, bf16[768,192]{1,0:T(8,128)(2,1)}, u32[]{:S(2)}, u32[]{:S(2)}) %collective-permute-start.23) | collective-permute-done | bytes 294944 | tf_op jit(solution)/shard_map/ppermute | solution.py:24
  211.2 5.1 dynamic_update_slice.120
  217.5 4.6 dynamic_update_slice.121
  222.2 4.6 dynamic_update_slice.122
  227.0 4.6 dynamic_update_slice.123
  231.6 4.5 multiply_convert_fusion.qkv_ref
  236.0 28.0 %attention_forward.3 = (bf16[4,192,512]{2,1,0:T(8,128)(2,1)S(1)}, f32[8,2048]{1,0:T(8,128)S(1)}) custom-call(s32[8]{0:T(128)S(1)} %stack.302.info, bf16[2048,576]{1,0:T(8,128)(2,1)S(1)} %multiply_convert_fusion.qkv_ref), custom_call_target="tpu_custom_call" | custom-call | flops 1610612736 | bytes 6291456 | tf_op jit(solution)/shard_map/attention_forward/pallas_call | solution.py:111
  267.8 3.7 collective-permute-done.20
  289.6 2.9 convert_reduce_fusion.5
  295.7 2.8 convert_reduce_fusion.3
  325.1 3.1 convolution_convert_fusion
  328.3 3.3 convolution_convert_fusion.1
  335.0 30.2 %attention_backward.2 = bf16[2048,576]{1,0:T(8,128)(2,1)S(1)} custom-call(s32[8]{0:T(128)S(1)} %stack.302.info, bf16[2048,576]{1,0:T(8,128)(2,1)} %copy-done.5, bf16[4,192,512]{2,1,0:T(8,128)(2,1)S(1)} %get-tuple-element.19.out_ref, bf16[4,192,512]{2,1,0:T(8,128)(2,1)S(1)} %pad_maximum_fusion.19.grad_ref, f32[8,2048]{1,0:T(8,128)S(1)} %get-tuple-element.20.lse_ref), custom_call_target="tpu_custom_call" | custom-call | flops 4026531840 | bytes 10485760 | tf_op jit(solution)/shard_map/attention_backward/pallas_call | solution.py:218
  365.3 4.5 fusion.258
  371.4 5.5 convolution_convert_fusion.8
  376.9 3.4 pad_maximum_fusion.10
  389.8 41.6 %reduce-scatter.9.cloned.1.call-done = bf16[192,576]{1,0:T(8,128)(2,1)} async-done(((bf16[768,576]{1,0:T(8,128)(2,1)}), bf16[192,576]{1,0:T(8,128)(2,1)}) %reduce-scatter.9.cloned.1.call-update) | async-done | bytes 221200 | tf_op jit(solution)/shard_map/reduce_scatter | solution.py:466
  435.7 2.8 collective-permute-done.54
  446.3 3.4 fusion.6
  451.0 6.9 collective-permute-done.56
  468.8 2.8 convert_reduce_fusion.10
  471.7 2.8 convert_reduce_fusion.12
  497.2 2.9 collective-permute-start.40
  506.6 3.8 collective-permute-done.39
  512.1 30.2 %attention_backward.3 = bf16[2048,576]{1,0:T(8,128)(2,1)S(1)} custom-call(s32[8]{0:T(128)S(1)} %stack.302.info, bf16[2048,576]{1,0:T(8,128)(2,1)} %copy-done.4, bf16[4,192,512]{2,1,0:T(8,128)(2,1)S(1)} %copy-done.3, bf16[4,192,512]{2,1,0:T(8,128)(2,1)S(1)} %pad_maximum_fusion.20.grad_ref, f32[8,2048]{1,0:T(8,128)S(1)} %get-tuple-element.21.lse_ref), custom_call_target="tpu_custom_call" | custom-call | flops 4026531840 | bytes 10485760 | tf_op jit(solution)/shard_map/attention_backward/pallas_call | solution.py:218
  542.4 5.2 convolution_convert_fusion.9
  547.7 3.9 pad_maximum_fusion.3
  553.5 4.5 fusion.259
  559.9 3.6 fusion.8
  575.5 4.6 copy.64
  580.1 3.7 stack_reshape.7
  584.6 2.8 fusion.140
  588.2 17.2 %collective-permute-done.64 = bf16[960,768]{1,0:T(8,128)(2,1)} collective-permute-done((bf16[960,768]{1,0:T(8,128)(2,1)}, bf16[960,768]{1,0:T(8,128)(2,1)}, u32[]{:S(2)}, u32[]{:S(2)}) %collective-permute-start.64) | collective-permute-done | bytes 1474592 | tf_op jit(solution)/shard_map/ppermute | solution.py:24
  605.5 3.9 fusion.2
  616.0 3.3 collective-permute-done.52
  619.8 2.9 copy.62
  623.6 3.9 fusion.25
  633.7 9.3 %collective-permute-done.69 = bf16[768,768]{1,0:T(8,128)(2,1)S(1)} collective-permute-done((bf16[768,768]{1,0:T(8,128)(2,1)S(1)}, bf16[768,768]{1,0:T(8,128)(2,1)S(1)}, u32[]{:S(2)}, u32[]{:S(2)}) %collective-permute-start.69) | collective-permute-done | bytes 1179680 | tf_op jit(solution)/shard_map/ppermute | solution.py:24
  652.6 22.0 %collective-permute-done.59 = bf16[960,768]{1,0:T(8,128)(2,1)} collective-permute-done((bf16[960,768]{1,0:T(8,128)(2,1)}, bf16[960,768]{1,0:T(8,128)(2,1)}, u32[]{:S(2)}, u32[]{:S(2)}) %collective-permute-start.59) | collective-permute-done | bytes 1474592 | tf_op jit(solution)/shard_map/ppermute | solution.py:24
  674.6 4.0 fusion.5
  680.7 15.7 %dynamic_update_slice.139 = f32[192,3,4,192]{3,2,1,0:T(4,128)S(1)} dynamic-update-slice(f32[192,3,4,192]{3,2,1,0:T(4,128)S(1)} %copy-done.26, f32[192,3,1,192]{3,2,1,0:T(1,128)S(1)} %copy.63, s32[]{:T(128)} %constant.575.clone.1, s32[]{:T(128)} %constant.575.clone.1, s32[]{:T(128)S(6)} %select_n.303, s32[]{:T(128)} %constant.575.clone.1) | dynamic-update-slice | bytes 884740 | tf_op jit(solution)/shard_map/dynamic_update_slice | solution.py:538
  696.4 2.8 stack_reshape.6
  699.2 13.5 %collective-permute-start.49 = (f32[144,128]{1,0:T(8,128)S(1)}, f32[144,128]{1,0:T(8,128)S(1)}, u32[]{:S(2)}, u32[]{:S(2)}) collective-permute-start(f32[144,128]{1,0:T(8,128)S(1)} %add.972), channel_id=1, source_target_pairs={{0,24},{8,0},{16,8},{24,16},{1,25},{9,1},{17,9},{25,17},{2,26},{10... | collective-permute-start | bytes 221192 | tf_op jit(solution)/shard_map/ppermute | solution.py:504
  714.2 4.0 pad_maximum_fusion
  720.9 5.6 collective-permute-done.47
  732.6 4.6 collective-permute-done.74
  738.2 3.1 collective-permute-start.75
  741.3 3.8 collective-permute-done.65
  753.3 6.7 collective-permute-done.70
  761.3 6.6 collective-permute-done.60
  (804 shorter events, 260.4 us)
Async XLA Ops:
  7.2 64.6 %all-gather.11.cloned.1.call-start = ((), (), s32[]{:S(2)}) async-start(), calls=%async_computation.6 | async-start | bytes 1474560 | tf_op jit(solution)/shard_map/all_gather | solution.py:339
  11.7 63.8 %all-gather.19.cloned.1.call-start = ((), (), s32[]{:S(2)}) async-start(), calls=%async_computation.16 | async-start | bytes 1474560 | tf_op jit(solution)/shard_map/all_gather | solution.py:351
  12.6 114.5 %all-gather.13.cloned.1.call-start = ((), (), s32[]{:S(2)}) async-start(), calls=%async_computation.7 | async-start | bytes 1474560 | tf_op jit(solution)/shard_map/all_gather | solution.py:351
  15.3 175.4 %all-gather.15.cloned.1.call-start = ((), (), s32[]{:S(2)}) async-start(), calls=%async_computation.8 | async-start | bytes 1474560 | tf_op jit(solution)/shard_map/all_gather | solution.py:339
  17.4 198.8 %all-gather.21.cloned.1.call-start = ((), (), s32[]{:S(2)}) async-start(), calls=%async_computation.17 | async-start | bytes 1474560 | tf_op jit(solution)/shard_map/all_gather | solution.py:351
  17.5 28.5 %collective-permute-start = (bf16[256,768]{1,0:T(8,128)(2,1)S(1)}, bf16[256,768]{1,0:T(8,128)(2,1)S(1)}, u32[]{:S(2)}, u32[]{:S(2)}) collective-permute-start(bf16[256,768]{1,0:T(8,128)(2,1)S(1)} %get-tuple-element.167), channel_id=1, source_target_pairs={{0,1},{1,0},{2,3},{3,2},{4,5},{5,4},{6,7},{7,6},{8,9},{9,8},{10,11... | collective-permute-start | bytes 1179656 | tf_op jit(solution)/shard_map/ppermute | solution.py:24
  19.6 207.1 %all-gather.17.cloned.1.call-start = ((), (), s32[]{:S(2)}) async-start(), calls=%async_computation.9 | async-start | bytes 1474560 | tf_op jit(solution)/shard_map/all_gather | solution.py:351
  47.0 13.1 %collective-permute-start.2 = (bf16[512,768]{1,0:T(8,128)(2,1)S(1)}, bf16[512,768]{1,0:T(8,128)(2,1)}, u32[]{:S(2)}, u32[]{:S(2)}) collective-permute-start(bf16[512,768]{1,0:T(8,128)(2,1)S(1)} %fusion.19), channel_id=1, source_target_pairs={{0,4},{4,0},{1,5},{5,1},{2,6},{6,2},{3,7},{7,3},{8,12},{12,8},{9,1... | collective-permute-start | bytes 2359304 | tf_op jit(solution)/shard_map/ppermute | solution.py:24
  49.1 382.3 %reduce-scatter.9.cloned.1.call-start = ((), (), s32[]{:S(2)}) async-start(), calls=%async_computation.11 | async-start | bytes 1228800 | tf_op jit(solution)/shard_map/reduce_scatter | solution.py:466
  49.9 32.8 %collective-permute-start.1 = (bf16[512,768]{1,0:T(8,128)(2,1)S(1)}, bf16[512,768]{1,0:T(8,128)(2,1)}, u32[]{:S(2)}, u32[]{:S(2)}) collective-permute-start(bf16[512,768]{1,0:T(8,128)(2,1)S(1)} %fusion.19), channel_id=1, source_target_pairs={{0,2},{2,0},{1,3},{3,1},{4,6},{6,4},{5,7},{7,5},{8,10},{10,8},{9,1... | collective-permute-start | bytes 2359304 | tf_op jit(solution)/shard_map/ppermute | solution.py:24
  60.2 22.5 %collective-permute-start.3 = (bf16[512,768]{1,0:T(8,128)(2,1)}, bf16[512,768]{1,0:T(8,128)(2,1)}, u32[]{:S(2)}, u32[]{:S(2)}) collective-permute-start(bf16[512,768]{1,0:T(8,128)(2,1)} %collective-permute-done.2), channel_id=1, source_target_pairs={{0,2},{2,0},{1,3},{3,1},{4,6},{6,4},{5,7},{7,5},{8,10},{10,8},{9,1... | collective-permute-start | bytes 2359304 | tf_op jit(solution)/shard_map/ppermute | solution.py:24
  73.1 43.6 %collective-permute-start.7 = (bf16[768,192]{1,0:T(8,128)(2,1)S(1)}, bf16[768,192]{1,0:T(8,128)(2,1)}, u32[]{:S(2)}, u32[]{:S(2)}) collective-permute-start(bf16[768,192]{1,0:T(8,128)(2,1)S(1)} %slice.567), channel_id=1, source_target_pairs={{0,2},{2,0},{1,3},{3,1},{4,6},{6,4},{5,7},{7,5},{8,10},{10,8},{9,1... | collective-permute-start | bytes 884744 | tf_op jit(solution)/shard_map/ppermute | solution.py:24
  73.2 48.6 %collective-permute-start.8 = (bf16[768,192]{1,0:T(8,128)(2,1)S(1)}, bf16[768,192]{1,0:T(8,128)(2,1)}, u32[]{:S(2)}, u32[]{:S(2)}) collective-permute-start(bf16[768,192]{1,0:T(8,128)(2,1)S(1)} %slice.567), channel_id=1, source_target_pairs={{0,4},{4,0},{1,5},{5,1},{2,6},{6,2},{3,7},{7,3},{8,12},{12,8},{9,1... | collective-permute-start | bytes 884744 | tf_op jit(solution)/shard_map/ppermute | solution.py:24
  75.4 67.7 %collective-permute-start.11 = (bf16[768,768]{1,0:T(8,128)(2,1)}, bf16[768,768]{1,0:T(8,128)(2,1)}, u32[]{:S(2)}, u32[]{:S(2)}) collective-permute-start(bf16[768,768]{1,0:T(8,128)(2,1)} %bitcast.24), channel_id=1, source_target_pairs={{0,1},{1,0},{2,3},{3,2},{4,5},{5,4},{6,7},{7,6},{8,9},{9,8},{10,11... | collective-permute-start | bytes 3538952 | tf_op jit(solution)/shard_map/ppermute | solution.py:24
  116.7 46.9 %collective-permute-start.13 = (bf16[768,768]{1,0:T(8,128)(2,1)}, bf16[768,768]{1,0:T(8,128)(2,1)}, u32[]{:S(2)}, u32[]{:S(2)}) collective-permute-start(bf16[768,768]{1,0:T(8,128)(2,1)} %bitcast.24), channel_id=1, source_target_pairs={{0,2},{2,0},{1,3},{3,1},{4,6},{6,4},{5,7},{7,5},{8,10},{10,8},{9,1... | collective-permute-start | bytes 3538952 | tf_op jit(solution)/shard_map/ppermute | solution.py:24
  127.1 27.8 %collective-permute-start.10 = (bf16[768,768]{1,0:T(8,128)(2,1)}, bf16[768,768]{1,0:T(8,128)(2,1)}, u32[]{:S(2)}, u32[]{:S(2)}) collective-permute-start(bf16[768,768]{1,0:T(8,128)(2,1)} %all-gather.13.cloned.1.call-done), channel_id=1, source_target_pairs={{0,1},{1,0},{2,3},{3,2},{4,5},{5,4},{6,7},{7,6},{8,9},{9,8},{10,11... | collective-permute-start | bytes 3538952 | tf_op jit(solution)/shard_map/ppermute | solution.py:24
  129.3 28.7 %collective-permute-start.12 = (bf16[768,768]{1,0:T(8,128)(2,1)}, bf16[768,768]{1,0:T(8,128)(2,1)}, u32[]{:S(2)}, u32[]{:S(2)}) collective-permute-start(bf16[768,768]{1,0:T(8,128)(2,1)} %all-gather.13.cloned.1.call-done), channel_id=1, source_target_pairs={{0,2},{2,0},{1,3},{3,1},{4,6},{6,4},{5,7},{7,5},{8,10},{10,8},{9,1... | collective-permute-start | bytes 3538952 | tf_op jit(solution)/shard_map/ppermute | solution.py:24
  143.1 23.9 %collective-permute-start.15 = (bf16[768,768]{1,0:T(8,128)(2,1)}, bf16[768,768]{1,0:T(8,128)(2,1)S(1)}, u32[]{:S(2)}, u32[]{:S(2)}) collective-permute-start(bf16[768,768]{1,0:T(8,128)(2,1)} %collective-permute-done.11), channel_id=1, source_target_pairs={{0,2},{2,0},{1,3},{3,1},{4,6},{6,4},{5,7},{7,5},{8,10},{10,8},{9,1... | collective-permute-start | bytes 3538952 | tf_op jit(solution)/shard_map/ppermute | solution.py:24
  170.0 20.1 %collective-permute-start.17 = (bf16[512,768]{1,0:T(8,128)(2,1)}, bf16[512,768]{1,0:T(8,128)(2,1)}, u32[]{:S(2)}, u32[]{:S(2)}) collective-permute-start(bf16[512,768]{1,0:T(8,128)(2,1)} %add_convert_fusion.1), channel_id=1, source_target_pairs={{0,4},{4,0},{1,5},{5,1},{2,6},{6,2},{3,7},{7,3},{8,12},{12,8},{9,1... | collective-permute-start | bytes 2359304 | tf_op jit(solution)/shard_map/ppermute | solution.py:24
  171.9 59.7 %collective-permute-start.16 = (bf16[512,768]{1,0:T(8,128)(2,1)}, bf16[512,768]{1,0:T(8,128)(2,1)}, u32[]{:S(2)}, u32[]{:S(2)}) collective-permute-start(bf16[512,768]{1,0:T(8,128)(2,1)} %add_convert_fusion.1), channel_id=1, source_target_pairs={{0,2},{2,0},{1,3},{3,1},{4,6},{6,4},{5,7},{7,5},{8,10},{10,8},{9,1... | collective-permute-start | bytes 2359304 | tf_op jit(solution)/shard_map/ppermute | solution.py:24
  190.1 41.4 %collective-permute-start.18 = (bf16[512,768]{1,0:T(8,128)(2,1)}, bf16[512,768]{1,0:T(8,128)(2,1)}, u32[]{:S(2)}, u32[]{:S(2)}) collective-permute-start(bf16[512,768]{1,0:T(8,128)(2,1)} %collective-permute-done.17), channel_id=1, source_target_pairs={{0,2},{2,0},{1,3},{3,1},{4,6},{6,4},{5,7},{7,5},{8,10},{10,8},{9,1... | collective-permute-start | bytes 2359304 | tf_op jit(solution)/shard_map/ppermute | solution.py:24
  193.4 22.9 %collective-permute-start.22 = (bf16[768,192]{1,0:T(8,128)(2,1)S(1)}, bf16[768,192]{1,0:T(8,128)(2,1)}, u32[]{:S(2)}, u32[]{:S(2)}) collective-permute-start(bf16[768,192]{1,0:T(8,128)(2,1)S(1)} %slice.584), channel_id=1, source_target_pairs={{0,2},{2,0},{1,3},{3,1},{4,6},{6,4},{5,7},{7,5},{8,10},{10,8},{9,1... | collective-permute-start | bytes 884744 | tf_op jit(solution)/shard_map/ppermute | solution.py:24
  202.8 23.9 %collective-permute-start.24 = (bf16[768,192]{1,0:T(8,128)(2,1)}, bf16[768,192]{1,0:T(8,128)(2,1)}, u32[]{:S(2)}, u32[]{:S(2)}) collective-permute-start(bf16[768,192]{1,0:T(8,128)(2,1)} %collective-permute-done.23), channel_id=1, source_target_pairs={{0,2},{2,0},{1,3},{3,1},{4,6},{6,4},{5,7},{7,5},{8,10},{10,8},{9,1... | collective-permute-start | bytes 884744 | tf_op jit(solution)/shard_map/ppermute | solution.py:24
  204.5 77.7 %collective-permute-start.32 = (bf16[256,768]{1,0:T(8,128)(2,1)}, bf16[256,768]{1,0:T(8,128)(2,1)}, u32[]{:S(2)}, u32[]{:S(2)}) collective-permute-start(bf16[256,768]{1,0:T(8,128)(2,1)} %get-tuple-element.157), channel_id=1, source_target_pairs={{0,1},{1,0},{2,3},{3,2},{4,5},{5,4},{6,7},{7,6},{8,9},{9,8},{10,11... | collective-permute-start | bytes 1179656 | tf_op jit(solution)/shard_map/ppermute | solution.py:24
  216.2 56.6 %collective-permute-start.26 = (bf16[768,768]{1,0:T(8,128)(2,1)}, bf16[768,768]{1,0:T(8,128)(2,1)}, u32[]{:S(2)}, u32[]{:S(2)}) collective-permute-start(bf16[768,768]{1,0:T(8,128)(2,1)} %bitcast.360), channel_id=1, source_target_pairs={{0,1},{1,0},{2,3},{3,2},{4,5},{5,4},{6,7},{7,6},{8,9},{9,8},{10,11... | collective-permute-start | bytes 3538952 | tf_op jit(solution)/shard_map/ppermute | solution.py:24
  226.7 46.2 %collective-permute-start.25 = (bf16[768,768]{1,0:T(8,128)(2,1)}, bf16[768,768]{1,0:T(8,128)(2,1)}, u32[]{:S(2)}, u32[]{:S(2)}) collective-permute-start(bf16[768,768]{1,0:T(8,128)(2,1)} %all-gather.17.cloned.1.call-done), channel_id=1, source_target_pairs={{0,1},{1,0},{2,3},{3,2},{4,5},{5,4},{6,7},{7,6},{8,9},{9,8},{10,11... | collective-permute-start | bytes 3538952 | tf_op jit(solution)/shard_map/ppermute | solution.py:24
  271.5 13.7 %collective-permute-start.28 = (bf16[768,768]{1,0:T(8,128)(2,1)S(1)}, bf16[768,768]{1,0:T(8,128)(2,1)S(1)}, u32[]{:S(2)}, u32[]{:S(2)}) collective-permute-start(bf16[768,768]{1,0:T(8,128)(2,1)S(1)} %bitcast.361), channel_id=1, source_target_pairs={{0,2},{2,0},{1,3},{3,1},{4,6},{6,4},{5,7},{7,5},{8,10},{10,8},{9,1... | collective-permute-start | bytes 3538952 | tf_op jit(solution)/shard_map/ppermute | solution.py:24
  273.0 22.7 %collective-permute-start.30 = (bf16[768,768]{1,0:T(8,128)(2,1)}, bf16[768,768]{1,0:T(8,128)(2,1)S(1)}, u32[]{:S(2)}, u32[]{:S(2)}) collective-permute-start(bf16[768,768]{1,0:T(8,128)(2,1)} %collective-permute-done.26), channel_id=1, source_target_pairs={{0,2},{2,0},{1,3},{3,1},{4,6},{6,4},{5,7},{7,5},{8,10},{10,8},{9,1... | collective-permute-start | bytes 3538952 | tf_op jit(solution)/shard_map/ppermute | solution.py:24
  275.9 18.9 %collective-permute-start.29 = (bf16[768,768]{1,0:T(8,128)(2,1)}, bf16[768,768]{1,0:T(8,128)(2,1)S(1)}, u32[]{:S(2)}, u32[]{:S(2)}) collective-permute-start(bf16[768,768]{1,0:T(8,128)(2,1)} %collective-permute-done.25), channel_id=1, source_target_pairs={{0,2},{2,0},{1,3},{3,1},{4,6},{6,4},{5,7},{7,5},{8,10},{10,8},{9,1... | collective-permute-start | bytes 3538952 | tf_op jit(solution)/shard_map/ppermute | solution.py:24
  315.2 72.5 %collective-permute-start.31 = (bf16[256,768]{1,0:T(8,128)(2,1)}, bf16[256,768]{1,0:T(8,128)(2,1)}, u32[]{:S(2)}, u32[]{:S(2)}) collective-permute-start(bf16[256,768]{1,0:T(8,128)(2,1)} %get-tuple-element.159), channel_id=1, source_target_pairs={{0,1},{1,0},{2,3},{3,2},{4,5},{5,4},{6,7},{7,6},{8,9},{9,8},{10,11... | collective-permute-start | bytes 1179656 | tf_op jit(solution)/shard_map/ppermute | solution.py:24
  317.3 16.5 %collective-permute-start.35 = (bf16[192,512]{1,0:T(8,128)(2,1)}, bf16[192,512]{1,0:T(8,128)(2,1)}, u32[]{:S(2)}, u32[]{:S(2)}) collective-permute-start(bf16[192,512]{1,0:T(8,128)(2,1)} %get-tuple-element.153), channel_id=1, source_target_pairs={{0,6},{2,4},{4,2},{6,0},{1,7},{3,5},{5,3},{7,1},{8,14},{10,12},{12... | collective-permute-start | bytes 589832 | tf_op jit(solution)/shard_map/ppermute | solution.py:448
  319.2 14.6 %collective-permute-start.34 = (bf16[192,512]{1,0:T(8,128)(2,1)}, bf16[192,512]{1,0:T(8,128)(2,1)}, u32[]{:S(2)}, u32[]{:S(2)}) collective-permute-start(bf16[192,512]{1,0:T(8,128)(2,1)} %get-tuple-element.154), channel_id=1, source_target_pairs={{0,4},{4,0},{1,5},{5,1},{2,6},{6,2},{3,7},{7,3},{8,12},{12,8},{9,1... | collective-permute-start | bytes 589832 | tf_op jit(solution)/shard_map/ppermute | solution.py:24
  319.2 14.6 %collective-permute-start.33 = (bf16[192,512]{1,0:T(8,128)(2,1)}, bf16[192,512]{1,0:T(8,128)(2,1)}, u32[]{:S(2)}, u32[]{:S(2)}) collective-permute-start(bf16[192,512]{1,0:T(8,128)(2,1)} %get-tuple-element.155), channel_id=1, source_target_pairs={{0,2},{2,0},{1,3},{3,1},{4,6},{6,4},{5,7},{7,5},{8,10},{10,8},{9,1... | collective-permute-start | bytes 589832 | tf_op jit(solution)/shard_map/ppermute | solution.py:24
  324.6 242.1 %collective-permute-start.63 = (bf16[1920,768]{1,0:T(8,128)(2,1)}, bf16[1920,768]{1,0:T(8,128)(2,1)}, u32[]{:S(2)}, u32[]{:S(2)}) collective-permute-start(bf16[1920,768]{1,0:T(8,128)(2,1)} %pad_maximum_fusion.7), channel_id=1, source_target_pairs={{0,2},{2,0},{1,3},{3,1},{4,6},{6,4},{5,7},{7,5},{8,10},{10,8},{9,1... | collective-permute-start | bytes 8847368 | tf_op jit(solution)/shard_map/ppermute | solution.py:24
  371.2 61.5 %collective-permute-start.36 = (bf16[1024,768]{1,0:T(8,128)(2,1)}, bf16[1024,768]{1,0:T(8,128)(2,1)}, u32[]{:S(2)}, u32[]{:S(2)}) collective-permute-start(bf16[1024,768]{1,0:T(8,128)(2,1)} %pad_maximum_fusion.11), channel_id=1, source_target_pairs={{0,2},{2,0},{1,3},{3,1},{4,6},{6,4},{5,7},{7,5},{8,10},{10,8},{9,1... | collective-permute-start | bytes 4718600 | tf_op jit(solution)/shard_map/ppermute | solution.py:24
  376.9 210.5 %reduce-scatter.7.cloned.1.call-start = ((), (), s32[]{:S(2)}) async-start(), calls=%async_computation.10 | async-start | bytes 1228800 | tf_op jit(solution)/shard_map/reduce_scatter | solution.py:466
  380.3 63.7 %collective-permute-start.72 = (bf16[1536,768]{1,0:T(8,128)(2,1)}, bf16[1536,768]{1,0:T(8,128)(2,1)}, u32[]{:S(2)}, u32[]{:S(2)}) collective-permute-start(bf16[1536,768]{1,0:T(8,128)(2,1)} %pad_maximum_fusion.10), channel_id=1, source_target_pairs={{0,2},{2,0},{1,3},{3,1},{4,6},{6,4},{5,7},{7,5},{8,10},{10,8},{9,1... | collective-permute-start | bytes 7077896 | tf_op jit(solution)/shard_map/ppermute | solution.py:24
  434.5 28.1 %collective-permute-start.37 = (bf16[512,768]{1,0:T(8,128)(2,1)S(1)}, bf16[512,768]{1,0:T(8,128)(2,1)S(1)}, u32[]{:S(2)}, u32[]{:S(2)}) collective-permute-start(bf16[512,768]{1,0:T(8,128)(2,1)S(1)} %fusion.142), channel_id=1, source_target_pairs={{0,4},{4,0},{1,5},{5,1},{2,6},{6,2},{3,7},{7,3},{8,12},{12,8},{9,1... | collective-permute-start | bytes 2359304 | tf_op jit(solution)/shard_map/ppermute | solution.py:24
  438.6 12.3 %collective-permute-start.55 = (bf16[192,576]{1,0:T(8,128)(2,1)S(1)}, bf16[192,576]{1,0:T(8,128)(2,1)S(1)}, u32[]{:S(2)}, u32[]{:S(2)}) collective-permute-start(bf16[192,576]{1,0:T(8,128)(2,1)S(1)} %get-tuple-element.111), channel_id=1, source_target_pairs={{0,2},{2,0},{1,3},{3,1},{4,6},{6,4},{5,7},{7,5},{8,10},{10,8},{9,1... | collective-permute-start | bytes 663560 | tf_op jit(solution)/shard_map/ppermute | solution.py:24
  440.3 17.7 %collective-permute-start.56 = (bf16[192,576]{1,0:T(8,128)(2,1)S(1)}, bf16[192,576]{1,0:T(8,128)(2,1)}, u32[]{:S(2)}, u32[]{:S(2)}) collective-permute-start(bf16[192,576]{1,0:T(8,128)(2,1)S(1)} %get-tuple-element.111), channel_id=1, source_target_pairs={{0,4},{4,0},{1,5},{5,1},{2,6},{6,2},{3,7},{7,3},{8,12},{12,8},{9,1... | collective-permute-start | bytes 663560 | tf_op jit(solution)/shard_map/ppermute | solution.py:24
  449.7 109.3 %collective-permute-start.73 = (bf16[768,768]{1,0:T(8,128)(2,1)}, bf16[768,768]{1,0:T(8,128)(2,1)}, u32[]{:S(2)}, u32[]{:S(2)}) collective-permute-start(bf16[768,768]{1,0:T(8,128)(2,1)} %fusion.6), channel_id=1, source_target_pairs={{0,1},{1,0},{2,3},{3,2},{4,5},{5,4},{6,7},{7,6},{8,9},{9,8},{10,11... | collective-permute-start | bytes 3538952 | tf_op jit(solution)/shard_map/ppermute | solution.py:24
  506.2 65.4 %collective-permute-start.57 = (bf16[192,576]{1,0:T(8,128)(2,1)}, bf16[192,576]{1,0:T(8,128)(2,1)}, u32[]{:S(2)}, u32[]{:S(2)}) collective-permute-start(bf16[192,576]{1,0:T(8,128)(2,1)} %collective-permute-done.56), channel_id=1, source_target_pairs={{0,2},{2,0},{1,3},{3,1},{4,6},{6,4},{5,7},{7,5},{8,10},{10,8},{9,1... | collective-permute-start | bytes 663560 | tf_op jit(solution)/shard_map/ppermute | solution.py:24
  510.4 117.2 %collective-permute-start.58 = (bf16[1920,768]{1,0:T(8,128)(2,1)}, bf16[1920,768]{1,0:T(8,128)(2,1)}, u32[]{:S(2)}, u32[]{:S(2)}) collective-permute-start(bf16[1920,768]{1,0:T(8,128)(2,1)} %pad_maximum_fusion.4), channel_id=1, source_target_pairs={{0,2},{2,0},{1,3},{3,1},{4,6},{6,4},{5,7},{7,5},{8,10},{10,8},{9,1... | collective-permute-start | bytes 8847368 | tf_op jit(solution)/shard_map/ppermute | solution.py:24
  510.8 101.5 %collective-permute-start.68 = (bf16[1536,768]{1,0:T(8,128)(2,1)}, bf16[1536,768]{1,0:T(8,128)(2,1)}, u32[]{:S(2)}, u32[]{:S(2)}) collective-permute-start(bf16[1536,768]{1,0:T(8,128)(2,1)} %pad_maximum_fusion.9), channel_id=1, source_target_pairs={{0,2},{2,0},{1,3},{3,1},{4,6},{6,4},{5,7},{7,5},{8,10},{10,8},{9,1... | collective-permute-start | bytes 7077896 | tf_op jit(solution)/shard_map/ppermute | solution.py:24
  547.6 181.6 %reduce-scatter.17.cloned.1.call-start = ((), (), s32[]{:S(2)}) async-start(), calls=%async_computation.15 | async-start | bytes 1474560 | tf_op jit(solution)/shard_map/reduce_scatter | solution.py:415
  563.5 167.6 %reduce-scatter.13.cloned.1.call-start = ((), (), s32[]{:S(2)}) async-start(), calls=%async_computation.13 | async-start | bytes 1843200 | tf_op jit(solution)/shard_map/reduce_scatter | solution.py:415
  566.3 18.3 %collective-permute-start.41 = (bf16[1024,768]{1,0:T(8,128)(2,1)}, bf16[1024,768]{1,0:T(8,128)(2,1)}, u32[]{:S(2)}, u32[]{:S(2)}) collective-permute-start(bf16[1024,768]{1,0:T(8,128)(2,1)} %pad_maximum_fusion.12), channel_id=1, source_target_pairs={{0,2},{2,0},{1,3},{3,1},{4,6},{6,4},{5,7},{7,5},{8,10},{10,8},{9,1... | collective-permute-start | bytes 4718600 | tf_op jit(solution)/shard_map/ppermute | solution.py:24
  571.3 34.2 %collective-permute-start.64 = (bf16[960,768]{1,0:T(8,128)(2,1)}, bf16[960,768]{1,0:T(8,128)(2,1)}, u32[]{:S(2)}, u32[]{:S(2)}) collective-permute-start(bf16[960,768]{1,0:T(8,128)(2,1)} %fusion), channel_id=1, source_target_pairs={{0,1},{1,0},{2,3},{3,2},{4,5},{5,4},{6,7},{7,6},{8,9},{9,8},{10,11... | collective-permute-start | bytes 4423688 | tf_op jit(solution)/shard_map/ppermute | solution.py:24
  587.4 36.2 %collective-permute-start.42 = (bf16[512,768]{1,0:T(8,128)(2,1)}, bf16[512,768]{1,0:T(8,128)(2,1)}, u32[]{:S(2)}, u32[]{:S(2)}) collective-permute-start(bf16[512,768]{1,0:T(8,128)(2,1)} %fusion.140), channel_id=1, source_target_pairs={{0,4},{4,0},{1,5},{5,1},{2,6},{6,2},{3,7},{7,3},{8,12},{12,8},{9,1... | collective-permute-start | bytes 2359304 | tf_op jit(solution)/shard_map/ppermute | solution.py:24
  587.4 23.4 %collective-permute-start.50 = (bf16[192,576]{1,0:T(8,128)(2,1)}, bf16[192,576]{1,0:T(8,128)(2,1)S(1)}, u32[]{:S(2)}, u32[]{:S(2)}) collective-permute-start(bf16[192,576]{1,0:T(8,128)(2,1)} %reduce-scatter.7.cloned.1.call-done), channel_id=1, source_target_pairs={{0,1},{1,0},{2,3},{3,2},{4,5},{5,4},{6,7},{7,6},{8,9},{9,8},{10,11... | collective-permute-start | bytes 663560 | tf_op jit(solution)/shard_map/ppermute | solution.py:24
  609.4 141.7 %reduce-scatter.15.cloned.1.call-start = ((), (), s32[]{:S(2)}) async-start(), calls=%async_computation.14 | async-start | bytes 1474560 | tf_op jit(solution)/shard_map/reduce_scatter | solution.py:415
  615.6 27.4 %collective-permute-start.69 = (bf16[768,768]{1,0:T(8,128)(2,1)S(1)}, bf16[768,768]{1,0:T(8,128)(2,1)S(1)}, u32[]{:S(2)}, u32[]{:S(2)}) collective-permute-start(bf16[768,768]{1,0:T(8,128)(2,1)S(1)} %fusion.9), channel_id=1, source_target_pairs={{0,1},{1,0},{2,3},{3,2},{4,5},{5,4},{6,7},{7,6},{8,9},{9,8},{10,11... | collective-permute-start | bytes 3538952 | tf_op jit(solution)/shard_map/ppermute | solution.py:24
  622.7 29.8 %collective-permute-start.53 = (bf16[192,576]{1,0:T(8,128)(2,1)S(1)}, bf16[192,576]{1,0:T(8,128)(2,1)S(1)}, u32[]{:S(2)}, u32[]{:S(2)}) collective-permute-start(bf16[192,576]{1,0:T(8,128)(2,1)S(1)} %collective-permute-done.52), channel_id=1, source_target_pairs={{0,2},{2,0},{1,3},{3,1},{4,6},{6,4},{5,7},{7,5},{8,10},{10,8},{9,1... | collective-permute-start | bytes 663560 | tf_op jit(solution)/shard_map/ppermute | solution.py:24
  633.4 41.2 %collective-permute-start.59 = (bf16[960,768]{1,0:T(8,128)(2,1)}, bf16[960,768]{1,0:T(8,128)(2,1)}, u32[]{:S(2)}, u32[]{:S(2)}) collective-permute-start(bf16[960,768]{1,0:T(8,128)(2,1)} %fusion.3), channel_id=1, source_target_pairs={{0,1},{1,0},{2,3},{3,2},{4,5},{5,4},{6,7},{7,6},{8,9},{9,8},{10,11... | collective-permute-start | bytes 4423688 | tf_op jit(solution)/shard_map/ppermute | solution.py:24
  645.0 107.6 %reduce-scatter.11.cloned.1.call-start = ((), (), s32[]{:S(2)}) async-start(), calls=%async_computation.12 | async-start | bytes 1843200 | tf_op jit(solution)/shard_map/reduce_scatter | solution.py:415
  650.0 98.5 %collective-permute-start.43 = (bf16[256,768]{1,0:T(8,128)(2,1)}, bf16[256,768]{1,0:T(8,128)(2,1)}, u32[]{:S(2)}, u32[]{:S(2)}) collective-permute-start(bf16[256,768]{1,0:T(8,128)(2,1)} %get-tuple-element.147), channel_id=1, source_target_pairs={{0,1},{1,0},{2,3},{3,2},{4,5},{5,4},{6,7},{7,6},{8,9},{9,8},{10,11... | collective-permute-start | bytes 1179656 | tf_op jit(solution)/shard_map/ppermute | solution.py:24
  650.9 27.7 %collective-permute-start.45 = (f32[144,128]{1,0:T(8,128)}, f32[144,128]{1,0:T(8,128)}, u32[]{:S(2)}, u32[]{:S(2)}) collective-permute-start(f32[144,128]{1,0:T(8,128)} %add.970), channel_id=1, source_target_pairs={{0,4},{4,0},{1,5},{5,1},{2,6},{6,2},{3,7},{7,3},{8,12},{12,8},{9,1... | collective-permute-start | bytes 221192 | tf_op jit(solution)/shard_map/ppermute | solution.py:24
  679.7 19.5 %collective-permute-start.46 = (f32[144,128]{1,0:T(8,128)S(1)}, f32[144,128]{1,0:T(8,128)S(1)}, u32[]{:S(2)}, u32[]{:S(2)}) collective-permute-start(f32[144,128]{1,0:T(8,128)S(1)} %add.971), channel_id=1, source_target_pairs={{0,1},{1,0},{2,3},{3,2},{4,5},{5,4},{6,7},{7,6},{8,9},{9,8},{10,11... | collective-permute-start | bytes 221192 | tf_op jit(solution)/shard_map/ppermute | solution.py:24
  699.2 19.1 %collective-permute-start.49 = (f32[144,128]{1,0:T(8,128)S(1)}, f32[144,128]{1,0:T(8,128)S(1)}, u32[]{:S(2)}, u32[]{:S(2)}) collective-permute-start(f32[144,128]{1,0:T(8,128)S(1)} %add.972), channel_id=1, source_target_pairs={{0,24},{8,0},{16,8},{24,16},{1,25},{9,1},{17,9},{25,17},{2,26},{10... | collective-permute-start | bytes 221192 | tf_op jit(solution)/shard_map/ppermute | solution.py:504
  712.7 13.9 %collective-permute-start.47 = (f32[144,128]{1,0:T(8,128)S(1)}, f32[144,128]{1,0:T(8,128)S(1)}, u32[]{:S(2)}, u32[]{:S(2)}) collective-permute-start(f32[144,128]{1,0:T(8,128)S(1)} %add.972), channel_id=1, source_target_pairs={{0,8},{8,16},{16,24},{24,0},{1,9},{9,17},{17,25},{25,1},{2,10},{10... | collective-permute-start | bytes 221192 | tf_op jit(solution)/shard_map/ppermute | solution.py:504
  731.1 13.9 %collective-permute-start.65 = (bf16[240,768]{1,0:T(8,128)(2,1)}, bf16[240,768]{1,0:T(8,128)(2,1)S(1)}, u32[]{:S(2)}, u32[]{:S(2)}) collective-permute-start(bf16[240,768]{1,0:T(8,128)(2,1)} %reduce-scatter.13.cloned.1.call-done), channel_id=1, source_target_pairs={{0,4},{4,0},{1,5},{5,1},{2,6},{6,2},{3,7},{7,3},{8,12},{12,8},{9,1... | collective-permute-start | bytes 1105928 | tf_op jit(solution)/shard_map/ppermute | solution.py:24
  738.2 12.8 %collective-permute-start.75 = (bf16[192,768]{1,0:T(8,128)(2,1)S(1)}, bf16[192,768]{1,0:T(8,128)(2,1)S(1)}, u32[]{:S(2)}, u32[]{:S(2)}) collective-permute-start(bf16[192,768]{1,0:T(8,128)(2,1)S(1)} %add_convert_fusion.5), channel_id=1, source_target_pairs={{0,2},{2,0},{1,3},{3,1},{4,6},{6,4},{5,7},{7,5},{8,10},{10,8},{9,1... | collective-permute-start | bytes 884744 | tf_op jit(solution)/shard_map/ppermute | solution.py:24
  752.6 15.3 %collective-permute-start.60 = (bf16[240,768]{1,0:T(8,128)(2,1)}, bf16[240,768]{1,0:T(8,128)(2,1)S(1)}, u32[]{:S(2)}, u32[]{:S(2)}) collective-permute-start(bf16[240,768]{1,0:T(8,128)(2,1)} %reduce-scatter.11.cloned.1.call-done), channel_id=1, source_target_pairs={{0,4},{4,0},{1,5},{5,1},{2,6},{6,2},{3,7},{7,3},{8,12},{12,8},{9,1... | collective-permute-start | bytes 1105928 | tf_op jit(solution)/shard_map/ppermute | solution.py:24
  752.9 16.0 %collective-permute-start.67 = (bf16[2,48,768]{2,1,0:T(8,128)(2,1)S(1)}, bf16[2,48,768]{2,1,0:T(8,128)(2,1)S(1)}, u32[]{:S(2)}, u32[]{:S(2)}) collective-permute-start(bf16[2,48,768]{2,1,0:T(8,128)(2,1)S(1)} %get-tuple-element.171), channel_id=1, source_target_pairs={{0,1},{1,0},{2,3},{3,2},{4,5},{5,4},{6,7},{7,6},{8,9},{9,8},{10,11... | collective-permute-start | bytes 442376 | tf_op jit(solution)/shard_map/ppermute | solution.py:24
  (165 other events, 1487.9 us)
Sparse Core Ops, SparseCore 0:
  11.8 31.6 all-gather.10
  45.7 29.7 all-gather.18
  77.6 29.5 all-gather.12
  109.2 29.5 all-gather.14
  140.8 29.6 all-gather.20
  171.9 29.5 all-gather.16
  377.0 54.4 reduce-scatter.8
  547.8 33.2 reduce-scatter.6
  584.0 27.7 reduce-scatter.16
  614.0 37.3 reduce-scatter.12
  653.8 30.3 reduce-scatter.14
  687.0 42.6 reduce-scatter.10

commit v2 on v1

v2 whole, which is shorter than its diff:
```python
from functools import partial, reduce

import jax
import jax.numpy as jnp
from jax import lax
from jax.experimental import pallas as pl
from jax.experimental.pallas import tpu as pltpu
from jax.sharding import Mesh
from jax.sharding import PartitionSpec as P

HEADS = 12
HEAD = 64
LAYERS = 2
BLK = 256
NEG = -1e30
TILES = 2
EPS = 1e-06
F32 = jnp.float32
BF16 = jnp.bfloat16


def dot(left, right, dims=((1,), (0,))):
    return lax.dot_general(left, right, (dims, ((), ())), preferred_element_type=F32)


def swap(value, axis):
    return lax.ppermute(value, axis, ((0, 1), (1, 0)))


def block_place(block, dev, half):
    return (((block // 2) ^ dev) * 2) + ((block % 2) ^ half)


def doc_range(first, ends, length):
    last = first + BLK - 1
    start, stop = jnp.int32(0), jnp.int32(length)
    for end in ends:
        start = jnp.maximum(start, jnp.where(first >= end, end, 0))
        stop = jnp.minimum(stop, jnp.where(last < end, end, length))
    return start // BLK, (stop + BLK - 1) // BLK


def seg_of(places, ends):
    seg = (places >= ends[0]).astype(jnp.int32)
    for end in ends[1:]:
        seg = seg + (places >= end).astype(jnp.int32)
    return seg


def three_heads(pair, single):
    blank = jnp.zeros_like(single)
    return (
        jnp.concatenate((pair[:HEAD], blank), axis=0),
        jnp.concatenate((blank, pair[HEAD:]), axis=0),
        jnp.concatenate((single, blank), axis=0),
    )


def norm_rows(rows, gain, bias):
    centred = rows - jnp.mean(rows, axis=-1, keepdims=True)
    inv_std = lax.rsqrt(jnp.mean(centred * centred, axis=-1, keepdims=True) + EPS)
    return centred * inv_std * gain + bias


def whole(shape):
    return pl.BlockSpec(shape, lambda *at: (0,) * len(shape))


HBM = pl.BlockSpec(memory_space=pl.ANY)


def attention_forward_kernel(norm, info, *refs):
    parts, (w_ref, bias_ref, gain_ref, shift_ref) = refs[:4], refs[4:8]
    at_out, qkv_out, out_ref, lse_ref, a_ref, at_ref, qkv_ref, v01_t, v2_t, sems, out_sems = refs[8:]
    length = qkv_ref.shape[0]
    ends = (info[0], info[1], info[2])
    dev, half = info[3], info[4]
    each = parts[0].shape[0]
    copies = [pltpu.make_async_copy(part, a_ref.at[at], sems.at[at]) for at, part in enumerate(parts)]
    for copy in copies:
        copy.start()
    for part in range(4):
        copies[part].wait()

        def project(at, nothing):
            rows = pl.ds(pl.multiple_of(at * BLK, BLK), BLK)
            goal = pl.ds(pl.multiple_of(part * each + at * BLK, BLK), BLK)
            values = a_ref[part, rows, :]
            if norm:
                values = norm_rows(values.astype(F32), gain_ref[...], shift_ref[...]).astype(BF16)
            found = dot(values, w_ref[...]) + bias_ref[...]
            at_ref[:, goal] = values.T
            qkv_ref[goal, 0:384] = found[:, 0:384].astype(BF16)
            qkv_ref[goal, 384:576] = (found[:, 384:576] * HEAD**-0.5).astype(BF16)
            v01_t[:, goal] = qkv_ref[goal, 256:384].T
            v2_t[:, goal] = qkv_ref[goal, 128:256].T
            return nothing

        lax.fori_loop(0, each // BLK, project, 0)
    out_copies = [
        pltpu.make_async_copy(at_ref, at_out, out_sems.at[0]),
        pltpu.make_async_copy(qkv_ref, qkv_out, out_sems.at[1]),
    ]
    for copy in out_copies:
        copy.start()

    blocks = length // BLK
    lse_ref[...] = jnp.zeros_like(lse_ref)

    def per_block(step, nothing):
        mine = pl.ds(pl.multiple_of(step * BLK, BLK), BLK)
        first = block_place(step, dev, half) * BLK
        seg_q = seg_of(first + lax.broadcasted_iota(jnp.int32, (1, BLK), 1), ends)
        queries = three_heads(qkv_ref[mine, 384:512].T, qkv_ref[mine, 512:576].T)
        low, high = doc_range(first, ends, length)

        def body(pair, carry):
            tiles = []
            for more in range(TILES):
                block = low + TILES * pair + more
                place = block_place(jnp.minimum(block, blocks - 1), dev, half)
                rows = pl.ds(pl.multiple_of(place * BLK, BLK), BLK)
                places = block * BLK + lax.broadcasted_iota(jnp.int32, (BLK, 1), 0)
                tiles.append((rows, seg_of(places, (*ends, length)) == seg_q))

            def score(head):
                lanes = slice(128, 256) if head == 2 else slice(0, 128)
                return [jnp.where(allowed, dot(qkv_ref[rows, lanes], queries[head]), NEG) for rows, allowed in tiles]

            def weigh(head, scores):
                top, total, acc = carry[head]
                new_top = jnp.maximum(top, jnp.max(reduce(jnp.maximum, scores), axis=0, keepdims=True))
                shrink = jnp.exp(top - new_top)
                exps = [jnp.exp(one - new_top) for one in scores]
                total = total * shrink + jnp.sum(reduce(jnp.add, exps), axis=0, keepdims=True)
                return new_top, total, acc * shrink, [exp.astype(BF16) for exp in exps]

            def gather(head, weighed):
                top, total, acc, exps = weighed
                for (rows, _), exp in zip(tiles, exps):
                    values = v2_t[HEAD:128, rows] if head == 2 else v01_t[head * HEAD : (head + 1) * HEAD, rows]
                    acc = acc + dot(values, exp)
                return top, total, acc

            s0 = score(0)
            s1 = score(1)
            w0 = weigh(0, s0)
            s2 = score(2)
            w1 = weigh(1, s1)
            r0 = gather(0, w0)
            w2 = weigh(2, s2)
            r1 = gather(1, w1)
            r2 = gather(2, w2)
            return r0, r1, r2

        start = tuple(
            (
                jnp.full((1, BLK), NEG, F32),
                jnp.zeros((1, BLK), F32),
                jnp.zeros((HEAD, BLK), F32),
            )
            for _ in range(3)
        )
        final = lax.fori_loop(0, (high - low + TILES - 1) // TILES, body, start)
        cols = pl.ds(pl.multiple_of((step % 2) * BLK, BLK), BLK)
        for head in range(3):
            top, total, acc = final[head]
            out_ref[step // 2, head * HEAD : (head + 1) * HEAD, cols] = (acc / total).astype(BF16)
            lse_ref[head : head + 1, mine] = top + jnp.log(total)
        return nothing

    lax.fori_loop(0, blocks, per_block, 0)
    for copy in out_copies:
        copy.wait()


def attention_forward(info, parts, w_qkv, bias, gain, shift, norm):
    each, width = parts[0].shape
    length = 4 * each
    return pl.pallas_call(
        partial(attention_forward_kernel, norm),
        name="attention_forward",
        grid_spec=pltpu.PrefetchScalarGridSpec(
            num_scalar_prefetch=1,
            grid=(1,),
            in_specs=[HBM] * 4 + [whole(w_qkv.shape), whole(bias.shape), whole(gain.shape), whole(shift.shape)],
            out_specs=[HBM, HBM, whole((4, 192, each)), whole((8, length))],
            scratch_shapes=[
                pltpu.VMEM((4, each, width), BF16),
                pltpu.VMEM((width, length), BF16),
                pltpu.VMEM((length, 576), BF16),
                pltpu.VMEM((128, length), BF16),
                pltpu.VMEM((128, length), BF16),
                pltpu.SemaphoreType.DMA((4,)),
                pltpu.SemaphoreType.DMA((2,)),
            ],
        ),
        out_shape=(
            jax.ShapeDtypeStruct((width, length), BF16),
            jax.ShapeDtypeStruct((length, 576), BF16),
            jax.ShapeDtypeStruct((4, 192, each), BF16),
            jax.ShapeDtypeStruct((8, length), F32),
        ),
        compiler_params=pltpu.CompilerParams(vmem_limit_bytes=48 << 20),
        cost_estimate=pl.CostEstimate(
            flops=14 * 10**9, transcendentals=3 * length * 1024, bytes_accessed=12 << 20
        ),
    )(info, *parts, w_qkv, bias, gain, shift)


def attention_backward_kernel(
    info, qkv_ref, out_ref, lse_ref, w_ref, g0, g1, g2, g3,
    du_out, core_out, far_out, own_out, sums_ref,
    q01_t, q2_t, delta, dq_t, grad_t, du_ref, core_ref, far_ref, own_ref, sems,
):
    length = qkv_ref.shape[0]
    each = length // 4
    ends = (info[0], info[1], info[2])
    dev, half = info[3], info[4]
    blocks = length // BLK
    q01_t[...] = qkv_ref[:, 384:512].T
    q2_t[...] = qkv_ref[:, 512:576].T
    dq_t[...] = jnp.zeros_like(dq_t)
    for part, grad in enumerate((g0, g1, g2, g3)):
        grad_t[part] = grad[...]
        for head in range(3):
            rows = slice(head * HEAD, (head + 1) * HEAD)
            both = out_ref[part, rows].astype(F32) * grad[rows].astype(F32)
            delta[head : head + 1, part * each : (part + 1) * each] = jnp.sum(both, axis=0, keepdims=True)

    def per_block(step, nothing):
        mine = pl.ds(pl.multiple_of(step * BLK, BLK), BLK)
        first = block_place(step, dev, half) * BLK
        seg_k = seg_of(first + lax.broadcasted_iota(jnp.int32, (BLK, 1), 0), ends)
        k01 = qkv_ref[mine, 0:128]
        k2v2 = qkv_ref[mine, 128:256]
        v01 = qkv_ref[mine, 256:384]
        k01_t = k01.T
        k2_t = k2v2.T[:HEAD]
        keys_t = (k01_t[:HEAD], k01_t[HEAD:], k2_t)
        low, high = doc_range(first, ends, length)

        def body(pair, carry):
            blank = jnp.zeros((HEAD, BLK), BF16)
            tiles = []
            for more in range(TILES):
                block = low + TILES * pair + more
                place = block_place(jnp.minimum(block, blocks - 1), dev, half)
                cols = pl.ds(pl.multiple_of(place * BLK, BLK), BLK)
                part_cols = pl.ds(pl.multiple_of((place % 2) * BLK, BLK), BLK)
                places = block * BLK + lax.broadcasted_iota(jnp.int32, (1, BLK), 1)
                allowed = seg_k == seg_of(places, (*ends, length))
                queries = three_heads(q01_t[:, cols], q2_t[:, cols])
                grads = grad_t[place // 2, :, part_cols]
                dos = (
                    jnp.concatenate((grads[:HEAD], blank), axis=0),
                    jnp.concatenate((blank, grads[HEAD:128]), axis=0),
                    jnp.concatenate((blank, grads[128:192]), axis=0),
                )
                tiles.append((cols, allowed, queries, dos))

            def first_dots(at):
                cols, allowed, queries, dos = tiles[at // 3]
                head = at % 3
                return (
                    dot(k2v2 if head == 2 else k01, queries[head]),
                    dot(k2v2 if head == 2 else v01, dos[head]),
                )

            def weigh(at, found):
                cols, allowed, queries, dos = tiles[at // 3]
                head = at % 3
                scores, grad_probs = found
                probs = jnp.where(allowed, jnp.exp(scores - lse_ref[head : head + 1, cols]), 0.0)
                grad_scores = (probs * (grad_probs - delta[head : head + 1, cols])).astype(BF16)
                return probs.astype(BF16), grad_scores

            def last_dots(at, found, sums):
                cols, allowed, queries, dos = tiles[at // 3]
                head = at % 3
                probs, grad_scores = found
                more_k = dot(grad_scores, queries[head], ((1,), (1,)))
                more_v = dot(probs, dos[head], ((1,), (1,)))
                more_q = dot(keys_t[head], grad_scores)
                dk01, dk2v2, dv01 = sums
                if head == 2:
                    dk2v2 = dk2v2 + more_k + more_v
                else:
                    dk01 = dk01 + more_k
                    dv01 = dv01 + more_v
                return (dk01, dk2v2, dv01), more_q

            count = 3 * TILES
            sums = carry
            more_q = []
            begun = {0: first_dots(0), 1: first_dots(1)}
            weighed = {}
            for at in range(count):
                if at + 2 < count:
                    begun[at + 2] = first_dots(at + 2)
                weighed[at] = weigh(at, begun[at])
                if at > 0:
                    sums, found = last_dots(at - 1, weighed[at - 1], sums)
                    more_q.append(found)
            sums, found = last_dots(count - 1, weighed[count - 1], sums)
            more_q.append(found)
            for tile in range(TILES):
                cols = tiles[tile][0]
                dq_t[:, cols] = dq_t[:, cols] + jnp.concatenate(more_q[3 * tile : 3 * tile + 3], axis=0)
            return sums

        zero = jnp.zeros((BLK, 128), F32)
        dk01, dk2v2, dv01 = lax.fori_loop(0, (high - low + TILES - 1) // TILES, body, (zero, zero, zero))
        du_ref[mine, 0:128] = dk01.astype(BF16)
        du_ref[mine, 128:256] = dk2v2.astype(BF16)
        du_ref[mine, 256:384] = dv01.astype(BF16)
        return nothing

    lax.fori_loop(0, blocks, per_block, 0)
    sums_ref[...] = jnp.zeros_like(sums_ref)
    scale = HEAD**-0.5

    def finish_rows(at, total):
        rows = pl.ds(pl.multiple_of(at * BLK, BLK), BLK)
        du_ref[rows, 384:512] = (dq_t[0:128, rows] * scale).T.astype(BF16)
        du_ref[rows, 512:576] = (dq_t[128:192, rows] * scale).T.astype(BF16)
        return total + jnp.sum(du_ref[rows, :].astype(F32), axis=0, keepdims=True)

    sums_ref[0:1, :] = lax.fori_loop(0, blocks, finish_rows, jnp.zeros((1, 576), F32))
    copies = [pltpu.make_async_copy(du_ref, du_out, sems.at[0])]
    copies[0].start()
    plan = ((1, core_ref.at[0], core_out.at[0]), (3, core_ref.at[1], core_out.at[1]), (2, far_ref, far_out), (0, own_ref, own_out))
    for at, (part, target, goal) in enumerate(plan):
        kind = target.dtype
        target[...] = dot(du_ref[part * each : (part + 1) * each, :], w_ref[...], ((1,), (1,))).astype(kind)
        copies.append(pltpu.make_async_copy(target, goal, sems.at[at + 1]))
        copies[-1].start()
    for copy in copies:
        copy.wait()


def attention_backward(info, qkv, out, lse, w_qkv, grads):
    length, each, width = qkv.shape[0], qkv.shape[0] // 4, w_qkv.shape[0]
    return pl.pallas_call(
        attention_backward_kernel,
        name="attention_backward",
        grid_spec=pltpu.PrefetchScalarGridSpec(
            num_scalar_prefetch=1,
            grid=(1,),
            in_specs=[whole(qkv.shape), whole(out.shape), whole(lse.shape), whole(w_qkv.shape)]
            + [whole((192, each))] * 4,
            out_specs=[HBM, HBM, HBM, HBM, whole((8, 576))],
            scratch_shapes=[
                pltpu.VMEM((128, length), BF16),
                pltpu.VMEM((64, length), BF16),
                pltpu.VMEM((8, length), F32),
                pltpu.VMEM((192, length), F32),
                pltpu.VMEM((4, 192, each), BF16),
                pltpu.VMEM((length, 576), BF16),
                pltpu.VMEM((2, each, width), BF16),
                pltpu.VMEM((each, width), F32),
                pltpu.VMEM((each, width), F32),
                pltpu.SemaphoreType.DMA((5,)),
            ],
        ),
        out_shape=(
            jax.ShapeDtypeStruct(qkv.shape, BF16),
            jax.ShapeDtypeStruct((2, each, width), BF16),
            jax.ShapeDtypeStruct((each, width), F32),
            jax.ShapeDtypeStruct((each, width), F32),
            jax.ShapeDtypeStruct((8, 576), F32),
        ),
        compiler_params=pltpu.CompilerParams(vmem_limit_bytes=56 << 20),
        cost_estimate=pl.CostEstimate(
            flops=20 * 10**9, transcendentals=3 * length * 1024, bytes_accessed=16 << 20
        ),
    )(info, qkv, out, lse, w_qkv, *grads)


def attention_weights_kernel(at_ref, du_ref, vec_ref, own_ref, core_ref, far_ref, out_ref, spread):
    blank = jnp.zeros((128 - vec_ref.shape[0], vec_ref.shape[1]), F32)
    out_ref[:, 768:896] = jnp.concatenate((vec_ref[...], blank), axis=0).T.astype(BF16)
    out_ref[:, 0:576] = dot(at_ref[...], du_ref[...]).astype(BF16)
    total = own_ref[...].astype(F32) + core_ref[...].astype(F32) + far_ref[...].astype(F32)
    quarter = own_ref.shape[0]
    for piece in range(4):
        rows = pl.ds(piece, quarter, stride=4)
        spread[0, rows, :] = total[:, piece * 192 : piece * 192 + 128]
        spread[1, rows, :] = jnp.concatenate(
            (total[:, piece * 192 + 128 : (piece + 1) * 192], jnp.zeros((quarter, 64), F32)), axis=1
        )
    out_ref[:, 576:704] = spread[0].astype(BF16)
    out_ref[:, 704:768] = spread[1, :, 0:64].astype(BF16)


def attention_weights(a_t, du, vectors, own, core, far):
    width = a_t.shape[0]
    return pl.pallas_call(
        attention_weights_kernel,
        name="attention_weights",
        grid=(1,),
        in_specs=[whole(v.shape) for v in (a_t, du, vectors, own, core, far)],
        out_specs=whole((width, width + 128)),
        out_shape=jax.ShapeDtypeStruct((width, width + 128), BF16),
        scratch_shapes=[pltpu.VMEM((2, width, 128), F32)],
        compiler_params=pltpu.CompilerParams(vmem_limit_bytes=48 << 20),
        cost_estimate=pl.CostEstimate(flops=18 * 10**8, transcendentals=0, bytes_accessed=8 << 20),
    )(a_t, du, vectors, own, core, far)


def out_kernel(info, p0, p1, p2, p3, w_ref, x_ref, vec_ref, ctx_ref, mid_ref, c_ref, ctx):
    dev = info[3]
    loc, toks = p0.shape
    for rel, part in enumerate((p0, p1, p2, p3)):
        ctx[dev ^ rel] = part[...]
    ctx_ref[...] = ctx[...].reshape(4 * loc, toks)

    def rows_of(at, nothing):
        rows = pl.ds(pl.multiple_of(at * 128, 128), 128)
        found = dot(ctx_ref[:, rows].T, w_ref[...])
        middle = x_ref[rows, :] + found + vec_ref[0:1, :]
        mid_ref[rows, :] = middle
        c_ref[rows, :] = norm_rows(middle, vec_ref[1:2, :], vec_ref[2:3, :]).astype(BF16)
        return nothing

    lax.fori_loop(0, toks // 128, rows_of, 0)


def out_forward(info, parts, w_out, current, vectors):
    loc, toks = parts[0].shape
    width = w_out.shape[1]
    return pl.pallas_call(
        out_kernel,
        name="out_forward",
        grid_spec=pltpu.PrefetchScalarGridSpec(
            num_scalar_prefetch=1,
            grid=(1,),
            in_specs=[whole((loc, toks))] * 4 + [whole(w_out.shape), whole(current.shape), whole(vectors.shape)],
            out_specs=[whole((width, toks)), whole((toks, width)), whole((toks, width))],
            scratch_shapes=[pltpu.VMEM((4, loc, toks), BF16)],
        ),
        out_shape=(
            jax.ShapeDtypeStruct((width, toks), BF16),
            jax.ShapeDtypeStruct((toks, width), F32),
            jax.ShapeDtypeStruct((toks, width), BF16),
        ),
        compiler_params=pltpu.CompilerParams(vmem_limit_bytes=48 << 20),
        cost_estimate=pl.CostEstimate(flops=10**9, transcendentals=0, bytes_accessed=7 << 20),
    )(info, *parts, w_out, current, vectors)


def norm_back(grad, values, gain):
    centred = values - jnp.mean(values, axis=-1, keepdims=True)
    inv_std = lax.rsqrt(jnp.mean(centred * centred, axis=-1, keepdims=True) + EPS)
    normed = centred * inv_std
    scaled = grad * gain
    grad_in = inv_std * (
        scaled
        - jnp.mean(scaled, axis=-1, keepdims=True)
        - normed * jnp.mean(scaled * normed, axis=-1, keepdims=True)
    )
    return grad_in, jnp.sum(grad * normed, axis=0, keepdims=True), jnp.sum(grad, axis=0, keepdims=True)


def norm_back_kernel(own, core, far, x_ref, gain_ref, mid_ref, grad_ref, sums_ref):
    toks, width = x_ref.shape

    def rows_of(at, sums):
        rows = pl.ds(pl.multiple_of(at * 64, 64), 64)
        found = own[rows, :] + core[0, rows, :].astype(F32) + far[rows, :].astype(F32)
        grad_in, gain_sum, bias_sum = norm_back(found, x_ref[rows, :], gain_ref[...])
        grad_ref[rows, :] = mid_ref[rows, :] + grad_in
        return sums[0] + gain_sum, sums[1] + bias_sum

    zero = jnp.zeros((1, width), F32)
    sums = lax.fori_loop(0, toks // 64, rows_of, (zero, zero))
    sums_ref[...] = jnp.zeros_like(sums_ref)
    sums_ref[0:1, :] = sums[0]
    sums_ref[1:2, :] = sums[1]


def norm_backward(own, core, far, values, gain, middle_grad):
    toks, width = values.shape
    return pl.pallas_call(
        norm_back_kernel,
        name="norm_backward",
        grid=(1,),
        in_specs=[
            whole((toks, width)),
            pl.BlockSpec((1, toks, width), lambda i: (0, 0, 0)),
            whole((toks, width)),
            whole((toks, width)),
            whole(gain.shape),
            whole((toks, width)),
        ],
        out_specs=[whole((toks, width)), whole((8, width))],
        out_shape=(jax.ShapeDtypeStruct((toks, width), F32), jax.ShapeDtypeStruct((8, width), F32)),
        compiler_params=pltpu.CompilerParams(vmem_limit_bytes=48 << 20),
        cost_estimate=pl.CostEstimate(flops=10**7, transcendentals=0, bytes_accessed=9 << 20),
    )(own, core, far, values, gain, middle_grad)


GELU_A = (2.0 / 3.141592653589793) ** 0.5
GELU_B = 0.044715


def gelu(t):
    square = t * t
    tanh = jnp.tanh(t * (GELU_A + GELU_A * GELU_B * square))
    half = 0.5 * t
    side = 0.5 + 0.5 * tanh
    slope = side + (half - half * tanh * tanh) * (GELU_A + 3.0 * GELU_A * GELU_B * square)
    return t * side, slope


def fetch(parts, held, sems):
    units = parts[0].shape[0]
    copies = [
        pltpu.make_async_copy(part, held.at[at // 2, pl.ds((at % 2) * units, units)], sems.at[at])
        for at, part in enumerate(parts)
    ]
    for copy in copies:
        copy.start()
    return copies


def feed_kernel(norm, c_ref, mid_ref, vec_ref, *refs):
    parts, refs = refs[:8], refs[8:]
    if norm:
        slope_out, act_out, x_ref, a_ref, slope_ref, act_ref, held, sems, out_sems = refs
    else:
        slope_out, act_out, x_ref, slope_ref, act_ref, held, sems, out_sems = refs
    toks, width = mid_ref.shape
    units = held.shape[1]
    copies = fetch(parts, held, sems)
    x_ref[...] = mid_ref[...] + vec_ref[0:1, :]
    outs = []

    def before(at):
        copies[2 * at].wait()
        copies[2 * at + 1].wait()
        bias = held[at, :, 2 * width : 2 * width + 128].T[0:1].astype(F32)
        return dot(c_ref[...], held[at, :, 0:width], ((1,), (1,))) + bias

    def after(at, pre):
        act, slope = gelu(pre)
        act = act.astype(BF16)
        slope_ref[at] = slope.astype(BF16)
        act_ref[at] = act.T
        outs.append(pltpu.make_async_copy(slope_ref.at[at], slope_out.at[at], out_sems.at[2 * at]))
        outs.append(pltpu.make_async_copy(act_ref.at[at], act_out.at[at], out_sems.at[2 * at + 1]))
        outs[-2].start()
        outs[-1].start()
        x_ref[...] += dot(act, held[at, :, width : 2 * width])

    pre = before(0)
    for at in range(4):
        later = before(at + 1) if at < 3 else None
        after(at, pre)
        pre = later

    if norm:

        def rows_of(at, nothing):
            rows = pl.ds(pl.multiple_of(at * 64, 64), 64)
            a_ref[rows, :] = norm_rows(x_ref[rows, :], vec_ref[1:2, :], vec_ref[2:3, :]).astype(BF16)
            return nothing

        lax.fori_loop(0, toks // 64, rows_of, 0)
    for copy in outs:
        copy.wait()


def feed_forward(c, middle, vectors, parts, norm):
    toks, width = middle.shape
    units = 2 * parts[0].shape[0]
    out_shape = [
        jax.ShapeDtypeStruct((4, toks, units), BF16),
        jax.ShapeDtypeStruct((4, units, toks), BF16),
        jax.ShapeDtypeStruct((toks, width), F32),
    ]
    if norm:
        out_shape.append(jax.ShapeDtypeStruct((toks, width), BF16))
    return pl.pallas_call(
        partial(feed_kernel, norm),
        name="feed_forward",
        grid=(1,),
        in_specs=[whole(c.shape), whole(middle.shape), whole(vectors.shape)] + [HBM] * 8,
        out_specs=[HBM, HBM] + [whole(shape.shape) for shape in out_shape[2:]],
        out_shape=out_shape,
        scratch_shapes=[
            pltpu.VMEM((4, toks, units), BF16),
            pltpu.VMEM((4, units, toks), BF16),
            pltpu.VMEM((4, units, parts[0].shape[1]), BF16),
            pltpu.SemaphoreType.DMA((8,)),
            pltpu.SemaphoreType.DMA((8,)),
        ],
        compiler_params=pltpu.CompilerParams(vmem_limit_bytes=56 << 20),
        cost_estimate=pl.CostEstimate(flops=5 * 10**9, transcendentals=2 * 10**6, bytes_accessed=20 << 20),
    )(c, middle, vectors, *parts)


def feed_back_kernel(info, grad_ref, slope_in, mid_ref, gain_ref, w_ref, *refs):
    parts, refs = refs[:8], refs[8:]
    dh_out, dm_ref, dmid_ref, da_ref, sums_ref, d0, d1, d2, d3 = refs[:9]
    slope_ref, dh_ref, held, dc, sems, slope_sems, out_sems = refs[9:]
    dev = info[3]
    toks, width = mid_ref.shape
    loc = d0.shape[0]
    copies = fetch(parts, held, sems)
    slopes = [pltpu.make_async_copy(slope_in.at[at], slope_ref.at[at], slope_sems.at[at]) for at in range(4)]
    for copy in slopes:
        copy.start()
    dm_ref[...] = grad_ref[...].astype(BF16)
    outs = []

    def before(at):
        copies[2 * at].wait()
        copies[2 * at + 1].wait()
        return dot(dm_ref[...], held[at, :, width : 2 * width], ((1,), (1,)))

    def after(at, dact):
        slopes[at].wait()
        dpre = (dact * slope_ref[at].astype(F32)).astype(BF16)
        dh_ref[at] = dpre
        outs.append(pltpu.make_async_copy(dh_ref.at[at], dh_out.at[at], out_sems.at[at]))
        outs[-1].start()
        term = dot(dpre, held[at, :, 0:width])
        if at == 0:
            dc[...] = term
        else:
            dc[...] += term

    dact = before(0)
    for at in range(4):
        later = before(at + 1) if at < 3 else None
        after(at, dact)
        dact = later

    def rows_of(at, sums):
        rows = pl.ds(pl.multiple_of(at * 64, 64), 64)
        grad_in, gain_sum, bias_sum = norm_back(dc[rows, :], mid_ref[rows, :], gain_ref[...])
        grad_mid = grad_ref[rows, :] + grad_in
        dmid_ref[rows, :] = grad_mid
        branch = grad_mid.astype(BF16)
        da_ref[rows, :] = branch
        out_sum = jnp.sum(branch.astype(F32), axis=0, keepdims=True)
        down_sum = jnp.sum(dm_ref[rows, :].astype(F32), axis=0, keepdims=True)
        return sums[0] + gain_sum, sums[1] + bias_sum, sums[2] + out_sum, sums[3] + down_sum

    zero = jnp.zeros((1, width), F32)
    sums = lax.fori_loop(0, toks // 64, rows_of, (zero,) * 4)
    sums_ref[...] = jnp.zeros_like(sums_ref)
    for at in range(4):
        sums_ref[at : at + 1, :] = sums[at]
    for rel, target in enumerate((d0, d1, d2, d3)):
        rows = pl.ds(pl.multiple_of((dev ^ rel) * loc, 64), loc)
        target[...] = dot(w_ref[rows, :], da_ref[...], ((1,), (1,))).astype(BF16)
    for copy in outs:
        copy.wait()


def feed_backward(info, grad, slope, middle, gain, w_out, parts):
    toks, width = middle.shape
    loc = width // 4
    units = 2 * parts[0].shape[0]
    shapes = [
        jax.ShapeDtypeStruct(slope.shape, BF16),
        jax.ShapeDtypeStruct((toks, width), BF16),
        jax.ShapeDtypeStruct((toks, width), F32),
        jax.ShapeDtypeStruct((toks, width), BF16),
        jax.ShapeDtypeStruct((8, width), F32),
    ] + [jax.ShapeDtypeStruct((loc, toks), BF16)] * 4
    return pl.pallas_call(
        feed_back_kernel,
        name="feed_backward",
        grid_spec=pltpu.PrefetchScalarGridSpec(
            num_scalar_prefetch=1,
            grid=(1,),
            in_specs=[whole(grad.shape), HBM, whole(middle.shape), whole(gain.shape), whole(w_out.shape)] + [HBM] * 8,
            out_specs=[HBM] + [whole(shape.shape) for shape in shapes[1:]],
            scratch_shapes=[
                pltpu.VMEM((4, toks, units), BF16),
                pltpu.VMEM((4, toks, units), BF16),
                pltpu.VMEM((4, units, parts[0].shape[1]), BF16),
                pltpu.VMEM((toks, width), F32),
                pltpu.SemaphoreType.DMA((8,)),
                pltpu.SemaphoreType.DMA((4,)),
                pltpu.SemaphoreType.DMA((4,)),
            ],
        ),
        out_shape=shapes,
        compiler_params=pltpu.CompilerParams(vmem_limit_bytes=60 << 20),
        cost_estimate=pl.CostEstimate(flops=6 * 10**9, transcendentals=2 * 10**6, bytes_accessed=24 << 20),
    )(info, grad, slope, middle, gain, w_out, *parts)


def feed_weights_kernel(add, dh_ref, act_ref, c_ref, dm_ref, *refs):
    width = c_ref.shape[1]
    out_ref = refs[-1]
    dh = dh_ref[0].T
    up = dot(dh, c_ref[...])
    down = dot(act_ref[0], dm_ref[...])
    bias = jnp.broadcast_to(jnp.sum(dh.astype(F32), axis=1, keepdims=True), (dh.shape[0], 128))
    if add:
        up = up + refs[0][:, 0:width].astype(F32)
        down = down + refs[0][:, width : 2 * width].astype(F32)
        bias = bias + refs[0][:, 2 * width :].astype(F32)
    out_ref[:, 0:width] = up.astype(BF16)
    out_ref[:, width : 2 * width] = down.astype(BF16)
    out_ref[:, 2 * width :] = bias.astype(BF16)


def feed_weights(dh, act, c, dm, quarter, add=None):
    units, toks, width = dh.shape[2], c.shape[0], c.shape[1]
    wide = 2 * width + 128
    step = 256
    out = pl.BlockSpec((step, wide), lambda i: (i, 0))
    return pl.pallas_call(
        partial(feed_weights_kernel, add is not None),
        name="feed_weights",
        grid=(units // step,),
        in_specs=[
            pl.BlockSpec((1, toks, step), lambda i: (quarter, 0, i)),
            pl.BlockSpec((1, step, toks), lambda i: (quarter, i, 0)),
            whole(c.shape),
            whole(dm.shape),
        ]
        + ([out] if add is not None else []),
        out_specs=out,
        out_shape=jax.ShapeDtypeStruct((units, wide), BF16),
        compiler_params=pltpu.CompilerParams(vmem_limit_bytes=48 << 20),
        cost_estimate=pl.CostEstimate(flops=24 * 10**8, transcendentals=0, bytes_accessed=6 << 20),
    )(dh, act, c, dm, *([add] if add is not None else []))


def finish_kernel(fill, info, *refs):
    attn, hidden, refs = refs[:4], refs[4:8], refs[8:]
    if fill:
        refs = refs[4:]
    qkv_ref, out_ref, up_ref, down_ref, bias_ref, vec_ref, qkv_at, out_at, hid_at = refs
    vectors = sum(part[:, 768:896].astype(F32) for part in attn)
    vec_ref[...] = vectors.T[0 : vec_ref.shape[0]]
    dev = info[3]
    spot = info[5]
    rows = attn[0].shape[0]
    loc = 192
    for rel in range(4):
        qkv_at[dev ^ rel] = attn[rel][:, 0:576].astype(F32)
        out_at[dev ^ rel, 0] = attn[rel][:, 576:704].astype(F32)
        out_at[dev ^ rel, 1, :, 0:64] = attn[rel][:, 704:768].astype(F32)
        hid_at[spot ^ rel] = hidden[rel][...].astype(F32)
    width = 4 * loc
    quarter = rows // 4
    units = hidden[0].shape[0]
    for at in range(4):
        cols = slice(at * loc, (at + 1) * loc)
        found = qkv_at[at]
        qkv_ref[0, :, at * loc : (at + 1) * loc] = found[:, 384:576]
        qkv_ref[0, :, width + at * loc : width + (at + 1) * loc] = found[:, 0:192]
        v_at = 2 * width + at * loc
        qkv_ref[0, :, v_at : v_at + 128] = found[:, 256:384]
        qkv_ref[0, :, v_at + 128 : v_at + 192] = found[:, 192:256]
        for piece in range(4):
            goal = slice(at * quarter, (at + 1) * quarter)
            lane = piece * loc
            out_ref[0, goal, lane : lane + 128] = out_at[at, 0, pl.ds(piece, quarter, stride=4), :]
            out_ref[0, goal, lane + 128 : lane + 192] = out_at[at, 1, pl.ds(piece, quarter, stride=4), :][:, 0:64]
        down_ref[0, at * units : (at + 1) * units, :] = hid_at[at, :, width : 2 * width]
        bias_ref[0, at * units : (at + 1) * units, :] = hid_at[at, :, 2 * width :]
    up = jnp.concatenate([hid_at[at, :, 0:width] for at in range(4)], axis=0)
    up_ref[0] = up.T


def finish(info, layer, attn, hidden, before):
    rows, width = attn[0].shape[0], attn[0].shape[1] - 128
    units = hidden[0].shape[0]
    shapes = [
        (LAYERS, rows, 3 * width),
        (LAYERS, rows, width),
        (LAYERS, width, 4 * units),
        (LAYERS, 4 * units, width),
        (LAYERS, 4 * units, 128),
    ]
    specs = [pl.BlockSpec((1, *shape[1:]), lambda i, info: (layer, 0, 0)) for shape in shapes]
    specs.append(whole((16, rows)))
    shapes.append((16, rows))
    fill = before is not None
    given = list(before[:4]) if fill else []
    return pl.pallas_call(
        partial(finish_kernel, fill),
        name="finish",
        grid_spec=pltpu.PrefetchScalarGridSpec(
            num_scalar_prefetch=1,
            grid=(1,),
            in_specs=[whole(attn[0].shape)] * 4 + [whole(hidden[0].shape)] * 4 + [HBM] * len(given),
            out_specs=specs,
            scratch_shapes=[
                pltpu.VMEM((4, rows, 576), F32),
                pltpu.VMEM((4, 2, rows, 128), F32),
                pltpu.VMEM((4, units, 2 * width + 128), F32),
            ],
        ),
        out_shape=[jax.ShapeDtypeStruct(shape, F32) for shape in shapes],
        input_output_aliases={9 + at: at for at in range(len(given))},
        compiler_params=pltpu.CompilerParams(vmem_limit_bytes=56 << 20),
        cost_estimate=pl.CostEstimate(flops=10**6, transcendentals=0, bytes_accessed=8 << 20),
    )(info, *attn, *hidden, *given)


PLANE = ("cx", "core", "tp")


def turned(value, first):
    pairs = []
    for x in range(2):
        for core in range(2):
            for y in range(2):
                flip_x = (core == 0) == first
                target = ((1 - x) if flip_x else x, core, y if flip_x else 1 - y)
                pairs.append((x * 4 + core * 2 + y, target[0] * 4 + target[1] * 2 + target[2]))
    return lax.ppermute(value, PLANE, pairs)


def after(value, *others):
    return lax.optimization_barrier((value, *others))[0]


def diagonal(value):
    return lax.ppermute(value, ("cx", "core"), ((0, 3), (1, 2), (2, 1), (3, 0)))


def around(own):
    far = swap(own, "cx")
    return own, swap(own, "core"), far, swap(far, "core")


def local(
    hidden_in,
    doc_lengths,
    ln1_gain,
    ln1_bias,
    qkv_weight,
    qv_bias,
    out_weight,
    out_bias,
    ln2_gain,
    ln2_bias,
    up_weight,
    up_bias,
    down_weight,
    down_bias,
    output_grad,
):
    shards = lax.axis_size("shard")
    ix, ic, iy = lax.axis_index("cx"), lax.axis_index("core"), lax.axis_index("tp")
    dev = ix * 2 + ic
    seqs, toks, width = hidden_in.shape
    rows = ln1_gain.shape[1]
    units = up_bias.shape[1] // 4
    loc = width // 4
    quarter = rows // 4

    def to_sequence(tokens):
        own = lax.dynamic_index_in_dim(tokens, iy, 0, keepdims=False)
        other = lax.dynamic_index_in_dim(tokens, 1 - iy, 0, keepdims=False)
        return jnp.concatenate((own, swap(other, "tp")), axis=0)

    def from_sequence(tokens):
        own, other = tokens[:toks], swap(tokens[toks:], "tp")
        return jnp.where(iy == 0, jnp.stack((own, other)), jnp.stack((other, own)))

    lengths = lax.dynamic_index_in_dim(doc_lengths, iy, 0, keepdims=False)
    end0 = lengths[0]
    end1 = end0 + lengths[1]
    end2 = end1 + lengths[2]
    info = jnp.stack((end0, end1, end2, dev, iy, ic * 2 + ix, dev, dev)).astype(jnp.int32)
    row_ids = jnp.arange(2 * toks, dtype=jnp.int32)
    places = dev * (2 * toks) + ((row_ids // toks) ^ iy) * toks + row_ids % toks
    keep = (places < end2).astype(F32)[:, None]

    def columns(array, start):
        return lax.dynamic_slice_in_dim(array, start, loc, 1)

    small = jnp.concatenate(
        [ln1_gain, ln1_bias, out_bias, ln2_gain, ln2_bias, down_bias, qv_bias.reshape(2 * LAYERS, rows)], axis=0
    )
    small = jnp.pad(small, ((0, 128 - small.shape[0]), (0, 0))).T

    def attention_piece(layer):
        weight = qkv_weight[layer]
        q, k, v = (columns(weight, which * width + loc * dev) for which in range(3))
        out = lax.dynamic_slice_in_dim(out_weight[layer], quarter * dev, quarter, 0).reshape(rows, loc)
        pieces = [k[:, :128], k[:, 128:], v[:, 128:], v[:, :128], q, out]
        if layer == 0:
            pieces.append(small)
        return jnp.concatenate(pieces, axis=1)

    def hidden_piece(layer):
        start = ic * 2 * units + ix * units
        up = lax.dynamic_slice_in_dim(up_weight[layer], start, units, 1).T
        down = lax.dynamic_slice_in_dim(down_weight[layer], start, units, 0)
        bias = lax.dynamic_slice_in_dim(up_bias[layer], start, units, 0)
        bias = jnp.broadcast_to(bias[:, None], (units, 128))
        return jnp.concatenate((up, down, bias), axis=1)

    def over_shards(piece):
        return lax.all_gather(piece, "shard", axis=0, tiled=True)

    def spread_hidden(own, one, *others):
        own, one = lax.optimization_barrier((own, one, *others))[:2]
        return own, one, turned(own, False), turned(one, False)

    def both_cores(parts):
        return tuple(parts) + tuple(swap(part, "core") for part in parts)

    def sum_shards(value):
        if shards != 4:
            return lax.psum_scatter(value, "shard", scatter_dimension=0, tiled=True)
        each = value.reshape(shards, -1, value.shape[1])
        index = lax.axis_index("shard")
        total = lax.dynamic_index_in_dim(each, index, 0, keepdims=False).astype(F32)
        for by in range(1, shards):
            piece = lax.dynamic_index_in_dim(each, (index + by) % shards, 0, keepdims=False)
            piece = lax.ppermute(piece, "shard", [(i, (i + by) % shards) for i in range(shards)])
            total = total + piece.astype(F32)
        return total.astype(value.dtype)

    hidden_own = to_sequence(hidden_in)
    grad = to_sequence(output_grad).astype(F32) * keep
    first_parts = around(hidden_own)
    attn0 = over_shards(attention_piece(0))
    feed0 = over_shards(after(hidden_piece(0), attn0, grad, *first_parts))

    def second_weights(*others):
        attn = attention_piece(1)
        piece = jnp.concatenate((hidden_piece(1), attn[:units], attn[units:]), axis=1)
        gathered = over_shards(after(piece, *others))
        wide = 2 * width + 128
        halves = [gathered[:, at : at + width].reshape(shards, 1, units, width) for at in (wide, wide + width)]
        return jnp.concatenate(halves, axis=1).reshape(width, width), gathered[:, :wide]

    def out_weights(own):
        full = jnp.zeros((shards, 4, quarter, width), BF16)
        for rel, part in enumerate(around(own)):
            full = lax.dynamic_update_slice(full, part, (0, dev ^ rel, 0, 0))
        return full.reshape(width, width)

    def out_own(gathered):
        return gathered[:, 3 * loc : 4 * loc].reshape(shards, 1, quarter, width)

    weights = []

    smalls = attn0[:, 4 * loc :].T.astype(F32)
    names = [[smalls[which * LAYERS + layer][None] for which in range(6)] for layer in range(LAYERS)]
    qv = smalls[6 * LAYERS : 8 * LAYERS].reshape(LAYERS, 2, shards, rows)
    qv = jnp.transpose(qv, (0, 2, 1, 3)).reshape(LAYERS, 2 * width)

    current = hidden_own.astype(F32)
    attn_parts = first_parts
    saved = []
    for layer in range(LAYERS):
        gain_one, bias_one, bias_out, gain_two, bias_two, bias_down = names[layer]
        w_qkv = (attn0 if layer == 0 else attn1)[:, : 3 * loc]
        q_bias = lax.dynamic_slice_in_dim(qv[layer], loc * dev, loc, 0)
        v_bias = lax.dynamic_slice_in_dim(qv[layer], width + loc * dev, loc, 0)
        bias = jnp.concatenate((jnp.zeros((192,), F32), v_bias[128:], v_bias[:128], q_bias))[None]
        attn_t, qkv, attended, lse = attention_forward(info, attn_parts, w_qkv, bias, gain_one, bias_one, layer == 0)
        if layer == 0:
            attn1, feed1 = second_weights(attended, feed0)
            w_out = out_own(attn0)
            attended, w_out = lax.optimization_barrier((attended, w_out))
            w_out = out_weights(w_out)
        else:
            own, one, two, three = w_feed1
            early_core = (swap(own, "core"), swap(one, "core"))
            attended, w_out, own, one, two, three, *early_core = lax.optimization_barrier(
                (attended, w_out1, own, one, two, three, *early_core)
            )
        parts = (
            attended[0],
            swap(attended[1], "core"),
            swap(attended[2], "cx"),
            diagonal(attended[3]),
        )
        if layer == 1:
            late_core = [swap(after(part, *parts), "core") for part in (two, three)]
            w_feed = (own, one, two, three, *early_core, *late_core)
        if layer == 0:
            own, *others = lax.optimization_barrier((feed0, *parts, w_out))
            one = turned(own, True)
            two = turned(own, False)
        vectors = jnp.concatenate((bias_out, gain_two, bias_two), axis=0)
        context, middle, mlp_in = out_forward(info, parts, w_out, current, vectors)
        if layer == 0:
            three = turned(after(one, mlp_in), False)
            w_feed = both_cores((own, one, two, three))
            vectors = jnp.concatenate((bias_down, names[1][0], names[1][1]), axis=0)
            mlp_in, feed1 = lax.optimization_barrier((mlp_in, feed1))
            slope, act, result, attn_own = feed_forward(mlp_in, middle, vectors, w_feed, True)
            one = turned(feed1, True)
            attn_parts = around(after(attn_own, one))
            w_out1 = out_weights(after(out_own(attn1), *attn_parts))
            w_feed1 = spread_hidden(feed1, one, *attn_parts)
        else:
            slope, act, result = feed_forward(mlp_in, middle, bias_down, w_feed, False)
        weights.append((w_qkv, w_out, w_feed))
        saved.append((current, attn_t, qkv, attended, lse, context, middle, mlp_in, slope, act))
        current = result
    hidden_out = from_sequence((current * keep).astype(BF16))

    n = shards * units

    attn_sums = [None] * LAYERS
    feed_sums = [None] * LAYERS
    by_attention, by_core = (), ()
    for layer in reversed(range(LAYERS)):
        x_in, attn_t, qkv, attended, lse, context, middle, mlp_in, slope, act = saved[layer]
        gain_one, _, _, gain_two, _, _ = names[layer]
        w_qkv, w_out, w_feed = weights[layer]
        dh, dm, middle_grad, branch_grad, sums_two, d0, d1, d2, d3 = feed_backward(
            info, grad, slope, middle, gain_two, w_out, w_feed
        )
        attn_grads = (d0, swap(d1, "core"), swap(d2, "cx"), diagonal(d3))
        other_late = swap(feed_weights(dh, act, mlp_in, dm, 3), "core")
        late = feed_weights(dh, act, mlp_in, dm, 1, other_late)
        w_out_grad = dot(context, branch_grad).astype(BF16).reshape(shards, 4, quarter, width)
        pieces = [lax.dynamic_index_in_dim(w_out_grad, dev ^ rel, 1, keepdims=False) for rel in range(4)]
        got = swap(jnp.stack((pieces[1], pieces[3])), "core")
        to_far_out = (pieces[2].astype(F32) + got[1].astype(F32)).astype(BF16)
        ready = [*attn_grads, late, to_far_out, *by_attention]
        if layer == 0:
            other_early = swap(feed_weights(dh, act, mlp_in, dm, 2), "core")
            early = feed_weights(dh, act, mlp_in, dm, 0, other_early)
            far = swap(to_far_out, "cx")
            ready += [early, far]
        *attn_grads, late, to_far_out = lax.optimization_barrier(tuple(ready))[:6]
        du, to_core, to_far, own, sums_u = attention_backward(info, qkv, attended, lse, w_qkv, attn_grads)
        late = turned(late, False)
        to_core = after(to_core, late, *by_core)
        from_core = swap(to_core, "core")
        to_far = (to_far + from_core[1].astype(F32)).astype(BF16)
        if layer == 0:
            part = (early[n:].astype(F32) + late[n:].astype(F32)).astype(BF16)
            kept = early[:n].astype(F32) + late[:n].astype(F32)
            arrived = turned(part, True)
            to_far = after(to_far, arrived)
        from_far = swap(to_far, "cx")
        if layer > 0:
            far = swap(after(to_far_out, to_far), "cx")
            du, dh_late, early_late = lax.optimization_barrier((du, dh, late, to_far))[:3]
            other_early = swap(feed_weights(dh_late, act, mlp_in, dm, 2), "core")
            early = feed_weights(dh_late, act, mlp_in, dm, 0, other_early)
            part = (early[n:].astype(F32) + early_late[n:].astype(F32)).astype(BF16)
            kept = early[:n].astype(F32) + early_late[:n].astype(F32)
        du_sum = sums_u[0]
        v_sum = jnp.concatenate((du_sum[256:384], du_sum[192:256]))
        q_row = lax.dynamic_update_slice_in_dim(jnp.zeros((width,), F32), du_sum[384:], loc * dev, 0)
        v_row = lax.dynamic_update_slice_in_dim(jnp.zeros((width,), F32), v_sum, loc * dev, 0)
        qv_rows = jnp.concatenate((q_row, v_row)).reshape(shards, 2, rows).transpose(1, 0, 2).reshape(2, width)
        vectors = jnp.concatenate((sums_two, qv_rows, jnp.zeros((6, width), F32)), axis=0)
        if layer == 0:
            vectors = jnp.concatenate((vectors[:10], sums_one[:2], vectors[12:]), axis=0)
        flat = [piece.reshape(shards * quarter, width) for piece in (pieces[0], got[0], far)]
        joined = attention_weights(attn_t, du, vectors, *flat)
        attn_sum = lax.psum_scatter(joined, "shard", scatter_dimension=0, tiled=True)
        if layer > 0:
            by_attention = (attn_sum,)
            from_far, part = lax.optimization_barrier((from_far, part))
            arrived = turned(part, True)
        attn_sum = (attn_sum.astype(F32) + swap(attn_sum, "tp").astype(F32)).astype(BF16)
        attn_sums[layer] = around(attn_sum)
        part = (kept + arrived.astype(F32)).astype(BF16)
        grad, sums_one = norm_backward(own, from_core, from_far, x_in, gain_one, middle_grad)
        if layer > 0:
            hidden = lax.psum_scatter(part, "shard", scatter_dimension=0, tiled=True)
        else:
            hidden = sum_shards(part)
            halves = sums_one[:2].reshape(2, shards, 2, units).transpose(1, 3, 0, 2).reshape(n, 4)
            lone = sum_shards(jnp.pad(halves, ((0, 0), (0, 124))))
            hidden = lax.dynamic_update_slice(hidden, lone[:, :4].astype(BF16), (0, 2 * width + 1))
        core, far = swap(hidden, "core"), swap(hidden, "cx")
        feed_sums[layer] = (hidden, far, core, swap(far, "core"))
        by_core = (hidden,)

    hidden_grad = from_sequence(grad.astype(BF16)).astype(F32)

    done = None
    columns_of = [None] * LAYERS
    biases = [None] * LAYERS
    for layer in reversed(range(LAYERS)):
        done = finish(info, layer, attn_sums[layer], feed_sums[layer], done)
        columns_of[layer] = done[5]
        biases[layer] = done[4][layer, :, 0]
    lone = feed_sums[0]
    lone = sum(part[:, 2 * width + 1 : 2 * width + 5].astype(F32) for part in lone)
    lone = lone + swap(lone, "tp")
    lone = lone.reshape(units, 2, 2).transpose(1, 2, 0).reshape(2, rows)
    first_gain = jnp.stack((lone[0], columns_of[0][10]))
    first_bias = jnp.stack((lone[1], columns_of[0][11]))
    rest = [jnp.stack((columns_of[0][at], columns_of[1][at])) for at in range(4)]
    qv_out = jnp.stack([jnp.concatenate((columns_of[layer][8], columns_of[layer][9])) for layer in range(LAYERS)])

    return (
        hidden_out,
        hidden_grad,
        first_gain,
        first_bias,
        done[0],
        qv_out,
        done[1],
        rest[2],
        rest[0],
        rest[1],
        done[2],
        jnp.stack(biases),
        done[3],
        rest[3],
    )


def solution(mesh):
    names = tuple(mesh.axis_names)
    shape = dict(mesh.shape)
    split = Mesh(
        mesh.devices.reshape(shape[names[0]], 2, shape[names[1]] // 2, shape[names[2]]),
        ("shard", "cx", "core", "tp"),
    )
    tokens = P("shard", ("cx", "core", "tp"), None)
    vector = P(None, "shard")
    attn = P(None, "shard", None)
    placed = (
        tokens,
        P("shard", None),
        vector,
        vector,
        attn,
        vector,
        attn,
        vector,
        vector,
        vector,
        P(None, None, ("shard", "tp")),
        P(None, ("shard", "tp")),
        P(None, ("shard", "tp"), None),
        vector,
        tokens,
    )
    return jax.shard_map(
        local,
        mesh=split,
        in_specs=placed,
        out_specs=(
            tokens,
            tokens,
            vector,
            vector,
            attn,
            vector,
            attn,
            vector,
            vector,
            vector,
            P(None, None, ("shard", "tp")),
            P(None, ("shard", "tp")),
            P(None, ("shard", "tp"), None),
            vector,
        ),
        check_vma=False,
    )
```

time: 794 us -> 628 us (0.79)
  the two profiles are of different devices: /device:TPU:9 before, /device:TPU:0 now
where the time goes in v2:
time: 628 us; the launch traced here: 619 us
  Pallas kernels  234 us (37%)
  waiting for transfers between devices  170 us (27%)
  starting transfers between devices  92.8 us (15%)
  local copies, waits for them, and re-layouts  64.8 us (10%)
  other arithmetic  36.9 us (6%)
  between operations  18 us (3%)
    ppermute x59, waiting for transfers between devices, swap(): return lax.ppermute(value, axis, ((0, 1), (1, 0)))  102 us
    pallas_call x2, Pallas kernels, attention_backward(): pl.pallas_call(attention_backward_kernel, name='attention_backward', grid...  54.3 us
    ppermute x59, starting transfers between devices, swap(): return lax.ppermute(value, axis, ((0, 1), (1, 0)))  49.9 us
    ppermute x10, waiting for transfers between devices, turned(): return lax.ppermute(value, PLANE, pairs)  42 us
    pallas_call x2, Pallas kernels, attention_forward(): pl.pallas_call(partial(attention_forward_kernel, norm), name='attention_f...  39.6 us
    pallas_call x2, Pallas kernels, feed_backward(): pl.pallas_call(feed_back_kernel, name='feed_backward', grid_spec=pltpu.Pr...  37.3 us
    pallas_call x8, Pallas kernels, feed_weights(): pl.pallas_call(partial(feed_weights_kernel, add is not None), name='feed_...  33.6 us
    ppermute x10, starting transfers between devices, turned(): return lax.ppermute(value, PLANE, pairs)  32.1 us
  transfers between devices with their start and end apart: 85, of which 30 were waited for; matrix products, arithmetic and copies ran while one was open for 12% of the time, Pallas kernels for 30%

profile of v2, /device:TPU:0, one launch (start us, length us, event | category | flops | bytes accessed | tf_op | source)
XLA Modules:
  0.0 618.8 jit_solution(15533144526215274837)
XLA Ops:
  9.2 3.0 collective-permute-start
  24.6 2.5 fusion.28
  34.4 2.4 convert_multiply_fusion.grad_ref
  36.8 9.4 %collective-permute-done.2.refs_2_ = bf16[512,768]{1,0:T(8,128)(2,1)S(1)} collective-permute-done((bf16[512,768]{1,0:T(8,128)(2,1)S(1)}, bf16[512,768]{1,0:T(8,128)(2,1)S(1)}, u32[]{:S(2)}, u32[]{:S(2)}) %collective-permute-start.2) | collective-permute-done | bytes 786464 | tf_op jit(solution)/shard_map/ppermute | solution.py:27
  46.2 6.5 %all-gather.4.cloned.1.call-done = bf16[768,896]{1,0:T(8,128)(2,1)} async-done(((bf16[192,896]{1,0:T(8,128)(2,1)}), bf16[768,896]{1,0:T(8,128)(2,1)}) %all-gather.4.cloned.1.call-update) | async-done | bytes 1376272 | tf_op jit(solution)/shard_map/all_gather | solution.py:908
  58.6 20.6 %attention_forward.2 = (bf16[768,2048]{1,0:T(8,128)(2,1)}, bf16[2048,576]{1,0:T(8,128)(2,1)}, bf16[4,192,512]{2,1,0:T(8,128)(2,1)S(1)}, f32[8,2048]{1,0:T(8,128)S(1)}) custom-call(s32[8]{0:T(128)S(1)} %stack.101.info, bf16[512,768]{1,0:T(8,128)(2,1)S(1)} %get-tuple-element.262.refs_0_, bf16[512,768]{1,0:T(8,128)(2,1)S(1)} %collective-permute-done.1.refs_1_, ...), custom_call_target="tpu_custom_call" | custom-call | flops 14000000000 | bytes 12582912 | tf_op jit(solution)/shard_map/attention_forward/pallas_call | solution.py:180
  83.7 5.5 collective-permute-done.8
  90.8 2.6 collective-permute-done.5.p2
  93.4 3.3 collective-permute-done.6.p3
  98.3 4.6 out_forward.2
  104.9 6.6 %collective-permute-start.12 = (bf16[384,1664]{1,0:T(8,128)(2,1)}, bf16[384,1664]{1,0:T(8,128)(2,1)}, u32[]{:S(2)}, u32[]{:S(2)}) collective-permute-start(bf16[384,1664]{1,0:T(8,128)(2,1)} %all-gather.6.cloned.1.call-done.refs_0_), channel_id=1, source_target_pairs={{0,1},{1,0},{2,6},{3,7},{4,5},{5,4},{6,2},{7,3},{8,9},{9,8},{10,14... | collective-permute-start | bytes 3833864 | tf_op jit(solution)/shard_map/ppermute | solution.py:822
  111.5 4.1 collective-permute-done.11.refs_1_
  115.6 13.1 %collective-permute-start.13 = (bf16[384,1664]{1,0:T(8,128)(2,1)}, bf16[384,1664]{1,0:T(8,128)(2,1)S(1)}, u32[]{:S(2)}, u32[]{:S(2)}) collective-permute-start(bf16[384,1664]{1,0:T(8,128)(2,1)} %collective-permute-done.11.refs_1_), channel_id=1, source_target_pairs={{0,1},{1,0},{2,6},{3,7},{4,5},{5,4},{6,2},{7,3},{8,9},{9,8},{10,14... | collective-permute-start | bytes 3833864 | tf_op jit(solution)/shard_map/ppermute | solution.py:822
  129.1 3.1 collective-permute-done.12.refs_2_
  132.2 13.6 %collective-permute-done.13.refs_3_ = bf16[384,1664]{1,0:T(8,128)(2,1)S(1)} collective-permute-done((bf16[384,1664]{1,0:T(8,128)(2,1)}, bf16[384,1664]{1,0:T(8,128)(2,1)S(1)}, u32[]{:S(2)}, u32[]{:S(2)}) %collective-permute-start.13) | collective-permute-done | bytes 1277984 | tf_op jit(solution)/shard_map/ppermute | solution.py:822
  149.9 14.7 %feed_forward.2 = (bf16[4,512,768]{2,1,0:T(8,128)(2,1)}, bf16[4,768,512]{2,1,0:T(8,128)(2,1)}, f32[512,768]{1,0:T(8,128)}, bf16[512,768]{1,0:T(8,128)(2,1)}) custom-call(bf16[512,768]{1,0:T(8,128)(2,1)} %copy-done.2, f32[512,768]{1,0:T(8,128)} %copy-done.31, f32[3,768]{1,0:T(4,128)} %pad_maximum_fusion.6.vec_ref, ...), custom_call_target="tpu_custom_call" | custom-call | flops 5000000000 | bytes 20971520 | tf_op jit(solution)/shard_map/feed_forward/pallas_call | solution.py:584
  166.5 18.3 %collective-permute-done.20.refs_2_ = bf16[512,768]{1,0:T(8,128)(2,1)S(1)} collective-permute-done((bf16[512,768]{1,0:T(8,128)(2,1)}, bf16[512,768]{1,0:T(8,128)(2,1)S(1)}, u32[]{:S(2)}, u32[]{:S(2)}) %collective-permute-start.20) | collective-permute-done | bytes 786464 | tf_op jit(solution)/shard_map/ppermute | solution.py:27
  195.1 19.0 %attention_forward.3 = (bf16[768,2048]{1,0:T(8,128)(2,1)}, bf16[2048,576]{1,0:T(8,128)(2,1)}, bf16[4,192,512]{2,1,0:T(8,128)(2,1)S(1)}, f32[8,2048]{1,0:T(8,128)S(1)}) custom-call(s32[8]{0:T(128)S(1)} %stack.101.info, bf16[512,768]{1,0:T(8,128)(2,1)S(1)} %copy-done.28, bf16[512,768]{1,0:T(8,128)(2,1)S(1)} %copy-done.30, ...), custom_call_target="tpu_custom_call" | custom-call | flops 14000000000 | bytes 12582912 | tf_op jit(solution)/shard_map/attention_forward/pallas_call | solution.py:180
  216.7 7.5 %collective-permute-done.26.refs_3_ = bf16[384,1664]{1,0:T(8,128)(2,1)S(1)} collective-permute-done((bf16[384,1664]{1,0:T(8,128)(2,1)}, bf16[384,1664]{1,0:T(8,128)(2,1)S(1)}, u32[]{:S(2)}, u32[]{:S(2)}) %collective-permute-start.26) | collective-permute-done | bytes 1277984 | tf_op jit(solution)/shard_map/ppermute | solution.py:822
  224.3 3.6 collective-permute-start.29
  229.4 6.3 %collective-permute-done.30.p2 = bf16[192,512]{1,0:T(8,128)(2,1)S(1)} collective-permute-done((bf16[192,512]{1,0:T(8,128)(2,1)S(1)}, bf16[192,512]{1,0:T(8,128)(2,1)S(1)}, u32[]{:S(2)}, u32[]{:S(2)}) %collective-permute-start.30) | collective-permute-done | bytes 196640 | tf_op jit(solution)/shard_map/ppermute | solution.py:27
  235.7 2.5 collective-permute-done.31.p3
  238.9 4.8 out_forward.3
  247.4 13.6 %feed_forward.3 = (bf16[4,512,768]{2,1,0:T(8,128)(2,1)}, bf16[4,768,512]{2,1,0:T(8,128)(2,1)}, f32[512,768]{1,0:T(8,128)}) custom-call(bf16[512,768]{1,0:T(8,128)(2,1)} %copy-done.4, f32[512,768]{1,0:T(8,128)} %copy-done.32, f32[1,768]{1,0:T(1,128)} %get-tuple-element.271.vec_ref, bf16[384,1664]{1,0:T(8,128)(2,1)} %copy-done.42, ...), custom_call_target="tpu_custom_call" | custom-call | flops 5000000000 | bytes 20971520 | tf_op jit(solution)/shard_map/feed_forward/pallas_call | solution.py:584
  261.0 18.7 %feed_backward.2 = (bf16[4,512,768]{2,1,0:T(8,128)(2,1)}, bf16[512,768]{1,0:T(8,128)(2,1)}, f32[512,768]{1,0:T(8,128)}, bf16[512,768]{1,0:T(8,128)(2,1)}, f32[8,...) custom-call(s32[8]{0:T(128)} %copy-done.26, ...), custom_call_target="tpu_custom_call" | custom-call | flops 6000000000 | bytes 25165824 | tf_op jit(solution)/shard_map/feed_backward/pallas_call | solution.py:674
  280.9 3.4 feed_weights.8
  292.5 3.9 feed_weights.9
  298.9 27.0 %attention_backward.2 = (bf16[2048,576]{1,0:T(8,128)(2,1)}, bf16[2,512,768]{2,1,0:T(8,128)(2,1)}, f32[512,768]{1,0:T(8,128)}, f32[512,768]{1,0:T(8,128)}, f32[8,576]{1,0:T(8,128)}) custom-call(s32[8]{0:T(128)} %copy-done.26, bf16[2048,576]{1,0:T(8,128)(2,1)} %get-tuple-element.154.qkv_ref, bf16[4,192,512]{2,1,0:T(8,128)(2,1)} %copy-done.25, ...), custom_call_target="tpu_custom_call" | custom-call | flops 20000000000 | bytes 16777216 | tf_op jit(solution)/shard_map/attention_backward/pallas_call | solution.py:344
  325.9 2.7 collective-permute-done.40
  328.7 3.6 collective-permute-done.41.core
  332.3 2.6 fusion.1
  334.9 4.5 feed_weights.10
  346.1 7.9 %collective-permute-done.49 = bf16[4,48,768]{2,1,0:T(8,128)(2,1)} collective-permute-done((bf16[4,48,768]{2,1,0:T(8,128)(2,1)}, bf16[4,48,768]{2,1,0:T(8,128)(2,1)}, u32[]{:S(2)}, u32[]{:S(2)}) %collective-permute-start.49) | collective-permute-done | bytes 294944 | tf_op jit(solution)/shard_map/ppermute | solution.py:27
  356.7 5.7 attention_weights.2
  362.5 4.2 feed_weights.11
  366.7 3.7 add_convert_fusion.3
  370.4 4.8 norm_backward.2
  376.3 18.6 %feed_backward.3 = (bf16[4,512,768]{2,1,0:T(8,128)(2,1)}, bf16[512,768]{1,0:T(8,128)(2,1)}, f32[512,768]{1,0:T(8,128)}, bf16[512,768]{1,0:T(8,128)(2,1)}, f32[8,...) custom-call(s32[8]{0:T(128)} %copy-done.26, ...), custom_call_target="tpu_custom_call" | custom-call | flops 6000000000 | bytes 25165824 | tf_op jit(solution)/shard_map/feed_backward/pallas_call | solution.py:674
  396.0 4.6 feed_weights.12
  400.7 4.7 feed_weights.14
  408.1 3.8 collective-permute-start.48
  414.6 10.5 %collective-permute-done.53 = bf16[384,1664]{1,0:T(8,128)(2,1)S(1)} collective-permute-done((bf16[384,1664]{1,0:T(8,128)(2,1)S(1)}, bf16[384,1664]{1,0:T(8,128)(2,1)S(1)}, u32[]{:S(2)}, u32[]{:S(2)}) %collective-permute-start.53) | collective-permute-done | bytes 1277984 | tf_op jit(solution)/shard_map/ppermute | solution.py:822
  426.4 2.9 add_convert_fusion.2
  430.5 4.3 feed_weights.13
  436.3 3.9 feed_weights.15
  441.8 3.8 collective-permute-start.52
  445.6 27.3 %attention_backward.3 = (bf16[2048,576]{1,0:T(8,128)(2,1)}, bf16[2,512,768]{2,1,0:T(8,128)(2,1)}, f32[512,768]{1,0:T(8,128)}, f32[512,768]{1,0:T(8,128)}, f32[8,576]{1,0:T(8,128)}) custom-call(s32[8]{0:T(128)} %copy-done.26, bf16[2048,576]{1,0:T(8,128)(2,1)} %get-tuple-element.152.qkv_ref, bf16[4,192,512]{2,1,0:T(8,128)(2,1)} %copy-done.24, ...), custom_call_target="tpu_custom_call" | custom-call | flops 20000000000 | bytes 16777216 | tf_op jit(solution)/shard_map/attention_backward/pallas_call | solution.py:344
  477.4 5.6 attention_weights.3
  485.7 8.6 %collective-permute-start.34 = (bf16[256,768]{1,0:T(8,128)(2,1)S(1)}, bf16[256,768]{1,0:T(8,128)(2,1)S(1)}, u32[]{:S(2)}, u32[]{:S(2)}) collective-permute-start(bf16[256,768]{1,0:T(8,128)(2,1)S(1)} %get-tuple-element.254), channel_id=1, source_target_pairs={{0,1},{1,0},{2,3},{3,2},{4,5},{5,4},{6,7},{7,6},{8,9},{9,8},{10,11... | collective-permute-start | bytes 1179656 | tf_op jit(solution)/shard_map/ppermute | solution.py:27
  494.4 2.7 add_convert_fusion.1
  498.0 13.6 %collective-permute-done.72 = bf16[192,896]{1,0:T(8,128)(2,1)S(1)} collective-permute-done((bf16[192,896]{1,0:T(8,128)(2,1)S(1)}, bf16[192,896]{1,0:T(8,128)(2,1)S(1)}, u32[]{:S(2)}, u32[]{:S(2)}) %collective-permute-start.72) | collective-permute-done | bytes 344096 | tf_op jit(solution)/shard_map/ppermute | solution.py:27
  513.9 9.3 %collective-permute-done.74.refs_2_ = bf16[192,896]{1,0:T(8,128)(2,1)} collective-permute-done((bf16[192,896]{1,0:T(8,128)(2,1)S(1)}, bf16[192,896]{1,0:T(8,128)(2,1)}, u32[]{:S(2)}, u32[]{:S(2)}) %collective-permute-start.74) | collective-permute-done | bytes 344096 | tf_op jit(solution)/shard_map/ppermute | solution.py:27
  523.9 4.9 collective-permute-done.76.refs_5_
  528.9 2.2 maximum_select_fusion
  531.1 5.6 finish.2
  541.5 2.2 add_convert_fusion
  544.8 2.7 collective-permute-start.62
  550.8 10.2 %collective-permute-done.56.far = bf16[512,768]{1,0:T(8,128)(2,1)S(1)} collective-permute-done((bf16[512,768]{1,0:T(8,128)(2,1)S(1)}, bf16[512,768]{1,0:T(8,128)(2,1)S(1)}, u32[]{:S(2)}, u32[]{:S(2)}) %collective-permute-start.56) | collective-permute-done | bytes 786464 | tf_op jit(solution)/shard_map/ppermute | solution.py:27
  561.0 4.5 norm_backward.3
  566.0 2.8 collective-permute-start.59
  568.8 8.9 %collective-permute-done.62 = bf16[96,1664]{1,0:T(8,128)(2,1)S(1)} collective-permute-done((bf16[96,1664]{1,0:T(8,128)(2,1)}, bf16[96,1664]{1,0:T(8,128)(2,1)S(1)}, u32[]{:S(2)}, u32[]{:S(2)}) %collective-permute-start.62) | collective-permute-done | bytes 319520 | tf_op jit(solution)/shard_map/ppermute | solution.py:925
  579.9 3.8 collective-permute-done.58
  588.9 2.9 collective-permute-done.64.refs_5_
  596.6 5.7 finish.3
  (509 shorter events, 136.2 us)
Async XLA Ops:
  7.2 45.4 %all-gather.4.cloned.1.call-start = ((), (), s32[]{:S(2)}) async-start(), calls=%async_computation.3 | async-start | bytes 1720320 | tf_op jit(solution)/shard_map/all_gather | solution.py:908
  9.2 15.4 %collective-permute-start = (bf16[256,768]{1,0:T(8,128)(2,1)}, bf16[256,768]{1,0:T(8,128)(2,1)}, u32[]{:S(2)}, u32[]{:S(2)}) collective-permute-start(bf16[256,768]{1,0:T(8,128)(2,1)} %get-tuple-element.268), channel_id=1, source_target_pairs={{0,1},{1,0},{2,3},{3,2},{4,5},{5,4},{6,7},{7,6},{8,9},{9,8},{10,11... | collective-permute-start | bytes 1179656 | tf_op jit(solution)/shard_map/ppermute | solution.py:27
  18.4 70.8 %all-gather.6.cloned.1.call-start = ((), (), s32[]{:S(2)}) async-start(), calls=%async_computation.4 | async-start | bytes 1597440 | tf_op jit(solution)/shard_map/all_gather | solution.py:908
  19.2 15.2 %collective-permute-start.10 = (bf16[256,768]{1,0:T(8,128)(2,1)}, bf16[256,768]{1,0:T(8,128)(2,1)}, u32[]{:S(2)}, u32[]{:S(2)}) collective-permute-start(bf16[256,768]{1,0:T(8,128)(2,1)} %get-tuple-element.260), channel_id=1, source_target_pairs={{0,1},{1,0},{2,3},{3,2},{4,5},{5,4},{6,7},{7,6},{8,9},{9,8},{10,11... | collective-permute-start | bytes 1179656 | tf_op jit(solution)/shard_map/ppermute | solution.py:27
  27.2 19.0 %collective-permute-start.2 = (bf16[512,768]{1,0:T(8,128)(2,1)S(1)}, bf16[512,768]{1,0:T(8,128)(2,1)S(1)}, u32[]{:S(2)}, u32[]{:S(2)}) collective-permute-start(bf16[512,768]{1,0:T(8,128)(2,1)S(1)} %get-tuple-element.262.refs_0_), channel_id=1, source_target_pairs={{0,4},{4,0},{1,5},{5,1},{2,6},{6,2},{3,7},{7,3},{8,12},{12,8},{9,1... | collective-permute-start | bytes 2359304 | tf_op jit(solution)/shard_map/ppermute | solution.py:27
  34.4 22.1 %collective-permute-start.1 = (bf16[512,768]{1,0:T(8,128)(2,1)S(1)}, bf16[512,768]{1,0:T(8,128)(2,1)S(1)}, u32[]{:S(2)}, u32[]{:S(2)}) collective-permute-start(bf16[512,768]{1,0:T(8,128)(2,1)S(1)} %get-tuple-element.262.refs_0_), channel_id=1, source_target_pairs={{0,2},{2,0},{1,3},{3,1},{4,6},{6,4},{5,7},{7,5},{8,10},{10,8},{9,1... | collective-permute-start | bytes 2359304 | tf_op jit(solution)/shard_map/ppermute | solution.py:27
  46.2 10.4 %collective-permute-start.3 = (bf16[512,768]{1,0:T(8,128)(2,1)S(1)}, bf16[512,768]{1,0:T(8,128)(2,1)}, u32[]{:S(2)}, u32[]{:S(2)}) collective-permute-start(bf16[512,768]{1,0:T(8,128)(2,1)S(1)} %collective-permute-done.2.refs_2_), channel_id=1, source_target_pairs={{0,2},{2,0},{1,3},{3,1},{4,6},{6,4},{5,7},{7,5},{8,10},{10,8},{9,1... | collective-permute-start | bytes 2359304 | tf_op jit(solution)/shard_map/ppermute | solution.py:27
  56.6 89.3 %all-gather.8.cloned.1.call-start = ((), (), s32[]{:S(2)}) async-start(), calls=%async_computation.5 | async-start | bytes 3072000 | tf_op jit(solution)/shard_map/all_gather | solution.py:908
  79.2 10.0 %collective-permute-start.7 = (bf16[4,1,48,768]{3,2,0,1:T(8,128)(2,1)S(1)}, bf16[4,1,48,768]{3,2,0,1:T(8,128)(2,1)S(1)}, u32[]{:S(2)}, u32[]{:S(2)}) collective-permute-start(bf16[4,1,48,768]{3,2,0,1:T(8,128)(2,1)S(1)} %reshape.199), channel_id=1, source_target_pairs={{0,2},{2,0},{1,3},{3,1},{4,6},{6,4},{5,7},{7,5},{8,10},{10,8},{9,1... | collective-permute-start | bytes 884744 | tf_op jit(solution)/shard_map/ppermute | solution.py:27
  79.3 9.9 %collective-permute-start.8 = (bf16[4,1,48,768]{3,2,0,1:T(8,128)(2,1)S(1)}, bf16[4,1,48,768]{3,2,0,1:T(8,128)(2,1)S(1)}, u32[]{:S(2)}, u32[]{:S(2)}) collective-permute-start(bf16[4,1,48,768]{3,2,0,1:T(8,128)(2,1)S(1)} %reshape.199), channel_id=1, source_target_pairs={{0,4},{4,0},{1,5},{5,1},{2,6},{6,2},{3,7},{7,3},{8,12},{12,8},{9,1... | collective-permute-start | bytes 884744 | tf_op jit(solution)/shard_map/ppermute | solution.py:27
  81.7 9.1 %collective-permute-start.4 = (bf16[192,512]{1,0:T(8,128)(2,1)}, bf16[192,512]{1,0:T(8,128)(2,1)S(1)}, u32[]{:S(2)}, u32[]{:S(2)}) collective-permute-start(bf16[192,512]{1,0:T(8,128)(2,1)} %get-tuple-element.265), channel_id=1, source_target_pairs={{0,2},{2,0},{1,3},{3,1},{4,6},{6,4},{5,7},{7,5},{8,10},{10,8},{9,1... | collective-permute-start | bytes 589832 | tf_op jit(solution)/shard_map/ppermute | solution.py:27
  81.9 11.5 %collective-permute-start.5 = (bf16[192,512]{1,0:T(8,128)(2,1)}, bf16[192,512]{1,0:T(8,128)(2,1)S(1)}, u32[]{:S(2)}, u32[]{:S(2)}) collective-permute-start(bf16[192,512]{1,0:T(8,128)(2,1)} %get-tuple-element.264), channel_id=1, source_target_pairs={{0,4},{4,0},{1,5},{5,1},{2,6},{6,2},{3,7},{7,3},{8,12},{12,8},{9,1... | collective-permute-start | bytes 589832 | tf_op jit(solution)/shard_map/ppermute | solution.py:27
  82.4 14.3 %collective-permute-start.6 = (bf16[192,512]{1,0:T(8,128)(2,1)S(1)}, bf16[192,512]{1,0:T(8,128)(2,1)S(1)}, u32[]{:S(2)}, u32[]{:S(2)}) collective-permute-start(bf16[192,512]{1,0:T(8,128)(2,1)S(1)} %get-tuple-element.263), channel_id=1, source_target_pairs={{0,6},{2,4},{4,2},{6,0},{1,7},{3,5},{5,3},{7,1},{8,14},{10,12},{12... | collective-permute-start | bytes 589832 | tf_op jit(solution)/shard_map/ppermute | solution.py:830
  89.2 352.6 %reduce-scatter.4.cloned.1.call-start = ((), (), s32[]{:S(2)}) async-start(), calls=%async_computation.6 | async-start | bytes 1720320 | tf_op jit(solution)/shard_map/reduce_scatter | solution.py:1066
  96.7 18.9 %collective-permute-start.11 = (bf16[384,1664]{1,0:T(8,128)(2,1)}, bf16[384,1664]{1,0:T(8,128)(2,1)}, u32[]{:S(2)}, u32[]{:S(2)}) collective-permute-start(bf16[384,1664]{1,0:T(8,128)(2,1)} %all-gather.6.cloned.1.call-done.refs_0_), channel_id=1, source_target_pairs={{0,4},{1,5},{2,3},{3,2},{4,0},{5,1},{6,7},{7,6},{8,12},{9,13},{10,... | collective-permute-start | bytes 3833864 | tf_op jit(solution)/shard_map/ppermute | solution.py:822
  104.9 27.3 %collective-permute-start.12 = (bf16[384,1664]{1,0:T(8,128)(2,1)}, bf16[384,1664]{1,0:T(8,128)(2,1)}, u32[]{:S(2)}, u32[]{:S(2)}) collective-permute-start(bf16[384,1664]{1,0:T(8,128)(2,1)} %all-gather.6.cloned.1.call-done.refs_0_), channel_id=1, source_target_pairs={{0,1},{1,0},{2,6},{3,7},{4,5},{5,4},{6,2},{7,3},{8,9},{9,8},{10,14... | collective-permute-start | bytes 3833864 | tf_op jit(solution)/shard_map/ppermute | solution.py:822
  115.6 30.3 %collective-permute-start.13 = (bf16[384,1664]{1,0:T(8,128)(2,1)}, bf16[384,1664]{1,0:T(8,128)(2,1)S(1)}, u32[]{:S(2)}, u32[]{:S(2)}) collective-permute-start(bf16[384,1664]{1,0:T(8,128)(2,1)} %collective-permute-done.11.refs_1_), channel_id=1, source_target_pairs={{0,1},{1,0},{2,6},{3,7},{4,5},{5,4},{6,2},{7,3},{8,9},{9,8},{10,14... | collective-permute-start | bytes 3833864 | tf_op jit(solution)/shard_map/ppermute | solution.py:822
  128.6 21.2 %collective-permute-start.14 = (bf16[384,1664]{1,0:T(8,128)(2,1)}, bf16[384,1664]{1,0:T(8,128)(2,1)}, u32[]{:S(2)}, u32[]{:S(2)}) collective-permute-start(bf16[384,1664]{1,0:T(8,128)(2,1)} %all-gather.6.cloned.1.call-done.refs_0_), channel_id=1, source_target_pairs={{0,2},{2,0},{1,3},{3,1},{4,6},{6,4},{5,7},{7,5},{8,10},{10,8},{9,1... | collective-permute-start | bytes 3833864 | tf_op jit(solution)/shard_map/ppermute | solution.py:27
  128.6 21.2 %collective-permute-start.15 = (bf16[384,1664]{1,0:T(8,128)(2,1)}, bf16[384,1664]{1,0:T(8,128)(2,1)}, u32[]{:S(2)}, u32[]{:S(2)}) collective-permute-start(bf16[384,1664]{1,0:T(8,128)(2,1)} %collective-permute-done.11.refs_1_), channel_id=1, source_target_pairs={{0,2},{2,0},{1,3},{3,1},{4,6},{6,4},{5,7},{7,5},{8,10},{10,8},{9,1... | collective-permute-start | bytes 3833864 | tf_op jit(solution)/shard_map/ppermute | solution.py:27
  132.2 17.6 %collective-permute-start.16 = (bf16[384,1664]{1,0:T(8,128)(2,1)}, bf16[384,1664]{1,0:T(8,128)(2,1)}, u32[]{:S(2)}, u32[]{:S(2)}) collective-permute-start(bf16[384,1664]{1,0:T(8,128)(2,1)} %collective-permute-done.12.refs_2_), channel_id=1, source_target_pairs={{0,2},{2,0},{1,3},{3,1},{4,6},{6,4},{5,7},{7,5},{8,10},{10,8},{9,1... | collective-permute-start | bytes 3833864 | tf_op jit(solution)/shard_map/ppermute | solution.py:27
  147.7 17.3 %collective-permute-start.18 = (bf16[384,1664]{1,0:T(8,128)(2,1)S(1)}, bf16[384,1664]{1,0:T(8,128)(2,1)S(1)}, u32[]{:S(2)}, u32[]{:S(2)}) collective-permute-start(bf16[384,1664]{1,0:T(8,128)(2,1)S(1)} %slice.486.refs_0_), channel_id=1, source_target_pairs={{0,4},{1,5},{2,3},{3,2},{4,0},{5,1},{6,7},{7,6},{8,12},{9,13},{10,... | collective-permute-start | bytes 3833864 | tf_op jit(solution)/shard_map/ppermute | solution.py:822
  165.0 19.8 %collective-permute-start.20 = (bf16[512,768]{1,0:T(8,128)(2,1)}, bf16[512,768]{1,0:T(8,128)(2,1)S(1)}, u32[]{:S(2)}, u32[]{:S(2)}) collective-permute-start(bf16[512,768]{1,0:T(8,128)(2,1)} %get-tuple-element.133.refs_0_), channel_id=1, source_target_pairs={{0,4},{4,0},{1,5},{5,1},{2,6},{6,2},{3,7},{7,3},{8,12},{12,8},{9,1... | collective-permute-start | bytes 2359304 | tf_op jit(solution)/shard_map/ppermute | solution.py:27
  166.5 22.8 %collective-permute-start.19 = (bf16[512,768]{1,0:T(8,128)(2,1)}, bf16[512,768]{1,0:T(8,128)(2,1)S(1)}, u32[]{:S(2)}, u32[]{:S(2)}) collective-permute-start(bf16[512,768]{1,0:T(8,128)(2,1)} %get-tuple-element.133.refs_0_), channel_id=1, source_target_pairs={{0,2},{2,0},{1,3},{3,1},{4,6},{6,4},{5,7},{7,5},{8,10},{10,8},{9,1... | collective-permute-start | bytes 2359304 | tf_op jit(solution)/shard_map/ppermute | solution.py:27
  191.5 23.4 %collective-permute-start.23 = (bf16[4,1,48,768]{3,2,0,1:T(8,128)(2,1)S(1)}, bf16[4,1,48,768]{3,2,0,1:T(8,128)(2,1)S(1)}, u32[]{:S(2)}, u32[]{:S(2)}) collective-permute-start(bf16[4,1,48,768]{3,2,0,1:T(8,128)(2,1)S(1)} %copy-done.47), channel_id=1, source_target_pairs={{0,4},{4,0},{1,5},{5,1},{2,6},{6,2},{3,7},{7,3},{8,12},{12,8},{9,1... | collective-permute-start | bytes 884744 | tf_op jit(solution)/shard_map/ppermute | solution.py:27
  193.0 23.6 %collective-permute-start.25 = (bf16[384,1664]{1,0:T(8,128)(2,1)}, bf16[384,1664]{1,0:T(8,128)(2,1)S(1)}, u32[]{:S(2)}, u32[]{:S(2)}) collective-permute-start(bf16[384,1664]{1,0:T(8,128)(2,1)} %copy-done.42), channel_id=1, source_target_pairs={{0,1},{1,0},{2,6},{3,7},{4,5},{5,4},{6,2},{7,3},{8,9},{9,8},{10,14... | collective-permute-start | bytes 3833864 | tf_op jit(solution)/shard_map/ppermute | solution.py:822
  194.3 29.9 %collective-permute-start.27 = (bf16[384,1664]{1,0:T(8,128)(2,1)}, bf16[384,1664]{1,0:T(8,128)(2,1)S(1)}, u32[]{:S(2)}, u32[]{:S(2)}) collective-permute-start(bf16[384,1664]{1,0:T(8,128)(2,1)} %copy-done.42), channel_id=1, source_target_pairs={{0,2},{2,0},{1,3},{3,1},{4,6},{6,4},{5,7},{7,5},{8,10},{10,8},{9,1... | collective-permute-start | bytes 3833864 | tf_op jit(solution)/shard_map/ppermute | solution.py:27
  194.3 29.9 %collective-permute-start.26 = (bf16[384,1664]{1,0:T(8,128)(2,1)}, bf16[384,1664]{1,0:T(8,128)(2,1)S(1)}, u32[]{:S(2)}, u32[]{:S(2)}) collective-permute-start(bf16[384,1664]{1,0:T(8,128)(2,1)} %copy-done.81), channel_id=1, source_target_pairs={{0,1},{1,0},{2,6},{3,7},{4,5},{5,4},{6,2},{7,3},{8,9},{9,8},{10,14... | collective-permute-start | bytes 3833864 | tf_op jit(solution)/shard_map/ppermute | solution.py:822
  195.1 29.1 %collective-permute-start.28 = (bf16[384,1664]{1,0:T(8,128)(2,1)}, bf16[384,1664]{1,0:T(8,128)(2,1)S(1)}, u32[]{:S(2)}, u32[]{:S(2)}) collective-permute-start(bf16[384,1664]{1,0:T(8,128)(2,1)} %copy-done.81), channel_id=1, source_target_pairs={{0,2},{2,0},{1,3},{3,1},{4,6},{6,4},{5,7},{7,5},{8,10},{10,8},{9,1... | collective-permute-start | bytes 3833864 | tf_op jit(solution)/shard_map/ppermute | solution.py:27
  229.4 8.8 %collective-permute-start.31 = (bf16[192,512]{1,0:T(8,128)(2,1)S(1)}, bf16[192,512]{1,0:T(8,128)(2,1)S(1)}, u32[]{:S(2)}, u32[]{:S(2)}) collective-permute-start(bf16[192,512]{1,0:T(8,128)(2,1)S(1)} %get-tuple-element.255), channel_id=1, source_target_pairs={{0,6},{2,4},{4,2},{6,0},{1,7},{3,5},{5,3},{7,1},{8,14},{10,12},{12... | collective-permute-start | bytes 589832 | tf_op jit(solution)/shard_map/ppermute | solution.py:830
  286.5 9.9 %collective-permute-start.35 = (bf16[192,512]{1,0:T(8,128)(2,1)S(1)}, bf16[192,512]{1,0:T(8,128)(2,1)S(1)}, u32[]{:S(2)}, u32[]{:S(2)}) collective-permute-start(bf16[192,512]{1,0:T(8,128)(2,1)S(1)} %copy-done.94), channel_id=1, source_target_pairs={{0,2},{2,0},{1,3},{3,1},{4,6},{6,4},{5,7},{7,5},{8,10},{10,8},{9,1... | collective-permute-start | bytes 589832 | tf_op jit(solution)/shard_map/ppermute | solution.py:27
  286.6 9.8 %collective-permute-start.36 = (bf16[192,512]{1,0:T(8,128)(2,1)S(1)}, bf16[192,512]{1,0:T(8,128)(2,1)S(1)}, u32[]{:S(2)}, u32[]{:S(2)}) collective-permute-start(bf16[192,512]{1,0:T(8,128)(2,1)S(1)} %copy-done.93), channel_id=1, source_target_pairs={{0,4},{4,0},{1,5},{5,1},{2,6},{6,2},{3,7},{7,3},{8,12},{12,8},{9,1... | collective-permute-start | bytes 589832 | tf_op jit(solution)/shard_map/ppermute | solution.py:27
  288.1 9.5 %collective-permute-start.37 = (bf16[192,512]{1,0:T(8,128)(2,1)S(1)}, bf16[192,512]{1,0:T(8,128)(2,1)S(1)}, u32[]{:S(2)}, u32[]{:S(2)}) collective-permute-start(bf16[192,512]{1,0:T(8,128)(2,1)S(1)} %copy-done.92), channel_id=1, source_target_pairs={{0,6},{2,4},{4,2},{6,0},{1,7},{3,5},{5,3},{7,1},{8,14},{10,12},{12... | collective-permute-start | bytes 589832 | tf_op jit(solution)/shard_map/ppermute | solution.py:830
  297.6 31.1 %collective-permute-start.40 = (bf16[768,1664]{1,0:T(8,128)(2,1)S(1)}, bf16[768,1664]{1,0:T(8,128)(2,1)}, u32[]{:S(2)}, u32[]{:S(2)}) collective-permute-start(bf16[768,1664]{1,0:T(8,128)(2,1)S(1)} %feed_weights.9), channel_id=1, source_target_pairs={{0,1},{1,0},{2,6},{3,7},{4,5},{5,4},{6,2},{7,3},{8,9},{9,8},{10,14... | collective-permute-start | bytes 7667720 | tf_op jit(solution)/shard_map/ppermute | solution.py:822
  339.4 23.1 %collective-permute-start.43 = (bf16[768,1664]{1,0:T(8,128)(2,1)}, bf16[768,1664]{1,0:T(8,128)(2,1)}, u32[]{:S(2)}, u32[]{:S(2)}) collective-permute-start(bf16[768,1664]{1,0:T(8,128)(2,1)} %feed_weights.10), channel_id=1, source_target_pairs={{0,2},{2,0},{1,3},{3,1},{4,6},{6,4},{5,7},{7,5},{8,10},{10,8},{9,1... | collective-permute-start | bytes 7667720 | tf_op jit(solution)/shard_map/ppermute | solution.py:27
  343.9 10.2 %collective-permute-start.49 = (bf16[4,48,768]{2,1,0:T(8,128)(2,1)}, bf16[4,48,768]{2,1,0:T(8,128)(2,1)}, u32[]{:S(2)}, u32[]{:S(2)}) collective-permute-start(bf16[4,48,768]{2,1,0:T(8,128)(2,1)} %fusion.7), channel_id=1, source_target_pairs={{0,4},{4,0},{1,5},{5,1},{2,6},{6,2},{3,7},{7,3},{8,12},{12,8},{9,1... | collective-permute-start | bytes 884744 | tf_op jit(solution)/shard_map/ppermute | solution.py:27
  345.5 24.8 %collective-permute-start.42 = (bf16[512,768]{1,0:T(8,128)(2,1)}, bf16[512,768]{1,0:T(8,128)(2,1)}, u32[]{:S(2)}, u32[]{:S(2)}) collective-permute-start(bf16[512,768]{1,0:T(8,128)(2,1)} %fusion.1), channel_id=1, source_target_pairs={{0,4},{4,0},{1,5},{5,1},{2,6},{6,2},{3,7},{7,3},{8,12},{12,8},{9,1... | collective-permute-start | bytes 2359304 | tf_op jit(solution)/shard_map/ppermute | solution.py:27
  362.4 122.4 %reduce-scatter.6.cloned.1.call-start = ((), (), s32[]{:S(2)}) async-start(), calls=%async_computation.7 | async-start | bytes 1597440 | tf_op jit(solution)/shard_map/reduce_scatter | solution.py:1076
  400.6 28.8 %collective-permute-start.47 = (bf16[768,1664]{1,0:T(8,128)(2,1)}, bf16[768,1664]{1,0:T(8,128)(2,1)}, u32[]{:S(2)}, u32[]{:S(2)}) collective-permute-start(bf16[768,1664]{1,0:T(8,128)(2,1)} %feed_weights.12), channel_id=1, source_target_pairs={{0,2},{2,0},{1,3},{3,1},{4,6},{6,4},{5,7},{7,5},{8,10},{10,8},{9,1... | collective-permute-start | bytes 7667720 | tf_op jit(solution)/shard_map/ppermute | solution.py:27
  405.4 31.0 %collective-permute-start.50 = (bf16[768,1664]{1,0:T(8,128)(2,1)}, bf16[768,1664]{1,0:T(8,128)(2,1)}, u32[]{:S(2)}, u32[]{:S(2)}) collective-permute-start(bf16[768,1664]{1,0:T(8,128)(2,1)} %feed_weights.14), channel_id=1, source_target_pairs={{0,2},{2,0},{1,3},{3,1},{4,6},{6,4},{5,7},{7,5},{8,10},{10,8},{9,1... | collective-permute-start | bytes 7667720 | tf_op jit(solution)/shard_map/ppermute | solution.py:27
  405.7 19.4 %collective-permute-start.53 = (bf16[384,1664]{1,0:T(8,128)(2,1)S(1)}, bf16[384,1664]{1,0:T(8,128)(2,1)S(1)}, u32[]{:S(2)}, u32[]{:S(2)}) collective-permute-start(bf16[384,1664]{1,0:T(8,128)(2,1)S(1)} %copy-done.43), channel_id=1, source_target_pairs={{0,4},{1,5},{2,3},{3,2},{4,0},{5,1},{6,7},{7,6},{8,12},{9,13},{10,... | collective-permute-start | bytes 3833864 | tf_op jit(solution)/shard_map/ppermute | solution.py:822
  411.9 29.8 %collective-permute-start.44 = (bf16[192,512]{1,0:T(8,128)(2,1)S(1)}, bf16[192,512]{1,0:T(8,128)(2,1)S(1)}, u32[]{:S(2)}, u32[]{:S(2)}) collective-permute-start(bf16[192,512]{1,0:T(8,128)(2,1)S(1)} %copy-done.90), channel_id=1, source_target_pairs={{0,2},{2,0},{1,3},{3,1},{4,6},{6,4},{5,7},{7,5},{8,10},{10,8},{9,1... | collective-permute-start | bytes 589832 | tf_op jit(solution)/shard_map/ppermute | solution.py:27
  413.5 28.3 %collective-permute-start.45 = (bf16[192,512]{1,0:T(8,128)(2,1)S(1)}, bf16[192,512]{1,0:T(8,128)(2,1)}, u32[]{:S(2)}, u32[]{:S(2)}) collective-permute-start(bf16[192,512]{1,0:T(8,128)(2,1)S(1)} %copy-done.89), channel_id=1, source_target_pairs={{0,4},{4,0},{1,5},{5,1},{2,6},{6,2},{3,7},{7,3},{8,12},{12,8},{9,1... | collective-permute-start | bytes 589832 | tf_op jit(solution)/shard_map/ppermute | solution.py:27
  425.1 16.7 %collective-permute-start.46 = (bf16[192,512]{1,0:T(8,128)(2,1)S(1)}, bf16[192,512]{1,0:T(8,128)(2,1)}, u32[]{:S(2)}, u32[]{:S(2)}) collective-permute-start(bf16[192,512]{1,0:T(8,128)(2,1)S(1)} %copy-done.88), channel_id=1, source_target_pairs={{0,6},{2,4},{4,2},{6,0},{1,7},{3,5},{5,3},{7,1},{8,14},{10,12},{12... | collective-permute-start | bytes 589832 | tf_op jit(solution)/shard_map/ppermute | solution.py:830
  429.3 107.4 %reduce-scatter.8.cloned.1.call-start = ((), (), s32[]{:S(2)}) async-start(), calls=%async_computation.8 | async-start | bytes 1720320 | tf_op jit(solution)/shard_map/reduce_scatter | solution.py:1066
  429.4 12.4 %collective-permute-start.51 = (bf16[4,48,768]{2,1,0:T(8,128)(2,1)S(1)}, bf16[4,48,768]{2,1,0:T(8,128)(2,1)S(1)}, u32[]{:S(2)}, u32[]{:S(2)}) collective-permute-start(bf16[4,48,768]{2,1,0:T(8,128)(2,1)S(1)} %fusion.6), channel_id=1, source_target_pairs={{0,4},{4,0},{1,5},{5,1},{2,6},{6,2},{3,7},{7,3},{8,12},{12,8},{9,1... | collective-permute-start | bytes 884744 | tf_op jit(solution)/shard_map/ppermute | solution.py:27
  441.8 43.0 %collective-permute-start.52 = (bf16[768,1664]{1,0:T(8,128)(2,1)}, bf16[768,1664]{1,0:T(8,128)(2,1)}, u32[]{:S(2)}, u32[]{:S(2)}) collective-permute-start(bf16[768,1664]{1,0:T(8,128)(2,1)} %copy-done.16), channel_id=1, source_target_pairs={{0,1},{1,0},{2,6},{3,7},{4,5},{5,4},{6,2},{7,3},{8,9},{9,8},{10,14... | collective-permute-start | bytes 7667720 | tf_op jit(solution)/shard_map/ppermute | solution.py:822
  484.8 53.9 %collective-permute-start.54 = (bf16[2,512,768]{2,1,0:T(8,128)(2,1)}, bf16[2,512,768]{2,1,0:T(8,128)(2,1)}, u32[]{:S(2)}, u32[]{:S(2)}) collective-permute-start(bf16[2,512,768]{2,1,0:T(8,128)(2,1)} %get-tuple-element.205), channel_id=1, source_target_pairs={{0,2},{2,0},{1,3},{3,1},{4,6},{6,4},{5,7},{7,5},{8,10},{10,8},{9,1... | collective-permute-start | bytes 4718600 | tf_op jit(solution)/shard_map/ppermute | solution.py:27
  485.7 27.0 %collective-permute-start.34 = (bf16[256,768]{1,0:T(8,128)(2,1)S(1)}, bf16[256,768]{1,0:T(8,128)(2,1)S(1)}, u32[]{:S(2)}, u32[]{:S(2)}) collective-permute-start(bf16[256,768]{1,0:T(8,128)(2,1)S(1)} %get-tuple-element.254), channel_id=1, source_target_pairs={{0,1},{1,0},{2,3},{3,2},{4,5},{5,4},{6,7},{7,6},{8,9},{9,8},{10,11... | collective-permute-start | bytes 1179656 | tf_op jit(solution)/shard_map/ppermute | solution.py:27
  494.3 17.3 %collective-permute-start.72 = (bf16[192,896]{1,0:T(8,128)(2,1)S(1)}, bf16[192,896]{1,0:T(8,128)(2,1)S(1)}, u32[]{:S(2)}, u32[]{:S(2)}) collective-permute-start(bf16[192,896]{1,0:T(8,128)(2,1)S(1)} %copy-done.62), channel_id=1, source_target_pairs={{0,1},{1,0},{2,3},{3,2},{4,5},{5,4},{6,7},{7,6},{8,9},{9,8},{10,11... | collective-permute-start | bytes 1032200 | tf_op jit(solution)/shard_map/ppermute | solution.py:27
  497.1 43.5 %collective-permute-start.55 = (bf16[384,1664]{1,0:T(8,128)(2,1)}, bf16[384,1664]{1,0:T(8,128)(2,1)}, u32[]{:S(2)}, u32[]{:S(2)}) collective-permute-start(bf16[384,1664]{1,0:T(8,128)(2,1)} %add_convert_fusion.1), channel_id=1, source_target_pairs={{0,4},{1,5},{2,3},{3,2},{4,0},{5,1},{6,7},{7,6},{8,12},{9,13},{10,... | collective-permute-start | bytes 3833864 | tf_op jit(solution)/shard_map/ppermute | solution.py:822
  511.7 11.5 %collective-permute-start.74 = (bf16[192,896]{1,0:T(8,128)(2,1)S(1)}, bf16[192,896]{1,0:T(8,128)(2,1)}, u32[]{:S(2)}, u32[]{:S(2)}) collective-permute-start(bf16[192,896]{1,0:T(8,128)(2,1)S(1)} %add_convert_fusion.4.refs_0_), channel_id=1, source_target_pairs={{0,4},{4,0},{1,5},{5,1},{2,6},{6,2},{3,7},{7,3},{8,12},{12,8},{9,1... | collective-permute-start | bytes 1032200 | tf_op jit(solution)/shard_map/ppermute | solution.py:27
  512.7 10.5 %collective-permute-start.73 = (bf16[192,896]{1,0:T(8,128)(2,1)S(1)}, bf16[192,896]{1,0:T(8,128)(2,1)S(1)}, u32[]{:S(2)}, u32[]{:S(2)}) collective-permute-start(bf16[192,896]{1,0:T(8,128)(2,1)S(1)} %add_convert_fusion.4.refs_0_), channel_id=1, source_target_pairs={{0,2},{2,0},{1,3},{3,1},{4,6},{6,4},{5,7},{7,5},{8,10},{10,8},{9,1... | collective-permute-start | bytes 1032200 | tf_op jit(solution)/shard_map/ppermute | solution.py:27
  512.7 16.2 %collective-permute-start.76 = (bf16[96,1664]{1,0:T(8,128)(2,1)}, bf16[96,1664]{1,0:T(8,128)(2,1)}, u32[]{:S(2)}, u32[]{:S(2)}) collective-permute-start(bf16[96,1664]{1,0:T(8,128)(2,1)} %reduce-scatter.6.cloned.1.call-done.refs_4_), channel_id=1, source_target_pairs={{0,4},{4,0},{1,5},{5,1},{2,6},{6,2},{3,7},{7,3},{8,12},{12,8},{9,1... | collective-permute-start | bytes 958472 | tf_op jit(solution)/shard_map/ppermute | solution.py:27
  523.2 8.0 %collective-permute-start.75 = (bf16[192,896]{1,0:T(8,128)(2,1)}, bf16[192,896]{1,0:T(8,128)(2,1)}, u32[]{:S(2)}, u32[]{:S(2)}) collective-permute-start(bf16[192,896]{1,0:T(8,128)(2,1)} %collective-permute-done.74.refs_2_), channel_id=1, source_target_pairs={{0,2},{2,0},{1,3},{3,1},{4,6},{6,4},{5,7},{7,5},{8,10},{10,8},{9,1... | collective-permute-start | bytes 1032200 | tf_op jit(solution)/shard_map/ppermute | solution.py:27
  523.2 7.9 %collective-permute-start.77 = (bf16[96,1664]{1,0:T(8,128)(2,1)}, bf16[96,1664]{1,0:T(8,128)(2,1)}, u32[]{:S(2)}, u32[]{:S(2)}) collective-permute-start(bf16[96,1664]{1,0:T(8,128)(2,1)} %reduce-scatter.6.cloned.1.call-done.refs_4_), channel_id=1, source_target_pairs={{0,2},{2,0},{1,3},{3,1},{4,6},{6,4},{5,7},{7,5},{8,10},{10,8},{9,1... | collective-permute-start | bytes 958472 | tf_op jit(solution)/shard_map/ppermute | solution.py:27
  536.8 12.8 %collective-permute-start.68 = (bf16[192,896]{1,0:T(8,128)(2,1)}, bf16[192,896]{1,0:T(8,128)(2,1)S(1)}, u32[]{:S(2)}, u32[]{:S(2)}) collective-permute-start(bf16[192,896]{1,0:T(8,128)(2,1)} %reduce-scatter.8.cloned.1.call-done), channel_id=1, source_target_pairs={{0,1},{1,0},{2,3},{3,2},{4,5},{5,4},{6,7},{7,6},{8,9},{9,8},{10,11... | collective-permute-start | bytes 1032200 | tf_op jit(solution)/shard_map/ppermute | solution.py:27
  540.5 20.4 %collective-permute-start.56 = (bf16[512,768]{1,0:T(8,128)(2,1)S(1)}, bf16[512,768]{1,0:T(8,128)(2,1)S(1)}, u32[]{:S(2)}, u32[]{:S(2)}) collective-permute-start(bf16[512,768]{1,0:T(8,128)(2,1)S(1)} %fusion), channel_id=1, source_target_pairs={{0,4},{4,0},{1,5},{5,1},{2,6},{6,2},{3,7},{7,3},{8,12},{12,8},{9,1... | collective-permute-start | bytes 2359304 | tf_op jit(solution)/shard_map/ppermute | solution.py:27
  544.8 21.2 %collective-permute-start.63 = (bf16[96,1664]{1,0:T(8,128)(2,1)}, bf16[96,1664]{1,0:T(8,128)(2,1)S(1)}, u32[]{:S(2)}, u32[]{:S(2)}) collective-permute-start(bf16[96,1664]{1,0:T(8,128)(2,1)} %get-tuple-element.233), channel_id=1, source_target_pairs={{0,24},{8,0},{16,8},{24,16},{1,25},{9,1},{17,9},{25,17},{2,26},{10... | collective-permute-start | bytes 958472 | tf_op jit(solution)/shard_map/ppermute | solution.py:925
  544.8 32.9 %collective-permute-start.62 = (bf16[96,1664]{1,0:T(8,128)(2,1)}, bf16[96,1664]{1,0:T(8,128)(2,1)S(1)}, u32[]{:S(2)}, u32[]{:S(2)}) collective-permute-start(bf16[96,1664]{1,0:T(8,128)(2,1)} %get-tuple-element.234), channel_id=1, source_target_pairs={{0,16},{8,24},{16,0},{24,8},{1,17},{9,25},{17,1},{25,9},{2,18},{10... | collective-permute-start | bytes 958472 | tf_op jit(solution)/shard_map/ppermute | solution.py:925
  547.5 30.9 %collective-permute-start.61 = (bf16[96,1664]{1,0:T(8,128)(2,1)}, bf16[96,1664]{1,0:T(8,128)(2,1)}, u32[]{:S(2)}, u32[]{:S(2)}) collective-permute-start(bf16[96,1664]{1,0:T(8,128)(2,1)} %get-tuple-element.232), channel_id=1, source_target_pairs={{0,8},{8,16},{16,24},{24,0},{1,9},{9,17},{17,25},{25,1},{2,10},{10... | collective-permute-start | bytes 958472 | tf_op jit(solution)/shard_map/ppermute | solution.py:925
  549.6 38.7 %collective-permute-start.70 = (bf16[192,896]{1,0:T(8,128)(2,1)S(1)}, bf16[192,896]{1,0:T(8,128)(2,1)S(1)}, u32[]{:S(2)}, u32[]{:S(2)}) collective-permute-start(bf16[192,896]{1,0:T(8,128)(2,1)S(1)} %add_convert_fusion.5.refs_0_), channel_id=1, source_target_pairs={{0,4},{4,0},{1,5},{5,1},{2,6},{6,2},{3,7},{7,3},{8,12},{12,8},{9,1... | collective-permute-start | bytes 1032200 | tf_op jit(solution)/shard_map/ppermute | solution.py:27
  565.9 13.9 %collective-permute-start.60 = (f32[96,128]{1,0:T(8,128)S(1)}, f32[96,128]{1,0:T(8,128)S(1)}, u32[]{:S(2)}, u32[]{:S(2)}) collective-permute-start(f32[96,128]{1,0:T(8,128)S(1)} %get-tuple-element.284), channel_id=1, source_target_pairs={{0,24},{8,0},{16,8},{24,16},{1,25},{9,1},{17,9},{25,17},{2,26},{10... | collective-permute-start | bytes 147464 | tf_op jit(solution)/shard_map/ppermute | solution.py:925
  566.0 13.8 %collective-permute-start.59 = (f32[96,128]{1,0:T(8,128)S(1)}, f32[96,128]{1,0:T(8,128)S(1)}, u32[]{:S(2)}, u32[]{:S(2)}) collective-permute-start(f32[96,128]{1,0:T(8,128)S(1)} %get-tuple-element.285), channel_id=1, source_target_pairs={{0,16},{8,24},{16,0},{24,8},{1,17},{9,25},{17,1},{25,9},{2,18},{10... | collective-permute-start | bytes 147464 | tf_op jit(solution)/shard_map/ppermute | solution.py:925
  585.3 8.9 %collective-permute-start.57 = (bf16[256,768]{1,0:T(8,128)(2,1)S(1)}, bf16[256,768]{1,0:T(8,128)(2,1)S(1)}, u32[]{:S(2)}, u32[]{:S(2)}) collective-permute-start(bf16[256,768]{1,0:T(8,128)(2,1)S(1)} %get-tuple-element.252), channel_id=1, source_target_pairs={{0,1},{1,0},{2,3},{3,2},{4,5},{5,4},{6,7},{7,6},{8,9},{9,8},{10,11... | collective-permute-start | bytes 1179656 | tf_op jit(solution)/shard_map/ppermute | solution.py:27
  (121 other events, 1221.0 us)
Sparse Core Ops, SparseCore 0:
  18.5 34.0 all-gather.3
  56.7 31.0 all-gather.5
  89.9 55.7 all-gather.7
  362.5 35.4 reduce-scatter.3
  429.4 33.2 reduce-scatter.5
  483.2 39.2 reduce-scatter.7

commit v3 on v2

--- a/solution.py
+++ b/solution.py
@@ -88,7 +88,7 @@
             values = a_ref[part, rows, :]
             if norm:
                 values = norm_rows(values.astype(F32), gain_ref[...], shift_ref[...]).astype(BF16)
-            found = dot(values, w_ref[...]) + bias_ref[...]
+            found = dot(values, w_ref[:, 0:576]) + bias_ref[...]
             at_ref[:, goal] = values.T
             qkv_ref[goal, 0:384] = found[:, 0:384].astype(BF16)
             qkv_ref[goal, 384:576] = (found[:, 384:576] * HEAD**-0.5).astype(BF16)
@@ -332,7 +332,7 @@
     plan = ((1, core_ref.at[0], core_out.at[0]), (3, core_ref.at[1], core_out.at[1]), (2, far_ref, far_out), (0, own_ref, own_out))
     for at, (part, target, goal) in enumerate(plan):
         kind = target.dtype
-        target[...] = dot(du_ref[part * each : (part + 1) * each, :], w_ref[...], ((1,), (1,))).astype(kind)
+        target[...] = dot(du_ref[part * each : (part + 1) * each, :], w_ref[:, 0:576], ((1,), (1,))).astype(kind)
         copies.append(pltpu.make_async_copy(target, goal, sems.at[at + 1]))
         copies[-1].start()
     for copy in copies:
@@ -462,39 +462,43 @@
     return grad_in, jnp.sum(grad * normed, axis=0, keepdims=True), jnp.sum(grad, axis=0, keepdims=True)
 
 
-def norm_back_kernel(own, core, far, x_ref, gain_ref, mid_ref, grad_ref, sums_ref):
+def norm_back_kernel(own, core, far, x_ref, gain_ref, mid_ref, grad_ref, low_ref, sums_ref):
     toks, width = x_ref.shape
+    step = pl.program_id(0)
+
+    @pl.when(step == 0)
+    def _():
+        sums_ref[...] = jnp.zeros_like(sums_ref)
 
     def rows_of(at, sums):
         rows = pl.ds(pl.multiple_of(at * 64, 64), 64)
         found = own[rows, :] + core[0, rows, :].astype(F32) + far[rows, :].astype(F32)
         grad_in, gain_sum, bias_sum = norm_back(found, x_ref[rows, :], gain_ref[...])
-        grad_ref[rows, :] = mid_ref[rows, :] + grad_in
+        grad = mid_ref[rows, :] + grad_in
+        grad_ref[rows, :] = grad
+        low_ref[rows, :] = grad.astype(BF16)
         return sums[0] + gain_sum, sums[1] + bias_sum
 
     zero = jnp.zeros((1, width), F32)
     sums = lax.fori_loop(0, toks // 64, rows_of, (zero, zero))
-    sums_ref[...] = jnp.zeros_like(sums_ref)
-    sums_ref[0:1, :] = sums[0]
-    sums_ref[1:2, :] = sums[1]
+    sums_ref[0:1, :] += sums[0]
+    sums_ref[1:2, :] += sums[1]
 
 
 def norm_backward(own, core, far, values, gain, middle_grad):
     toks, width = values.shape
+    rows = pl.BlockSpec((toks // 4, width), lambda i: (i, 0))
     return pl.pallas_call(
         norm_back_kernel,
         name="norm_backward",
-        grid=(1,),
-        in_specs=[
-            whole((toks, width)),
-            pl.BlockSpec((1, toks, width), lambda i: (0, 0, 0)),
-            whole((toks, width)),
-            whole((toks, width)),
-            whole(gain.shape),
-            whole((toks, width)),
-        ],
-        out_specs=[whole((toks, width)), whole((8, width))],
-        out_shape=(jax.ShapeDtypeStruct((toks, width), F32), jax.ShapeDtypeStruct((8, width), F32)),
+        grid=(4,),
+        in_specs=[rows, pl.BlockSpec((1, toks // 4, width), lambda i: (0, i, 0)), rows, rows, whole(gain.shape), rows],
+        out_specs=[rows, rows, whole((8, width))],
+        out_shape=(
+            jax.ShapeDtypeStruct((toks, width), F32),
+            jax.ShapeDtypeStruct((toks, width), BF16),
+            jax.ShapeDtypeStruct((8, width), F32),
+        ),
         compiler_params=pltpu.CompilerParams(vmem_limit_bytes=48 << 20),
         cost_estimate=pl.CostEstimate(flops=10**7, transcendentals=0, bytes_accessed=9 << 20),
     )(own, core, far, values, gain, middle_grad)
@@ -524,14 +528,10 @@
     return copies
 
 
-def feed_kernel(norm, c_ref, mid_ref, vec_ref, *refs):
+def feed_kernel(c_ref, mid_ref, vec_ref, *refs):
     parts, refs = refs[:8], refs[8:]
-    if norm:
-        slope_out, act_out, x_ref, a_ref, slope_ref, act_ref, held, sems, out_sems = refs
-    else:
-        slope_out, act_out, x_ref, slope_ref, act_ref, held, sems, out_sems = refs
+    slope_out, own_out, other_out, x_ref, a_ref, slope_ref, act_ref, held, sems, out_sems = refs
     toks, width = mid_ref.shape
-    units = held.shape[1]
     copies = fetch(parts, held, sems)
     x_ref[...] = mid_ref[...] + vec_ref[0:1, :]
     outs = []
@@ -548,7 +548,8 @@
         slope_ref[at] = slope.astype(BF16)
         act_ref[at] = act.T
         outs.append(pltpu.make_async_copy(slope_ref.at[at], slope_out.at[at], out_sems.at[2 * at]))
-        outs.append(pltpu.make_async_copy(act_ref.at[at], act_out.at[at], out_sems.at[2 * at + 1]))
+        goal = (own_out, other_out)[at // 2].at[at % 2]
+        outs.append(pltpu.make_async_copy(act_ref.at[at], goal, out_sems.at[2 * at + 1]))
         outs[-2].start()
         outs[-1].start()
         x_ref[...] += dot(act, held[at, :, width : 2 * width])
@@ -559,35 +560,32 @@
         after(at, pre)
         pre = later
 
-    if norm:
-
-        def rows_of(at, nothing):
-            rows = pl.ds(pl.multiple_of(at * 64, 64), 64)
-            a_ref[rows, :] = norm_rows(x_ref[rows, :], vec_ref[1:2, :], vec_ref[2:3, :]).astype(BF16)
-            return nothing
-
-        lax.fori_loop(0, toks // 64, rows_of, 0)
+    def rows_of(at, nothing):
+        rows = pl.ds(pl.multiple_of(at * 64, 64), 64)
+        a_ref[rows, :] = norm_rows(x_ref[rows, :], vec_ref[1:2, :], vec_ref[2:3, :]).astype(BF16)
+        return nothing
+
+    lax.fori_loop(0, toks // 64, rows_of, 0)
     for copy in outs:
         copy.wait()
 
 
-def feed_forward(c, middle, vectors, parts, norm):
+def feed_forward(c, middle, vectors, parts):
     toks, width = middle.shape
     units = 2 * parts[0].shape[0]
-    out_shape = [
-        jax.ShapeDtypeStruct((4, toks, units), BF16),
-        jax.ShapeDtypeStruct((4, units, toks), BF16),
-        jax.ShapeDtypeStruct((toks, width), F32),
-    ]
-    if norm:
-        out_shape.append(jax.ShapeDtypeStruct((toks, width), BF16))
     return pl.pallas_call(
-        partial(feed_kernel, norm),
+        feed_kernel,
         name="feed_forward",
         grid=(1,),
         in_specs=[whole(c.shape), whole(middle.shape), whole(vectors.shape)] + [HBM] * 8,
-        out_specs=[HBM, HBM] + [whole(shape.shape) for shape in out_shape[2:]],
-        out_shape=out_shape,
+        out_specs=[HBM, HBM, HBM, whole((toks, width)), whole((toks, width))],
+        out_shape=[
+            jax.ShapeDtypeStruct((4, toks, units), BF16),
+            jax.ShapeDtypeStruct((2, units, toks), BF16),
+            jax.ShapeDtypeStruct((2, units, toks), BF16),
+            jax.ShapeDtypeStruct((toks, width), F32),
+            jax.ShapeDtypeStruct((toks, width), BF16),
+        ],
         scratch_shapes=[
             pltpu.VMEM((4, toks, units), BF16),
             pltpu.VMEM((4, units, toks), BF16),
@@ -600,42 +598,9 @@
     )(c, middle, vectors, *parts)
 
 
-def feed_back_kernel(info, grad_ref, slope_in, mid_ref, gain_ref, w_ref, *refs):
-    parts, refs = refs[:8], refs[8:]
-    dh_out, dm_ref, dmid_ref, da_ref, sums_ref, d0, d1, d2, d3 = refs[:9]
-    slope_ref, dh_ref, held, dc, sems, slope_sems, out_sems = refs[9:]
-    dev = info[3]
+def finish_back(dev, grad_ref, mid_ref, gain_ref, w_ref, dm_ref, dc, dmid_ref, da_ref, sums_ref, targets):
     toks, width = mid_ref.shape
-    loc = d0.shape[0]
-    copies = fetch(parts, held, sems)
-    slopes = [pltpu.make_async_copy(slope_in.at[at], slope_ref.at[at], slope_sems.at[at]) for at in range(4)]
-    for copy in slopes:
-        copy.start()
-    dm_ref[...] = grad_ref[...].astype(BF16)
-    outs = []
-
-    def before(at):
-        copies[2 * at].wait()
-        copies[2 * at + 1].wait()
-        return dot(dm_ref[...], held[at, :, width : 2 * width], ((1,), (1,)))
-
-    def after(at, dact):
-        slopes[at].wait()
-        dpre = (dact * slope_ref[at].astype(F32)).astype(BF16)
-        dh_ref[at] = dpre
-        outs.append(pltpu.make_async_copy(dh_ref.at[at], dh_out.at[at], out_sems.at[at]))
-        outs[-1].start()
-        term = dot(dpre, held[at, :, 0:width])
-        if at == 0:
-            dc[...] = term
-        else:
-            dc[...] += term
-
-    dact = before(0)
-    for at in range(4):
-        later = before(at + 1) if at < 3 else None
-        after(at, dact)
-        dact = later
+    loc = targets[0].shape[0]
 
     def rows_of(at, sums):
         rows = pl.ds(pl.multiple_of(at * 64, 64), 64)
@@ -653,94 +618,218 @@
     sums_ref[...] = jnp.zeros_like(sums_ref)
     for at in range(4):
         sums_ref[at : at + 1, :] = sums[at]
-    for rel, target in enumerate((d0, d1, d2, d3)):
+    for rel, target in enumerate(targets):
         rows = pl.ds(pl.multiple_of((dev ^ rel) * loc, 64), loc)
         target[...] = dot(w_ref[rows, :], da_ref[...], ((1,), (1,))).astype(BF16)
-    for copy in outs:
-        copy.wait()
-
-
-def feed_backward(info, grad, slope, middle, gain, w_out, parts):
-    toks, width = middle.shape
-    loc = width // 4
-    units = 2 * parts[0].shape[0]
-    shapes = [
-        jax.ShapeDtypeStruct(slope.shape, BF16),
-        jax.ShapeDtypeStruct((toks, width), BF16),
+
+
+def back_outputs(toks, width, units):
+    return [
+        jax.ShapeDtypeStruct((2, toks, units), BF16),
+        jax.ShapeDtypeStruct((2, toks, units), BF16),
         jax.ShapeDtypeStruct((toks, width), F32),
         jax.ShapeDtypeStruct((toks, width), BF16),
         jax.ShapeDtypeStruct((8, width), F32),
-    ] + [jax.ShapeDtypeStruct((loc, toks), BF16)] * 4
+    ] + [jax.ShapeDtypeStruct((width // 4, toks), BF16)] * 4
+
+
+def feed_back_kernel(info, grad_ref, dm_ref, slope_in, mid_in, gain_ref, w_in, *refs):
+    parts, refs = refs[:8], refs[8:]
+    own_out, other_out, dmid_ref, da_ref, sums_ref, *targets = refs[:9]
+    slope_ref, dh_ref, held, dc, mid_ref, w_ref, sems, slope_sems, out_sems, in_sems = refs[9:]
+    width = mid_ref.shape[1]
+    copies = fetch(parts, held, sems)
+    slopes = [pltpu.make_async_copy(slope_in.at[at], slope_ref.at[at], slope_sems.at[at]) for at in range(4)]
+    late_in = [pltpu.make_async_copy(mid_in, mid_ref, in_sems.at[0]), pltpu.make_async_copy(w_in, w_ref, in_sems.at[1])]
+    for copy in slopes + late_in:
+        copy.start()
+    outs = []
+    goals = (own_out.at[0], own_out.at[1], other_out.at[0], other_out.at[1])
+
+    def before(at):
+        copies[2 * at].wait()
+        copies[2 * at + 1].wait()
+        return dot(dm_ref[...], held[at, :, width : 2 * width], ((1,), (1,)))
+
+    def after(at, dact):
+        slopes[at].wait()
+        dpre = (dact * slope_ref[at].astype(F32)).astype(BF16)
+        dh_ref[at] = dpre
+        outs.append(pltpu.make_async_copy(dh_ref.at[at], goals[at], out_sems.at[at]))
+        outs[-1].start()
+        term = dot(dpre, held[at, :, 0:width])
+        if at == 0:
+            dc[...] = term
+        else:
+            dc[...] += term
+
+    dact = before(0)
+    for at in range(4):
+        later = before(at + 1) if at < 3 else None
+        after(at, dact)
+        dact = later
+    for copy in late_in:
+        copy.wait()
+    finish_back(info[3], grad_ref, mid_ref, gain_ref, w_ref, dm_ref, dc, dmid_ref, da_ref, sums_ref, targets)
+    for copy in outs:
+        copy.wait()
+
+
+def feed_backward(info, grad, dm, slope, middle, gain, w_out, parts):
+    toks, width = middle.shape
+    units = 2 * parts[0].shape[0]
+    shapes = back_outputs(toks, width, units)
     return pl.pallas_call(
         feed_back_kernel,
         name="feed_backward",
         grid_spec=pltpu.PrefetchScalarGridSpec(
             num_scalar_prefetch=1,
             grid=(1,),
-            in_specs=[whole(grad.shape), HBM, whole(middle.shape), whole(gain.shape), whole(w_out.shape)] + [HBM] * 8,
-            out_specs=[HBM] + [whole(shape.shape) for shape in shapes[1:]],
+            in_specs=[whole(grad.shape), whole(dm.shape), HBM, HBM, whole(gain.shape), HBM] + [HBM] * 8,
+            out_specs=[HBM] * 2 + [whole(shape.shape) for shape in shapes[2:]],
             scratch_shapes=[
                 pltpu.VMEM((4, toks, units), BF16),
                 pltpu.VMEM((4, toks, units), BF16),
                 pltpu.VMEM((4, units, parts[0].shape[1]), BF16),
                 pltpu.VMEM((toks, width), F32),
+                pltpu.VMEM((toks, width), F32),
+                pltpu.VMEM((width, width), BF16),
                 pltpu.SemaphoreType.DMA((8,)),
                 pltpu.SemaphoreType.DMA((4,)),
                 pltpu.SemaphoreType.DMA((4,)),
+                pltpu.SemaphoreType.DMA((2,)),
             ],
         ),
         out_shape=shapes,
         compiler_params=pltpu.CompilerParams(vmem_limit_bytes=60 << 20),
         cost_estimate=pl.CostEstimate(flops=6 * 10**9, transcendentals=2 * 10**6, bytes_accessed=24 << 20),
-    )(info, grad, slope, middle, gain, w_out, *parts)
-
-
-def feed_weights_kernel(add, dh_ref, act_ref, c_ref, dm_ref, *refs):
-    width = c_ref.shape[1]
-    out_ref = refs[-1]
-    dh = dh_ref[0].T
-    up = dot(dh, c_ref[...])
-    down = dot(act_ref[0], dm_ref[...])
-    bias = jnp.broadcast_to(jnp.sum(dh.astype(F32), axis=1, keepdims=True), (dh.shape[0], 128))
-    if add:
-        up = up + refs[0][:, 0:width].astype(F32)
-        down = down + refs[0][:, width : 2 * width].astype(F32)
-        bias = bias + refs[0][:, 2 * width :].astype(F32)
-    out_ref[:, 0:width] = up.astype(BF16)
-    out_ref[:, width : 2 * width] = down.astype(BF16)
-    out_ref[:, 2 * width :] = bias.astype(BF16)
-
-
-def feed_weights(dh, act, c, dm, quarter, add=None):
-    units, toks, width = dh.shape[2], c.shape[0], c.shape[1]
+    )(info, grad, dm, slope, middle, gain, w_out, *parts)
+
+
+def feed_both_kernel(info, c_ref, grad_ref, dm_ref, mid_ref, vec_ref, w_in, *refs):
+    parts, refs = refs[:8], refs[8:]
+    own_out, other_out, dmid_ref, da_ref, sums_ref, *targets = refs[:9]
+    act_own, act_other, x_ref = refs[9:12]
+    act_ref, dh_ref, held, dc, w_ref, sems, out_sems, in_sem = refs[12:]
+    toks, width = mid_ref.shape
+    copies = fetch(parts, held, sems)
+    late_in = pltpu.make_async_copy(w_in, w_ref, in_sem.at[0])
+    late_in.start()
+    x_ref[...] = mid_ref[...] + vec_ref[0:1, :]
+    outs = []
+    goals = (own_out.at[0], own_out.at[1], other_out.at[0], other_out.at[1])
+
+    def before(at):
+        copies[2 * at].wait()
+        copies[2 * at + 1].wait()
+        bias = held[at, :, 2 * width : 2 * width + 128].T[0:1].astype(F32)
+        pre = dot(c_ref[...], held[at, :, 0:width], ((1,), (1,))) + bias
+        return pre, dot(dm_ref[...], held[at, :, width : 2 * width], ((1,), (1,)))
+
+    def after(at, found):
+        pre, dact = found
+        act, slope = gelu(pre)
+        act = act.astype(BF16)
+        act_ref[at] = act.T
+        dpre = (dact * slope).astype(BF16)
+        dh_ref[at] = dpre
+        goal = (act_own, act_other)[at // 2].at[at % 2]
+        outs.append(pltpu.make_async_copy(dh_ref.at[at], goals[at], out_sems.at[2 * at]))
+        outs.append(pltpu.make_async_copy(act_ref.at[at], goal, out_sems.at[2 * at + 1]))
+        outs[-2].start()
+        outs[-1].start()
+        x_ref[...] += dot(act, held[at, :, width : 2 * width])
+        term = dot(dpre, held[at, :, 0:width])
+        if at == 0:
+            dc[...] = term
+        else:
+            dc[...] += term
+
+    found = before(0)
+    for at in range(4):
+        later = before(at + 1) if at < 3 else None
+        after(at, found)
+        found = later
+    late_in.wait()
+    finish_back(info[3], grad_ref, mid_ref, vec_ref.at[1:2], w_ref, dm_ref, dc, dmid_ref, da_ref, sums_ref, targets)
+    for copy in outs:
+        copy.wait()
+
+
+def feed_both(info, c, grad, dm, middle, vectors, w_out, parts):
+    toks, width = middle.shape
+    units = 2 * parts[0].shape[0]
+    shapes = back_outputs(toks, width, units) + [
+        jax.ShapeDtypeStruct((2, units, toks), BF16),
+        jax.ShapeDtypeStruct((2, units, toks), BF16),
+        jax.ShapeDtypeStruct((toks, width), F32),
+    ]
+    return pl.pallas_call(
+        feed_both_kernel,
+        name="feed_both",
+        grid_spec=pltpu.PrefetchScalarGridSpec(
+            num_scalar_prefetch=1,
+            grid=(1,),
+            in_specs=[whole(v.shape) for v in (c, grad, dm, middle, vectors)] + [HBM] * 9,
+            out_specs=[HBM] * 2 + [whole(shape.shape) for shape in shapes[2:9]] + [HBM, HBM, whole((toks, width))],
+            scratch_shapes=[
+                pltpu.VMEM((4, units, toks), BF16),
+                pltpu.VMEM((4, toks, units), BF16),
+                pltpu.VMEM((4, units, parts[0].shape[1]), BF16),
+                pltpu.VMEM((toks, width), F32),
+                pltpu.VMEM((width, width), BF16),
+                pltpu.SemaphoreType.DMA((8,)),
+                pltpu.SemaphoreType.DMA((8,)),
+                pltpu.SemaphoreType.DMA((1,)),
+            ],
+        ),
+        out_shape=shapes,
+        compiler_params=pltpu.CompilerParams(vmem_limit_bytes=60 << 20),
+        cost_estimate=pl.CostEstimate(flops=10**10, transcendentals=2 * 10**6, bytes_accessed=24 << 20),
+    )(info, c, grad, dm, middle, vectors, w_out, *parts)
+
+
+def feed_weights_kernel(dh, dh2, act, act2, c, c2, dm, dm2, out_ref):
+    width = c.shape[1]
+    one, two = dh[0].T, dh2[0].T
+    out_ref[:, 0:width] = (dot(one, c[...]) + dot(two, c2[...])).astype(BF16)
+    out_ref[:, width : 2 * width] = (dot(act[0], dm[...]) + dot(act2[0], dm2[...])).astype(BF16)
+    bias = jnp.sum(one.astype(F32), axis=1, keepdims=True) + jnp.sum(two.astype(F32), axis=1, keepdims=True)
+    out_ref[:, 2 * width :] = jnp.broadcast_to(bias, (bias.shape[0], 128)).astype(BF16)
+
+
+def feed_weights(half, dh, dh2, act, act2, c, c2, dm, dm2):
+    toks, units, width = dh.shape[1], dh.shape[2], c.shape[1]
     wide = 2 * width + 128
     step = 256
-    out = pl.BlockSpec((step, wide), lambda i: (i, 0))
+    act_spec = pl.BlockSpec((1, step, toks), lambda i: (half, i, 0))
     return pl.pallas_call(
-        partial(feed_weights_kernel, add is not None),
+        feed_weights_kernel,
         name="feed_weights",
         grid=(units // step,),
         in_specs=[
-            pl.BlockSpec((1, toks, step), lambda i: (quarter, 0, i)),
-            pl.BlockSpec((1, step, toks), lambda i: (quarter, i, 0)),
-            whole(c.shape),
-            whole(dm.shape),
+            pl.BlockSpec((1, toks, step), lambda i: (half, 0, i)),
+            pl.BlockSpec((1, toks, step), lambda i: (half, 0, i)),
+            act_spec,
+            act_spec,
         ]
-        + ([out] if add is not None else []),
-        out_specs=out,
+        + [pl.BlockSpec(v.shape, lambda i: (0, 0)) for v in (c, c2, dm, dm2)],
+        out_specs=pl.BlockSpec((step, wide), lambda i: (i, 0)),
         out_shape=jax.ShapeDtypeStruct((units, wide), BF16),
         compiler_params=pltpu.CompilerParams(vmem_limit_bytes=48 << 20),
-        cost_estimate=pl.CostEstimate(flops=24 * 10**8, transcendentals=0, bytes_accessed=6 << 20),
-    )(dh, act, c, dm, *([add] if add is not None else []))
-
-
-def finish_kernel(fill, info, *refs):
+        cost_estimate=pl.CostEstimate(flops=24 * 10**8, transcendentals=0, bytes_accessed=9 << 20),
+    )(dh, dh2, act, act2, c, c2, dm, dm2)
+
+
+def finish_kernel(last, info, *refs):
     attn, hidden, refs = refs[:4], refs[4:8], refs[8:]
-    if fill:
-        refs = refs[4:]
-    qkv_ref, out_ref, up_ref, down_ref, bias_ref, vec_ref, qkv_at, out_at, hid_at = refs
-    vectors = sum(part[:, 768:896].astype(F32) for part in attn)
-    vec_ref[...] = vectors.T[0 : vec_ref.shape[0]]
+    if last:
+        (other_vec, other_bias), refs = refs[:2], refs[6:]
+        qkv_ref, out_ref, up_ref, down_ref = refs[:4]
+        vectors_out, qv_out, bias_out = refs[4:10], refs[10], refs[11]
+        qkv_at, out_at, hid_at = refs[12:]
+    else:
+        qkv_ref, out_ref, up_ref, down_ref, vec_ref, bias_ref, qkv_at, out_at, hid_at = refs
     dev = info[3]
     spot = info[5]
     rows = attn[0].shape[0]
@@ -754,7 +843,6 @@
     quarter = rows // 4
     units = hidden[0].shape[0]
     for at in range(4):
-        cols = slice(at * loc, (at + 1) * loc)
         found = qkv_at[at]
         qkv_ref[0, :, at * loc : (at + 1) * loc] = found[:, 384:576]
         qkv_ref[0, :, width + at * loc : width + (at + 1) * loc] = found[:, 0:192]
@@ -767,9 +855,25 @@
             out_ref[0, goal, lane : lane + 128] = out_at[at, 0, pl.ds(piece, quarter, stride=4), :]
             out_ref[0, goal, lane + 128 : lane + 192] = out_at[at, 1, pl.ds(piece, quarter, stride=4), :][:, 0:64]
         down_ref[0, at * units : (at + 1) * units, :] = hid_at[at, :, width : 2 * width]
-        bias_ref[0, at * units : (at + 1) * units, :] = hid_at[at, :, 2 * width :]
     up = jnp.concatenate([hid_at[at, :, 0:width] for at in range(4)], axis=0)
     up_ref[0] = up.T
+    bias = jnp.concatenate([hid_at[at, :, 2 * width :] for at in range(4)], axis=0).T[0:8]
+    vectors = sum(part[:, 768:896].astype(F32) for part in attn).T[0:16]
+    if not last:
+        vec_ref[...] = vectors
+        bias_ref[...] = bias
+        return
+    bias_out[0:1, :] = bias[0:1]
+    bias_out[1:2, :] = other_bias[0:1, :]
+    order = (((12, 0), (10, 0)), ((13, 0), (11, 0)), ((0, 0), (0, 1)), ((1, 0), (1, 1)), ((2, 0), (2, 1)), ((3, 0), (3, 1)))
+    for target, picks in zip(vectors_out, order):
+        for layer, (row, from_other) in enumerate(picks):
+            source = other_vec[row : row + 1, :] if from_other else vectors[row : row + 1]
+            target[layer : layer + 1, :] = source
+    for half in range(2):
+        lanes = slice(half * rows, (half + 1) * rows)
+        qv_out[0:1, lanes] = vectors[8 + half : 9 + half]
+        qv_out[1:2, lanes] = other_vec[8 + half : 9 + half, :]
 
 
 def finish(info, layer, attn, hidden, before):
@@ -780,29 +884,29 @@
         (LAYERS, rows, width),
         (LAYERS, width, 4 * units),
         (LAYERS, 4 * units, width),
-        (LAYERS, 4 * units, 128),
     ]
     specs = [pl.BlockSpec((1, *shape[1:]), lambda i, info: (layer, 0, 0)) for shape in shapes]
-    specs.append(whole((16, rows)))
-    shapes.append((16, rows))
-    fill = before is not None
-    given = list(before[:4]) if fill else []
+    last = before is not None
+    more = [(LAYERS, rows)] * 6 + [(LAYERS, 2 * rows), (LAYERS, 4 * units)] if last else [(16, rows), (8, 4 * units)]
+    given = [*before[4:6], *before[:4]] if last else []
     return pl.pallas_call(
-        partial(finish_kernel, fill),
+        partial(finish_kernel, last),
         name="finish",
         grid_spec=pltpu.PrefetchScalarGridSpec(
             num_scalar_prefetch=1,
             grid=(1,),
-            in_specs=[whole(attn[0].shape)] * 4 + [whole(hidden[0].shape)] * 4 + [HBM] * len(given),
-            out_specs=specs,
+            in_specs=[whole(attn[0].shape)] * 4
+            + [whole(hidden[0].shape)] * 4
+            + ([whole(v.shape) for v in given[:2]] + [HBM] * 4 if last else []),
+            out_specs=specs + [whole(shape) for shape in more],
             scratch_shapes=[
                 pltpu.VMEM((4, rows, 576), F32),
                 pltpu.VMEM((4, 2, rows, 128), F32),
                 pltpu.VMEM((4, units, 2 * width + 128), F32),
             ],
         ),
-        out_shape=[jax.ShapeDtypeStruct(shape, F32) for shape in shapes],
-        input_output_aliases={9 + at: at for at in range(len(given))},
+        out_shape=[jax.ShapeDtypeStruct(shape, F32) for shape in shapes + more],
+        input_output_aliases={11 + at: at for at in range(4)} if last else {},
         compiler_params=pltpu.CompilerParams(vmem_limit_bytes=56 << 20),
         cost_estimate=pl.CostEstimate(flops=10**6, transcendentals=0, bytes_accessed=8 << 20),
     )(info, *attn, *hidden, *given)
@@ -907,38 +1011,37 @@
     def over_shards(piece):
         return lax.all_gather(piece, "shard", axis=0, tiled=True)
 
-    def spread_hidden(own, one, *others):
-        own, one = lax.optimization_barrier((own, one, *others))[:2]
-        return own, one, turned(own, False), turned(one, False)
-
-    def both_cores(parts):
-        return tuple(parts) + tuple(swap(part, "core") for part in parts)
-
-    def sum_shards(value):
+    def send_shards(value, count):
+        if shards != 4:
+            return ()
+        index = lax.axis_index("shard")
+        return tuple(
+            lax.ppermute(
+                lax.dynamic_slice_in_dim(value, (index + by) % shards * count, count, 0),
+                "shard",
+                [(i, (i + by) % shards) for i in range(shards)],
+            )
+            for by in range(1, shards)
+        )
+
+    def sum_shards(value, count, arriving):
         if shards != 4:
             return lax.psum_scatter(value, "shard", scatter_dimension=0, tiled=True)
-        each = value.reshape(shards, -1, value.shape[1])
-        index = lax.axis_index("shard")
-        total = lax.dynamic_index_in_dim(each, index, 0, keepdims=False).astype(F32)
-        for by in range(1, shards):
-            piece = lax.dynamic_index_in_dim(each, (index + by) % shards, 0, keepdims=False)
-            piece = lax.ppermute(piece, "shard", [(i, (i + by) % shards) for i in range(shards)])
-            total = total + piece.astype(F32)
-        return total.astype(value.dtype)
+        own = lax.dynamic_slice_in_dim(value, lax.axis_index("shard") * count, count, 0).astype(F32)
+        return (own + sum(piece.astype(F32) for piece in arriving)).astype(value.dtype)
+
+    def around_hidden(own):
+        core, far = swap(own, "core"), swap(own, "cx")
+        return own, far, core, swap(far, "core")
 
     hidden_own = to_sequence(hidden_in)
-    grad = to_sequence(output_grad).astype(F32) * keep
-    first_parts = around(hidden_own)
-    attn0 = over_shards(attention_piece(0))
-    feed0 = over_shards(after(hidden_piece(0), attn0, grad, *first_parts))
-
-    def second_weights(*others):
-        attn = attention_piece(1)
-        piece = jnp.concatenate((hidden_piece(1), attn[:units], attn[units:]), axis=1)
-        gathered = over_shards(after(piece, *others))
-        wide = 2 * width + 128
-        halves = [gathered[:, at : at + width].reshape(shards, 1, units, width) for at in (wide, wide + width)]
-        return jnp.concatenate(halves, axis=1).reshape(width, width), gathered[:, :wide]
+    first_piece, attn_piece = hidden_piece(0), attention_piece(0)
+    first_parts = around(after(hidden_own, first_piece, attn_piece))
+    feed0 = over_shards(first_piece)
+    attn0 = over_shards(after(attn_piece, feed0, *first_parts))
+    feed_piece, attn_piece = hidden_piece(1), attention_piece(1)
+    feed1 = over_shards(after(feed_piece, attn0))
+    one0, two0 = turned(feed0, True), turned(feed0, False)
 
     def out_weights(own):
         full = jnp.zeros((shards, 4, quarter, width), BF16)
@@ -961,22 +1064,29 @@
     saved = []
     for layer in range(LAYERS):
         gain_one, bias_one, bias_out, gain_two, bias_two, bias_down = names[layer]
-        w_qkv = (attn0 if layer == 0 else attn1)[:, : 3 * loc]
+        w_qkv = attn0 if layer == 0 else attn1
         q_bias = lax.dynamic_slice_in_dim(qv[layer], loc * dev, loc, 0)
         v_bias = lax.dynamic_slice_in_dim(qv[layer], width + loc * dev, loc, 0)
         bias = jnp.concatenate((jnp.zeros((192,), F32), v_bias[128:], v_bias[:128], q_bias))[None]
+        if layer == 0:
+            one0, two0, attn_piece, *attn_parts = lax.optimization_barrier((one0, two0, attn_piece, *attn_parts))
+            three0 = turned(one0, False)
+            early_core = [swap(part, "core") for part in (feed0, one0, two0)]
         attn_t, qkv, attended, lse = attention_forward(info, attn_parts, w_qkv, bias, gain_one, bias_one, layer == 0)
         if layer == 0:
-            attn1, feed1 = second_weights(attended, feed0)
-            w_out = out_own(attn0)
-            attended, w_out = lax.optimization_barrier((attended, w_out))
-            w_out = out_weights(w_out)
+            attn1 = over_shards(after(attn_piece, attended))
+            w_out = out_weights(out_own(attn0))
+            attended, w_out, three0, *early_core = lax.optimization_barrier((attended, w_out, three0, *early_core))
+            w_feed = (feed0, one0, two0, three0, *early_core, swap(three0, "core"))
         else:
             own, one, two, three = w_feed1
             early_core = (swap(own, "core"), swap(one, "core"))
-            attended, w_out, own, one, two, three, *early_core = lax.optimization_barrier(
-                (attended, w_out1, own, one, two, three, *early_core)
+            attended, w_out, raw_grad, own, one, two, three, *early_core = lax.optimization_barrier(
+                (attended, w_out1, raw_grad, own, one, two, three, *early_core)
             )
+            grad = raw_grad.astype(F32) * keep
+            low_grad = grad.astype(BF16)
+            low_other = swap(low_grad, "core")
         parts = (
             attended[0],
             swap(attended[1], "core"),
@@ -986,73 +1096,70 @@
         if layer == 1:
             late_core = [swap(after(part, *parts), "core") for part in (two, three)]
             w_feed = (own, one, two, three, *early_core, *late_core)
-        if layer == 0:
-            own, *others = lax.optimization_barrier((feed0, *parts, w_out))
-            one = turned(own, True)
-            two = turned(own, False)
         vectors = jnp.concatenate((bias_out, gain_two, bias_two), axis=0)
         context, middle, mlp_in = out_forward(info, parts, w_out, current, vectors)
         if layer == 0:
-            three = turned(after(one, mlp_in), False)
-            w_feed = both_cores((own, one, two, three))
             vectors = jnp.concatenate((bias_down, names[1][0], names[1][1]), axis=0)
             mlp_in, feed1 = lax.optimization_barrier((mlp_in, feed1))
-            slope, act, result, attn_own = feed_forward(mlp_in, middle, vectors, w_feed, True)
-            one = turned(feed1, True)
-            attn_parts = around(after(attn_own, one))
-            w_out1 = out_weights(after(out_own(attn1), *attn_parts))
-            w_feed1 = spread_hidden(feed1, one, *attn_parts)
+            one1 = turned(feed1, True)
+            slope, act, act_other, result, attn_own = feed_forward(mlp_in, middle, vectors, w_feed)
+            act_other, mlp_other = swap(act_other, "core"), swap(mlp_in, "core")
+            attn_own = after(attn_own, one1)
+            attn_parts = around(attn_own)
+            own_out1 = out_own(attn1)
+            own_out1, act_other, mlp_other, given, *attn_parts = lax.optimization_barrier(
+                (own_out1, act_other, mlp_other, output_grad, *attn_parts)
+            )
+            raw_grad = to_sequence(given)
+            w_out1 = out_weights(own_out1)
+            feed1, one1 = lax.optimization_barrier((feed1, one1, *attn_parts))[:2]
+            w_feed1 = (feed1, one1, turned(feed1, False), turned(one1, False))
         else:
-            slope, act, result = feed_forward(mlp_in, middle, bias_down, w_feed, False)
+            slope = act = act_other = result = None
+            mlp_other = swap(mlp_in, "core")
         weights.append((w_qkv, w_out, w_feed))
-        saved.append((current, attn_t, qkv, attended, lse, context, middle, mlp_in, slope, act))
+        saved.append((current, attn_t, qkv, attended, lse, context, middle, mlp_in, mlp_other, slope, act, act_other))
         current = result
-    hidden_out = from_sequence((current * keep).astype(BF16))
-
     n = shards * units
 
-    attn_sums = [None] * LAYERS
-    feed_sums = [None] * LAYERS
-    by_attention, by_core = (), ()
     for layer in reversed(range(LAYERS)):
-        x_in, attn_t, qkv, attended, lse, context, middle, mlp_in, slope, act = saved[layer]
+        x_in, attn_t, qkv, attended, lse, context, middle, mlp_in, mlp_other, slope, act, act_other = saved[layer]
         gain_one, _, _, gain_two, _, _ = names[layer]
         w_qkv, w_out, w_feed = weights[layer]
-        dh, dm, middle_grad, branch_grad, sums_two, d0, d1, d2, d3 = feed_backward(
-            info, grad, slope, middle, gain_two, w_out, w_feed
-        )
+        if layer == 0:
+            found = feed_backward(info, grad, low_grad, slope, middle, gain_two, w_out, w_feed)
+        else:
+            vectors = jnp.concatenate((names[1][5], gain_two), axis=0)
+            *found, act, act_other, result = feed_both(info, mlp_in, grad, low_grad, middle, vectors, w_out, w_feed)
+            act_other = swap(act_other, "core")
+        dh, dh_other, middle_grad, branch_grad, sums_two, d0, d1, d2, d3 = found
         attn_grads = (d0, swap(d1, "core"), swap(d2, "cx"), diagonal(d3))
-        other_late = swap(feed_weights(dh, act, mlp_in, dm, 3), "core")
-        late = feed_weights(dh, act, mlp_in, dm, 1, other_late)
+        tokens = (mlp_in, mlp_other, low_grad, low_other)
+        dh_other = swap(dh_other, "core")
+        *attn_grads, dh_other = lax.optimization_barrier((*attn_grads, dh_other))
+        late = feed_weights(1, dh, dh_other, act, act_other, *tokens)
         w_out_grad = dot(context, branch_grad).astype(BF16).reshape(shards, 4, quarter, width)
         pieces = [lax.dynamic_index_in_dim(w_out_grad, dev ^ rel, 1, keepdims=False) for rel in range(4)]
         got = swap(jnp.stack((pieces[1], pieces[3])), "core")
-        to_far_out = (pieces[2].astype(F32) + got[1].astype(F32)).astype(BF16)
-        ready = [*attn_grads, late, to_far_out, *by_attention]
+        far = swap((pieces[2].astype(F32) + got[1].astype(F32)).astype(BF16), "cx")
+        ready = [*attn_grads, late, far]
         if layer == 0:
-            other_early = swap(feed_weights(dh, act, mlp_in, dm, 2), "core")
-            early = feed_weights(dh, act, mlp_in, dm, 0, other_early)
-            far = swap(to_far_out, "cx")
-            ready += [early, far]
-        *attn_grads, late, to_far_out = lax.optimization_barrier(tuple(ready))[:6]
+            early = feed_weights(0, dh, dh_other, act, act_other, *tokens)
+            ready += [early]
+        *attn_grads, late, far = lax.optimization_barrier(tuple(ready))[:6]
         du, to_core, to_far, own, sums_u = attention_backward(info, qkv, attended, lse, w_qkv, attn_grads)
         late = turned(late, False)
-        to_core = after(to_core, late, *by_core)
+        to_core = after(to_core, late)
         from_core = swap(to_core, "core")
         to_far = (to_far + from_core[1].astype(F32)).astype(BF16)
         if layer == 0:
             part = (early[n:].astype(F32) + late[n:].astype(F32)).astype(BF16)
-            kept = early[:n].astype(F32) + late[:n].astype(F32)
             arrived = turned(part, True)
-            to_far = after(to_far, arrived)
         from_far = swap(to_far, "cx")
         if layer > 0:
-            far = swap(after(to_far_out, to_far), "cx")
-            du, dh_late, early_late = lax.optimization_barrier((du, dh, late, to_far))[:3]
-            other_early = swap(feed_weights(dh_late, act, mlp_in, dm, 2), "core")
-            early = feed_weights(dh_late, act, mlp_in, dm, 0, other_early)
+            du, dh_now, early_late = lax.optimization_barrier((du, dh, late, to_far))[:3]
+            early = feed_weights(0, dh_now, dh_other, act, act_other, *tokens)
             part = (early[n:].astype(F32) + early_late[n:].astype(F32)).astype(BF16)
-            kept = early[:n].astype(F32) + early_late[:n].astype(F32)
         du_sum = sums_u[0]
         v_sum = jnp.concatenate((du_sum[256:384], du_sum[192:256]))
         q_row = lax.dynamic_update_slice_in_dim(jnp.zeros((width,), F32), du_sum[384:], loc * dev, 0)
@@ -1062,44 +1169,44 @@
         if layer == 0:
             vectors = jnp.concatenate((vectors[:10], sums_one[:2], vectors[12:]), axis=0)
         flat = [piece.reshape(shards * quarter, width) for piece in (pieces[0], got[0], far)]
-        joined = attention_weights(attn_t, du, vectors, *flat)
-        attn_sum = lax.psum_scatter(joined, "shard", scatter_dimension=0, tiled=True)
         if layer > 0:
-            by_attention = (attn_sum,)
-            from_far, part = lax.optimization_barrier((from_far, part))
+            joined = attention_weights(attn_t, after(du, part), vectors, *flat)
+            attn_sum1 = lax.psum_scatter(joined, "shard", scatter_dimension=0, tiled=True)
+            hidden_out = from_sequence((after(result, to_far) * keep).astype(BF16))
+            from_far, part, hidden_out = lax.optimization_barrier((from_far, part, hidden_out))
             arrived = turned(part, True)
-        attn_sum = (attn_sum.astype(F32) + swap(attn_sum, "tp").astype(F32)).astype(BF16)
-        attn_sums[layer] = around(attn_sum)
-        part = (kept + arrived.astype(F32)).astype(BF16)
-        grad, sums_one = norm_backward(own, from_core, from_far, x_in, gain_one, middle_grad)
+        else:
+            joined = attention_weights(attn_t, after(du, from_core, part), vectors, *flat)
+            attn_sum = lax.psum_scatter(joined, "shard", scatter_dimension=0, tiled=True)
+        grad, low_grad, sums_one = norm_backward(own, from_core, from_far, x_in, gain_one, middle_grad)
         if layer > 0:
-            hidden = lax.psum_scatter(part, "shard", scatter_dimension=0, tiled=True)
+            low_other = swap(low_grad, "core")
+            grad, low_grad, arrived = lax.optimization_barrier((grad, low_grad, arrived))
+            part = early[:n].astype(F32) + early_late[:n].astype(F32) + arrived.astype(F32)
+            feed_sum1 = lax.psum_scatter(part.astype(BF16), "shard", scatter_dimension=0, tiled=True)
         else:
-            hidden = sum_shards(part)
+            part = (early[:n].astype(F32) + late[:n].astype(F32) + arrived.astype(F32)).astype(BF16)
             halves = sums_one[:2].reshape(2, shards, 2, units).transpose(1, 3, 0, 2).reshape(n, 4)
-            lone = sum_shards(jnp.pad(halves, ((0, 0), (0, 124))))
-            hidden = lax.dynamic_update_slice(hidden, lone[:, :4].astype(BF16), (0, 2 * width + 1))
-        core, far = swap(hidden, "core"), swap(hidden, "cx")
-        feed_sums[layer] = (hidden, far, core, swap(far, "core"))
-        by_core = (hidden,)
-
-    hidden_grad = from_sequence(grad.astype(BF16)).astype(F32)
-
-    done = None
-    columns_of = [None] * LAYERS
-    biases = [None] * LAYERS
-    for layer in reversed(range(LAYERS)):
-        done = finish(info, layer, attn_sums[layer], feed_sums[layer], done)
-        columns_of[layer] = done[5]
-        biases[layer] = done[4][layer, :, 0]
-    lone = feed_sums[0]
-    lone = sum(part[:, 2 * width + 1 : 2 * width + 5].astype(F32) for part in lone)
+            part = lax.dynamic_update_slice(part, halves.astype(BF16), (0, 2 * width + 1))
+            attn_sum1 = (attn_sum1.astype(F32) + swap(attn_sum1, "tp").astype(F32)).astype(BF16)
+            part, attn_sum1, feed_sum1 = lax.optimization_barrier((part, attn_sum1, feed_sum1))
+            arriving = send_shards(part, units)
+            attn_parts1, hidden_parts1 = around(attn_sum1), around_hidden(feed_sum1)
+            arriving = lax.optimization_barrier((*arriving, *attn_parts1, *hidden_parts1))[: len(arriving)]
+            feed_sum = sum_shards(part, units, arriving)
+            done = finish(info, 1, attn_parts1, hidden_parts1, None)
+            attn_sum = after(attn_sum, feed_sum)
+            attn_sum = (attn_sum.astype(F32) + swap(attn_sum, "tp").astype(F32)).astype(BF16)
+
+    hidden_grad = from_sequence(low_grad).astype(F32)
+
+    feed_sums = around_hidden(feed_sum)
+    lone = sum(part[:, 2 * width + 1 : 2 * width + 5].astype(F32) for part in feed_sums)
     lone = lone + swap(lone, "tp")
     lone = lone.reshape(units, 2, 2).transpose(1, 2, 0).reshape(2, rows)
-    first_gain = jnp.stack((lone[0], columns_of[0][10]))
-    first_bias = jnp.stack((lone[1], columns_of[0][11]))
-    rest = [jnp.stack((columns_of[0][at], columns_of[1][at])) for at in range(4)]
-    qv_out = jnp.stack([jnp.concatenate((columns_of[layer][8], columns_of[layer][9])) for layer in range(LAYERS)])
+    done = finish(info, 0, around(attn_sum), feed_sums, done)
+    first_gain = jnp.stack((lone[0], done[4][1]))
+    first_bias = jnp.stack((lone[1], done[5][1]))
 
     return (
         hidden_out,
@@ -1107,15 +1214,15 @@
         first_gain,
         first_bias,
         done[0],
-        qv_out,
+        done[10],
         done[1],
-        rest[2],
-        rest[0],
-        rest[1],
+        done[8],
+        done[6],
+        done[7],
         done[2],
-        jnp.stack(biases),
+        done[11],
         done[3],
-        rest[3],
+        done[9],
     )
 
 

time: 628 us -> 589 us (0.938)
  the two profiles are of different devices: /device:TPU:0 before, /device:TPU:9 now
where the time goes in v3:
time: 589 us; the launch traced here: 580 us
  Pallas kernels  230 us (39%)
  waiting for transfers between devices  155 us (26%)
  starting transfers between devices  88.5 us (15%)
  local copies, waits for them, and re-layouts  54.9 us (9%)
  other arithmetic  30.1 us (5%)
  between operations  18 us (3%)
    ppermute x63, waiting for transfers between devices, swap(): return lax.ppermute(value, axis, ((0, 1), (1, 0)))  95.8 us
    pallas_call x2, Pallas kernels, attention_backward(): pl.pallas_call(attention_backward_kernel, name='attention_backward', grid...  63.4 us
    ppermute x63, starting transfers between devices, swap(): return lax.ppermute(value, axis, ((0, 1), (1, 0)))  58.4 us
    pallas_call x2, Pallas kernels, attention_forward(): pl.pallas_call(partial(attention_forward_kernel, norm), name='attention_f...  46.4 us
    unnamed x207, local copies, waits for them, and re-layouts  27 us
    pallas_call x1, Pallas kernels, feed_both(): pl.pallas_call(feed_both_kernel, name='feed_both', grid_spec=pltpu.Prefet...  23.2 us
    pallas_call x4, Pallas kernels, feed_weights(): pl.pallas_call(feed_weights_kernel, name='feed_weights', grid=(units // s...  22.4 us
    ppermute x10, waiting for transfers between devices, turned(): return lax.ppermute(value, PLANE, pairs)  20.2 us
  transfers between devices with their start and end apart: 87, of which 33 were waited for; matrix products, arithmetic and copies ran while one was open for 10% of the time, Pallas kernels for 35%

profile of v3, /device:TPU:9, one launch (start us, length us, event | category | flops | bytes accessed | tf_op | source)
XLA Modules:
  0.0 579.6 jit_solution(8659335625617343014)
XLA Ops:
  7.3 2.1 dynamic-slice_bitcast_fusion.3
  17.8 1.9 collective-permute-done.2
  19.7 2.3 fusion.25
  25.1 14.4 %collective-permute-done.4.refs_2_ = bf16[512,768]{1,0:T(8,128)(2,1)S(1)} collective-permute-done((bf16[512,768]{1,0:T(8,128)(2,1)S(1)}, bf16[512,768]{1,0:T(8,128)(2,1)S(1)}, u32[]{:S(2)}, u32[]{:S(2)}) %collective-permute-start.4) | collective-permute-done | bytes 786464 | tf_op jit(solution)/shard_map/ppermute | solution.py:27
  39.5 2.5 collective-permute-start.5
  42.0 3.6 all-gather.5.cloned.1.call-done.refs_0_
  57.1 16.2 %collective-permute-done.refs_1_ = bf16[384,1664]{1,0:T(8,128)(2,1)} collective-permute-done((bf16[384,1664]{1,0:T(8,128)(2,1)}, bf16[384,1664]{1,0:T(8,128)(2,1)}, u32[]{:S(2)}, u32[]{:S(2)}) %collective-permute-start) | collective-permute-done | bytes 1277984 | tf_op jit(solution)/shard_map/ppermute | solution.py:926
  73.3 3.9 collective-permute-done.1.refs_2_
  88.9 24.0 %attention_forward.2 = (bf16[768,2048]{1,0:T(8,128)(2,1)}, bf16[2048,576]{1,0:T(8,128)(2,1)}, bf16[4,192,512]{2,1,0:T(8,128)(2,1)S(1)}, f32[8,2048]{1,0:T(8,128)S(1)}) custom-call(s32[8]{0:T(128)S(1)} %stack.77.info, bf16[512,768]{1,0:T(8,128)(2,1)S(1)} %get-tuple-element.173.refs_0_, bf16[512,768]{1,0:T(8,128)(2,1)S(1)} %copy-done.37, ...), custom_call_target="tpu_custom_call" | custom-call | flops 14000000000 | bytes 12582912 | tf_op jit(solution)/shard_map/attention_forward/pallas_call | solution.py:180
  119.0 3.5 collective-permute-done.14.p2
  122.5 4.7 collective-permute-done.15.p3
  127.2 4.4 out_forward.2
  136.4 14.7 %feed_forward.1 = (bf16[4,512,768]{2,1,0:T(8,128)(2,1)}, bf16[2,768,512]{2,1,0:T(8,128)(2,1)}, bf16[2,768,512]{2,1,0:T(8,128)(2,1)}, f32[512,768]{1,0:T(8,128)}, bf16[512,768]{1,0:T(8,128)(2,1)}) custom-call(bf16[512,768]{1,0:T(8,128)(2,1)} %copy-done.5, f32[512,768]{1,0:T(8,128)} %copy-done.39, f32[3,768]{1,0:T(4,128)} %pad_maximum_fusion.7.vec_ref, ...), custom_call_target="tpu_custom_call" | custom-call | flops 5000000000 | bytes 20971520 | tf_op jit(solution)/shard_map/feed_forward/pallas_call | solution.py:576
  153.4 17.8 %collective-permute-done.21.refs_2_ = bf16[512,768]{1,0:T(8,128)(2,1)S(1)} collective-permute-done((bf16[512,768]{1,0:T(8,128)(2,1)}, bf16[512,768]{1,0:T(8,128)(2,1)S(1)}, u32[]{:S(2)}, u32[]{:S(2)}) %collective-permute-start.21) | collective-permute-done | bytes 786464 | tf_op jit(solution)/shard_map/ppermute | solution.py:27
  180.1 22.4 %attention_forward.3 = (bf16[768,2048]{1,0:T(8,128)(2,1)}, bf16[2048,576]{1,0:T(8,128)(2,1)}, bf16[4,192,512]{2,1,0:T(8,128)(2,1)S(1)}, f32[8,2048]{1,0:T(8,128)S(1)}) custom-call(s32[8]{0:T(128)S(1)} %stack.77.info, bf16[512,768]{1,0:T(8,128)(2,1)S(1)} %copy-done.38, bf16[512,768]{1,0:T(8,128)(2,1)} %collective-permute-done.20.refs_1_, ...), custom_call_target="tpu_custom_call" | custom-call | flops 14000000000 | bytes 12582912 | tf_op jit(solution)/shard_map/attention_forward/pallas_call | solution.py:180
  202.6 8.2 %collective-permute-done.24 = bf16[4,1,48,768]{3,2,0,1:T(8,128)(2,1)S(1)} collective-permute-done((bf16[4,1,48,768]{3,2,0,1:T(8,128)(2,1)S(1)}, bf16[4,1,48,768]{3,2,0,1:T(8,128)(2,1)S(1)}, u32[]{:S(2)}, u32[]{:S(2)}) %collective-permute-start.24) | collective-permute-done | bytes 294944 | tf_op jit(solution)/shard_map/ppermute | solution.py:27
  211.9 5.5 collective-permute-done.26
  221.4 4.1 collective-permute-done.32.p2
  225.5 4.7 collective-permute-done.33.p3
  231.4 2.8 fusion.24
  234.1 4.8 out_forward.3
  241.9 23.2 %feed_both.1 = (bf16[2,512,768]{2,1,0:T(8,128)(2,1)}, bf16[2,512,768]{2,1,0:T(8,128)(2,1)}, f32[512,768]{1,0:T(8,128)}, bf16[512,768]{1,0:T(8,128)(2,1)}, f32[8,...) custom-call(s32[8]{0:T(128)} %copy-done.34, ...), custom_call_target="tpu_custom_call" | custom-call | flops 10000000000 | bytes 25165824 | tf_op jit(solution)/shard_map/feed_both/pallas_call | solution.py:767
  266.8 1.9 convolution_convert_fusion.1
  269.6 2.0 collective-permute-done.36.g1
  274.4 5.5 collective-permute-done.38.g3
  282.6 5.5 feed_weights.4
  290.2 31.4 %attention_backward.2 = (bf16[2048,576]{1,0:T(8,128)(2,1)}, bf16[2,512,768]{2,1,0:T(8,128)(2,1)}, f32[512,768]{1,0:T(8,128)}, f32[512,768]{1,0:T(8,128)}, f32[8,576]{1,0:T(8,128)}) custom-call(s32[8]{0:T(128)} %copy-done.34, bf16[2048,576]{1,0:T(8,128)(2,1)} %get-tuple-element.200.qkv_ref, bf16[4,192,512]{2,1,0:T(8,128)(2,1)} %copy-done.25, ...), custom_call_target="tpu_custom_call" | custom-call | flops 20000000000 | bytes 16777216 | tf_op jit(solution)/shard_map/attention_backward/pallas_call | solution.py:344
  322.7 3.4 collective-permute-done.46.core
  330.1 5.5 feed_weights.5
  335.7 3.0 add_convert_fusion.3
  339.8 7.0 %collective-permute-done.47.far = bf16[512,768]{1,0:T(8,128)(2,1)S(1)} collective-permute-done((bf16[512,768]{1,0:T(8,128)(2,1)S(1)}, bf16[512,768]{1,0:T(8,128)(2,1)S(1)}, u32[]{:S(2)}, u32[]{:S(2)}) %collective-permute-start.47) | collective-permute-done | bytes 786464 | tf_op jit(solution)/shard_map/ppermute | solution.py:27
  352.3 5.7 attention_weights.2
  359.1 4.5 norm_backward.2
  365.7 17.7 %feed_backward.1 = (bf16[2,512,768]{2,1,0:T(8,128)(2,1)}, bf16[2,512,768]{2,1,0:T(8,128)(2,1)}, f32[512,768]{1,0:T(8,128)}, bf16[512,768]{1,0:T(8,128)(2,1)}, f3...) custom-call(s32[8]{0:T(128)} %copy-done.34, ...), custom_call_target="tpu_custom_call" | custom-call | flops 6000000000 | bytes 25165824 | tf_op jit(solution)/shard_map/feed_backward/pallas_call | solution.py:682
  383.5 2.1 collective-permute-start.53
  385.6 1.9 convolution_convert_fusion
  392.2 3.5 collective-permute-done.51.g2
  395.6 4.8 collective-permute-done.52.g3
  401.7 5.5 feed_weights.7
  407.2 5.8 feed_weights.6
  414.8 3.2 add_convert_fusion
  418.1 32.0 %attention_backward.3 = (bf16[2048,576]{1,0:T(8,128)(2,1)}, bf16[2,512,768]{2,1,0:T(8,128)(2,1)}, f32[512,768]{1,0:T(8,128)}, f32[512,768]{1,0:T(8,128)}, f32[8,576]{1,0:T(8,128)}) custom-call(s32[8]{0:T(128)} %copy-done.34, bf16[2048,576]{1,0:T(8,128)(2,1)} %get-tuple-element.250.qkv_ref, bf16[4,192,512]{2,1,0:T(8,128)(2,1)} %copy-done.24, ...), custom_call_target="tpu_custom_call" | custom-call | flops 20000000000 | bytes 16777216 | tf_op jit(solution)/shard_map/attention_backward/pallas_call | solution.py:344
  452.3 2.8 add_convert_fusion.2
  457.4 5.6 attention_weights.3
  464.6 1.9 fusion
  467.0 12.1 %collective-permute-done.62 = bf16[192,896]{1,0:T(8,128)(2,1)S(1)} collective-permute-done((bf16[192,896]{1,0:T(8,128)(2,1)}, bf16[192,896]{1,0:T(8,128)(2,1)S(1)}, u32[]{:S(2)}, u32[]{:S(2)}) %collective-permute-start.62) | collective-permute-done | bytes 344096 | tf_op jit(solution)/shard_map/ppermute | solution.py:27
  479.2 2.3 add_convert_fusion.1
  481.5 4.8 collective-permute-done.59.far
  486.3 5.2 norm_backward.3
  494.0 7.2 %collective-permute-start.63 = (bf16[96,1664]{1,0:T(8,128)(2,1)S(1)}, bf16[96,1664]{1,0:T(8,128)(2,1)S(1)}, u32[]{:S(2)}, u32[]{:S(2)}) collective-permute-start(bf16[96,1664]{1,0:T(8,128)(2,1)S(1)} %get-tuple-element.332), channel_id=1, source_target_pairs={{0,8},{8,16},{16,24},{24,0},{1,9},{9,17},{17,25},{25,1},{2,10},{10... | collective-permute-start | bytes 958472 | tf_op jit(solution)/shard_map/ppermute | solution.py:1019
  501.1 5.5 collective-permute-start.64
  508.0 4.1 collective-permute-start.66
  512.2 5.6 collective-permute-start.65
  517.8 9.9 %collective-permute-done.64 = bf16[96,1664]{1,0:T(8,128)(2,1)} collective-permute-done((bf16[96,1664]{1,0:T(8,128)(2,1)S(1)}, bf16[96,1664]{1,0:T(8,128)(2,1)}, u32[]{:S(2)}, u32[]{:S(2)}) %collective-permute-start.64) | collective-permute-done | bytes 319520 | tf_op jit(solution)/shard_map/ppermute | solution.py:1019
  527.7 2.1 collective-permute-start.70
  529.8 3.6 collective-permute-done.65
  538.0 2.3 collective-permute-start.73
  540.3 2.2 collective-permute-done.72.refs_5_
  542.4 2.6 collective-permute-start.74
  548.1 1.9 collective-permute-start.77
  550.1 2.1 collective-permute-done.78.refs_2_
  552.2 3.6 collective-permute-start.79
  557.0 5.5 finish.2
  563.6 6.0 %finish.3 = (f32[2,192,2304]{2,1,0:T(8,128)}, f32[2,192,768]{2,1,0:T(8,128)}, f32[2,768,384]{2,1,0:T(8,128)}, f32[2,384,768]{2,1,0:T(8,128)}, f32[2,192]{1,0:T(2...) custom-call(s32[8]{0:T(128)} %copy-done.34, ...), custom_call_target="tpu_custom_call", output_to_operand_aliasing={{0}: (11, {}), {1}: (12, {}), {2}: (13, {}), {3}: (14, {})} | custom-call | flops 1000000 | bytes 8388608 | tf_op jit(solution)/shard_map/finish/pallas_call | solution.py:892
  (493 shorter events, 118.7 us)
Async XLA Ops:
  7.2 38.4 %all-gather.5.cloned.1.call-start = ((), (), s32[]{:S(2)}) async-start(), calls=%async_computation.3 | async-start | bytes 1597440 | tf_op jit(solution)/shard_map/all_gather | solution.py:1012
  9.4 10.3 %collective-permute-start.2 = (bf16[256,768]{1,0:T(8,128)(2,1)}, bf16[256,768]{1,0:T(8,128)(2,1)}, u32[]{:S(2)}, u32[]{:S(2)}) collective-permute-start(bf16[256,768]{1,0:T(8,128)(2,1)} %get-tuple-element.368), channel_id=1, source_target_pairs={{0,1},{1,0},{2,3},{3,2},{4,5},{5,4},{6,7},{7,6},{8,9},{9,8},{10,11... | collective-permute-start | bytes 1179656 | tf_op jit(solution)/shard_map/ppermute | solution.py:27
  13.7 66.8 %all-gather.7.cloned.1.call-start = ((), (), s32[]{:S(2)}) async-start(), calls=%async_computation.4 | async-start | bytes 1720320 | tf_op jit(solution)/shard_map/all_gather | solution.py:1012
  22.1 17.5 %collective-permute-start.4 = (bf16[512,768]{1,0:T(8,128)(2,1)S(1)}, bf16[512,768]{1,0:T(8,128)(2,1)S(1)}, u32[]{:S(2)}, u32[]{:S(2)}) collective-permute-start(bf16[512,768]{1,0:T(8,128)(2,1)S(1)} %get-tuple-element.173.refs_0_), channel_id=1, source_target_pairs={{0,4},{4,0},{1,5},{5,1},{2,6},{6,2},{3,7},{7,3},{8,12},{12,8},{9,1... | collective-permute-start | bytes 2359304 | tf_op jit(solution)/shard_map/ppermute | solution.py:27
  23.3 18.7 %collective-permute-start.3 = (bf16[512,768]{1,0:T(8,128)(2,1)S(1)}, bf16[512,768]{1,0:T(8,128)(2,1)S(1)}, u32[]{:S(2)}, u32[]{:S(2)}) collective-permute-start(bf16[512,768]{1,0:T(8,128)(2,1)S(1)} %get-tuple-element.173.refs_0_), channel_id=1, source_target_pairs={{0,2},{2,0},{1,3},{3,1},{4,6},{6,4},{5,7},{7,5},{8,10},{10,8},{9,1... | collective-permute-start | bytes 2359304 | tf_op jit(solution)/shard_map/ppermute | solution.py:27
  45.7 88.8 %all-gather.11.cloned.1.call-start = ((), (), s32[]{:S(2)}) async-start(), calls=%async_computation.6 | async-start | bytes 1597440 | tf_op jit(solution)/shard_map/all_gather | solution.py:1012
  45.7 27.6 %collective-permute-start = (bf16[384,1664]{1,0:T(8,128)(2,1)}, bf16[384,1664]{1,0:T(8,128)(2,1)}, u32[]{:S(2)}, u32[]{:S(2)}) collective-permute-start(bf16[384,1664]{1,0:T(8,128)(2,1)} %all-gather.5.cloned.1.call-done.refs_0_), channel_id=1, source_target_pairs={{0,4},{1,5},{2,3},{3,2},{4,0},{5,1},{6,7},{7,6},{8,12},{9,13},{10,... | collective-permute-start | bytes 3833864 | tf_op jit(solution)/shard_map/ppermute | solution.py:926
  47.0 30.2 %collective-permute-start.1 = (bf16[384,1664]{1,0:T(8,128)(2,1)}, bf16[384,1664]{1,0:T(8,128)(2,1)}, u32[]{:S(2)}, u32[]{:S(2)}) collective-permute-start(bf16[384,1664]{1,0:T(8,128)(2,1)} %all-gather.5.cloned.1.call-done.refs_0_), channel_id=1, source_target_pairs={{0,1},{1,0},{2,6},{3,7},{4,5},{5,4},{6,2},{7,3},{8,9},{9,8},{10,14... | collective-permute-start | bytes 3833864 | tf_op jit(solution)/shard_map/ppermute | solution.py:926
  55.6 60.0 %collective-permute-start.10 = (bf16[384,1664]{1,0:T(8,128)(2,1)}, bf16[384,1664]{1,0:T(8,128)(2,1)}, u32[]{:S(2)}, u32[]{:S(2)}) collective-permute-start(bf16[384,1664]{1,0:T(8,128)(2,1)} %all-gather.5.cloned.1.call-done.refs_0_), channel_id=1, source_target_pairs={{0,2},{2,0},{1,3},{3,1},{4,6},{6,4},{5,7},{7,5},{8,10},{10,8},{9,1... | collective-permute-start | bytes 3833864 | tf_op jit(solution)/shard_map/ppermute | solution.py:27
  77.2 38.4 %collective-permute-start.11 = (bf16[384,1664]{1,0:T(8,128)(2,1)}, bf16[384,1664]{1,0:T(8,128)(2,1)}, u32[]{:S(2)}, u32[]{:S(2)}) collective-permute-start(bf16[384,1664]{1,0:T(8,128)(2,1)} %collective-permute-done.refs_1_), channel_id=1, source_target_pairs={{0,2},{2,0},{1,3},{3,1},{4,6},{6,4},{5,7},{7,5},{8,10},{10,8},{9,1... | collective-permute-start | bytes 3833864 | tf_op jit(solution)/shard_map/ppermute | solution.py:27
  77.8 37.9 %collective-permute-start.9 = (bf16[384,1664]{1,0:T(8,128)(2,1)}, bf16[384,1664]{1,0:T(8,128)(2,1)}, u32[]{:S(2)}, u32[]{:S(2)}) collective-permute-start(bf16[384,1664]{1,0:T(8,128)(2,1)} %collective-permute-done.refs_1_), channel_id=1, source_target_pairs={{0,1},{1,0},{2,6},{3,7},{4,5},{5,4},{6,2},{7,3},{8,9},{9,8},{10,14... | collective-permute-start | bytes 3833864 | tf_op jit(solution)/shard_map/ppermute | solution.py:926
  79.0 36.7 %collective-permute-start.12 = (bf16[384,1664]{1,0:T(8,128)(2,1)}, bf16[384,1664]{1,0:T(8,128)(2,1)}, u32[]{:S(2)}, u32[]{:S(2)}) collective-permute-start(bf16[384,1664]{1,0:T(8,128)(2,1)} %collective-permute-done.1.refs_2_), channel_id=1, source_target_pairs={{0,2},{2,0},{1,3},{3,1},{4,6},{6,4},{5,7},{7,5},{8,10},{10,8},{9,1... | collective-permute-start | bytes 3833864 | tf_op jit(solution)/shard_map/ppermute | solution.py:27
  85.3 86.8 %all-gather.9.cloned.1.call-start = ((), (), s32[]{:S(2)}) async-start(), calls=%async_computation.5 | async-start | bytes 1474560 | tf_op jit(solution)/shard_map/all_gather | solution.py:1012
  86.6 27.1 %collective-permute-start.7 = (bf16[4,1,48,768]{3,2,0,1:T(8,128)(2,1)}, bf16[4,1,48,768]{3,2,0,1:T(8,128)(2,1)S(1)}, u32[]{:S(2)}, u32[]{:S(2)}) collective-permute-start(bf16[4,1,48,768]{3,2,0,1:T(8,128)(2,1)} %reshape.182), channel_id=1, source_target_pairs={{0,4},{4,0},{1,5},{5,1},{2,6},{6,2},{3,7},{7,3},{8,12},{12,8},{9,1... | collective-permute-start | bytes 884744 | tf_op jit(solution)/shard_map/ppermute | solution.py:27
  115.7 19.7 %collective-permute-start.16 = (bf16[384,1664]{1,0:T(8,128)(2,1)}, bf16[384,1664]{1,0:T(8,128)(2,1)S(1)}, u32[]{:S(2)}, u32[]{:S(2)}) collective-permute-start(bf16[384,1664]{1,0:T(8,128)(2,1)} %collective-permute-done.9.refs_3_), channel_id=1, source_target_pairs={{0,2},{2,0},{1,3},{3,1},{4,6},{6,4},{5,7},{7,5},{8,10},{10,8},{9,1... | collective-permute-start | bytes 3833864 | tf_op jit(solution)/shard_map/ppermute | solution.py:27
  116.8 10.4 %collective-permute-start.15 = (bf16[192,512]{1,0:T(8,128)(2,1)S(1)}, bf16[192,512]{1,0:T(8,128)(2,1)S(1)}, u32[]{:S(2)}, u32[]{:S(2)}) collective-permute-start(bf16[192,512]{1,0:T(8,128)(2,1)S(1)} %get-tuple-element.363), channel_id=1, source_target_pairs={{0,6},{2,4},{4,2},{6,0},{1,7},{3,5},{5,3},{7,1},{8,14},{10,12},{12... | collective-permute-start | bytes 589832 | tf_op jit(solution)/shard_map/ppermute | solution.py:934
  134.5 17.4 %collective-permute-start.19 = (bf16[384,1664]{1,0:T(8,128)(2,1)}, bf16[384,1664]{1,0:T(8,128)(2,1)}, u32[]{:S(2)}, u32[]{:S(2)}) collective-permute-start(bf16[384,1664]{1,0:T(8,128)(2,1)} %all-gather.11.cloned.1.call-done.refs_0_), channel_id=1, source_target_pairs={{0,4},{1,5},{2,3},{3,2},{4,0},{5,1},{6,7},{7,6},{8,12},{9,13},{10,... | collective-permute-start | bytes 3833864 | tf_op jit(solution)/shard_map/ppermute | solution.py:926
  134.5 328.5 %reduce-scatter.4.cloned.1.call-start = ((), (), s32[]{:S(2)}) async-start(), calls=%async_computation.7 | async-start | bytes 1720320 | tf_op jit(solution)/shard_map/reduce_scatter | solution.py:1174
  151.2 22.4 %collective-permute-start.17 = (bf16[2,768,512]{2,1,0:T(8,128)(2,1)}, bf16[2,768,512]{2,1,0:T(8,128)(2,1)}, u32[]{:S(2)}, u32[]{:S(2)}) collective-permute-start(bf16[2,768,512]{2,1,0:T(8,128)(2,1)} %get-tuple-element.192), channel_id=1, source_target_pairs={{0,2},{2,0},{1,3},{3,1},{4,6},{6,4},{5,7},{7,5},{8,10},{10,8},{9,1... | collective-permute-start | bytes 4718600 | tf_op jit(solution)/shard_map/ppermute | solution.py:27
  151.9 19.3 %collective-permute-start.21 = (bf16[512,768]{1,0:T(8,128)(2,1)}, bf16[512,768]{1,0:T(8,128)(2,1)S(1)}, u32[]{:S(2)}, u32[]{:S(2)}) collective-permute-start(bf16[512,768]{1,0:T(8,128)(2,1)} %get-tuple-element.196.refs_0_), channel_id=1, source_target_pairs={{0,4},{4,0},{1,5},{5,1},{2,6},{6,2},{3,7},{7,3},{8,12},{12,8},{9,1... | collective-permute-start | bytes 2359304 | tf_op jit(solution)/shard_map/ppermute | solution.py:27
  152.9 20.7 %collective-permute-start.18 = (bf16[512,768]{1,0:T(8,128)(2,1)S(1)}, bf16[512,768]{1,0:T(8,128)(2,1)S(1)}, u32[]{:S(2)}, u32[]{:S(2)}) collective-permute-start(bf16[512,768]{1,0:T(8,128)(2,1)S(1)} %copy-done.6), channel_id=1, source_target_pairs={{0,2},{2,0},{1,3},{3,1},{4,6},{6,4},{5,7},{7,5},{8,10},{10,8},{9,1... | collective-permute-start | bytes 2359304 | tf_op jit(solution)/shard_map/ppermute | solution.py:27
  153.2 20.4 %collective-permute-start.20 = (bf16[512,768]{1,0:T(8,128)(2,1)}, bf16[512,768]{1,0:T(8,128)(2,1)}, u32[]{:S(2)}, u32[]{:S(2)}) collective-permute-start(bf16[512,768]{1,0:T(8,128)(2,1)} %get-tuple-element.196.refs_0_), channel_id=1, source_target_pairs={{0,2},{2,0},{1,3},{3,1},{4,6},{6,4},{5,7},{7,5},{8,10},{10,8},{9,1... | collective-permute-start | bytes 2359304 | tf_op jit(solution)/shard_map/ppermute | solution.py:27
  174.5 44.6 %collective-permute-start.27 = (bf16[384,1664]{1,0:T(8,128)(2,1)}, bf16[384,1664]{1,0:T(8,128)(2,1)}, u32[]{:S(2)}, u32[]{:S(2)}) collective-permute-start(bf16[384,1664]{1,0:T(8,128)(2,1)} %all-gather.11.cloned.1.call-done.refs_0_), channel_id=1, source_target_pairs={{0,1},{1,0},{2,6},{3,7},{4,5},{5,4},{6,2},{7,3},{8,9},{9,8},{10,14... | collective-permute-start | bytes 3833864 | tf_op jit(solution)/shard_map/ppermute | solution.py:926
  175.5 43.6 %collective-permute-start.29 = (bf16[384,1664]{1,0:T(8,128)(2,1)}, bf16[384,1664]{1,0:T(8,128)(2,1)S(1)}, u32[]{:S(2)}, u32[]{:S(2)}) collective-permute-start(bf16[384,1664]{1,0:T(8,128)(2,1)} %all-gather.11.cloned.1.call-done.refs_0_), channel_id=1, source_target_pairs={{0,2},{2,0},{1,3},{3,1},{4,6},{6,4},{5,7},{7,5},{8,10},{10,8},{9,1... | collective-permute-start | bytes 3833864 | tf_op jit(solution)/shard_map/ppermute | solution.py:27
  175.8 43.2 %collective-permute-start.28 = (bf16[384,1664]{1,0:T(8,128)(2,1)}, bf16[384,1664]{1,0:T(8,128)(2,1)}, u32[]{:S(2)}, u32[]{:S(2)}) collective-permute-start(bf16[384,1664]{1,0:T(8,128)(2,1)} %collective-permute-done.19.refs_1_), channel_id=1, source_target_pairs={{0,1},{1,0},{2,6},{3,7},{4,5},{5,4},{6,2},{7,3},{8,9},{9,8},{10,14... | collective-permute-start | bytes 3833864 | tf_op jit(solution)/shard_map/ppermute | solution.py:926
  176.2 42.8 %collective-permute-start.30 = (bf16[384,1664]{1,0:T(8,128)(2,1)}, bf16[384,1664]{1,0:T(8,128)(2,1)S(1)}, u32[]{:S(2)}, u32[]{:S(2)}) collective-permute-start(bf16[384,1664]{1,0:T(8,128)(2,1)} %collective-permute-done.19.refs_1_), channel_id=1, source_target_pairs={{0,2},{2,0},{1,3},{3,1},{4,6},{6,4},{5,7},{7,5},{8,10},{10,8},{9,1... | collective-permute-start | bytes 3833864 | tf_op jit(solution)/shard_map/ppermute | solution.py:27
  176.6 34.2 %collective-permute-start.24 = (bf16[4,1,48,768]{3,2,0,1:T(8,128)(2,1)S(1)}, bf16[4,1,48,768]{3,2,0,1:T(8,128)(2,1)S(1)}, u32[]{:S(2)}, u32[]{:S(2)}) collective-permute-start(bf16[4,1,48,768]{3,2,0,1:T(8,128)(2,1)S(1)} %reshape.181), channel_id=1, source_target_pairs={{0,4},{4,0},{1,5},{5,1},{2,6},{6,2},{3,7},{7,3},{8,12},{12,8},{9,1... | collective-permute-start | bytes 884744 | tf_op jit(solution)/shard_map/ppermute | solution.py:27
  220.4 9.8 %collective-permute-start.33 = (bf16[192,512]{1,0:T(8,128)(2,1)S(1)}, bf16[192,512]{1,0:T(8,128)(2,1)S(1)}, u32[]{:S(2)}, u32[]{:S(2)}) collective-permute-start(bf16[192,512]{1,0:T(8,128)(2,1)S(1)} %get-tuple-element.355), channel_id=1, source_target_pairs={{0,6},{2,4},{4,2},{6,0},{1,7},{3,5},{5,3},{7,1},{8,14},{10,12},{12... | collective-permute-start | bytes 589832 | tf_op jit(solution)/shard_map/ppermute | solution.py:934
  230.2 11.6 %collective-permute-start.35 = (bf16[384,1664]{1,0:T(8,128)(2,1)}, bf16[384,1664]{1,0:T(8,128)(2,1)}, u32[]{:S(2)}, u32[]{:S(2)}) collective-permute-start(bf16[384,1664]{1,0:T(8,128)(2,1)} %collective-permute-done.28.refs_3_), channel_id=1, source_target_pairs={{0,2},{2,0},{1,3},{3,1},{4,6},{6,4},{5,7},{7,5},{8,10},{10,8},{9,1... | collective-permute-start | bytes 3833864 | tf_op jit(solution)/shard_map/ppermute | solution.py:27
  230.2 11.6 %collective-permute-start.34 = (bf16[384,1664]{1,0:T(8,128)(2,1)}, bf16[384,1664]{1,0:T(8,128)(2,1)}, u32[]{:S(2)}, u32[]{:S(2)}) collective-permute-start(bf16[384,1664]{1,0:T(8,128)(2,1)} %collective-permute-done.27.refs_2_), channel_id=1, source_target_pairs={{0,2},{2,0},{1,3},{3,1},{4,6},{6,4},{5,7},{7,5},{8,10},{10,8},{9,1... | collective-permute-start | bytes 3833864 | tf_op jit(solution)/shard_map/ppermute | solution.py:27
  265.1 15.8 %collective-permute-start.39 = (bf16[2,512,768]{2,1,0:T(8,128)(2,1)}, bf16[2,512,768]{2,1,0:T(8,128)(2,1)S(1)}, u32[]{:S(2)}, u32[]{:S(2)}) collective-permute-start(bf16[2,512,768]{2,1,0:T(8,128)(2,1)} %get-tuple-element.225), channel_id=1, source_target_pairs={{0,2},{2,0},{1,3},{3,1},{4,6},{6,4},{5,7},{7,5},{8,10},{10,8},{9,1... | collective-permute-start | bytes 4718600 | tf_op jit(solution)/shard_map/ppermute | solution.py:27
  265.2 15.7 %collective-permute-start.40 = (bf16[2,768,512]{2,1,0:T(8,128)(2,1)}, bf16[2,768,512]{2,1,0:T(8,128)(2,1)S(1)}, u32[]{:S(2)}, u32[]{:S(2)}) collective-permute-start(bf16[2,768,512]{2,1,0:T(8,128)(2,1)} %get-tuple-element.233), channel_id=1, source_target_pairs={{0,2},{2,0},{1,3},{3,1},{4,6},{6,4},{5,7},{7,5},{8,10},{10,8},{9,1... | collective-permute-start | bytes 4718600 | tf_op jit(solution)/shard_map/ppermute | solution.py:27
  271.6 9.3 %collective-permute-start.42 = (bf16[512,768]{1,0:T(8,128)(2,1)S(1)}, bf16[512,768]{1,0:T(8,128)(2,1)S(1)}, u32[]{:S(2)}, u32[]{:S(2)}) collective-permute-start(bf16[512,768]{1,0:T(8,128)(2,1)S(1)} %copy-done.2), channel_id=1, source_target_pairs={{0,2},{2,0},{1,3},{3,1},{4,6},{6,4},{5,7},{7,5},{8,10},{10,8},{9,1... | collective-permute-start | bytes 2359304 | tf_op jit(solution)/shard_map/ppermute | solution.py:27
  272.0 8.9 %collective-permute-start.41 = (bf16[512,768]{1,0:T(8,128)(2,1)S(1)}, bf16[512,768]{1,0:T(8,128)(2,1)S(1)}, u32[]{:S(2)}, u32[]{:S(2)}) collective-permute-start(bf16[512,768]{1,0:T(8,128)(2,1)S(1)} %copy-done.10), channel_id=1, source_target_pairs={{0,2},{2,0},{1,3},{3,1},{4,6},{6,4},{5,7},{7,5},{8,10},{10,8},{9,1... | collective-permute-start | bytes 2359304 | tf_op jit(solution)/shard_map/ppermute | solution.py:27
  279.9 8.6 %collective-permute-start.44 = (bf16[4,48,768]{2,1,0:T(8,128)(2,1)S(1)}, bf16[4,48,768]{2,1,0:T(8,128)(2,1)S(1)}, u32[]{:S(2)}, u32[]{:S(2)}) collective-permute-start(bf16[4,48,768]{2,1,0:T(8,128)(2,1)S(1)} %fusion.4), channel_id=1, source_target_pairs={{0,4},{4,0},{1,5},{5,1},{2,6},{6,2},{3,7},{7,3},{8,12},{12,8},{9,1... | collective-permute-start | bytes 884744 | tf_op jit(solution)/shard_map/ppermute | solution.py:27
  289.2 32.4 %collective-permute-start.45 = (bf16[768,1664]{1,0:T(8,128)(2,1)}, bf16[768,1664]{1,0:T(8,128)(2,1)}, u32[]{:S(2)}, u32[]{:S(2)}) collective-permute-start(bf16[768,1664]{1,0:T(8,128)(2,1)} %feed_weights.4), channel_id=1, source_target_pairs={{0,1},{1,0},{2,6},{3,7},{4,5},{5,4},{6,2},{7,3},{8,9},{9,8},{10,14... | collective-permute-start | bytes 7667720 | tf_op jit(solution)/shard_map/ppermute | solution.py:926
  328.0 18.8 %collective-permute-start.47 = (bf16[512,768]{1,0:T(8,128)(2,1)S(1)}, bf16[512,768]{1,0:T(8,128)(2,1)S(1)}, u32[]{:S(2)}, u32[]{:S(2)}) collective-permute-start(bf16[512,768]{1,0:T(8,128)(2,1)S(1)} %fusion.1), channel_id=1, source_target_pairs={{0,4},{4,0},{1,5},{5,1},{2,6},{6,2},{3,7},{7,3},{8,12},{12,8},{9,1... | collective-permute-start | bytes 2359304 | tf_op jit(solution)/shard_map/ppermute | solution.py:27
  328.7 10.1 %collective-permute-start.48 = (bf16[256,768]{1,0:T(8,128)(2,1)S(1)}, bf16[256,768]{1,0:T(8,128)(2,1)S(1)}, u32[]{:S(2)}, u32[]{:S(2)}) collective-permute-start(bf16[256,768]{1,0:T(8,128)(2,1)S(1)} %get-tuple-element.354), channel_id=1, source_target_pairs={{0,1},{1,0},{2,3},{3,2},{4,5},{5,4},{6,7},{7,6},{8,9},{9,8},{10,11... | collective-permute-start | bytes 1179656 | tf_op jit(solution)/shard_map/ppermute | solution.py:27
  347.7 18.1 %collective-permute-start.49 = (bf16[384,1664]{1,0:T(8,128)(2,1)}, bf16[384,1664]{1,0:T(8,128)(2,1)}, u32[]{:S(2)}, u32[]{:S(2)}) collective-permute-start(bf16[384,1664]{1,0:T(8,128)(2,1)} %add_convert_fusion.3), channel_id=1, source_target_pairs={{0,4},{1,5},{2,3},{3,2},{4,0},{5,1},{6,7},{7,6},{8,12},{9,13},{10,... | collective-permute-start | bytes 3833864 | tf_op jit(solution)/shard_map/ppermute | solution.py:926
  358.0 134.6 %reduce-scatter.6.cloned.1.call-start = ((), (), s32[]{:S(2)}) async-start(), calls=%async_computation.8 | async-start | bytes 1597440 | tf_op jit(solution)/shard_map/reduce_scatter | solution.py:1186
  383.5 17.0 %collective-permute-start.53 = (bf16[2,512,768]{2,1,0:T(8,128)(2,1)}, bf16[2,512,768]{2,1,0:T(8,128)(2,1)S(1)}, u32[]{:S(2)}, u32[]{:S(2)}) collective-permute-start(bf16[2,512,768]{2,1,0:T(8,128)(2,1)} %get-tuple-element.265), channel_id=1, source_target_pairs={{0,2},{2,0},{1,3},{3,1},{4,6},{6,4},{5,7},{7,5},{8,10},{10,8},{9,1... | collective-permute-start | bytes 4718600 | tf_op jit(solution)/shard_map/ppermute | solution.py:27
  388.6 11.8 %collective-permute-start.54 = (bf16[512,768]{1,0:T(8,128)(2,1)S(1)}, bf16[512,768]{1,0:T(8,128)(2,1)S(1)}, u32[]{:S(2)}, u32[]{:S(2)}) collective-permute-start(bf16[512,768]{1,0:T(8,128)(2,1)S(1)} %copy-done.13), channel_id=1, source_target_pairs={{0,2},{2,0},{1,3},{3,1},{4,6},{6,4},{5,7},{7,5},{8,10},{10,8},{9,1... | collective-permute-start | bytes 2359304 | tf_op jit(solution)/shard_map/ppermute | solution.py:27
  390.2 10.2 %collective-permute-start.52 = (bf16[192,512]{1,0:T(8,128)(2,1)S(1)}, bf16[192,512]{1,0:T(8,128)(2,1)S(1)}, u32[]{:S(2)}, u32[]{:S(2)}) collective-permute-start(bf16[192,512]{1,0:T(8,128)(2,1)S(1)} %copy-done.98), channel_id=1, source_target_pairs={{0,6},{2,4},{4,2},{6,0},{1,7},{3,5},{5,3},{7,1},{8,14},{10,12},{12... | collective-permute-start | bytes 589832 | tf_op jit(solution)/shard_map/ppermute | solution.py:934
  391.0 22.0 %collective-permute-start.56 = (bf16[4,48,768]{2,1,0:T(8,128)(2,1)S(1)}, bf16[4,48,768]{2,1,0:T(8,128)(2,1)S(1)}, u32[]{:S(2)}, u32[]{:S(2)}) collective-permute-start(bf16[4,48,768]{2,1,0:T(8,128)(2,1)S(1)} %fusion.3), channel_id=1, source_target_pairs={{0,4},{4,0},{1,5},{5,1},{2,6},{6,2},{3,7},{7,3},{8,12},{12,8},{9,1... | collective-permute-start | bytes 884744 | tf_op jit(solution)/shard_map/ppermute | solution.py:27
  413.7 36.4 %collective-permute-start.57 = (bf16[768,1664]{1,0:T(8,128)(2,1)}, bf16[768,1664]{1,0:T(8,128)(2,1)S(1)}, u32[]{:S(2)}, u32[]{:S(2)}) collective-permute-start(bf16[768,1664]{1,0:T(8,128)(2,1)} %feed_weights.6), channel_id=1, source_target_pairs={{0,1},{1,0},{2,6},{3,7},{4,5},{5,4},{6,2},{7,3},{8,9},{9,8},{10,14... | collective-permute-start | bytes 7667720 | tf_op jit(solution)/shard_map/ppermute | solution.py:926
  418.1 116.9 %reduce-scatter.8.cloned.1.call-start = ((), (), s32[]{:S(2)}) async-start(), calls=%async_computation.9 | async-start | bytes 1720320 | tf_op jit(solution)/shard_map/reduce_scatter | solution.py:1180
  455.1 24.1 %collective-permute-start.61 = (bf16[384,1664]{1,0:T(8,128)(2,1)}, bf16[384,1664]{1,0:T(8,128)(2,1)}, u32[]{:S(2)}, u32[]{:S(2)}) collective-permute-start(bf16[384,1664]{1,0:T(8,128)(2,1)} %add_convert_fusion.2), channel_id=1, source_target_pairs={{0,4},{1,5},{2,3},{3,2},{4,0},{5,1},{6,7},{7,6},{8,12},{9,13},{10,... | collective-permute-start | bytes 3833864 | tf_op jit(solution)/shard_map/ppermute | solution.py:926
  463.1 16.0 %collective-permute-start.62 = (bf16[192,896]{1,0:T(8,128)(2,1)}, bf16[192,896]{1,0:T(8,128)(2,1)S(1)}, u32[]{:S(2)}, u32[]{:S(2)}) collective-permute-start(bf16[192,896]{1,0:T(8,128)(2,1)} %reduce-scatter.4.cloned.1.call-done), channel_id=1, source_target_pairs={{0,1},{1,0},{2,3},{3,2},{4,5},{5,4},{6,7},{7,6},{8,9},{9,8},{10,11... | collective-permute-start | bytes 1032200 | tf_op jit(solution)/shard_map/ppermute | solution.py:27
  466.5 19.8 %collective-permute-start.59 = (bf16[512,768]{1,0:T(8,128)(2,1)S(1)}, bf16[512,768]{1,0:T(8,128)(2,1)S(1)}, u32[]{:S(2)}, u32[]{:S(2)}) collective-permute-start(bf16[512,768]{1,0:T(8,128)(2,1)S(1)} %fusion), channel_id=1, source_target_pairs={{0,4},{4,0},{1,5},{5,1},{2,6},{6,2},{3,7},{7,3},{8,12},{12,8},{9,1... | collective-permute-start | bytes 2359304 | tf_op jit(solution)/shard_map/ppermute | solution.py:27
  492.6 19.5 %collective-permute-start.67 = (bf16[192,896]{1,0:T(8,128)(2,1)S(1)}, bf16[192,896]{1,0:T(8,128)(2,1)S(1)}, u32[]{:S(2)}, u32[]{:S(2)}) collective-permute-start(bf16[192,896]{1,0:T(8,128)(2,1)S(1)} %add_convert_fusion.5.refs_0_), channel_id=1, source_target_pairs={{0,4},{4,0},{1,5},{5,1},{2,6},{6,2},{3,7},{7,3},{8,12},{12,8},{9,1... | collective-permute-start | bytes 1032200 | tf_op jit(solution)/shard_map/ppermute | solution.py:27
  494.0 18.2 %collective-permute-start.63 = (bf16[96,1664]{1,0:T(8,128)(2,1)S(1)}, bf16[96,1664]{1,0:T(8,128)(2,1)S(1)}, u32[]{:S(2)}, u32[]{:S(2)}) collective-permute-start(bf16[96,1664]{1,0:T(8,128)(2,1)S(1)} %get-tuple-element.332), channel_id=1, source_target_pairs={{0,8},{8,16},{16,24},{24,0},{1,9},{9,17},{17,25},{25,1},{2,10},{10... | collective-permute-start | bytes 958472 | tf_op jit(solution)/shard_map/ppermute | solution.py:1019
  501.1 26.6 %collective-permute-start.64 = (bf16[96,1664]{1,0:T(8,128)(2,1)S(1)}, bf16[96,1664]{1,0:T(8,128)(2,1)}, u32[]{:S(2)}, u32[]{:S(2)}) collective-permute-start(bf16[96,1664]{1,0:T(8,128)(2,1)S(1)} %get-tuple-element.331), channel_id=1, source_target_pairs={{0,16},{8,24},{16,0},{24,8},{1,17},{9,25},{17,1},{25,9},{2,18},{10... | collective-permute-start | bytes 958472 | tf_op jit(solution)/shard_map/ppermute | solution.py:1019
  506.6 23.2 %collective-permute-start.69 = (bf16[96,1664]{1,0:T(8,128)(2,1)}, bf16[96,1664]{1,0:T(8,128)(2,1)}, u32[]{:S(2)}, u32[]{:S(2)}) collective-permute-start(bf16[96,1664]{1,0:T(8,128)(2,1)} %reduce-scatter.6.cloned.1.call-done.refs_4_), channel_id=1, source_target_pairs={{0,4},{4,0},{1,5},{5,1},{2,6},{6,2},{3,7},{7,3},{8,12},{12,8},{9,1... | collective-permute-start | bytes 958472 | tf_op jit(solution)/shard_map/ppermute | solution.py:27
  508.0 25.5 %collective-permute-start.66 = (bf16[192,896]{1,0:T(8,128)(2,1)S(1)}, bf16[192,896]{1,0:T(8,128)(2,1)S(1)}, u32[]{:S(2)}, u32[]{:S(2)}) collective-permute-start(bf16[192,896]{1,0:T(8,128)(2,1)S(1)} %add_convert_fusion.5.refs_0_), channel_id=1, source_target_pairs={{0,2},{2,0},{1,3},{3,1},{4,6},{6,4},{5,7},{7,5},{8,10},{10,8},{9,1... | collective-permute-start | bytes 1032200 | tf_op jit(solution)/shard_map/ppermute | solution.py:27
  512.1 21.3 %collective-permute-start.68 = (bf16[192,896]{1,0:T(8,128)(2,1)S(1)}, bf16[192,896]{1,0:T(8,128)(2,1)}, u32[]{:S(2)}, u32[]{:S(2)}) collective-permute-start(bf16[192,896]{1,0:T(8,128)(2,1)S(1)} %collective-permute-done.67.refs_2_), channel_id=1, source_target_pairs={{0,2},{2,0},{1,3},{3,1},{4,6},{6,4},{5,7},{7,5},{8,10},{10,8},{9,1... | collective-permute-start | bytes 1032200 | tf_op jit(solution)/shard_map/ppermute | solution.py:27
  512.2 21.2 %collective-permute-start.65 = (bf16[96,1664]{1,0:T(8,128)(2,1)}, bf16[96,1664]{1,0:T(8,128)(2,1)}, u32[]{:S(2)}, u32[]{:S(2)}) collective-permute-start(bf16[96,1664]{1,0:T(8,128)(2,1)} %get-tuple-element.330), channel_id=1, source_target_pairs={{0,24},{8,0},{16,8},{24,16},{1,25},{9,1},{17,9},{25,17},{2,26},{10... | collective-permute-start | bytes 958472 | tf_op jit(solution)/shard_map/ppermute | solution.py:1019
  535.0 10.1 %collective-permute-start.76 = (bf16[192,896]{1,0:T(8,128)(2,1)}, bf16[192,896]{1,0:T(8,128)(2,1)S(1)}, u32[]{:S(2)}, u32[]{:S(2)}) collective-permute-start(bf16[192,896]{1,0:T(8,128)(2,1)} %reduce-scatter.8.cloned.1.call-done), channel_id=1, source_target_pairs={{0,1},{1,0},{2,3},{3,2},{4,5},{5,4},{6,7},{7,6},{8,9},{9,8},{10,11... | collective-permute-start | bytes 1032200 | tf_op jit(solution)/shard_map/ppermute | solution.py:27
  535.1 7.3 %collective-permute-start.72 = (bf16[96,1664]{1,0:T(8,128)(2,1)S(1)}, bf16[96,1664]{1,0:T(8,128)(2,1)S(1)}, u32[]{:S(2)}, u32[]{:S(2)}) collective-permute-start(bf16[96,1664]{1,0:T(8,128)(2,1)S(1)} %add_convert_fusion.6.refs_4_), channel_id=1, source_target_pairs={{0,4},{4,0},{1,5},{5,1},{2,6},{6,2},{3,7},{7,3},{8,12},{12,8},{9,1... | collective-permute-start | bytes 958472 | tf_op jit(solution)/shard_map/ppermute | solution.py:27
  536.5 19.2 %collective-permute-start.60 = (bf16[256,768]{1,0:T(8,128)(2,1)S(1)}, bf16[256,768]{1,0:T(8,128)(2,1)S(1)}, u32[]{:S(2)}, u32[]{:S(2)}) collective-permute-start(bf16[256,768]{1,0:T(8,128)(2,1)S(1)} %get-tuple-element.352), channel_id=1, source_target_pairs={{0,1},{1,0},{2,3},{3,2},{4,5},{5,4},{6,7},{7,6},{8,9},{9,8},{10,11... | collective-permute-start | bytes 1179656 | tf_op jit(solution)/shard_map/ppermute | solution.py:27
  538.0 8.6 %collective-permute-start.73 = (bf16[96,1664]{1,0:T(8,128)(2,1)S(1)}, bf16[96,1664]{1,0:T(8,128)(2,1)S(1)}, u32[]{:S(2)}, u32[]{:S(2)}) collective-permute-start(bf16[96,1664]{1,0:T(8,128)(2,1)S(1)} %add_convert_fusion.6.refs_4_), channel_id=1, source_target_pairs={{0,2},{2,0},{1,3},{3,1},{4,6},{6,4},{5,7},{7,5},{8,10},{10,8},{9,1... | collective-permute-start | bytes 958472 | tf_op jit(solution)/shard_map/ppermute | solution.py:27
  545.2 7.0 %collective-permute-start.78 = (bf16[192,896]{1,0:T(8,128)(2,1)S(1)}, bf16[192,896]{1,0:T(8,128)(2,1)S(1)}, u32[]{:S(2)}, u32[]{:S(2)}) collective-permute-start(bf16[192,896]{1,0:T(8,128)(2,1)S(1)} %add_convert_fusion.4.refs_0_), channel_id=1, source_target_pairs={{0,4},{4,0},{1,5},{5,1},{2,6},{6,2},{3,7},{7,3},{8,12},{12,8},{9,1... | collective-permute-start | bytes 1032200 | tf_op jit(solution)/shard_map/ppermute | solution.py:27
  546.7 15.9 %collective-permute-start.75 = (f32[96,4]{1,0:T(8,128)S(1)}, f32[96,4]{1,0:T(8,128)S(1)}, u32[]{:S(2)}, u32[]{:S(2)}) collective-permute-start(f32[96,4]{1,0:T(8,128)S(1)} %convert_add_fusion.4), channel_id=1, source_target_pairs={{0,1},{1,0},{2,3},{3,2},{4,5},{5,4},{6,7},{7,6},{8,9},{9,8},{10,11... | collective-permute-start | bytes 4616 | tf_op jit(solution)/shard_map/ppermute | solution.py:27
  548.1 14.7 %collective-permute-start.77 = (bf16[192,896]{1,0:T(8,128)(2,1)S(1)}, bf16[192,896]{1,0:T(8,128)(2,1)S(1)}, u32[]{:S(2)}, u32[]{:S(2)}) collective-permute-start(bf16[192,896]{1,0:T(8,128)(2,1)S(1)} %add_convert_fusion.4.refs_0_), channel_id=1, source_target_pairs={{0,2},{2,0},{1,3},{3,1},{4,6},{6,4},{5,7},{7,5},{8,10},{10,8},{9,1... | collective-permute-start | bytes 1032200 | tf_op jit(solution)/shard_map/ppermute | solution.py:27
  552.2 10.7 %collective-permute-start.79 = (bf16[192,896]{1,0:T(8,128)(2,1)S(1)}, bf16[192,896]{1,0:T(8,128)(2,1)}, u32[]{:S(2)}, u32[]{:S(2)}) collective-permute-start(bf16[192,896]{1,0:T(8,128)(2,1)S(1)} %collective-permute-done.78.refs_2_), channel_id=1, source_target_pairs={{0,2},{2,0},{1,3},{3,1},{4,6},{6,4},{5,7},{7,5},{8,10},{10,8},{9,1... | collective-permute-start | bytes 1032200 | tf_op jit(solution)/shard_map/ppermute | solution.py:27
  (126 other events, 1242.9 us)
Sparse Core Ops, SparseCore 0:
  13.9 31.7 all-gather.4
  47.8 32.6 all-gather.6
  85.4 30.4 all-gather.10
  134.6 30.9 all-gather.8
  358.1 35.6 reduce-scatter.3
  418.2 32.3 reduce-scatter.5
  463.2 37.8 reduce-scatter.7

commit v4 on v3

--- a/solution.py
+++ b/solution.py
@@ -13,7 +13,6 @@
 LAYERS = 2
 BLK = 256
 NEG = -1e30
-TILES = 2
 EPS = 1e-06
 F32 = jnp.float32
 BF16 = jnp.bfloat16
@@ -71,7 +70,7 @@
 
 def attention_forward_kernel(norm, info, *refs):
     parts, (w_ref, bias_ref, gain_ref, shift_ref) = refs[:4], refs[4:8]
-    at_out, qkv_out, out_ref, lse_ref, a_ref, at_ref, qkv_ref, v01_t, v2_t, sems, out_sems = refs[8:]
+    at_out, qkv_out, out_ref, lse_ref, a_ref, at_ref, qkv_ref, v_t, sems, out_sems = refs[8:]
     length = qkv_ref.shape[0]
     ends = (info[0], info[1], info[2])
     dev, half = info[3], info[4]
@@ -92,8 +91,11 @@
             at_ref[:, goal] = values.T
             qkv_ref[goal, 0:384] = found[:, 0:384].astype(BF16)
             qkv_ref[goal, 384:576] = (found[:, 384:576] * HEAD**-0.5).astype(BF16)
-            v01_t[:, goal] = qkv_ref[goal, 256:384].T
-            v2_t[:, goal] = qkv_ref[goal, 128:256].T
+            pair = qkv_ref[goal, 256:384].T
+            ones = jnp.ones((16, BLK), BF16)
+            for head, found in enumerate((pair[:HEAD], pair[HEAD:], qkv_ref[goal, 128:256].T[HEAD:])):
+                v_t[head, 0:HEAD, goal] = found
+                v_t[head, HEAD : HEAD + 16, goal] = ones
             return nothing
 
         lax.fori_loop(0, each // BLK, project, 0)
@@ -114,33 +116,31 @@
         queries = three_heads(qkv_ref[mine, 384:512].T, qkv_ref[mine, 512:576].T)
         low, high = doc_range(first, ends, length)
 
-        def body(pair, carry):
+        def body(count, begin, at, carry):
             tiles = []
-            for more in range(TILES):
-                block = low + TILES * pair + more
-                place = block_place(jnp.minimum(block, blocks - 1), dev, half)
+            for more in range(count):
+                block = begin + count * at + more
+                place = block_place(block, dev, half)
                 rows = pl.ds(pl.multiple_of(place * BLK, BLK), BLK)
                 places = block * BLK + lax.broadcasted_iota(jnp.int32, (BLK, 1), 0)
-                tiles.append((rows, seg_of(places, (*ends, length)) == seg_q))
+                tiles.append((rows, seg_of(places, ends) == seg_q))
 
             def score(head):
                 lanes = slice(128, 256) if head == 2 else slice(0, 128)
                 return [jnp.where(allowed, dot(qkv_ref[rows, lanes], queries[head]), NEG) for rows, allowed in tiles]
 
             def weigh(head, scores):
-                top, total, acc = carry[head]
+                top, acc = carry[head]
                 new_top = jnp.maximum(top, jnp.max(reduce(jnp.maximum, scores), axis=0, keepdims=True))
                 shrink = jnp.exp(top - new_top)
                 exps = [jnp.exp(one - new_top) for one in scores]
-                total = total * shrink + jnp.sum(reduce(jnp.add, exps), axis=0, keepdims=True)
-                return new_top, total, acc * shrink, [exp.astype(BF16) for exp in exps]
+                return new_top, acc * shrink, [exp.astype(BF16) for exp in exps]
 
             def gather(head, weighed):
-                top, total, acc, exps = weighed
+                top, acc, exps = weighed
                 for (rows, _), exp in zip(tiles, exps):
-                    values = v2_t[HEAD:128, rows] if head == 2 else v01_t[head * HEAD : (head + 1) * HEAD, rows]
-                    acc = acc + dot(values, exp)
-                return top, total, acc
+                    acc = acc + dot(v_t[head, :, rows], exp)
+                return top, acc
 
             s0 = score(0)
             s1 = score(1)
@@ -156,16 +156,18 @@
         start = tuple(
             (
                 jnp.full((1, BLK), NEG, F32),
-                jnp.zeros((1, BLK), F32),
-                jnp.zeros((HEAD, BLK), F32),
+                jnp.zeros((HEAD + 16, BLK), F32),
             )
             for _ in range(3)
         )
-        final = lax.fori_loop(0, (high - low + TILES - 1) // TILES, body, start)
+        pairs, odd = (high - low) // 2, (high - low) % 2
+        final = lax.fori_loop(0, pairs, partial(body, 2, low), start)
+        final = lax.fori_loop(0, odd, partial(body, 1, high - 1), final)
         cols = pl.ds(pl.multiple_of((step % 2) * BLK, BLK), BLK)
         for head in range(3):
-            top, total, acc = final[head]
-            out_ref[step // 2, head * HEAD : (head + 1) * HEAD, cols] = (acc / total).astype(BF16)
+            top, acc = final[head]
+            total = acc[HEAD : HEAD + 1]
+            out_ref[step // 2, head * HEAD : (head + 1) * HEAD, cols] = (acc[:HEAD] / total).astype(BF16)
             lse_ref[head : head + 1, mine] = top + jnp.log(total)
         return nothing
 
@@ -189,8 +191,7 @@
                 pltpu.VMEM((4, each, width), BF16),
                 pltpu.VMEM((width, length), BF16),
                 pltpu.VMEM((length, 576), BF16),
-                pltpu.VMEM((128, length), BF16),
-                pltpu.VMEM((128, length), BF16),
+                pltpu.VMEM((3, HEAD + 16, length), BF16),
                 pltpu.SemaphoreType.DMA((4,)),
                 pltpu.SemaphoreType.DMA((2,)),
             ],
@@ -208,11 +209,17 @@
     )(info, *parts, w_qkv, bias, gain, shift)
 
 
-def attention_backward_kernel(
-    info, qkv_ref, out_ref, lse_ref, w_ref, g0, g1, g2, g3,
-    du_out, core_out, far_out, own_out, sums_ref,
-    q01_t, q2_t, delta, dq_t, grad_t, du_ref, core_ref, far_ref, own_ref, sems,
-):
+def attention_backward_kernel(norm, info, qkv_ref, out_ref, lse_ref, w_ref, g0, g1, g2, g3, *refs):
+    if norm:
+        tokens, refs = refs[:4], refs[4:]
+        norm_sums, refs = refs[5], refs[:5] + refs[6:]
+        x_ref, da_ref, x_sems = refs[-3:]
+        token_copies = [pltpu.make_async_copy(part, x_ref.at[at], x_sems.at[at]) for at, part in enumerate(tokens)]
+        for copy in token_copies:
+            copy.start()
+        refs = refs[:-3]
+    du_out, core_out, far_out, own_out, sums_ref = refs[:5]
+    q01_t, q2_t, delta, dq_t, grad_t, du_ref, core_ref, far_ref, own_ref, sems = refs[5:]
     length = qkv_ref.shape[0]
     each = length // 4
     ends = (info[0], info[1], info[2])
@@ -240,16 +247,16 @@
         keys_t = (k01_t[:HEAD], k01_t[HEAD:], k2_t)
         low, high = doc_range(first, ends, length)
 
-        def body(pair, carry):
+        def body(width, begin, at, carry):
             blank = jnp.zeros((HEAD, BLK), BF16)
             tiles = []
-            for more in range(TILES):
-                block = low + TILES * pair + more
-                place = block_place(jnp.minimum(block, blocks - 1), dev, half)
+            for more in range(width):
+                block = begin + width * at + more
+                place = block_place(block, dev, half)
                 cols = pl.ds(pl.multiple_of(place * BLK, BLK), BLK)
                 part_cols = pl.ds(pl.multiple_of((place % 2) * BLK, BLK), BLK)
                 places = block * BLK + lax.broadcasted_iota(jnp.int32, (1, BLK), 1)
-                allowed = seg_k == seg_of(places, (*ends, length))
+                allowed = seg_k == seg_of(places, ends)
                 queries = three_heads(q01_t[:, cols], q2_t[:, cols])
                 grads = grad_t[place // 2, :, part_cols]
                 dos = (
@@ -290,7 +297,7 @@
                     dv01 = dv01 + more_v
                 return (dk01, dk2v2, dv01), more_q
 
-            count = 3 * TILES
+            count = 3 * width
             sums = carry
             more_q = []
             begun = {0: first_dots(0), 1: first_dots(1)}
@@ -304,13 +311,15 @@
                     more_q.append(found)
             sums, found = last_dots(count - 1, weighed[count - 1], sums)
             more_q.append(found)
-            for tile in range(TILES):
+            for tile in range(width):
                 cols = tiles[tile][0]
                 dq_t[:, cols] = dq_t[:, cols] + jnp.concatenate(more_q[3 * tile : 3 * tile + 3], axis=0)
             return sums
 
         zero = jnp.zeros((BLK, 128), F32)
-        dk01, dk2v2, dv01 = lax.fori_loop(0, (high - low + TILES - 1) // TILES, body, (zero, zero, zero))
+        pairs, odd = (high - low) // 2, (high - low) % 2
+        sums = lax.fori_loop(0, pairs, partial(body, 2, low), (zero, zero, zero))
+        dk01, dk2v2, dv01 = lax.fori_loop(0, odd, partial(body, 1, high - 1), sums)
         du_ref[mine, 0:128] = dk01.astype(BF16)
         du_ref[mine, 128:256] = dk2v2.astype(BF16)
         du_ref[mine, 256:384] = dv01.astype(BF16)
@@ -330,26 +339,52 @@
     copies = [pltpu.make_async_copy(du_ref, du_out, sems.at[0])]
     copies[0].start()
     plan = ((1, core_ref.at[0], core_out.at[0]), (3, core_ref.at[1], core_out.at[1]), (2, far_ref, far_out), (0, own_ref, own_out))
+    if norm:
+        for copy in token_copies:
+            copy.wait()
+        width = da_ref.shape[1]
+        totals = (jnp.zeros((1, width), F32), jnp.zeros((1, width), F32))
     for at, (part, target, goal) in enumerate(plan):
         kind = target.dtype
-        target[...] = dot(du_ref[part * each : (part + 1) * each, :], w_ref[:, 0:576], ((1,), (1,))).astype(kind)
+        found = dot(du_ref[part * each : (part + 1) * each, :], w_ref[:, 0:576], ((1,), (1,)))
+        if norm:
+            da_ref[...] = found
+
+            def rows_of(step, sums, part=part):
+                rows = pl.ds(pl.multiple_of(step * 64, 64), 64)
+                grad = da_ref[rows, :]
+                normed = norm_rows(x_ref[part, rows, :].astype(F32), 1.0, 0.0)
+                return (
+                    sums[0] + jnp.sum(grad * normed, axis=0, keepdims=True),
+                    sums[1] + jnp.sum(grad, axis=0, keepdims=True),
+                )
+
+            totals = lax.fori_loop(0, each // 64, rows_of, totals)
+            found = da_ref[...]
+        target[...] = found.astype(kind)
         copies.append(pltpu.make_async_copy(target, goal, sems.at[at + 1]))
         copies[-1].start()
+    if norm:
+        norm_sums[...] = jnp.zeros_like(norm_sums)
+        norm_sums[0:1, :] = totals[0]
+        norm_sums[1:2, :] = totals[1]
     for copy in copies:
         copy.wait()
 
 
-def attention_backward(info, qkv, out, lse, w_qkv, grads):
+def attention_backward(info, qkv, out, lse, w_qkv, grads, tokens=()):
+    norm = len(tokens) > 0
     length, each, width = qkv.shape[0], qkv.shape[0] // 4, w_qkv.shape[0]
     return pl.pallas_call(
-        attention_backward_kernel,
+        partial(attention_backward_kernel, norm),
         name="attention_backward",
         grid_spec=pltpu.PrefetchScalarGridSpec(
             num_scalar_prefetch=1,
             grid=(1,),
             in_specs=[whole(qkv.shape), whole(out.shape), whole(lse.shape), whole(w_qkv.shape)]
-            + [whole((192, each))] * 4,
-            out_specs=[HBM, HBM, HBM, HBM, whole((8, 576))],
+            + [whole((192, each))] * 4
+            + [HBM] * len(tokens),
+            out_specs=[HBM, HBM, HBM, HBM, whole((8, 576))] + [whole((8, width))] * norm,
             scratch_shapes=[
                 pltpu.VMEM((128, length), BF16),
                 pltpu.VMEM((64, length), BF16),
@@ -361,7 +396,8 @@
                 pltpu.VMEM((each, width), F32),
                 pltpu.VMEM((each, width), F32),
                 pltpu.SemaphoreType.DMA((5,)),
-            ],
+            ]
+            + [pltpu.VMEM((4, each, width), BF16), pltpu.VMEM((each, width), F32), pltpu.SemaphoreType.DMA((4,))] * norm,
         ),
         out_shape=(
             jax.ShapeDtypeStruct(qkv.shape, BF16),
@@ -369,12 +405,13 @@
             jax.ShapeDtypeStruct((each, width), F32),
             jax.ShapeDtypeStruct((each, width), F32),
             jax.ShapeDtypeStruct((8, 576), F32),
-        ),
+        )
+        + (jax.ShapeDtypeStruct((8, width), F32),) * norm,
         compiler_params=pltpu.CompilerParams(vmem_limit_bytes=56 << 20),
         cost_estimate=pl.CostEstimate(
             flops=20 * 10**9, transcendentals=3 * length * 1024, bytes_accessed=16 << 20
         ),
-    )(info, qkv, out, lse, w_qkv, *grads)
+    )(info, qkv, out, lse, w_qkv, *grads, *tokens)
 
 
 def attention_weights_kernel(at_ref, du_ref, vec_ref, own_ref, core_ref, far_ref, out_ref, spread):
@@ -605,7 +642,7 @@
     def rows_of(at, sums):
         rows = pl.ds(pl.multiple_of(at * 64, 64), 64)
         grad_in, gain_sum, bias_sum = norm_back(dc[rows, :], mid_ref[rows, :], gain_ref[...])
-        grad_mid = grad_ref[rows, :] + grad_in
+        grad_mid = grad_ref[rows, :].astype(F32) + grad_in
         dmid_ref[rows, :] = grad_mid
         branch = grad_mid.astype(BF16)
         da_ref[rows, :] = branch
@@ -706,7 +743,7 @@
     )(info, grad, dm, slope, middle, gain, w_out, *parts)
 
 
-def feed_both_kernel(info, c_ref, grad_ref, dm_ref, mid_ref, vec_ref, w_in, *refs):
+def feed_both_kernel(info, c_ref, dm_ref, mid_ref, vec_ref, w_in, *refs):
     parts, refs = refs[:8], refs[8:]
     own_out, other_out, dmid_ref, da_ref, sums_ref, *targets = refs[:9]
     act_own, act_other, x_ref = refs[9:12]
@@ -751,12 +788,12 @@
         after(at, found)
         found = later
     late_in.wait()
-    finish_back(info[3], grad_ref, mid_ref, vec_ref.at[1:2], w_ref, dm_ref, dc, dmid_ref, da_ref, sums_ref, targets)
+    finish_back(info[3], dm_ref, mid_ref, vec_ref.at[1:2], w_ref, dm_ref, dc, dmid_ref, da_ref, sums_ref, targets)
     for copy in outs:
         copy.wait()
 
 
-def feed_both(info, c, grad, dm, middle, vectors, w_out, parts):
+def feed_both(info, c, dm, middle, vectors, w_out, parts):
     toks, width = middle.shape
     units = 2 * parts[0].shape[0]
     shapes = back_outputs(toks, width, units) + [
@@ -770,7 +807,7 @@
         grid_spec=pltpu.PrefetchScalarGridSpec(
             num_scalar_prefetch=1,
             grid=(1,),
-            in_specs=[whole(v.shape) for v in (c, grad, dm, middle, vectors)] + [HBM] * 9,
+            in_specs=[whole(v.shape) for v in (c, dm, middle, vectors)] + [HBM] * 9,
             out_specs=[HBM] * 2 + [whole(shape.shape) for shape in shapes[2:9]] + [HBM, HBM, whole((toks, width))],
             scratch_shapes=[
                 pltpu.VMEM((4, units, toks), BF16),
@@ -786,7 +823,7 @@
         out_shape=shapes,
         compiler_params=pltpu.CompilerParams(vmem_limit_bytes=60 << 20),
         cost_estimate=pl.CostEstimate(flops=10**10, transcendentals=2 * 10**6, bytes_accessed=24 << 20),
-    )(info, c, grad, dm, middle, vectors, w_out, *parts)
+    )(info, c, dm, middle, vectors, w_out, *parts)
 
 
 def feed_weights_kernel(dh, dh2, act, act2, c, c2, dm, dm2, out_ref):
@@ -965,14 +1002,19 @@
     loc = width // 4
     quarter = rows // 4
 
-    def to_sequence(tokens):
-        own = lax.dynamic_index_in_dim(tokens, iy, 0, keepdims=False)
-        other = lax.dynamic_index_in_dim(tokens, 1 - iy, 0, keepdims=False)
-        return jnp.concatenate((own, swap(other, "tp")), axis=0)
+    def to_sequence(*arrays):
+        given = jnp.stack([lax.dynamic_index_in_dim(array, 1 - iy, 0, keepdims=False) for array in arrays])
+        given = swap(given, "tp")
+        return [
+            jnp.concatenate((lax.dynamic_index_in_dim(array, iy, 0, keepdims=False), other), axis=0)
+            for array, other in zip(arrays, given)
+        ]
+
+    def own_first(own, other):
+        return jnp.where(iy == 0, jnp.stack((own, other)), jnp.stack((other, own)))
 
     def from_sequence(tokens):
-        own, other = tokens[:toks], swap(tokens[toks:], "tp")
-        return jnp.where(iy == 0, jnp.stack((own, other)), jnp.stack((other, own)))
+        return own_first(tokens[:toks], swap(tokens[toks:], "tp"))
 
     lengths = lax.dynamic_index_in_dim(doc_lengths, iy, 0, keepdims=False)
     end0 = lengths[0]
@@ -1030,11 +1072,11 @@
         own = lax.dynamic_slice_in_dim(value, lax.axis_index("shard") * count, count, 0).astype(F32)
         return (own + sum(piece.astype(F32) for piece in arriving)).astype(value.dtype)
 
-    def around_hidden(own):
+    def around_hidden(own, *others):
         core, far = swap(own, "core"), swap(own, "cx")
-        return own, far, core, swap(far, "core")
-
-    hidden_own = to_sequence(hidden_in)
+        return own, far, core, swap(after(far, *others), "core")
+
+    hidden_own, raw_grad = to_sequence(hidden_in, output_grad)
     first_piece, attn_piece = hidden_piece(0), attention_piece(0)
     first_parts = around(after(hidden_own, first_piece, attn_piece))
     feed0 = over_shards(first_piece)
@@ -1081,12 +1123,9 @@
         else:
             own, one, two, three = w_feed1
             early_core = (swap(own, "core"), swap(one, "core"))
-            attended, w_out, raw_grad, own, one, two, three, *early_core = lax.optimization_barrier(
-                (attended, w_out1, raw_grad, own, one, two, three, *early_core)
+            attended, w_out, own, one, two, three, *early_core = lax.optimization_barrier(
+                (attended, w_out1, own, one, two, three, *early_core)
             )
-            grad = raw_grad.astype(F32) * keep
-            low_grad = grad.astype(BF16)
-            low_other = swap(low_grad, "core")
         parts = (
             attended[0],
             swap(attended[1], "core"),
@@ -1095,6 +1134,8 @@
         )
         if layer == 1:
             late_core = [swap(after(part, *parts), "core") for part in (two, three)]
+            low_grad = raw_grad * keep.astype(BF16)
+            low_other = swap(low_grad, "core")
             w_feed = (own, one, two, three, *early_core, *late_core)
         vectors = jnp.concatenate((bias_out, gain_two, bias_two), axis=0)
         context, middle, mlp_in = out_forward(info, parts, w_out, current, vectors)
@@ -1106,12 +1147,10 @@
             act_other, mlp_other = swap(act_other, "core"), swap(mlp_in, "core")
             attn_own = after(attn_own, one1)
             attn_parts = around(attn_own)
-            own_out1 = out_own(attn1)
-            own_out1, act_other, mlp_other, given, *attn_parts = lax.optimization_barrier(
-                (own_out1, act_other, mlp_other, output_grad, *attn_parts)
+            w_out1 = out_weights(out_own(after(attn1, attn_own)))
+            w_out1, act_other, mlp_other, *attn_parts = lax.optimization_barrier(
+                (w_out1, act_other, mlp_other, *attn_parts)
             )
-            raw_grad = to_sequence(given)
-            w_out1 = out_weights(own_out1)
             feed1, one1 = lax.optimization_barrier((feed1, one1, *attn_parts))[:2]
             w_feed1 = (feed1, one1, turned(feed1, False), turned(one1, False))
         else:
@@ -1122,6 +1161,7 @@
         current = result
     n = shards * units
 
+    before = ()
     for layer in reversed(range(LAYERS)):
         x_in, attn_t, qkv, attended, lse, context, middle, mlp_in, mlp_other, slope, act, act_other = saved[layer]
         gain_one, _, _, gain_two, _, _ = names[layer]
@@ -1130,13 +1170,13 @@
             found = feed_backward(info, grad, low_grad, slope, middle, gain_two, w_out, w_feed)
         else:
             vectors = jnp.concatenate((names[1][5], gain_two), axis=0)
-            *found, act, act_other, result = feed_both(info, mlp_in, grad, low_grad, middle, vectors, w_out, w_feed)
+            *found, act, act_other, result = feed_both(info, mlp_in, low_grad, middle, vectors, w_out, w_feed)
             act_other = swap(act_other, "core")
         dh, dh_other, middle_grad, branch_grad, sums_two, d0, d1, d2, d3 = found
         attn_grads = (d0, swap(d1, "core"), swap(d2, "cx"), diagonal(d3))
         tokens = (mlp_in, mlp_other, low_grad, low_other)
         dh_other = swap(dh_other, "core")
-        *attn_grads, dh_other = lax.optimization_barrier((*attn_grads, dh_other))
+        *attn_grads, dh_other = lax.optimization_barrier((*attn_grads, dh_other, *before))[:5]
         late = feed_weights(1, dh, dh_other, act, act_other, *tokens)
         w_out_grad = dot(context, branch_grad).astype(BF16).reshape(shards, 4, quarter, width)
         pieces = [lax.dynamic_index_in_dim(w_out_grad, dev ^ rel, 1, keepdims=False) for rel in range(4)]
@@ -1144,22 +1184,18 @@
         far = swap((pieces[2].astype(F32) + got[1].astype(F32)).astype(BF16), "cx")
         ready = [*attn_grads, late, far]
         if layer == 0:
+            attn_sum1 = after(attn_sum1, *attn_grads)
+            attn_sum1 = (attn_sum1.astype(F32) + swap(attn_sum1, "tp").astype(F32)).astype(BF16)
+            ready.append(attn_sum1)
             early = feed_weights(0, dh, dh_other, act, act_other, *tokens)
-            ready += [early]
+            ready.append(early)
         *attn_grads, late, far = lax.optimization_barrier(tuple(ready))[:6]
-        du, to_core, to_far, own, sums_u = attention_backward(info, qkv, attended, lse, w_qkv, attn_grads)
+        du, to_core, to_far, own, sums_u, *norm_sums = attention_backward(
+            info, qkv, attended, lse, w_qkv, attn_grads, first_parts if layer == 0 else ()
+        )
         late = turned(late, False)
         to_core = after(to_core, late)
         from_core = swap(to_core, "core")
-        to_far = (to_far + from_core[1].astype(F32)).astype(BF16)
-        if layer == 0:
-            part = (early[n:].astype(F32) + late[n:].astype(F32)).astype(BF16)
-            arrived = turned(part, True)
-        from_far = swap(to_far, "cx")
-        if layer > 0:
-            du, dh_now, early_late = lax.optimization_barrier((du, dh, late, to_far))[:3]
-            early = feed_weights(0, dh_now, dh_other, act, act_other, *tokens)
-            part = (early[n:].astype(F32) + early_late[n:].astype(F32)).astype(BF16)
         du_sum = sums_u[0]
         v_sum = jnp.concatenate((du_sum[256:384], du_sum[192:256]))
         q_row = lax.dynamic_update_slice_in_dim(jnp.zeros((width,), F32), du_sum[384:], loc * dev, 0)
@@ -1167,52 +1203,63 @@
         qv_rows = jnp.concatenate((q_row, v_row)).reshape(shards, 2, rows).transpose(1, 0, 2).reshape(2, width)
         vectors = jnp.concatenate((sums_two, qv_rows, jnp.zeros((6, width), F32)), axis=0)
         if layer == 0:
-            vectors = jnp.concatenate((vectors[:10], sums_one[:2], vectors[12:]), axis=0)
+            vectors = jnp.concatenate((vectors[:10], sums_one[:2], norm_sums[0][:2], vectors[14:]), axis=0)
         flat = [piece.reshape(shards * quarter, width) for piece in (pieces[0], got[0], far)]
+        if layer == 0:
+            joined = attention_weights(attn_t, du, vectors, *flat)
+            attn_sum = lax.psum_scatter(joined, "shard", scatter_dimension=0, tiled=True)
+            to_far = after(to_far, joined)
+        to_far = (to_far + from_core[1].astype(F32)).astype(BF16)
+        if layer == 0:
+            attn_sum1, feed_sum1 = lax.optimization_barrier((attn_sum1, feed_sum1, late))[:2]
+            attn_parts1, hidden_parts1 = around(attn_sum1), around_hidden(feed_sum1)
+            part = (early[n:].astype(F32) + after(late, joined)[n:].astype(F32)).astype(BF16)
+            part = after(part, *attn_parts1, *hidden_parts1)
+            early_late = late
+            arrived = turned(part, True)
+            to_far = after(to_far, arrived)
+            done = finish(info, 1, attn_parts1, hidden_parts1, None)
+        from_far = swap(to_far, "cx")
+        if layer == 0:
+            from_far = after(from_far, done[5])
         if layer > 0:
-            joined = attention_weights(attn_t, after(du, part), vectors, *flat)
-            attn_sum1 = lax.psum_scatter(joined, "shard", scatter_dimension=0, tiled=True)
-            hidden_out = from_sequence((after(result, to_far) * keep).astype(BF16))
-            from_far, part, hidden_out = lax.optimization_barrier((from_far, part, hidden_out))
+            du, dh_now, early_late = lax.optimization_barrier((du, dh, late, to_far))[:3]
+            early = feed_weights(0, dh_now, dh_other, act, act_other, *tokens)
+            part = (early[n:].astype(F32) + early_late[n:].astype(F32)).astype(BF16)
+        if layer > 0:
+            hidden_own_out = (after(result, to_far) * keep).astype(BF16)
+            hidden_other_out = swap(hidden_own_out[toks:], "tp")
+            from_far, part, hidden_other_out = lax.optimization_barrier((from_far, part, hidden_other_out))
             arrived = turned(part, True)
-        else:
-            joined = attention_weights(attn_t, after(du, from_core, part), vectors, *flat)
-            attn_sum = lax.psum_scatter(joined, "shard", scatter_dimension=0, tiled=True)
         grad, low_grad, sums_one = norm_backward(own, from_core, from_far, x_in, gain_one, middle_grad)
         if layer > 0:
             low_other = swap(low_grad, "core")
-            grad, low_grad, arrived = lax.optimization_barrier((grad, low_grad, arrived))
+            joined = attention_weights(attn_t, after(du, low_grad), vectors, *flat)
+            attn_sum1 = lax.psum_scatter(joined, "shard", scatter_dimension=0, tiled=True)
+            grad, low_grad, arrived = lax.optimization_barrier((grad, low_grad, arrived, joined))[:3]
             part = early[:n].astype(F32) + early_late[:n].astype(F32) + arrived.astype(F32)
-            feed_sum1 = lax.psum_scatter(part.astype(BF16), "shard", scatter_dimension=0, tiled=True)
+            part = part.astype(BF16)
+            before = (part,)
+            feed_sum1 = lax.psum_scatter(part, "shard", scatter_dimension=0, tiled=True)
         else:
             part = (early[:n].astype(F32) + late[:n].astype(F32) + arrived.astype(F32)).astype(BF16)
-            halves = sums_one[:2].reshape(2, shards, 2, units).transpose(1, 3, 0, 2).reshape(n, 4)
-            part = lax.dynamic_update_slice(part, halves.astype(BF16), (0, 2 * width + 1))
-            attn_sum1 = (attn_sum1.astype(F32) + swap(attn_sum1, "tp").astype(F32)).astype(BF16)
-            part, attn_sum1, feed_sum1 = lax.optimization_barrier((part, attn_sum1, feed_sum1))
             arriving = send_shards(part, units)
-            attn_parts1, hidden_parts1 = around(attn_sum1), around_hidden(feed_sum1)
-            arriving = lax.optimization_barrier((*arriving, *attn_parts1, *hidden_parts1))[: len(arriving)]
+            attn_sum = after(attn_sum, from_far)
+            attn_sum = (attn_sum.astype(F32) + swap(attn_sum, "tp").astype(F32)).astype(BF16)
+            attn_parts0 = around(attn_sum)
+            arriving = lax.optimization_barrier((*arriving, low_grad))[: len(arriving)]
             feed_sum = sum_shards(part, units, arriving)
-            done = finish(info, 1, attn_parts1, hidden_parts1, None)
-            attn_sum = after(attn_sum, feed_sum)
-            attn_sum = (attn_sum.astype(F32) + swap(attn_sum, "tp").astype(F32)).astype(BF16)
+            hidden_out = own_first(hidden_own_out[:toks], after(hidden_other_out, part))
 
     hidden_grad = from_sequence(low_grad).astype(F32)
 
-    feed_sums = around_hidden(feed_sum)
-    lone = sum(part[:, 2 * width + 1 : 2 * width + 5].astype(F32) for part in feed_sums)
-    lone = lone + swap(lone, "tp")
-    lone = lone.reshape(units, 2, 2).transpose(1, 2, 0).reshape(2, rows)
-    done = finish(info, 0, around(attn_sum), feed_sums, done)
-    first_gain = jnp.stack((lone[0], done[4][1]))
-    first_bias = jnp.stack((lone[1], done[5][1]))
+    done = finish(info, 0, attn_parts0, around_hidden(feed_sum), done)
 
     return (
         hidden_out,
         hidden_grad,
-        first_gain,
-        first_bias,
+        done[4],
+        done[5],
         done[0],
         done[10],
         done[1],

time: 589 us -> 580 us (0.985)
  Pallas kernels: 230 us -> 216 us
  waiting for transfers between devices: 155 us -> 166 us
  starting transfers between devices: 88.5 us -> 82 us
    ppermute x10, waiting for transfers between devices: 20.2 us -> 46.4 us  [turned(): return lax.ppermute(value, PLANE, pairs)]
    ppermute x63 -> x61, waiting for transfers between devices: 95.8 us -> 83 us  [swap(): return lax.ppermute(value, axis, ((0, 1), (1, 0)))]
    ppermute x10, starting transfers between devices: 7.18 us -> 19.7 us  [turned(): return lax.ppermute(value, PLANE, pairs)]
    pallas_call x2, Pallas kernels: 46.4 us -> 35.1 us  [attention_forward(): pl.pallas_call(partial(attention_forward_kernel, norm), name='attention_f...]
    ppermute x63 -> x61, starting transfers between devices: 58.4 us -> 48.6 us  [swap(): return lax.ppermute(value, axis, ((0, 1), (1, 0)))]
    ppermute x3, starting transfers between devices: 18.2 us -> 8.51 us  [send_shards(): lax.ppermute(lax.dynamic_slice_in_dim(value, (index + by) % shards * coun...]
    unnamed x207 -> x205, local copies, waits for them, and re-layouts: 27 us -> 23.2 us
  transfers between devices with their start and end apart: 87 -> 85, of which waited for: 33 -> 31; matrix products, arithmetic and copies ran while one was open for 10% -> 11% of each run, Pallas kernels for 35% -> 33%
where the time goes in v4:
time: 580 us; the launch traced here: 571 us
  Pallas kernels  216 us (37%)
  waiting for transfers between devices  166 us (29%)
  starting transfers between devices  82 us (14%)
  local copies, waits for them, and re-layouts  54.5 us (9%)
  other arithmetic  30.8 us (5%)
  between operations  17.8 us (3%)
    ppermute x61, waiting for transfers between devices, swap(): return lax.ppermute(value, axis, ((0, 1), (1, 0)))  83 us
    pallas_call x2, Pallas kernels, attention_backward(): pl.pallas_call(partial(attention_backward_kernel, norm), name='attention_...  59.3 us
    ppermute x61, starting transfers between devices, swap(): return lax.ppermute(value, axis, ((0, 1), (1, 0)))  48.6 us
    ppermute x10, waiting for transfers between devices, turned(): return lax.ppermute(value, PLANE, pairs)  46.4 us
    pallas_call x2, Pallas kernels, attention_forward(): pl.pallas_call(partial(attention_forward_kernel, norm), name='attention_f...  35.1 us
    pallas_call x4, Pallas kernels, feed_weights(): pl.pallas_call(feed_weights_kernel, name='feed_weights', grid=(units // s...  23.5 us
    unnamed x205, local copies, waits for them, and re-layouts  23.2 us
    pallas_call x1, Pallas kernels, feed_both(): pl.pallas_call(feed_both_kernel, name='feed_both', grid_spec=pltpu.Prefet...  23.1 us
  transfers between devices with their start and end apart: 85, of which 31 were waited for; matrix products, arithmetic and copies ran while one was open for 11% of the time, Pallas kernels for 33%

profile of v4, /device:TPU:9, one launch (start us, length us, event | category | flops | bytes accessed | tf_op | source)
XLA Modules:
  0.0 570.8 jit_solution(17627728221055329453)
XLA Ops:
  7.2 2.3 dynamic-slice_bitcast_fusion
  17.6 11.6 %collective-permute-done.2 = bf16[2,256,768]{2,1,0:T(8,128)(2,1)} collective-permute-done((bf16[2,256,768]{2,1,0:T(8,128)(2,1)}, bf16[2,256,768]{2,1,0:T(8,128)(2,1)}, u32[]{:S(2)}, u32[]{:S(2)}) %collective-permute-start.2) | collective-permute-done | bytes 786464 | tf_op jit(solution)/shard_map/ppermute | solution.py:26
  29.3 1.9 slice_bitcast_fusion.3
  35.6 14.4 %collective-permute-done.4.refs_2_ = bf16[512,768]{1,0:T(8,128)(2,1)S(1)} collective-permute-done((bf16[512,768]{1,0:T(8,128)(2,1)S(1)}, bf16[512,768]{1,0:T(8,128)(2,1)S(1)}, u32[]{:S(2)}, u32[]{:S(2)}) %collective-permute-start.4) | collective-permute-done | bytes 786464 | tf_op jit(solution)/shard_map/ppermute | solution.py:26
  50.0 2.5 collective-permute-start.5
  52.5 2.0 collective-permute-done.5.refs_3_
  65.5 17.2 %collective-permute-done.refs_1_ = bf16[384,1664]{1,0:T(8,128)(2,1)} collective-permute-done((bf16[384,1664]{1,0:T(8,128)(2,1)}, bf16[384,1664]{1,0:T(8,128)(2,1)}, u32[]{:S(2)}, u32[]{:S(2)}) %collective-permute-start) | collective-permute-done | bytes 1277984 | tf_op jit(solution)/shard_map/ppermute | solution.py:963
  82.7 3.2 collective-permute-done.1.refs_2_
  97.2 18.1 %attention_forward.2 = (bf16[768,2048]{1,0:T(8,128)(2,1)}, bf16[2048,576]{1,0:T(8,128)(2,1)}, bf16[4,192,512]{2,1,0:T(8,128)(2,1)S(1)}, f32[8,2048]{1,0:T(8,128)S(1)}) custom-call(s32[8]{0:T(128)S(1)} %stack.76.info, bf16[512,768]{1,0:T(8,128)(2,1)S(1)} %get-tuple-element.177.refs_0_, bf16[512,768]{1,0:T(8,128)(2,1)S(1)} %copy-done.36, ...), custom_call_target="tpu_custom_call" | custom-call | flops 14000000000 | bytes 12582912 | tf_op jit(solution)/shard_map/attention_forward/pallas_call | solution.py:182
  120.6 3.6 collective-permute-done.14.p2
  124.2 4.6 collective-permute-done.15.p3
  128.8 4.4 out_forward.2
  136.2 5.7 collective-permute-start.17
  142.4 14.8 %feed_forward.1 = (bf16[4,512,768]{2,1,0:T(8,128)(2,1)}, bf16[2,768,512]{2,1,0:T(8,128)(2,1)}, bf16[2,768,512]{2,1,0:T(8,128)(2,1)}, f32[512,768]{1,0:T(8,128)}, bf16[512,768]{1,0:T(8,128)(2,1)}) custom-call(bf16[512,768]{1,0:T(8,128)(2,1)} %copy-done.5, f32[512,768]{1,0:T(8,128)} %copy-done.38, f32[3,768]{1,0:T(4,128)} %pad_maximum_fusion.7.vec_ref, ...), custom_call_target="tpu_custom_call" | custom-call | flops 5000000000 | bytes 20971520 | tf_op jit(solution)/shard_map/feed_forward/pallas_call | solution.py:613
  161.6 15.2 %collective-permute-done.24.refs_2_ = bf16[512,768]{1,0:T(8,128)(2,1)S(1)} collective-permute-done((bf16[512,768]{1,0:T(8,128)(2,1)}, bf16[512,768]{1,0:T(8,128)(2,1)S(1)}, u32[]{:S(2)}, u32[]{:S(2)}) %collective-permute-start.24) | collective-permute-done | bytes 786464 | tf_op jit(solution)/shard_map/ppermute | solution.py:26
  177.0 2.9 collective-permute-done.19
  182.8 5.1 collective-permute-start.28
  188.3 16.9 %attention_forward.3 = (bf16[768,2048]{1,0:T(8,128)(2,1)}, bf16[2048,576]{1,0:T(8,128)(2,1)}, bf16[4,192,512]{2,1,0:T(8,128)(2,1)S(1)}, f32[8,2048]{1,0:T(8,128)S(1)}) custom-call(s32[8]{0:T(128)S(1)} %stack.76.info, bf16[512,768]{1,0:T(8,128)(2,1)S(1)} %copy-done.37, bf16[512,768]{1,0:T(8,128)(2,1)S(1)} %collective-permute-done.23.refs_1_, ...), custom_call_target="tpu_custom_call" | custom-call | flops 14000000000 | bytes 12582912 | tf_op jit(solution)/shard_map/attention_forward/pallas_call | solution.py:182
  205.9 6.8 %collective-permute-done.27.refs_3_ = bf16[384,1664]{1,0:T(8,128)(2,1)} collective-permute-done((bf16[384,1664]{1,0:T(8,128)(2,1)}, bf16[384,1664]{1,0:T(8,128)(2,1)}, u32[]{:S(2)}, u32[]{:S(2)}) %collective-permute-start.27) | collective-permute-done | bytes 1277984 | tf_op jit(solution)/shard_map/ppermute | solution.py:963
  212.8 4.3 collective-permute-start.30
  218.7 4.8 collective-permute-done.31.p2
  223.5 4.4 collective-permute-done.32.p3
  231.5 4.4 out_forward.3
  239.9 23.1 %feed_both.1 = (bf16[2,512,768]{2,1,0:T(8,128)(2,1)}, bf16[2,512,768]{2,1,0:T(8,128)(2,1)}, f32[512,768]{1,0:T(8,128)}, bf16[512,768]{1,0:T(8,128)(2,1)}, f32[8,...) custom-call(s32[8]{0:T(128)} %copy-done.32, ...), custom_call_target="tpu_custom_call" | custom-call | flops 10000000000 | bytes 25165824 | tf_op jit(solution)/shard_map/feed_both/pallas_call | solution.py:804
  264.1 1.9 convolution_convert_fusion.1
  266.8 2.6 collective-permute-done.35.g1
  271.7 6.2 %collective-permute-done.37.g3 = bf16[192,512]{1,0:T(8,128)(2,1)S(1)} collective-permute-done((bf16[192,512]{1,0:T(8,128)(2,1)S(1)}, bf16[192,512]{1,0:T(8,128)(2,1)S(1)}, u32[]{:S(2)}, u32[]{:S(2)}) %collective-permute-start.37) | collective-permute-done | bytes 196640 | tf_op jit(solution)/shard_map/ppermute | solution.py:971
  280.0 5.6 feed_weights.4
  287.6 25.6 %attention_backward.2 = (bf16[2048,576]{1,0:T(8,128)(2,1)}, bf16[2,512,768]{2,1,0:T(8,128)(2,1)}, f32[512,768]{1,0:T(8,128)}, f32[512,768]{1,0:T(8,128)}, f32[8,576]{1,0:T(8,128)}) custom-call(s32[8]{0:T(128)} %copy-done.32, bf16[2048,576]{1,0:T(8,128)(2,1)} %get-tuple-element.223.qkv_ref, bf16[4,192,512]{2,1,0:T(8,128)(2,1)} %copy-done.24, ...), custom_call_target="tpu_custom_call" | custom-call | flops 20000000000 | bytes 16777216 | tf_op jit(solution)/shard_map/attention_backward/pallas_call | solution.py:378
  313.2 4.5 collective-permute-done.44
  323.9 1.9 fusion.1
  327.2 2.5 collective-permute-start.47
  329.7 5.6 feed_weights.5
  335.3 3.2 add_convert_fusion.3
  338.6 6.5 %collective-permute-done.46.far = bf16[512,768]{1,0:T(8,128)(2,1)S(1)} collective-permute-done((bf16[512,768]{1,0:T(8,128)(2,1)S(1)}, bf16[512,768]{1,0:T(8,128)(2,1)S(1)}, u32[]{:S(2)}, u32[]{:S(2)}) %collective-permute-start.46) | collective-permute-done | bytes 786464 | tf_op jit(solution)/shard_map/ppermute | solution.py:26
  345.9 2.2 collective-permute-start.48
  349.5 5.3 norm_backward.2
  356.0 5.6 attention_weights.2
  363.4 17.9 %feed_backward.1 = (bf16[2,512,768]{2,1,0:T(8,128)(2,1)}, bf16[2,512,768]{2,1,0:T(8,128)(2,1)}, f32[512,768]{1,0:T(8,128)}, bf16[512,768]{1,0:T(8,128)(2,1)}, f3...) custom-call(s32[8]{0:T(128)} %copy-done.32, ...), custom_call_target="tpu_custom_call" | custom-call | flops 6000000000 | bytes 25165824 | tf_op jit(solution)/shard_map/feed_backward/pallas_call | solution.py:719
  383.2 1.9 convolution_convert_fusion
  387.5 3.4 add_convert_fusion.2
  392.4 1.8 fusion.3
  394.6 4.0 collective-permute-done.51.g3
  398.5 2.5 collective-permute-start.56
  401.0 6.1 %feed_weights.7 = bf16[768,1664]{1,0:T(8,128)(2,1)} custom-call(bf16[2,512,768]{2,1,0:T(8,128)(2,1)S(1)} %copy-done.4, bf16[2,512,768]{2,1,0:T(8,128)(2,1)} %collective-permute-done.52.dh2, bf16[2,768,512]{2,1,0:T(8,128)(2,1)} %get-tuple-element.276.act, bf16[2,768,512]{2,1,0:T(8,128)(2,1)} %collective-permute-done.21.act2, bf16[512,768]{1,0:T(8,128)(2,1)S(1)} %copy-done.6, ...), custom_call_target="tpu_custom_call" | custom-call | flops 2400000000 | bytes 9437184 | tf_op jit(solution)/shard_map/feed_weights/pallas_call | solution.py:843
  407.2 6.2 %feed_weights.6 = bf16[768,1664]{1,0:T(8,128)(2,1)} custom-call(bf16[2,512,768]{2,1,0:T(8,128)(2,1)S(1)} %copy-done.4, bf16[2,512,768]{2,1,0:T(8,128)(2,1)} %collective-permute-done.52.dh2, bf16[2,768,512]{2,1,0:T(8,128)(2,1)} %get-tuple-element.276.act, bf16[2,768,512]{2,1,0:T(8,128)(2,1)} %collective-permute-done.21.act2, bf16[512,768]{1,0:T(8,128)(2,1)S(1)} %copy-done.6, ...), custom_call_target="tpu_custom_call" | custom-call | flops 2400000000 | bytes 9437184 | tf_op jit(solution)/shard_map/feed_weights/pallas_call | solution.py:843
  415.3 33.7 %attention_backward.3 = (bf16[2048,576]{1,0:T(8,128)(2,1)}, bf16[2,512,768]{2,1,0:T(8,128)(2,1)}, f32[512,768]{1,0:T(8,128)}, f32[512,768]{1,0:T(8,128)}, f32[8,576]{1,0:T(8,128)}, /*index=5*/f32[8,768]{1,0:T(8,128)}) custom-call(s32[8]{0:T(128)} %copy-done.32, bf16[2048,576]{1,0:T(8,128)(2,1)} %get-tuple-element.288.qkv_ref, ...), custom_call_target="tpu_custom_call" | custom-call | flops 20000000000 | bytes 16777216 | tf_op jit(solution)/shard_map/attention_backward/pallas_call | solution.py:378
  456.2 5.7 attention_weights.3
  462.4 5.0 collective-permute-done.61.refs_5_
  468.0 3.1 add_convert_fusion.1
  472.8 6.2 %collective-permute-start.64 = (bf16[384,1664]{1,0:T(8,128)(2,1)}, bf16[384,1664]{1,0:T(8,128)(2,1)}, u32[]{:S(2)}, u32[]{:S(2)}) collective-permute-start(bf16[384,1664]{1,0:T(8,128)(2,1)} %add_convert_fusion.1), channel_id=1, source_target_pairs={{0,4},{1,5},{2,3},{3,2},{4,0},{5,1},{6,7},{7,6},{8,12},{9,13},{10,... | collective-permute-start | bytes 3833864 | tf_op jit(solution)/shard_map/ppermute | solution.py:963
  478.9 2.2 fusion
  481.1 13.0 %collective-permute-done.64 = bf16[384,1664]{1,0:T(8,128)(2,1)} collective-permute-done((bf16[384,1664]{1,0:T(8,128)(2,1)}, bf16[384,1664]{1,0:T(8,128)(2,1)}, u32[]{:S(2)}, u32[]{:S(2)}) %collective-permute-start.64) | collective-permute-done | bytes 1277984 | tf_op jit(solution)/shard_map/ppermute | solution.py:963
  494.8 2.2 add_convert_fusion
  499.0 8.5 %collective-permute-start.73 = (bf16[96,1664]{1,0:T(8,128)(2,1)}, bf16[96,1664]{1,0:T(8,128)(2,1)}, u32[]{:S(2)}, u32[]{:S(2)}) collective-permute-start(bf16[96,1664]{1,0:T(8,128)(2,1)} %get-tuple-element.339), channel_id=1, source_target_pairs={{0,16},{8,24},{16,0},{24,8},{1,17},{9,25},{17,1},{25,9},{2,18},{10... | collective-permute-start | bytes 958472 | tf_op jit(solution)/shard_map/ppermute | solution.py:1061
  507.5 5.5 finish.2
  513.1 5.3 norm_backward.3
  518.4 2.5 collective-permute-done.73
  520.9 13.7 %collective-permute-done.74 = bf16[96,1664]{1,0:T(8,128)(2,1)} collective-permute-done((bf16[96,1664]{1,0:T(8,128)(2,1)}, bf16[96,1664]{1,0:T(8,128)(2,1)}, u32[]{:S(2)}, u32[]{:S(2)}) %collective-permute-start.74) | collective-permute-done | bytes 319520 | tf_op jit(solution)/shard_map/ppermute | solution.py:1061
  537.0 6.0 %collective-permute-done.68 = bf16[192,896]{1,0:T(8,128)(2,1)S(1)} collective-permute-done((bf16[192,896]{1,0:T(8,128)(2,1)}, bf16[192,896]{1,0:T(8,128)(2,1)S(1)}, u32[]{:S(2)}, u32[]{:S(2)}) %collective-permute-start.68) | collective-permute-done | bytes 344096 | tf_op jit(solution)/shard_map/ppermute | solution.py:26
  544.5 2.6 collective-permute-start.69
  547.1 3.5 collective-permute-done.70.refs_2_
  550.5 3.2 collective-permute-start.71
  557.5 6.0 %finish.3 = (f32[2,192,2304]{2,1,0:T(8,128)}, f32[2,192,768]{2,1,0:T(8,128)}, f32[2,768,384]{2,1,0:T(8,128)}, f32[2,384,768]{2,1,0:T(8,128)}, f32[2,192]{1,0:T(2...) custom-call(s32[8]{0:T(128)} %copy-done.32, ...), custom_call_target="tpu_custom_call", output_to_operand_aliasing={{0}: (11, {}), {1}: (12, {}), {2}: (13, {}), {3}: (14, {})} | custom-call | flops 1000000 | bytes 8388608 | tf_op jit(solution)/shard_map/finish/pallas_call | solution.py:929
  (472 shorter events, 107.9 us)
Async XLA Ops:
  7.2 45.3 %all-gather.5.cloned.1.call-start = ((), (), s32[]{:S(2)}) async-start(), calls=%async_computation.3 | async-start | bytes 1597440 | tf_op jit(solution)/shard_map/all_gather | solution.py:1054
  10.5 18.7 %collective-permute-start.2 = (bf16[2,256,768]{2,1,0:T(8,128)(2,1)}, bf16[2,256,768]{2,1,0:T(8,128)(2,1)}, u32[]{:S(2)}, u32[]{:S(2)}) collective-permute-start(bf16[2,256,768]{2,1,0:T(8,128)(2,1)} %pad_maximum_fusion), channel_id=1, source_target_pairs={{0,1},{1,0},{2,3},{3,2},{4,5},{5,4},{6,7},{7,6},{8,9},{9,8},{10,11... | collective-permute-start | bytes 2359304 | tf_op jit(solution)/shard_map/ppermute | solution.py:26
  14.9 73.5 %all-gather.7.cloned.1.call-start = ((), (), s32[]{:S(2)}) async-start(), calls=%async_computation.4 | async-start | bytes 1720320 | tf_op jit(solution)/shard_map/all_gather | solution.py:1054
  32.5 17.5 %collective-permute-start.4 = (bf16[512,768]{1,0:T(8,128)(2,1)S(1)}, bf16[512,768]{1,0:T(8,128)(2,1)S(1)}, u32[]{:S(2)}, u32[]{:S(2)}) collective-permute-start(bf16[512,768]{1,0:T(8,128)(2,1)S(1)} %get-tuple-element.177.refs_0_), channel_id=1, source_target_pairs={{0,4},{4,0},{1,5},{5,1},{2,6},{6,2},{3,7},{7,3},{8,12},{12,8},{9,1... | collective-permute-start | bytes 2359304 | tf_op jit(solution)/shard_map/ppermute | solution.py:26
  33.7 18.8 %collective-permute-start.3 = (bf16[512,768]{1,0:T(8,128)(2,1)S(1)}, bf16[512,768]{1,0:T(8,128)(2,1)S(1)}, u32[]{:S(2)}, u32[]{:S(2)}) collective-permute-start(bf16[512,768]{1,0:T(8,128)(2,1)S(1)} %get-tuple-element.177.refs_0_), channel_id=1, source_target_pairs={{0,2},{2,0},{1,3},{3,1},{4,6},{6,4},{5,7},{7,5},{8,10},{10,8},{9,1... | collective-permute-start | bytes 2359304 | tf_op jit(solution)/shard_map/ppermute | solution.py:26
  54.5 81.6 %all-gather.11.cloned.1.call-start = ((), (), s32[]{:S(2)}) async-start(), calls=%async_computation.6 | async-start | bytes 1597440 | tf_op jit(solution)/shard_map/all_gather | solution.py:1054
  54.6 28.1 %collective-permute-start = (bf16[384,1664]{1,0:T(8,128)(2,1)}, bf16[384,1664]{1,0:T(8,128)(2,1)}, u32[]{:S(2)}, u32[]{:S(2)}) collective-permute-start(bf16[384,1664]{1,0:T(8,128)(2,1)} %all-gather.5.cloned.1.call-done.refs_0_), channel_id=1, source_target_pairs={{0,4},{1,5},{2,3},{3,2},{4,0},{5,1},{6,7},{7,6},{8,12},{9,13},{10,... | collective-permute-start | bytes 3833864 | tf_op jit(solution)/shard_map/ppermute | solution.py:963
  55.9 30.0 %collective-permute-start.1 = (bf16[384,1664]{1,0:T(8,128)(2,1)}, bf16[384,1664]{1,0:T(8,128)(2,1)}, u32[]{:S(2)}, u32[]{:S(2)}) collective-permute-start(bf16[384,1664]{1,0:T(8,128)(2,1)} %all-gather.5.cloned.1.call-done.refs_0_), channel_id=1, source_target_pairs={{0,1},{1,0},{2,6},{3,7},{4,5},{5,4},{6,2},{7,3},{8,9},{9,8},{10,14... | collective-permute-start | bytes 3833864 | tf_op jit(solution)/shard_map/ppermute | solution.py:963
  64.5 52.7 %collective-permute-start.10 = (bf16[384,1664]{1,0:T(8,128)(2,1)}, bf16[384,1664]{1,0:T(8,128)(2,1)}, u32[]{:S(2)}, u32[]{:S(2)}) collective-permute-start(bf16[384,1664]{1,0:T(8,128)(2,1)} %all-gather.5.cloned.1.call-done.refs_0_), channel_id=1, source_target_pairs={{0,2},{2,0},{1,3},{3,1},{4,6},{6,4},{5,7},{7,5},{8,10},{10,8},{9,1... | collective-permute-start | bytes 3833864 | tf_op jit(solution)/shard_map/ppermute | solution.py:26
  85.9 31.4 %collective-permute-start.11 = (bf16[384,1664]{1,0:T(8,128)(2,1)}, bf16[384,1664]{1,0:T(8,128)(2,1)}, u32[]{:S(2)}, u32[]{:S(2)}) collective-permute-start(bf16[384,1664]{1,0:T(8,128)(2,1)} %collective-permute-done.refs_1_), channel_id=1, source_target_pairs={{0,2},{2,0},{1,3},{3,1},{4,6},{6,4},{5,7},{7,5},{8,10},{10,8},{9,1... | collective-permute-start | bytes 3833864 | tf_op jit(solution)/shard_map/ppermute | solution.py:26
  86.0 31.3 %collective-permute-start.9 = (bf16[384,1664]{1,0:T(8,128)(2,1)}, bf16[384,1664]{1,0:T(8,128)(2,1)}, u32[]{:S(2)}, u32[]{:S(2)}) collective-permute-start(bf16[384,1664]{1,0:T(8,128)(2,1)} %collective-permute-done.refs_1_), channel_id=1, source_target_pairs={{0,1},{1,0},{2,6},{3,7},{4,5},{5,4},{6,2},{7,3},{8,9},{9,8},{10,14... | collective-permute-start | bytes 3833864 | tf_op jit(solution)/shard_map/ppermute | solution.py:963
  87.2 30.1 %collective-permute-start.12 = (bf16[384,1664]{1,0:T(8,128)(2,1)}, bf16[384,1664]{1,0:T(8,128)(2,1)}, u32[]{:S(2)}, u32[]{:S(2)}) collective-permute-start(bf16[384,1664]{1,0:T(8,128)(2,1)} %collective-permute-done.1.refs_2_), channel_id=1, source_target_pairs={{0,2},{2,0},{1,3},{3,1},{4,6},{6,4},{5,7},{7,5},{8,10},{10,8},{9,1... | collective-permute-start | bytes 3833864 | tf_op jit(solution)/shard_map/ppermute | solution.py:26
  93.1 65.2 %all-gather.9.cloned.1.call-start = ((), (), s32[]{:S(2)}) async-start(), calls=%async_computation.5 | async-start | bytes 1474560 | tf_op jit(solution)/shard_map/all_gather | solution.py:1054
  94.8 20.7 %collective-permute-start.7 = (bf16[4,1,48,768]{3,2,0,1:T(8,128)(2,1)}, bf16[4,1,48,768]{3,2,0,1:T(8,128)(2,1)S(1)}, u32[]{:S(2)}, u32[]{:S(2)}) collective-permute-start(bf16[4,1,48,768]{3,2,0,1:T(8,128)(2,1)} %reshape.175), channel_id=1, source_target_pairs={{0,4},{4,0},{1,5},{5,1},{2,6},{6,2},{3,7},{7,3},{8,12},{12,8},{9,1... | collective-permute-start | bytes 884744 | tf_op jit(solution)/shard_map/ppermute | solution.py:26
  117.3 25.1 %collective-permute-start.16 = (bf16[384,1664]{1,0:T(8,128)(2,1)}, bf16[384,1664]{1,0:T(8,128)(2,1)}, u32[]{:S(2)}, u32[]{:S(2)}) collective-permute-start(bf16[384,1664]{1,0:T(8,128)(2,1)} %collective-permute-done.9.refs_3_), channel_id=1, source_target_pairs={{0,2},{2,0},{1,3},{3,1},{4,6},{6,4},{5,7},{7,5},{8,10},{10,8},{9,1... | collective-permute-start | bytes 3833864 | tf_op jit(solution)/shard_map/ppermute | solution.py:26
  118.3 10.6 %collective-permute-start.15 = (bf16[192,512]{1,0:T(8,128)(2,1)S(1)}, bf16[192,512]{1,0:T(8,128)(2,1)S(1)}, u32[]{:S(2)}, u32[]{:S(2)}) collective-permute-start(bf16[192,512]{1,0:T(8,128)(2,1)S(1)} %get-tuple-element.371), channel_id=1, source_target_pairs={{0,6},{2,4},{4,2},{6,0},{1,7},{3,5},{5,3},{7,1},{8,14},{10,12},{12... | collective-permute-start | bytes 589832 | tf_op jit(solution)/shard_map/ppermute | solution.py:971
  119.9 278.6 %reduce-scatter.4.cloned.1.call-start = ((), (), s32[]{:S(2)}) async-start(), calls=%async_computation.7 | async-start | bytes 1720320 | tf_op jit(solution)/shard_map/reduce_scatter | solution.py:1238
  136.2 21.1 %collective-permute-start.17 = (bf16[384,1664]{1,0:T(8,128)(2,1)}, bf16[384,1664]{1,0:T(8,128)(2,1)S(1)}, u32[]{:S(2)}, u32[]{:S(2)}) collective-permute-start(bf16[384,1664]{1,0:T(8,128)(2,1)} %all-gather.11.cloned.1.call-done.refs_0_), channel_id=1, source_target_pairs={{0,4},{1,5},{2,3},{3,2},{4,0},{5,1},{6,7},{7,6},{8,12},{9,13},{10,... | collective-permute-start | bytes 3833864 | tf_op jit(solution)/shard_map/ppermute | solution.py:963
  157.2 19.6 %collective-permute-start.24 = (bf16[512,768]{1,0:T(8,128)(2,1)}, bf16[512,768]{1,0:T(8,128)(2,1)S(1)}, u32[]{:S(2)}, u32[]{:S(2)}) collective-permute-start(bf16[512,768]{1,0:T(8,128)(2,1)} %get-tuple-element.201.refs_0_), channel_id=1, source_target_pairs={{0,4},{4,0},{1,5},{5,1},{2,6},{6,2},{3,7},{7,3},{8,12},{12,8},{9,1... | collective-permute-start | bytes 2359304 | tf_op jit(solution)/shard_map/ppermute | solution.py:26
  157.7 24.7 %collective-permute-start.21 = (bf16[2,768,512]{2,1,0:T(8,128)(2,1)}, bf16[2,768,512]{2,1,0:T(8,128)(2,1)}, u32[]{:S(2)}, u32[]{:S(2)}) collective-permute-start(bf16[2,768,512]{2,1,0:T(8,128)(2,1)} %get-tuple-element.200), channel_id=1, source_target_pairs={{0,2},{2,0},{1,3},{3,1},{4,6},{6,4},{5,7},{7,5},{8,10},{10,8},{9,1... | collective-permute-start | bytes 4718600 | tf_op jit(solution)/shard_map/ppermute | solution.py:26
  159.9 19.9 %collective-permute-start.19 = (bf16[4,1,48,768]{3,2,0,1:T(8,128)(2,1)S(1)}, bf16[4,1,48,768]{3,2,0,1:T(8,128)(2,1)S(1)}, u32[]{:S(2)}, u32[]{:S(2)}) collective-permute-start(bf16[4,1,48,768]{3,2,0,1:T(8,128)(2,1)S(1)} %reshape.177), channel_id=1, source_target_pairs={{0,4},{4,0},{1,5},{5,1},{2,6},{6,2},{3,7},{7,3},{8,12},{12,8},{9,1... | collective-permute-start | bytes 884744 | tf_op jit(solution)/shard_map/ppermute | solution.py:26
  160.9 20.5 %collective-permute-start.22 = (bf16[512,768]{1,0:T(8,128)(2,1)S(1)}, bf16[512,768]{1,0:T(8,128)(2,1)S(1)}, u32[]{:S(2)}, u32[]{:S(2)}) collective-permute-start(bf16[512,768]{1,0:T(8,128)(2,1)S(1)} %copy-done.6), channel_id=1, source_target_pairs={{0,2},{2,0},{1,3},{3,1},{4,6},{6,4},{5,7},{7,5},{8,10},{10,8},{9,1... | collective-permute-start | bytes 2359304 | tf_op jit(solution)/shard_map/ppermute | solution.py:26
  161.5 20.9 %collective-permute-start.23 = (bf16[512,768]{1,0:T(8,128)(2,1)}, bf16[512,768]{1,0:T(8,128)(2,1)S(1)}, u32[]{:S(2)}, u32[]{:S(2)}) collective-permute-start(bf16[512,768]{1,0:T(8,128)(2,1)} %get-tuple-element.201.refs_0_), channel_id=1, source_target_pairs={{0,2},{2,0},{1,3},{3,1},{4,6},{6,4},{5,7},{7,5},{8,10},{10,8},{9,1... | collective-permute-start | bytes 2359304 | tf_op jit(solution)/shard_map/ppermute | solution.py:26
  182.4 23.5 %collective-permute-start.26 = (bf16[384,1664]{1,0:T(8,128)(2,1)S(1)}, bf16[384,1664]{1,0:T(8,128)(2,1)}, u32[]{:S(2)}, u32[]{:S(2)}) collective-permute-start(bf16[384,1664]{1,0:T(8,128)(2,1)S(1)} %copy-done.94), channel_id=1, source_target_pairs={{0,1},{1,0},{2,6},{3,7},{4,5},{5,4},{6,2},{7,3},{8,9},{9,8},{10,14... | collective-permute-start | bytes 3833864 | tf_op jit(solution)/shard_map/ppermute | solution.py:963
  182.8 29.9 %collective-permute-start.28 = (bf16[384,1664]{1,0:T(8,128)(2,1)S(1)}, bf16[384,1664]{1,0:T(8,128)(2,1)S(1)}, u32[]{:S(2)}, u32[]{:S(2)}) collective-permute-start(bf16[384,1664]{1,0:T(8,128)(2,1)S(1)} %copy-done.94), channel_id=1, source_target_pairs={{0,2},{2,0},{1,3},{3,1},{4,6},{6,4},{5,7},{7,5},{8,10},{10,8},{9,1... | collective-permute-start | bytes 3833864 | tf_op jit(solution)/shard_map/ppermute | solution.py:26
  187.8 24.8 %collective-permute-start.27 = (bf16[384,1664]{1,0:T(8,128)(2,1)}, bf16[384,1664]{1,0:T(8,128)(2,1)}, u32[]{:S(2)}, u32[]{:S(2)}) collective-permute-start(bf16[384,1664]{1,0:T(8,128)(2,1)} %copy-done.95), channel_id=1, source_target_pairs={{0,1},{1,0},{2,6},{3,7},{4,5},{5,4},{6,2},{7,3},{8,9},{9,8},{10,14... | collective-permute-start | bytes 3833864 | tf_op jit(solution)/shard_map/ppermute | solution.py:963
  188.1 24.5 %collective-permute-start.29 = (bf16[384,1664]{1,0:T(8,128)(2,1)}, bf16[384,1664]{1,0:T(8,128)(2,1)S(1)}, u32[]{:S(2)}, u32[]{:S(2)}) collective-permute-start(bf16[384,1664]{1,0:T(8,128)(2,1)} %copy-done.95), channel_id=1, source_target_pairs={{0,2},{2,0},{1,3},{3,1},{4,6},{6,4},{5,7},{7,5},{8,10},{10,8},{9,1... | collective-permute-start | bytes 3833864 | tf_op jit(solution)/shard_map/ppermute | solution.py:26
  217.4 10.5 %collective-permute-start.32 = (bf16[192,512]{1,0:T(8,128)(2,1)S(1)}, bf16[192,512]{1,0:T(8,128)(2,1)S(1)}, u32[]{:S(2)}, u32[]{:S(2)}) collective-permute-start(bf16[192,512]{1,0:T(8,128)(2,1)S(1)} %get-tuple-element.365), channel_id=1, source_target_pairs={{0,6},{2,4},{4,2},{6,0},{1,7},{3,5},{5,3},{7,1},{8,14},{10,12},{12... | collective-permute-start | bytes 589832 | tf_op jit(solution)/shard_map/ppermute | solution.py:971
  227.9 12.0 %collective-permute-start.34 = (bf16[384,1664]{1,0:T(8,128)(2,1)}, bf16[384,1664]{1,0:T(8,128)(2,1)}, u32[]{:S(2)}, u32[]{:S(2)}) collective-permute-start(bf16[384,1664]{1,0:T(8,128)(2,1)} %collective-permute-done.27.refs_3_), channel_id=1, source_target_pairs={{0,2},{2,0},{1,3},{3,1},{4,6},{6,4},{5,7},{7,5},{8,10},{10,8},{9,1... | collective-permute-start | bytes 3833864 | tf_op jit(solution)/shard_map/ppermute | solution.py:26
  228.1 11.8 %collective-permute-start.33 = (bf16[384,1664]{1,0:T(8,128)(2,1)}, bf16[384,1664]{1,0:T(8,128)(2,1)}, u32[]{:S(2)}, u32[]{:S(2)}) collective-permute-start(bf16[384,1664]{1,0:T(8,128)(2,1)} %collective-permute-done.26.refs_2_), channel_id=1, source_target_pairs={{0,2},{2,0},{1,3},{3,1},{4,6},{6,4},{5,7},{7,5},{8,10},{10,8},{9,1... | collective-permute-start | bytes 3833864 | tf_op jit(solution)/shard_map/ppermute | solution.py:26
  263.0 15.3 %collective-permute-start.38 = (bf16[2,512,768]{2,1,0:T(8,128)(2,1)}, bf16[2,512,768]{2,1,0:T(8,128)(2,1)S(1)}, u32[]{:S(2)}, u32[]{:S(2)}) collective-permute-start(bf16[2,512,768]{2,1,0:T(8,128)(2,1)} %get-tuple-element.229), channel_id=1, source_target_pairs={{0,2},{2,0},{1,3},{3,1},{4,6},{6,4},{5,7},{7,5},{8,10},{10,8},{9,1... | collective-permute-start | bytes 4718600 | tf_op jit(solution)/shard_map/ppermute | solution.py:26
  263.3 15.1 %collective-permute-start.39 = (bf16[2,768,512]{2,1,0:T(8,128)(2,1)}, bf16[2,768,512]{2,1,0:T(8,128)(2,1)S(1)}, u32[]{:S(2)}, u32[]{:S(2)}) collective-permute-start(bf16[2,768,512]{2,1,0:T(8,128)(2,1)} %get-tuple-element.237), channel_id=1, source_target_pairs={{0,2},{2,0},{1,3},{3,1},{4,6},{6,4},{5,7},{7,5},{8,10},{10,8},{9,1... | collective-permute-start | bytes 4718600 | tf_op jit(solution)/shard_map/ppermute | solution.py:26
  269.5 8.8 %collective-permute-start.41 = (bf16[512,768]{1,0:T(8,128)(2,1)S(1)}, bf16[512,768]{1,0:T(8,128)(2,1)S(1)}, u32[]{:S(2)}, u32[]{:S(2)}) collective-permute-start(bf16[512,768]{1,0:T(8,128)(2,1)S(1)} %copy-done.2), channel_id=1, source_target_pairs={{0,2},{2,0},{1,3},{3,1},{4,6},{6,4},{5,7},{7,5},{8,10},{10,8},{9,1... | collective-permute-start | bytes 2359304 | tf_op jit(solution)/shard_map/ppermute | solution.py:26
  270.2 8.1 %collective-permute-start.40 = (bf16[512,768]{1,0:T(8,128)(2,1)S(1)}, bf16[512,768]{1,0:T(8,128)(2,1)S(1)}, u32[]{:S(2)}, u32[]{:S(2)}) collective-permute-start(bf16[512,768]{1,0:T(8,128)(2,1)S(1)} %copy-done.10), channel_id=1, source_target_pairs={{0,2},{2,0},{1,3},{3,1},{4,6},{6,4},{5,7},{7,5},{8,10},{10,8},{9,1... | collective-permute-start | bytes 2359304 | tf_op jit(solution)/shard_map/ppermute | solution.py:26
  277.9 8.6 %collective-permute-start.43 = (bf16[4,48,768]{2,1,0:T(8,128)(2,1)S(1)}, bf16[4,48,768]{2,1,0:T(8,128)(2,1)S(1)}, u32[]{:S(2)}, u32[]{:S(2)}) collective-permute-start(bf16[4,48,768]{2,1,0:T(8,128)(2,1)S(1)} %fusion.4), channel_id=1, source_target_pairs={{0,4},{4,0},{1,5},{5,1},{2,6},{6,2},{3,7},{7,3},{8,12},{12,8},{9,1... | collective-permute-start | bytes 884744 | tf_op jit(solution)/shard_map/ppermute | solution.py:26
  287.2 30.4 %collective-permute-start.44 = (bf16[768,1664]{1,0:T(8,128)(2,1)}, bf16[768,1664]{1,0:T(8,128)(2,1)}, u32[]{:S(2)}, u32[]{:S(2)}) collective-permute-start(bf16[768,1664]{1,0:T(8,128)(2,1)} %feed_weights.4), channel_id=1, source_target_pairs={{0,1},{1,0},{2,6},{3,7},{4,5},{5,4},{6,2},{7,3},{8,9},{9,8},{10,14... | collective-permute-start | bytes 7667720 | tf_op jit(solution)/shard_map/ppermute | solution.py:963
  325.8 19.2 %collective-permute-start.46 = (bf16[512,768]{1,0:T(8,128)(2,1)S(1)}, bf16[512,768]{1,0:T(8,128)(2,1)S(1)}, u32[]{:S(2)}, u32[]{:S(2)}) collective-permute-start(bf16[512,768]{1,0:T(8,128)(2,1)S(1)} %fusion.1), channel_id=1, source_target_pairs={{0,4},{4,0},{1,5},{5,1},{2,6},{6,2},{3,7},{7,3},{8,12},{12,8},{9,1... | collective-permute-start | bytes 2359304 | tf_op jit(solution)/shard_map/ppermute | solution.py:26
  327.2 11.4 %collective-permute-start.47 = (bf16[256,768]{1,0:T(8,128)(2,1)S(1)}, bf16[256,768]{1,0:T(8,128)(2,1)S(1)}, u32[]{:S(2)}, u32[]{:S(2)}) collective-permute-start(bf16[256,768]{1,0:T(8,128)(2,1)S(1)} %get-tuple-element.360), channel_id=1, source_target_pairs={{0,1},{1,0},{2,3},{3,2},{4,5},{5,4},{6,7},{7,6},{8,9},{9,8},{10,11... | collective-permute-start | bytes 1179656 | tf_op jit(solution)/shard_map/ppermute | solution.py:26
  345.9 17.5 %collective-permute-start.48 = (bf16[384,1664]{1,0:T(8,128)(2,1)}, bf16[384,1664]{1,0:T(8,128)(2,1)}, u32[]{:S(2)}, u32[]{:S(2)}) collective-permute-start(bf16[384,1664]{1,0:T(8,128)(2,1)} %add_convert_fusion.3), channel_id=1, source_target_pairs={{0,4},{1,5},{2,3},{3,2},{4,0},{5,1},{6,7},{7,6},{8,12},{9,13},{10,... | collective-permute-start | bytes 3833864 | tf_op jit(solution)/shard_map/ppermute | solution.py:963
  361.7 88.8 %reduce-scatter.6.cloned.1.call-start = ((), (), s32[]{:S(2)}) async-start(), calls=%async_computation.8 | async-start | bytes 1597440 | tf_op jit(solution)/shard_map/reduce_scatter | solution.py:1243
  381.4 17.2 %collective-permute-start.52 = (bf16[2,512,768]{2,1,0:T(8,128)(2,1)}, bf16[2,512,768]{2,1,0:T(8,128)(2,1)}, u32[]{:S(2)}, u32[]{:S(2)}) collective-permute-start(bf16[2,512,768]{2,1,0:T(8,128)(2,1)} %get-tuple-element.273), channel_id=1, source_target_pairs={{0,2},{2,0},{1,3},{3,1},{4,6},{6,4},{5,7},{7,5},{8,10},{10,8},{9,1... | collective-permute-start | bytes 4718600 | tf_op jit(solution)/shard_map/ppermute | solution.py:26
  382.3 18.7 %collective-permute-start.53 = (bf16[512,768]{1,0:T(8,128)(2,1)}, bf16[512,768]{1,0:T(8,128)(2,1)}, u32[]{:S(2)}, u32[]{:S(2)}) collective-permute-start(bf16[512,768]{1,0:T(8,128)(2,1)} %get-tuple-element.266.dm_ref.dm), channel_id=1, source_target_pairs={{0,2},{2,0},{1,3},{3,1},{4,6},{6,4},{5,7},{7,5},{8,10},{10,8},{9,1... | collective-permute-start | bytes 2359304 | tf_op jit(solution)/shard_map/ppermute | solution.py:26
  382.4 11.8 %collective-permute-start.49 = (bf16[192,512]{1,0:T(8,128)(2,1)}, bf16[192,512]{1,0:T(8,128)(2,1)}, u32[]{:S(2)}, u32[]{:S(2)}) collective-permute-start(bf16[192,512]{1,0:T(8,128)(2,1)} %get-tuple-element.270), channel_id=1, source_target_pairs={{0,2},{2,0},{1,3},{3,1},{4,6},{6,4},{5,7},{7,5},{8,10},{10,8},{9,1... | collective-permute-start | bytes 589832 | tf_op jit(solution)/shard_map/ppermute | solution.py:26
  382.8 11.7 %collective-permute-start.50 = (bf16[192,512]{1,0:T(8,128)(2,1)}, bf16[192,512]{1,0:T(8,128)(2,1)}, u32[]{:S(2)}, u32[]{:S(2)}) collective-permute-start(bf16[192,512]{1,0:T(8,128)(2,1)} %get-tuple-element.271), channel_id=1, source_target_pairs={{0,4},{4,0},{1,5},{5,1},{2,6},{6,2},{3,7},{7,3},{8,12},{12,8},{9,1... | collective-permute-start | bytes 589832 | tf_op jit(solution)/shard_map/ppermute | solution.py:26
  390.9 143.7 %reduce-scatter.8.cloned.1.call-start = ((), (), s32[]{:S(2)}) async-start(), calls=%async_computation.9 | async-start | bytes 1720320 | tf_op jit(solution)/shard_map/reduce_scatter | solution.py:1210
  390.9 7.6 %collective-permute-start.51 = (bf16[192,512]{1,0:T(8,128)(2,1)}, bf16[192,512]{1,0:T(8,128)(2,1)}, u32[]{:S(2)}, u32[]{:S(2)}) collective-permute-start(bf16[192,512]{1,0:T(8,128)(2,1)} %get-tuple-element.272), channel_id=1, source_target_pairs={{0,6},{2,4},{4,2},{6,0},{1,7},{3,5},{5,3},{7,1},{8,14},{10,12},{12... | collective-permute-start | bytes 589832 | tf_op jit(solution)/shard_map/ppermute | solution.py:971
  394.2 19.3 %collective-permute-start.55 = (bf16[4,48,768]{2,1,0:T(8,128)(2,1)}, bf16[4,48,768]{2,1,0:T(8,128)(2,1)}, u32[]{:S(2)}, u32[]{:S(2)}) collective-permute-start(bf16[4,48,768]{2,1,0:T(8,128)(2,1)} %fusion.3), channel_id=1, source_target_pairs={{0,4},{4,0},{1,5},{5,1},{2,6},{6,2},{3,7},{7,3},{8,12},{12,8},{9,1... | collective-permute-start | bytes 884744 | tf_op jit(solution)/shard_map/ppermute | solution.py:26
  398.5 14.9 %collective-permute-start.56 = (bf16[192,896]{1,0:T(8,128)(2,1)}, bf16[192,896]{1,0:T(8,128)(2,1)S(1)}, u32[]{:S(2)}, u32[]{:S(2)}) collective-permute-start(bf16[192,896]{1,0:T(8,128)(2,1)} %reduce-scatter.4.cloned.1.call-done), channel_id=1, source_target_pairs={{0,1},{1,0},{2,3},{3,2},{4,5},{5,4},{6,7},{7,6},{8,9},{9,8},{10,11... | collective-permute-start | bytes 1032200 | tf_op jit(solution)/shard_map/ppermute | solution.py:26
  413.5 37.0 %collective-permute-start.57 = (bf16[768,1664]{1,0:T(8,128)(2,1)}, bf16[768,1664]{1,0:T(8,128)(2,1)}, u32[]{:S(2)}, u32[]{:S(2)}) collective-permute-start(bf16[768,1664]{1,0:T(8,128)(2,1)} %feed_weights.7), channel_id=1, source_target_pairs={{0,1},{1,0},{2,6},{3,7},{4,5},{5,4},{6,2},{7,3},{8,9},{9,8},{10,14... | collective-permute-start | bytes 7667720 | tf_op jit(solution)/shard_map/ppermute | solution.py:963
  450.5 17.4 %collective-permute-start.59 = (bf16[192,896]{1,0:T(8,128)(2,1)S(1)}, bf16[192,896]{1,0:T(8,128)(2,1)S(1)}, u32[]{:S(2)}, u32[]{:S(2)}) collective-permute-start(bf16[192,896]{1,0:T(8,128)(2,1)S(1)} %add_convert_fusion.5.refs_0_), channel_id=1, source_target_pairs={{0,4},{4,0},{1,5},{5,1},{2,6},{6,2},{3,7},{7,3},{8,12},{12,8},{9,1... | collective-permute-start | bytes 1032200 | tf_op jit(solution)/shard_map/ppermute | solution.py:26
  451.2 16.3 %collective-permute-start.61 = (bf16[96,1664]{1,0:T(8,128)(2,1)}, bf16[96,1664]{1,0:T(8,128)(2,1)}, u32[]{:S(2)}, u32[]{:S(2)}) collective-permute-start(bf16[96,1664]{1,0:T(8,128)(2,1)} %reduce-scatter.6.cloned.1.call-done.refs_4_), channel_id=1, source_target_pairs={{0,4},{4,0},{1,5},{5,1},{2,6},{6,2},{3,7},{7,3},{8,12},{12,8},{9,1... | collective-permute-start | bytes 958472 | tf_op jit(solution)/shard_map/ppermute | solution.py:26
  454.3 24.7 %collective-permute-start.65 = (bf16[2,512,768]{2,1,0:T(8,128)(2,1)}, bf16[2,512,768]{2,1,0:T(8,128)(2,1)S(1)}, u32[]{:S(2)}, u32[]{:S(2)}) collective-permute-start(bf16[2,512,768]{2,1,0:T(8,128)(2,1)} %get-tuple-element.307), channel_id=1, source_target_pairs={{0,2},{2,0},{1,3},{3,1},{4,6},{6,4},{5,7},{7,5},{8,10},{10,8},{9,1... | collective-permute-start | bytes 4718600 | tf_op jit(solution)/shard_map/ppermute | solution.py:26
  461.9 9.2 %collective-permute-start.58 = (bf16[192,896]{1,0:T(8,128)(2,1)S(1)}, bf16[192,896]{1,0:T(8,128)(2,1)S(1)}, u32[]{:S(2)}, u32[]{:S(2)}) collective-permute-start(bf16[192,896]{1,0:T(8,128)(2,1)S(1)} %add_convert_fusion.5.refs_0_), channel_id=1, source_target_pairs={{0,2},{2,0},{1,3},{3,1},{4,6},{6,4},{5,7},{7,5},{8,10},{10,8},{9,1... | collective-permute-start | bytes 1032200 | tf_op jit(solution)/shard_map/ppermute | solution.py:26
  462.3 8.8 %collective-permute-start.62 = (bf16[96,1664]{1,0:T(8,128)(2,1)}, bf16[96,1664]{1,0:T(8,128)(2,1)S(1)}, u32[]{:S(2)}, u32[]{:S(2)}) collective-permute-start(bf16[96,1664]{1,0:T(8,128)(2,1)} %reduce-scatter.6.cloned.1.call-done.refs_4_), channel_id=1, source_target_pairs={{0,2},{2,0},{1,3},{3,1},{4,6},{6,4},{5,7},{7,5},{8,10},{10,8},{9,1... | collective-permute-start | bytes 958472 | tf_op jit(solution)/shard_map/ppermute | solution.py:26
  472.8 21.4 %collective-permute-start.64 = (bf16[384,1664]{1,0:T(8,128)(2,1)}, bf16[384,1664]{1,0:T(8,128)(2,1)}, u32[]{:S(2)}, u32[]{:S(2)}) collective-permute-start(bf16[384,1664]{1,0:T(8,128)(2,1)} %add_convert_fusion.1), channel_id=1, source_target_pairs={{0,4},{1,5},{2,3},{3,2},{4,0},{5,1},{6,7},{7,6},{8,12},{9,13},{10,... | collective-permute-start | bytes 3833864 | tf_op jit(solution)/shard_map/ppermute | solution.py:963
  494.2 18.9 %collective-permute-start.66 = (bf16[512,768]{1,0:T(8,128)(2,1)S(1)}, bf16[512,768]{1,0:T(8,128)(2,1)S(1)}, u32[]{:S(2)}, u32[]{:S(2)}) collective-permute-start(bf16[512,768]{1,0:T(8,128)(2,1)S(1)} %fusion), channel_id=1, source_target_pairs={{0,4},{4,0},{1,5},{5,1},{2,6},{6,2},{3,7},{7,3},{8,12},{12,8},{9,1... | collective-permute-start | bytes 2359304 | tf_op jit(solution)/shard_map/ppermute | solution.py:26
  499.0 19.3 %collective-permute-start.72 = (bf16[96,1664]{1,0:T(8,128)(2,1)}, bf16[96,1664]{1,0:T(8,128)(2,1)}, u32[]{:S(2)}, u32[]{:S(2)}) collective-permute-start(bf16[96,1664]{1,0:T(8,128)(2,1)} %get-tuple-element.340), channel_id=1, source_target_pairs={{0,8},{8,16},{16,24},{24,0},{1,9},{9,17},{17,25},{25,1},{2,10},{10... | collective-permute-start | bytes 958472 | tf_op jit(solution)/shard_map/ppermute | solution.py:1061
  499.0 21.9 %collective-permute-start.73 = (bf16[96,1664]{1,0:T(8,128)(2,1)}, bf16[96,1664]{1,0:T(8,128)(2,1)}, u32[]{:S(2)}, u32[]{:S(2)}) collective-permute-start(bf16[96,1664]{1,0:T(8,128)(2,1)} %get-tuple-element.339), channel_id=1, source_target_pairs={{0,16},{8,24},{16,0},{24,8},{1,17},{9,25},{17,1},{25,9},{2,18},{10... | collective-permute-start | bytes 958472 | tf_op jit(solution)/shard_map/ppermute | solution.py:1061
  507.5 27.0 %collective-permute-start.74 = (bf16[96,1664]{1,0:T(8,128)(2,1)}, bf16[96,1664]{1,0:T(8,128)(2,1)}, u32[]{:S(2)}, u32[]{:S(2)}) collective-permute-start(bf16[96,1664]{1,0:T(8,128)(2,1)} %get-tuple-element.338), channel_id=1, source_target_pairs={{0,24},{8,0},{16,8},{24,16},{1,25},{9,1},{17,9},{25,17},{2,26},{10... | collective-permute-start | bytes 958472 | tf_op jit(solution)/shard_map/ppermute | solution.py:1061
  534.6 8.4 %collective-permute-start.68 = (bf16[192,896]{1,0:T(8,128)(2,1)}, bf16[192,896]{1,0:T(8,128)(2,1)S(1)}, u32[]{:S(2)}, u32[]{:S(2)}) collective-permute-start(bf16[192,896]{1,0:T(8,128)(2,1)} %reduce-scatter.8.cloned.1.call-done), channel_id=1, source_target_pairs={{0,1},{1,0},{2,3},{3,2},{4,5},{5,4},{6,7},{7,6},{8,9},{9,8},{10,11... | collective-permute-start | bytes 1032200 | tf_op jit(solution)/shard_map/ppermute | solution.py:26
  536.1 17.7 %collective-permute-start.75 = (bf16[96,1664]{1,0:T(8,128)(2,1)S(1)}, bf16[96,1664]{1,0:T(8,128)(2,1)}, u32[]{:S(2)}, u32[]{:S(2)}) collective-permute-start(bf16[96,1664]{1,0:T(8,128)(2,1)S(1)} %add_convert_fusion.6.refs_4_), channel_id=1, source_target_pairs={{0,4},{4,0},{1,5},{5,1},{2,6},{6,2},{3,7},{7,3},{8,12},{12,8},{9,1... | collective-permute-start | bytes 958472 | tf_op jit(solution)/shard_map/ppermute | solution.py:26
  543.1 7.4 %collective-permute-start.70 = (bf16[192,896]{1,0:T(8,128)(2,1)S(1)}, bf16[192,896]{1,0:T(8,128)(2,1)}, u32[]{:S(2)}, u32[]{:S(2)}) collective-permute-start(bf16[192,896]{1,0:T(8,128)(2,1)S(1)} %add_convert_fusion.4.refs_0_), channel_id=1, source_target_pairs={{0,4},{4,0},{1,5},{5,1},{2,6},{6,2},{3,7},{7,3},{8,12},{12,8},{9,1... | collective-permute-start | bytes 1032200 | tf_op jit(solution)/shard_map/ppermute | solution.py:26
  544.1 11.2 %collective-permute-start.67 = (bf16[256,768]{1,0:T(8,128)(2,1)S(1)}, bf16[256,768]{1,0:T(8,128)(2,1)S(1)}, u32[]{:S(2)}, u32[]{:S(2)}) collective-permute-start(bf16[256,768]{1,0:T(8,128)(2,1)S(1)} %get-tuple-element.358), channel_id=1, source_target_pairs={{0,1},{1,0},{2,3},{3,2},{4,5},{5,4},{6,7},{7,6},{8,9},{9,8},{10,11... | collective-permute-start | bytes 1179656 | tf_op jit(solution)/shard_map/ppermute | solution.py:26
  544.5 12.1 %collective-permute-start.69 = (bf16[192,896]{1,0:T(8,128)(2,1)S(1)}, bf16[192,896]{1,0:T(8,128)(2,1)S(1)}, u32[]{:S(2)}, u32[]{:S(2)}) collective-permute-start(bf16[192,896]{1,0:T(8,128)(2,1)S(1)} %add_convert_fusion.4.refs_0_), channel_id=1, source_target_pairs={{0,2},{2,0},{1,3},{3,1},{4,6},{6,4},{5,7},{7,5},{8,10},{10,8},{9,1... | collective-permute-start | bytes 1032200 | tf_op jit(solution)/shard_map/ppermute | solution.py:26
  (123 other events, 1282.7 us)
Sparse Core Ops, SparseCore 0:
  15.0 31.7 all-gather.4
  54.6 33.6 all-gather.6
  93.2 30.4 all-gather.10
  125.1 29.6 all-gather.8
  361.8 30.9 reduce-scatter.3
  395.1 29.5 reduce-scatter.5
  462.0 39.1 reduce-scatter.7

commit v5 on v4

--- a/solution.py
+++ b/solution.py
@@ -70,7 +70,10 @@
 
 def attention_forward_kernel(norm, info, *refs):
     parts, (w_ref, bias_ref, gain_ref, shift_ref) = refs[:4], refs[4:8]
-    at_out, qkv_out, out_ref, lse_ref, a_ref, at_ref, qkv_ref, v_t, sems, out_sems = refs[8:]
+    at_out, qkv_out, out_ref, lse_ref = refs[8:12]
+    if norm:
+        n_out = refs[12]
+    a_ref, at_ref, qkv_ref, v_t, sems, out_sems = refs[13:19] if norm else refs[12:18]
     length = qkv_ref.shape[0]
     ends = (info[0], info[1], info[2])
     dev, half = info[3], info[4]
@@ -86,7 +89,9 @@
             goal = pl.ds(pl.multiple_of(part * each + at * BLK, BLK), BLK)
             values = a_ref[part, rows, :]
             if norm:
-                values = norm_rows(values.astype(F32), gain_ref[...], shift_ref[...]).astype(BF16)
+                normed = norm_rows(values.astype(F32), 1.0, 0.0)
+                a_ref[part, rows, :] = normed.astype(BF16)
+                values = (normed * gain_ref[...] + shift_ref[...]).astype(BF16)
             found = dot(values, w_ref[:, 0:576]) + bias_ref[...]
             at_ref[:, goal] = values.T
             qkv_ref[goal, 0:384] = found[:, 0:384].astype(BF16)
@@ -103,6 +108,8 @@
         pltpu.make_async_copy(at_ref, at_out, out_sems.at[0]),
         pltpu.make_async_copy(qkv_ref, qkv_out, out_sems.at[1]),
     ]
+    if norm:
+        out_copies.append(pltpu.make_async_copy(a_ref, n_out, out_sems.at[2]))
     for copy in out_copies:
         copy.start()
 
@@ -186,14 +193,14 @@
             num_scalar_prefetch=1,
             grid=(1,),
             in_specs=[HBM] * 4 + [whole(w_qkv.shape), whole(bias.shape), whole(gain.shape), whole(shift.shape)],
-            out_specs=[HBM, HBM, whole((4, 192, each)), whole((8, length))],
+            out_specs=[HBM, HBM, whole((4, 192, each)), whole((8, length))] + [HBM] * norm,
             scratch_shapes=[
                 pltpu.VMEM((4, each, width), BF16),
                 pltpu.VMEM((width, length), BF16),
                 pltpu.VMEM((length, 576), BF16),
                 pltpu.VMEM((3, HEAD + 16, length), BF16),
                 pltpu.SemaphoreType.DMA((4,)),
-                pltpu.SemaphoreType.DMA((2,)),
+                pltpu.SemaphoreType.DMA((3,)),
             ],
         ),
         out_shape=(
@@ -201,7 +208,8 @@
             jax.ShapeDtypeStruct((length, 576), BF16),
             jax.ShapeDtypeStruct((4, 192, each), BF16),
             jax.ShapeDtypeStruct((8, length), F32),
-        ),
+        )
+        + (jax.ShapeDtypeStruct((4, each, width), BF16),) * norm,
         compiler_params=pltpu.CompilerParams(vmem_limit_bytes=48 << 20),
         cost_estimate=pl.CostEstimate(
             flops=14 * 10**9, transcendentals=3 * length * 1024, bytes_accessed=12 << 20
@@ -211,10 +219,10 @@
 
 def attention_backward_kernel(norm, info, qkv_ref, out_ref, lse_ref, w_ref, g0, g1, g2, g3, *refs):
     if norm:
-        tokens, refs = refs[:4], refs[4:]
+        tokens, refs = refs[0], refs[1:]
         norm_sums, refs = refs[5], refs[:5] + refs[6:]
         x_ref, da_ref, x_sems = refs[-3:]
-        token_copies = [pltpu.make_async_copy(part, x_ref.at[at], x_sems.at[at]) for at, part in enumerate(tokens)]
+        token_copies = [pltpu.make_async_copy(tokens, x_ref, x_sems.at[0])]
         for copy in token_copies:
             copy.start()
         refs = refs[:-3]
@@ -351,15 +359,15 @@
             da_ref[...] = found
 
             def rows_of(step, sums, part=part):
-                rows = pl.ds(pl.multiple_of(step * 64, 64), 64)
+                rows = pl.ds(pl.multiple_of(step * 128, 128), 128)
                 grad = da_ref[rows, :]
-                normed = norm_rows(x_ref[part, rows, :].astype(F32), 1.0, 0.0)
+                normed = x_ref[part, rows, :].astype(F32)
                 return (
                     sums[0] + jnp.sum(grad * normed, axis=0, keepdims=True),
                     sums[1] + jnp.sum(grad, axis=0, keepdims=True),
                 )
 
-            totals = lax.fori_loop(0, each // 64, rows_of, totals)
+            totals = lax.fori_loop(0, each // 128, rows_of, totals)
             found = da_ref[...]
         target[...] = found.astype(kind)
         copies.append(pltpu.make_async_copy(target, goal, sems.at[at + 1]))
@@ -397,7 +405,7 @@
                 pltpu.VMEM((each, width), F32),
                 pltpu.SemaphoreType.DMA((5,)),
             ]
-            + [pltpu.VMEM((4, each, width), BF16), pltpu.VMEM((each, width), F32), pltpu.SemaphoreType.DMA((4,))] * norm,
+            + [pltpu.VMEM((4, each, width), BF16), pltpu.VMEM((each, width), F32), pltpu.SemaphoreType.DMA((1,))] * norm,
         ),
         out_shape=(
             jax.ShapeDtypeStruct(qkv.shape, BF16),
@@ -1114,7 +1122,7 @@
             one0, two0, attn_piece, *attn_parts = lax.optimization_barrier((one0, two0, attn_piece, *attn_parts))
             three0 = turned(one0, False)
             early_core = [swap(part, "core") for part in (feed0, one0, two0)]
-        attn_t, qkv, attended, lse = attention_forward(info, attn_parts, w_qkv, bias, gain_one, bias_one, layer == 0)
+        attn_t, qkv, attended, lse, *normed_all = attention_forward(info, attn_parts, w_qkv, bias, gain_one, bias_one, layer == 0)
         if layer == 0:
             attn1 = over_shards(after(attn_piece, attended))
             w_out = out_weights(out_own(attn0))
@@ -1156,6 +1164,8 @@
         else:
             slope = act = act_other = result = None
             mlp_other = swap(mlp_in, "core")
+        if layer == 0:
+            first_normed = normed_all
         weights.append((w_qkv, w_out, w_feed))
         saved.append((current, attn_t, qkv, attended, lse, context, middle, mlp_in, mlp_other, slope, act, act_other))
         current = result
@@ -1191,7 +1201,7 @@
             ready.append(early)
         *attn_grads, late, far = lax.optimization_barrier(tuple(ready))[:6]
         du, to_core, to_far, own, sums_u, *norm_sums = attention_backward(
-            info, qkv, attended, lse, w_qkv, attn_grads, first_parts if layer == 0 else ()
+            info, qkv, attended, lse, w_qkv, attn_grads, first_normed if layer == 0 else ()
         )
         late = turned(late, False)
         to_core = after(to_core, late)

time: 580 us -> 575 us (level)
  Pallas kernels: 216 us -> 238 us
  starting transfers between devices: 82 us -> 61.1 us
  waiting for transfers between devices: 166 us -> 157 us
    ppermute x10, starting transfers between devices: 19.7 us -> 6.07 us  [turned(): return lax.ppermute(value, PLANE, pairs)]
    pallas_call x2, Pallas kernels: 35.1 us -> 46.7 us  [attention_forward(): pl.pallas_call(partial(attention_forward_kernel, norm), name='attention_f...]
    pallas_call x2, Pallas kernels: 59.3 us -> 70.2 us  [attention_backward(): pl.pallas_call(partial(attention_backward_kernel, norm), name='attention_...]
    ppermute x3, waiting for transfers between devices: 16.2 us -> 8.46 us  [send_shards(): lax.ppermute(lax.dynamic_slice_in_dim(value, (index + by) % shards * coun...]
    ppermute x3, starting transfers between devices: 8.51 us -> 1.47 us  [send_shards(): lax.ppermute(lax.dynamic_slice_in_dim(value, (index + by) % shards * coun...]
    unnamed x205 -> x201, local copies, waits for them, and re-layouts: 23.2 us -> 23.2 us
  transfers between devices with their start and end apart: 85 -> 85, of which waited for: 31 -> 31; matrix products, arithmetic and copies ran while one was open for 11% -> 11% of each run, Pallas kernels for 33% -> 37%
where the time goes in v5:
time: 575 us; the launch traced here: 563 us
  Pallas kernels  238 us (41%)
  waiting for transfers between devices  157 us (27%)
  starting transfers between devices  61.1 us (11%)
  local copies, waits for them, and re-layouts  54.4 us (9%)
  other arithmetic  30.6 us (5%)
  between operations  17.9 us (3%)
    ppermute x61, waiting for transfers between devices, swap(): return lax.ppermute(value, axis, ((0, 1), (1, 0)))  84.5 us
    pallas_call x2, Pallas kernels, attention_backward(): pl.pallas_call(partial(attention_backward_kernel, norm), name='attention_...  70.2 us
    ppermute x61, starting transfers between devices, swap(): return lax.ppermute(value, axis, ((0, 1), (1, 0)))  48.7 us
    pallas_call x2, Pallas kernels, attention_forward(): pl.pallas_call(partial(attention_forward_kernel, norm), name='attention_f...  46.7 us
    ppermute x10, waiting for transfers between devices, turned(): return lax.ppermute(value, PLANE, pairs)  43.8 us
    pallas_call x4, Pallas kernels, feed_weights(): pl.pallas_call(feed_weights_kernel, name='feed_weights', grid=(units // s...  23.4 us
    unnamed x201, local copies, waits for them, and re-layouts  23.2 us
    pallas_call x1, Pallas kernels, feed_both(): pl.pallas_call(feed_both_kernel, name='feed_both', grid_spec=pltpu.Prefet...  23 us
  transfers between devices with their start and end apart: 85, of which 31 were waited for; matrix products, arithmetic and copies ran while one was open for 11% of the time, Pallas kernels for 37%

profile of v5, /device:TPU:9, one launch (start us, length us, event | category | flops | bytes accessed | tf_op | source)
XLA Modules:
  0.0 563.4 jit_solution(10219382741584735969)
XLA Ops:
  7.2 2.3 dynamic-slice_bitcast_fusion
  17.6 11.6 %collective-permute-done.2 = bf16[2,256,768]{2,1,0:T(8,128)(2,1)} collective-permute-done((bf16[2,256,768]{2,1,0:T(8,128)(2,1)}, bf16[2,256,768]{2,1,0:T(8,128)(2,1)}, u32[]{:S(2)}, u32[]{:S(2)}) %collective-permute-start.2) | collective-permute-done | bytes 786464 | tf_op jit(solution)/shard_map/ppermute | solution.py:26
  29.3 1.9 slice_bitcast_fusion.3
  33.7 1.8 collective-permute-start.3
  35.6 14.4 %collective-permute-done.4.refs_2_ = bf16[512,768]{1,0:T(8,128)(2,1)S(1)} collective-permute-done((bf16[512,768]{1,0:T(8,128)(2,1)S(1)}, bf16[512,768]{1,0:T(8,128)(2,1)S(1)}, u32[]{:S(2)}, u32[]{:S(2)}) %collective-permute-start.4) | collective-permute-done | bytes 786464 | tf_op jit(solution)/shard_map/ppermute | solution.py:26
  50.0 2.5 collective-permute-start.5
  52.5 2.0 collective-permute-done.5.refs_3_
  65.5 17.2 %collective-permute-done.refs_1_ = bf16[384,1664]{1,0:T(8,128)(2,1)} collective-permute-done((bf16[384,1664]{1,0:T(8,128)(2,1)}, bf16[384,1664]{1,0:T(8,128)(2,1)}, u32[]{:S(2)}, u32[]{:S(2)}) %collective-permute-start) | collective-permute-done | bytes 1277984 | tf_op jit(solution)/shard_map/ppermute | solution.py:971
  82.7 3.2 collective-permute-done.1.refs_2_
  93.1 1.7 fusion.30
  97.3 24.0 %attention_forward.2 = (bf16[768,2048]{1,0:T(8,128)(2,1)}, bf16[2048,576]{1,0:T(8,128)(2,1)}, bf16[4,192,512]{2,1,0:T(8,128)(2,1)S(1)}, f32[8,2048]{1,0:T(8,128)S(1)}, bf16[4,512,768]{2,1,0:T(8,128)(2,1)}) custom-call(s32[8]{0:T(128)S(1)} %stack.76.info, bf16[512,768]{1,0:T(8,128)(2,1)S(1)} %get-tuple-element.178.refs_0_, bf16[512,768]{1,0:T(8,128)(2,1)S(1)} %copy-done.34, ...), custom_call_target="tpu_custom_call" | custom-call | flops 14000000000 | bytes 12582912 | tf_op jit(solution)/shard_map/attention_forward/pallas_call | solution.py:189
  126.5 3.6 collective-permute-done.14.p2
  130.0 4.6 collective-permute-done.15.p3
  134.7 4.4 out_forward.2
  142.6 14.7 %feed_forward.1 = (bf16[4,512,768]{2,1,0:T(8,128)(2,1)}, bf16[2,768,512]{2,1,0:T(8,128)(2,1)}, bf16[2,768,512]{2,1,0:T(8,128)(2,1)}, f32[512,768]{1,0:T(8,128)}, bf16[512,768]{1,0:T(8,128)(2,1)}) custom-call(bf16[512,768]{1,0:T(8,128)(2,1)} %copy-done.5, f32[512,768]{1,0:T(8,128)} %copy-done.36, f32[3,768]{1,0:T(4,128)} %pad_maximum_fusion.7.vec_ref, ...), custom_call_target="tpu_custom_call" | custom-call | flops 5000000000 | bytes 20971520 | tf_op jit(solution)/shard_map/feed_forward/pallas_call | solution.py:621
  163.8 13.2 %collective-permute-done.24.refs_2_ = bf16[512,768]{1,0:T(8,128)(2,1)S(1)} collective-permute-done((bf16[512,768]{1,0:T(8,128)(2,1)}, bf16[512,768]{1,0:T(8,128)(2,1)S(1)}, u32[]{:S(2)}, u32[]{:S(2)}) %collective-permute-start.24) | collective-permute-done | bytes 786464 | tf_op jit(solution)/shard_map/ppermute | solution.py:26
  177.0 3.1 collective-permute-start.25
  180.2 3.1 collective-permute-done.19
  183.4 1.7 collective-permute-start.20
  189.7 22.7 %attention_forward.3 = (bf16[768,2048]{1,0:T(8,128)(2,1)}, bf16[2048,576]{1,0:T(8,128)(2,1)}, bf16[4,192,512]{2,1,0:T(8,128)(2,1)S(1)}, f32[8,2048]{1,0:T(8,128)S(1)}) custom-call(s32[8]{0:T(128)S(1)} %stack.76.info, bf16[512,768]{1,0:T(8,128)(2,1)S(1)} %copy-done.35, bf16[512,768]{1,0:T(8,128)(2,1)S(1)} %collective-permute-done.23.refs_1_, ...), custom_call_target="tpu_custom_call" | custom-call | flops 14000000000 | bytes 12582912 | tf_op jit(solution)/shard_map/attention_forward/pallas_call | solution.py:189
  213.1 4.4 collective-permute-done.27.refs_3_
  220.6 4.8 collective-permute-done.31.p2
  225.4 4.4 collective-permute-done.32.p3
  233.4 4.4 out_forward.3
  241.8 23.0 %feed_both.1 = (bf16[2,512,768]{2,1,0:T(8,128)(2,1)}, bf16[2,512,768]{2,1,0:T(8,128)(2,1)}, f32[512,768]{1,0:T(8,128)}, bf16[512,768]{1,0:T(8,128)(2,1)}, f32[8,...) custom-call(s32[8]{0:T(128)} %copy-done.31, ...), custom_call_target="tpu_custom_call" | custom-call | flops 10000000000 | bytes 25165824 | tf_op jit(solution)/shard_map/feed_both/pallas_call | solution.py:812
  265.9 1.9 convolution_convert_fusion.1
  268.6 2.7 collective-permute-done.35.g1
  273.5 6.3 %collective-permute-done.37.g3 = bf16[192,512]{1,0:T(8,128)(2,1)S(1)} collective-permute-done((bf16[192,512]{1,0:T(8,128)(2,1)S(1)}, bf16[192,512]{1,0:T(8,128)(2,1)S(1)}, u32[]{:S(2)}, u32[]{:S(2)}) %collective-permute-start.37) | collective-permute-done | bytes 196640 | tf_op jit(solution)/shard_map/ppermute | solution.py:979
  281.7 5.6 feed_weights.4
  289.3 33.5 %attention_backward.2 = (bf16[2048,576]{1,0:T(8,128)(2,1)}, bf16[2,512,768]{2,1,0:T(8,128)(2,1)}, f32[512,768]{1,0:T(8,128)}, f32[512,768]{1,0:T(8,128)}, f32[8,576]{1,0:T(8,128)}) custom-call(s32[8]{0:T(128)} %copy-done.31, bf16[2048,576]{1,0:T(8,128)(2,1)} %get-tuple-element.224.qkv_ref, bf16[4,192,512]{2,1,0:T(8,128)(2,1)} %copy-done.24, ...), custom_call_target="tpu_custom_call" | custom-call | flops 20000000000 | bytes 16777216 | tf_op jit(solution)/shard_map/attention_backward/pallas_call | solution.py:386
  323.6 1.7 slice.370
  328.1 1.9 fusion.1
  332.4 5.6 feed_weights.5
  338.0 3.2 add_convert_fusion.3
  341.5 7.7 %collective-permute-done.46.far = bf16[512,768]{1,0:T(8,128)(2,1)S(1)} collective-permute-done((bf16[512,768]{1,0:T(8,128)(2,1)S(1)}, bf16[512,768]{1,0:T(8,128)(2,1)S(1)}, u32[]{:S(2)}, u32[]{:S(2)}) %collective-permute-start.46) | collective-permute-done | bytes 786464 | tf_op jit(solution)/shard_map/ppermute | solution.py:26
  351.4 5.3 norm_backward.2
  357.8 5.7 %attention_weights.2 = bf16[768,896]{1,0:T(8,128)(2,1)} custom-call(bf16[768,2048]{1,0:T(8,128)(2,1)} %get-tuple-element.260.at_ref, bf16[2048,576]{1,0:T(8,128)(2,1)S(1)} %copy-done.16, f32[16,768]{1,0:T(8,128)S(1)} %maximum_maximum_fusion.vec_ref, bf16[192,768]{1,0:T(8,128)(2,1)S(1)} %bitcast.156, bf16[192,768]{1,0:T(8,128)(2,1)S(1)} %bitcast.158, ...), custom_call_target="tpu_custom_call" | custom-call | flops 1800000000 | bytes 8388608 | tf_op jit(solution)/shard_map/attention_weights/pallas_call | solution.py:443
  363.6 3.2 collective-permute-done.48
  366.8 18.0 %feed_backward.1 = (bf16[2,512,768]{2,1,0:T(8,128)(2,1)}, bf16[2,512,768]{2,1,0:T(8,128)(2,1)}, f32[512,768]{1,0:T(8,128)}, bf16[512,768]{1,0:T(8,128)(2,1)}, f3...) custom-call(s32[8]{0:T(128)} %copy-done.31, ...), custom_call_target="tpu_custom_call" | custom-call | flops 6000000000 | bytes 25165824 | tf_op jit(solution)/shard_map/feed_backward/pallas_call | solution.py:727
  387.8 1.9 convolution_convert_fusion
  392.1 3.3 add_convert_fusion.2
  396.5 1.8 fusion.3
  399.1 4.0 collective-permute-done.51.g3
  403.1 6.1 %feed_weights.7 = bf16[768,1664]{1,0:T(8,128)(2,1)} custom-call(bf16[2,512,768]{2,1,0:T(8,128)(2,1)S(1)} %copy-done.4, bf16[2,512,768]{2,1,0:T(8,128)(2,1)} %collective-permute-done.52.dh2, bf16[2,768,512]{2,1,0:T(8,128)(2,1)} %get-tuple-element.277.act, bf16[2,768,512]{2,1,0:T(8,128)(2,1)} %collective-permute-done.21.act2, bf16[512,768]{1,0:T(8,128)(2,1)S(1)} %copy-done.6, ...), custom_call_target="tpu_custom_call" | custom-call | flops 2400000000 | bytes 9437184 | tf_op jit(solution)/shard_map/feed_weights/pallas_call | solution.py:851
  409.2 6.1 %feed_weights.6 = bf16[768,1664]{1,0:T(8,128)(2,1)} custom-call(bf16[2,512,768]{2,1,0:T(8,128)(2,1)S(1)} %copy-done.4, bf16[2,512,768]{2,1,0:T(8,128)(2,1)} %collective-permute-done.52.dh2, bf16[2,768,512]{2,1,0:T(8,128)(2,1)} %get-tuple-element.277.act, bf16[2,768,512]{2,1,0:T(8,128)(2,1)} %collective-permute-done.21.act2, bf16[512,768]{1,0:T(8,128)(2,1)S(1)} %copy-done.6, ...), custom_call_target="tpu_custom_call" | custom-call | flops 2400000000 | bytes 9437184 | tf_op jit(solution)/shard_map/feed_weights/pallas_call | solution.py:851
  417.2 36.7 %attention_backward.3 = (bf16[2048,576]{1,0:T(8,128)(2,1)}, bf16[2,512,768]{2,1,0:T(8,128)(2,1)}, f32[512,768]{1,0:T(8,128)}, f32[512,768]{1,0:T(8,128)}, f32[8,576]{1,0:T(8,128)}, /*index=5*/f32[8,768]{1,0:T(8,128)}) custom-call(s32[8]{0:T(128)} %copy-done.31, bf16[2048,576]{1,0:T(8,128)(2,1)} %get-tuple-element.289.qkv_ref, ...), custom_call_target="tpu_custom_call" | custom-call | flops 20000000000 | bytes 16777216 | tf_op jit(solution)/shard_map/attention_backward/pallas_call | solution.py:386
  459.1 2.0 collective-permute-start.65
  461.1 1.7 copy-done.17
  462.8 5.7 %attention_weights.3 = bf16[768,896]{1,0:T(8,128)(2,1)} custom-call(bf16[768,2048]{1,0:T(8,128)(2,1)} %get-tuple-element.288.at_ref, bf16[2048,576]{1,0:T(8,128)(2,1)S(1)} %copy-done.17, f32[16,768]{1,0:T(8,128)S(1)} %concatenate.91.vec_ref, bf16[192,768]{1,0:T(8,128)(2,1)S(1)} %bitcast.157, bf16[192,768]{1,0:T(8,128)(2,1)S(1)} %bitcast.159, ...), custom_call_target="tpu_custom_call" | custom-call | flops 1800000000 | bytes 8388608 | tf_op jit(solution)/shard_map/attention_weights/pallas_call | solution.py:443
  470.5 2.3 collective-permute-start.63
  472.8 3.1 add_convert_fusion.1
  477.6 2.2 fusion
  479.8 14.5 %collective-permute-done.64 = bf16[384,1664]{1,0:T(8,128)(2,1)} collective-permute-done((bf16[384,1664]{1,0:T(8,128)(2,1)}, bf16[384,1664]{1,0:T(8,128)(2,1)}, u32[]{:S(2)}, u32[]{:S(2)}) %collective-permute-start.64) | collective-permute-done | bytes 1277984 | tf_op jit(solution)/shard_map/ppermute | solution.py:971
  495.1 2.2 add_convert_fusion
  500.8 5.5 finish.2
  506.4 5.8 %collective-permute-done.66.far = bf16[512,768]{1,0:T(8,128)(2,1)S(1)} collective-permute-done((bf16[512,768]{1,0:T(8,128)(2,1)S(1)}, bf16[512,768]{1,0:T(8,128)(2,1)S(1)}, u32[]{:S(2)}, u32[]{:S(2)}) %collective-permute-start.66) | collective-permute-done | bytes 786464 | tf_op jit(solution)/shard_map/ppermute | solution.py:26
  512.2 5.2 norm_backward.3
  517.4 8.5 %collective-permute-done.73 = bf16[96,1664]{1,0:T(8,128)(2,1)} collective-permute-done((bf16[96,1664]{1,0:T(8,128)(2,1)}, bf16[96,1664]{1,0:T(8,128)(2,1)}, u32[]{:S(2)}, u32[]{:S(2)}) %collective-permute-start.73) | collective-permute-done | bytes 319520 | tf_op jit(solution)/shard_map/ppermute | solution.py:1069
  529.7 4.8 collective-permute-done.68
  535.8 2.3 collective-permute-start.67
  538.0 1.7 collective-permute-start.69
  539.8 4.6 collective-permute-done.70.refs_2_
  544.3 2.0 collective-permute-start.71
  550.0 6.0 %finish.3 = (f32[2,192,2304]{2,1,0:T(8,128)}, f32[2,192,768]{2,1,0:T(8,128)}, f32[2,768,384]{2,1,0:T(8,128)}, f32[2,384,768]{2,1,0:T(8,128)}, f32[2,192]{1,0:T(2...) custom-call(s32[8]{0:T(128)} %copy-done.31, ...), custom_call_target="tpu_custom_call", output_to_operand_aliasing={{0}: (11, {}), {1}: (12, {}), {2}: (13, {}), {3}: (14, {})} | custom-call | flops 1000000 | bytes 8388608 | tf_op jit(solution)/shard_map/finish/pallas_call | solution.py:937
  (468 shorter events, 108.3 us)
Async XLA Ops:
  7.2 45.3 %all-gather.5.cloned.1.call-start = ((), (), s32[]{:S(2)}) async-start(), calls=%async_computation.3 | async-start | bytes 1597440 | tf_op jit(solution)/shard_map/all_gather | solution.py:1062
  10.5 18.7 %collective-permute-start.2 = (bf16[2,256,768]{2,1,0:T(8,128)(2,1)}, bf16[2,256,768]{2,1,0:T(8,128)(2,1)}, u32[]{:S(2)}, u32[]{:S(2)}) collective-permute-start(bf16[2,256,768]{2,1,0:T(8,128)(2,1)} %pad_maximum_fusion), channel_id=1, source_target_pairs={{0,1},{1,0},{2,3},{3,2},{4,5},{5,4},{6,7},{7,6},{8,9},{9,8},{10,11... | collective-permute-start | bytes 2359304 | tf_op jit(solution)/shard_map/ppermute | solution.py:26
  14.9 73.5 %all-gather.7.cloned.1.call-start = ((), (), s32[]{:S(2)}) async-start(), calls=%async_computation.4 | async-start | bytes 1720320 | tf_op jit(solution)/shard_map/all_gather | solution.py:1062
  32.5 17.5 %collective-permute-start.4 = (bf16[512,768]{1,0:T(8,128)(2,1)S(1)}, bf16[512,768]{1,0:T(8,128)(2,1)S(1)}, u32[]{:S(2)}, u32[]{:S(2)}) collective-permute-start(bf16[512,768]{1,0:T(8,128)(2,1)S(1)} %get-tuple-element.178.refs_0_), channel_id=1, source_target_pairs={{0,4},{4,0},{1,5},{5,1},{2,6},{6,2},{3,7},{7,3},{8,12},{12,8},{9,1... | collective-permute-start | bytes 2359304 | tf_op jit(solution)/shard_map/ppermute | solution.py:26
  33.7 18.7 %collective-permute-start.3 = (bf16[512,768]{1,0:T(8,128)(2,1)S(1)}, bf16[512,768]{1,0:T(8,128)(2,1)S(1)}, u32[]{:S(2)}, u32[]{:S(2)}) collective-permute-start(bf16[512,768]{1,0:T(8,128)(2,1)S(1)} %get-tuple-element.178.refs_0_), channel_id=1, source_target_pairs={{0,2},{2,0},{1,3},{3,1},{4,6},{6,4},{5,7},{7,5},{8,10},{10,8},{9,1... | collective-permute-start | bytes 2359304 | tf_op jit(solution)/shard_map/ppermute | solution.py:26
  54.6 87.4 %all-gather.11.cloned.1.call-start = ((), (), s32[]{:S(2)}) async-start(), calls=%async_computation.6 | async-start | bytes 1597440 | tf_op jit(solution)/shard_map/all_gather | solution.py:1062
  54.6 28.1 %collective-permute-start = (bf16[384,1664]{1,0:T(8,128)(2,1)}, bf16[384,1664]{1,0:T(8,128)(2,1)}, u32[]{:S(2)}, u32[]{:S(2)}) collective-permute-start(bf16[384,1664]{1,0:T(8,128)(2,1)} %all-gather.5.cloned.1.call-done.refs_0_), channel_id=1, source_target_pairs={{0,4},{1,5},{2,3},{3,2},{4,0},{5,1},{6,7},{7,6},{8,12},{9,13},{10,... | collective-permute-start | bytes 3833864 | tf_op jit(solution)/shard_map/ppermute | solution.py:971
  55.9 30.0 %collective-permute-start.1 = (bf16[384,1664]{1,0:T(8,128)(2,1)}, bf16[384,1664]{1,0:T(8,128)(2,1)}, u32[]{:S(2)}, u32[]{:S(2)}) collective-permute-start(bf16[384,1664]{1,0:T(8,128)(2,1)} %all-gather.5.cloned.1.call-done.refs_0_), channel_id=1, source_target_pairs={{0,1},{1,0},{2,6},{3,7},{4,5},{5,4},{6,2},{7,3},{8,9},{9,8},{10,14... | collective-permute-start | bytes 3833864 | tf_op jit(solution)/shard_map/ppermute | solution.py:971
  64.5 58.6 %collective-permute-start.10 = (bf16[384,1664]{1,0:T(8,128)(2,1)}, bf16[384,1664]{1,0:T(8,128)(2,1)}, u32[]{:S(2)}, u32[]{:S(2)}) collective-permute-start(bf16[384,1664]{1,0:T(8,128)(2,1)} %all-gather.5.cloned.1.call-done.refs_0_), channel_id=1, source_target_pairs={{0,2},{2,0},{1,3},{3,1},{4,6},{6,4},{5,7},{7,5},{8,10},{10,8},{9,1... | collective-permute-start | bytes 3833864 | tf_op jit(solution)/shard_map/ppermute | solution.py:26
  85.9 37.2 %collective-permute-start.11 = (bf16[384,1664]{1,0:T(8,128)(2,1)}, bf16[384,1664]{1,0:T(8,128)(2,1)}, u32[]{:S(2)}, u32[]{:S(2)}) collective-permute-start(bf16[384,1664]{1,0:T(8,128)(2,1)} %collective-permute-done.refs_1_), channel_id=1, source_target_pairs={{0,2},{2,0},{1,3},{3,1},{4,6},{6,4},{5,7},{7,5},{8,10},{10,8},{9,1... | collective-permute-start | bytes 3833864 | tf_op jit(solution)/shard_map/ppermute | solution.py:26
  86.0 37.1 %collective-permute-start.9 = (bf16[384,1664]{1,0:T(8,128)(2,1)}, bf16[384,1664]{1,0:T(8,128)(2,1)}, u32[]{:S(2)}, u32[]{:S(2)}) collective-permute-start(bf16[384,1664]{1,0:T(8,128)(2,1)} %collective-permute-done.refs_1_), channel_id=1, source_target_pairs={{0,1},{1,0},{2,6},{3,7},{4,5},{5,4},{6,2},{7,3},{8,9},{9,8},{10,14... | collective-permute-start | bytes 3833864 | tf_op jit(solution)/shard_map/ppermute | solution.py:971
  87.2 35.9 %collective-permute-start.12 = (bf16[384,1664]{1,0:T(8,128)(2,1)}, bf16[384,1664]{1,0:T(8,128)(2,1)}, u32[]{:S(2)}, u32[]{:S(2)}) collective-permute-start(bf16[384,1664]{1,0:T(8,128)(2,1)} %collective-permute-done.1.refs_2_), channel_id=1, source_target_pairs={{0,2},{2,0},{1,3},{3,1},{4,6},{6,4},{5,7},{7,5},{8,10},{10,8},{9,1... | collective-permute-start | bytes 3833864 | tf_op jit(solution)/shard_map/ppermute | solution.py:26
  93.1 66.9 %all-gather.9.cloned.1.call-start = ((), (), s32[]{:S(2)}) async-start(), calls=%async_computation.5 | async-start | bytes 1474560 | tf_op jit(solution)/shard_map/all_gather | solution.py:1062
  94.9 26.5 %collective-permute-start.7 = (bf16[4,1,48,768]{3,2,0,1:T(8,128)(2,1)}, bf16[4,1,48,768]{3,2,0,1:T(8,128)(2,1)S(1)}, u32[]{:S(2)}, u32[]{:S(2)}) collective-permute-start(bf16[4,1,48,768]{3,2,0,1:T(8,128)(2,1)} %reshape.175), channel_id=1, source_target_pairs={{0,4},{4,0},{1,5},{5,1},{2,6},{6,2},{3,7},{7,3},{8,12},{12,8},{9,1... | collective-permute-start | bytes 884744 | tf_op jit(solution)/shard_map/ppermute | solution.py:26
  123.1 19.5 %collective-permute-start.16 = (bf16[384,1664]{1,0:T(8,128)(2,1)}, bf16[384,1664]{1,0:T(8,128)(2,1)}, u32[]{:S(2)}, u32[]{:S(2)}) collective-permute-start(bf16[384,1664]{1,0:T(8,128)(2,1)} %collective-permute-done.9.refs_3_), channel_id=1, source_target_pairs={{0,2},{2,0},{1,3},{3,1},{4,6},{6,4},{5,7},{7,5},{8,10},{10,8},{9,1... | collective-permute-start | bytes 3833864 | tf_op jit(solution)/shard_map/ppermute | solution.py:26
  124.1 10.6 %collective-permute-start.15 = (bf16[192,512]{1,0:T(8,128)(2,1)S(1)}, bf16[192,512]{1,0:T(8,128)(2,1)S(1)}, u32[]{:S(2)}, u32[]{:S(2)}) collective-permute-start(bf16[192,512]{1,0:T(8,128)(2,1)S(1)} %get-tuple-element.373), channel_id=1, source_target_pairs={{0,6},{2,4},{4,2},{6,0},{1,7},{3,5},{5,3},{7,1},{8,14},{10,12},{12... | collective-permute-start | bytes 589832 | tf_op jit(solution)/shard_map/ppermute | solution.py:979
  125.8 277.3 %reduce-scatter.4.cloned.1.call-start = ((), (), s32[]{:S(2)}) async-start(), calls=%async_computation.7 | async-start | bytes 1720320 | tf_op jit(solution)/shard_map/reduce_scatter | solution.py:1248
  142.0 16.6 %collective-permute-start.17 = (bf16[384,1664]{1,0:T(8,128)(2,1)}, bf16[384,1664]{1,0:T(8,128)(2,1)S(1)}, u32[]{:S(2)}, u32[]{:S(2)}) collective-permute-start(bf16[384,1664]{1,0:T(8,128)(2,1)} %all-gather.11.cloned.1.call-done.refs_0_), channel_id=1, source_target_pairs={{0,4},{1,5},{2,3},{3,2},{4,0},{5,1},{6,7},{7,6},{8,12},{9,13},{10,... | collective-permute-start | bytes 3833864 | tf_op jit(solution)/shard_map/ppermute | solution.py:971
  158.6 18.4 %collective-permute-start.24 = (bf16[512,768]{1,0:T(8,128)(2,1)}, bf16[512,768]{1,0:T(8,128)(2,1)S(1)}, u32[]{:S(2)}, u32[]{:S(2)}) collective-permute-start(bf16[512,768]{1,0:T(8,128)(2,1)} %get-tuple-element.202.refs_0_), channel_id=1, source_target_pairs={{0,4},{4,0},{1,5},{5,1},{2,6},{6,2},{3,7},{7,3},{8,12},{12,8},{9,1... | collective-permute-start | bytes 2359304 | tf_op jit(solution)/shard_map/ppermute | solution.py:26
  158.9 28.4 %collective-permute-start.21 = (bf16[2,768,512]{2,1,0:T(8,128)(2,1)}, bf16[2,768,512]{2,1,0:T(8,128)(2,1)}, u32[]{:S(2)}, u32[]{:S(2)}) collective-permute-start(bf16[2,768,512]{2,1,0:T(8,128)(2,1)} %get-tuple-element.201), channel_id=1, source_target_pairs={{0,2},{2,0},{1,3},{3,1},{4,6},{6,4},{5,7},{7,5},{8,10},{10,8},{9,1... | collective-permute-start | bytes 4718600 | tf_op jit(solution)/shard_map/ppermute | solution.py:26
  162.1 21.3 %collective-permute-start.19 = (bf16[4,1,48,768]{3,2,0,1:T(8,128)(2,1)S(1)}, bf16[4,1,48,768]{3,2,0,1:T(8,128)(2,1)S(1)}, u32[]{:S(2)}, u32[]{:S(2)}) collective-permute-start(bf16[4,1,48,768]{3,2,0,1:T(8,128)(2,1)S(1)} %reshape.177), channel_id=1, source_target_pairs={{0,4},{4,0},{1,5},{5,1},{2,6},{6,2},{3,7},{7,3},{8,12},{12,8},{9,1... | collective-permute-start | bytes 884744 | tf_op jit(solution)/shard_map/ppermute | solution.py:26
  162.9 23.4 %collective-permute-start.22 = (bf16[512,768]{1,0:T(8,128)(2,1)S(1)}, bf16[512,768]{1,0:T(8,128)(2,1)S(1)}, u32[]{:S(2)}, u32[]{:S(2)}) collective-permute-start(bf16[512,768]{1,0:T(8,128)(2,1)S(1)} %copy-done.6), channel_id=1, source_target_pairs={{0,2},{2,0},{1,3},{3,1},{4,6},{6,4},{5,7},{7,5},{8,10},{10,8},{9,1... | collective-permute-start | bytes 2359304 | tf_op jit(solution)/shard_map/ppermute | solution.py:26
  163.7 23.5 %collective-permute-start.23 = (bf16[512,768]{1,0:T(8,128)(2,1)}, bf16[512,768]{1,0:T(8,128)(2,1)S(1)}, u32[]{:S(2)}, u32[]{:S(2)}) collective-permute-start(bf16[512,768]{1,0:T(8,128)(2,1)} %get-tuple-element.202.refs_0_), channel_id=1, source_target_pairs={{0,2},{2,0},{1,3},{3,1},{4,6},{6,4},{5,7},{7,5},{8,10},{10,8},{9,1... | collective-permute-start | bytes 2359304 | tf_op jit(solution)/shard_map/ppermute | solution.py:26
  177.0 10.2 %collective-permute-start.25 = (bf16[512,768]{1,0:T(8,128)(2,1)S(1)}, bf16[512,768]{1,0:T(8,128)(2,1)S(1)}, u32[]{:S(2)}, u32[]{:S(2)}) collective-permute-start(bf16[512,768]{1,0:T(8,128)(2,1)S(1)} %collective-permute-done.24.refs_2_), channel_id=1, source_target_pairs={{0,2},{2,0},{1,3},{3,1},{4,6},{6,4},{5,7},{7,5},{8,10},{10,8},{9,1... | collective-permute-start | bytes 2359304 | tf_op jit(solution)/shard_map/ppermute | solution.py:26
  187.3 25.8 %collective-permute-start.26 = (bf16[384,1664]{1,0:T(8,128)(2,1)S(1)}, bf16[384,1664]{1,0:T(8,128)(2,1)}, u32[]{:S(2)}, u32[]{:S(2)}) collective-permute-start(bf16[384,1664]{1,0:T(8,128)(2,1)S(1)} %copy-done.92), channel_id=1, source_target_pairs={{0,1},{1,0},{2,6},{3,7},{4,5},{5,4},{6,2},{7,3},{8,9},{9,8},{10,14... | collective-permute-start | bytes 3833864 | tf_op jit(solution)/shard_map/ppermute | solution.py:971
  187.6 29.9 %collective-permute-start.28 = (bf16[384,1664]{1,0:T(8,128)(2,1)S(1)}, bf16[384,1664]{1,0:T(8,128)(2,1)S(1)}, u32[]{:S(2)}, u32[]{:S(2)}) collective-permute-start(bf16[384,1664]{1,0:T(8,128)(2,1)S(1)} %copy-done.92), channel_id=1, source_target_pairs={{0,2},{2,0},{1,3},{3,1},{4,6},{6,4},{5,7},{7,5},{8,10},{10,8},{9,1... | collective-permute-start | bytes 3833864 | tf_op jit(solution)/shard_map/ppermute | solution.py:26
  187.8 29.7 %collective-permute-start.27 = (bf16[384,1664]{1,0:T(8,128)(2,1)}, bf16[384,1664]{1,0:T(8,128)(2,1)}, u32[]{:S(2)}, u32[]{:S(2)}) collective-permute-start(bf16[384,1664]{1,0:T(8,128)(2,1)} %copy-done.93), channel_id=1, source_target_pairs={{0,1},{1,0},{2,6},{3,7},{4,5},{5,4},{6,2},{7,3},{8,9},{9,8},{10,14... | collective-permute-start | bytes 3833864 | tf_op jit(solution)/shard_map/ppermute | solution.py:971
  188.8 28.7 %collective-permute-start.29 = (bf16[384,1664]{1,0:T(8,128)(2,1)}, bf16[384,1664]{1,0:T(8,128)(2,1)S(1)}, u32[]{:S(2)}, u32[]{:S(2)}) collective-permute-start(bf16[384,1664]{1,0:T(8,128)(2,1)} %copy-done.93), channel_id=1, source_target_pairs={{0,2},{2,0},{1,3},{3,1},{4,6},{6,4},{5,7},{7,5},{8,10},{10,8},{9,1... | collective-permute-start | bytes 3833864 | tf_op jit(solution)/shard_map/ppermute | solution.py:26
  219.2 10.6 %collective-permute-start.32 = (bf16[192,512]{1,0:T(8,128)(2,1)S(1)}, bf16[192,512]{1,0:T(8,128)(2,1)S(1)}, u32[]{:S(2)}, u32[]{:S(2)}) collective-permute-start(bf16[192,512]{1,0:T(8,128)(2,1)S(1)} %get-tuple-element.367), channel_id=1, source_target_pairs={{0,6},{2,4},{4,2},{6,0},{1,7},{3,5},{5,3},{7,1},{8,14},{10,12},{12... | collective-permute-start | bytes 589832 | tf_op jit(solution)/shard_map/ppermute | solution.py:979
  229.8 12.0 %collective-permute-start.34 = (bf16[384,1664]{1,0:T(8,128)(2,1)}, bf16[384,1664]{1,0:T(8,128)(2,1)}, u32[]{:S(2)}, u32[]{:S(2)}) collective-permute-start(bf16[384,1664]{1,0:T(8,128)(2,1)} %collective-permute-done.27.refs_3_), channel_id=1, source_target_pairs={{0,2},{2,0},{1,3},{3,1},{4,6},{6,4},{5,7},{7,5},{8,10},{10,8},{9,1... | collective-permute-start | bytes 3833864 | tf_op jit(solution)/shard_map/ppermute | solution.py:26
  230.0 11.8 %collective-permute-start.33 = (bf16[384,1664]{1,0:T(8,128)(2,1)}, bf16[384,1664]{1,0:T(8,128)(2,1)}, u32[]{:S(2)}, u32[]{:S(2)}) collective-permute-start(bf16[384,1664]{1,0:T(8,128)(2,1)} %collective-permute-done.26.refs_2_), channel_id=1, source_target_pairs={{0,2},{2,0},{1,3},{3,1},{4,6},{6,4},{5,7},{7,5},{8,10},{10,8},{9,1... | collective-permute-start | bytes 3833864 | tf_op jit(solution)/shard_map/ppermute | solution.py:26
  264.8 15.2 %collective-permute-start.38 = (bf16[2,512,768]{2,1,0:T(8,128)(2,1)}, bf16[2,512,768]{2,1,0:T(8,128)(2,1)S(1)}, u32[]{:S(2)}, u32[]{:S(2)}) collective-permute-start(bf16[2,512,768]{2,1,0:T(8,128)(2,1)} %get-tuple-element.230), channel_id=1, source_target_pairs={{0,2},{2,0},{1,3},{3,1},{4,6},{6,4},{5,7},{7,5},{8,10},{10,8},{9,1... | collective-permute-start | bytes 4718600 | tf_op jit(solution)/shard_map/ppermute | solution.py:26
  265.1 15.0 %collective-permute-start.39 = (bf16[2,768,512]{2,1,0:T(8,128)(2,1)}, bf16[2,768,512]{2,1,0:T(8,128)(2,1)S(1)}, u32[]{:S(2)}, u32[]{:S(2)}) collective-permute-start(bf16[2,768,512]{2,1,0:T(8,128)(2,1)} %get-tuple-element.238), channel_id=1, source_target_pairs={{0,2},{2,0},{1,3},{3,1},{4,6},{6,4},{5,7},{7,5},{8,10},{10,8},{9,1... | collective-permute-start | bytes 4718600 | tf_op jit(solution)/shard_map/ppermute | solution.py:26
  271.3 8.7 %collective-permute-start.41 = (bf16[512,768]{1,0:T(8,128)(2,1)S(1)}, bf16[512,768]{1,0:T(8,128)(2,1)S(1)}, u32[]{:S(2)}, u32[]{:S(2)}) collective-permute-start(bf16[512,768]{1,0:T(8,128)(2,1)S(1)} %copy-done.2), channel_id=1, source_target_pairs={{0,2},{2,0},{1,3},{3,1},{4,6},{6,4},{5,7},{7,5},{8,10},{10,8},{9,1... | collective-permute-start | bytes 2359304 | tf_op jit(solution)/shard_map/ppermute | solution.py:26
  272.1 8.0 %collective-permute-start.40 = (bf16[512,768]{1,0:T(8,128)(2,1)S(1)}, bf16[512,768]{1,0:T(8,128)(2,1)S(1)}, u32[]{:S(2)}, u32[]{:S(2)}) collective-permute-start(bf16[512,768]{1,0:T(8,128)(2,1)S(1)} %copy-done.10), channel_id=1, source_target_pairs={{0,2},{2,0},{1,3},{3,1},{4,6},{6,4},{5,7},{7,5},{8,10},{10,8},{9,1... | collective-permute-start | bytes 2359304 | tf_op jit(solution)/shard_map/ppermute | solution.py:26
  279.8 8.6 %collective-permute-start.43 = (bf16[4,48,768]{2,1,0:T(8,128)(2,1)S(1)}, bf16[4,48,768]{2,1,0:T(8,128)(2,1)S(1)}, u32[]{:S(2)}, u32[]{:S(2)}) collective-permute-start(bf16[4,48,768]{2,1,0:T(8,128)(2,1)S(1)} %fusion.4), channel_id=1, source_target_pairs={{0,4},{4,0},{1,5},{5,1},{2,6},{6,2},{3,7},{7,3},{8,12},{12,8},{9,1... | collective-permute-start | bytes 884744 | tf_op jit(solution)/shard_map/ppermute | solution.py:26
  289.1 33.8 %collective-permute-start.44 = (bf16[768,1664]{1,0:T(8,128)(2,1)}, bf16[768,1664]{1,0:T(8,128)(2,1)}, u32[]{:S(2)}, u32[]{:S(2)}) collective-permute-start(bf16[768,1664]{1,0:T(8,128)(2,1)} %feed_weights.4), channel_id=1, source_target_pairs={{0,1},{1,0},{2,6},{3,7},{4,5},{5,4},{6,2},{7,3},{8,9},{9,8},{10,14... | collective-permute-start | bytes 7667720 | tf_op jit(solution)/shard_map/ppermute | solution.py:971
  330.0 19.2 %collective-permute-start.46 = (bf16[512,768]{1,0:T(8,128)(2,1)S(1)}, bf16[512,768]{1,0:T(8,128)(2,1)S(1)}, u32[]{:S(2)}, u32[]{:S(2)}) collective-permute-start(bf16[512,768]{1,0:T(8,128)(2,1)S(1)} %fusion.1), channel_id=1, source_target_pairs={{0,4},{4,0},{1,5},{5,1},{2,6},{6,2},{3,7},{7,3},{8,12},{12,8},{9,1... | collective-permute-start | bytes 2359304 | tf_op jit(solution)/shard_map/ppermute | solution.py:26
  331.6 9.9 %collective-permute-start.47 = (bf16[256,768]{1,0:T(8,128)(2,1)S(1)}, bf16[256,768]{1,0:T(8,128)(2,1)S(1)}, u32[]{:S(2)}, u32[]{:S(2)}) collective-permute-start(bf16[256,768]{1,0:T(8,128)(2,1)S(1)} %get-tuple-element.362), channel_id=1, source_target_pairs={{0,1},{1,0},{2,3},{3,2},{4,5},{5,4},{6,7},{7,6},{8,9},{9,8},{10,11... | collective-permute-start | bytes 1179656 | tf_op jit(solution)/shard_map/ppermute | solution.py:26
  350.1 16.7 %collective-permute-start.48 = (bf16[384,1664]{1,0:T(8,128)(2,1)}, bf16[384,1664]{1,0:T(8,128)(2,1)}, u32[]{:S(2)}, u32[]{:S(2)}) collective-permute-start(bf16[384,1664]{1,0:T(8,128)(2,1)} %add_convert_fusion.3), channel_id=1, source_target_pairs={{0,4},{1,5},{2,3},{3,2},{4,0},{5,1},{6,7},{7,6},{8,12},{9,13},{10,... | collective-permute-start | bytes 3833864 | tf_op jit(solution)/shard_map/ppermute | solution.py:971
  363.6 91.7 %reduce-scatter.6.cloned.1.call-start = ((), (), s32[]{:S(2)}) async-start(), calls=%async_computation.8 | async-start | bytes 1597440 | tf_op jit(solution)/shard_map/reduce_scatter | solution.py:1253
  384.8 18.3 %collective-permute-start.52 = (bf16[2,512,768]{2,1,0:T(8,128)(2,1)}, bf16[2,512,768]{2,1,0:T(8,128)(2,1)}, u32[]{:S(2)}, u32[]{:S(2)}) collective-permute-start(bf16[2,512,768]{2,1,0:T(8,128)(2,1)} %get-tuple-element.274), channel_id=1, source_target_pairs={{0,2},{2,0},{1,3},{3,1},{4,6},{6,4},{5,7},{7,5},{8,10},{10,8},{9,1... | collective-permute-start | bytes 4718600 | tf_op jit(solution)/shard_map/ppermute | solution.py:26
  386.5 16.6 %collective-permute-start.53 = (bf16[512,768]{1,0:T(8,128)(2,1)}, bf16[512,768]{1,0:T(8,128)(2,1)}, u32[]{:S(2)}, u32[]{:S(2)}) collective-permute-start(bf16[512,768]{1,0:T(8,128)(2,1)} %get-tuple-element.267.dm_ref.dm), channel_id=1, source_target_pairs={{0,2},{2,0},{1,3},{3,1},{4,6},{6,4},{5,7},{7,5},{8,10},{10,8},{9,1... | collective-permute-start | bytes 2359304 | tf_op jit(solution)/shard_map/ppermute | solution.py:26
  386.6 11.7 %collective-permute-start.49 = (bf16[192,512]{1,0:T(8,128)(2,1)}, bf16[192,512]{1,0:T(8,128)(2,1)}, u32[]{:S(2)}, u32[]{:S(2)}) collective-permute-start(bf16[192,512]{1,0:T(8,128)(2,1)} %get-tuple-element.271), channel_id=1, source_target_pairs={{0,2},{2,0},{1,3},{3,1},{4,6},{6,4},{5,7},{7,5},{8,10},{10,8},{9,1... | collective-permute-start | bytes 589832 | tf_op jit(solution)/shard_map/ppermute | solution.py:26
  387.0 12.1 %collective-permute-start.50 = (bf16[192,512]{1,0:T(8,128)(2,1)}, bf16[192,512]{1,0:T(8,128)(2,1)}, u32[]{:S(2)}, u32[]{:S(2)}) collective-permute-start(bf16[192,512]{1,0:T(8,128)(2,1)} %get-tuple-element.272), channel_id=1, source_target_pairs={{0,4},{4,0},{1,5},{5,1},{2,6},{6,2},{3,7},{7,3},{8,12},{12,8},{9,1... | collective-permute-start | bytes 589832 | tf_op jit(solution)/shard_map/ppermute | solution.py:26
  395.4 130.4 %reduce-scatter.8.cloned.1.call-start = ((), (), s32[]{:S(2)}) async-start(), calls=%async_computation.9 | async-start | bytes 1720320 | tf_op jit(solution)/shard_map/reduce_scatter | solution.py:1220
  395.5 7.6 %collective-permute-start.51 = (bf16[192,512]{1,0:T(8,128)(2,1)}, bf16[192,512]{1,0:T(8,128)(2,1)}, u32[]{:S(2)}, u32[]{:S(2)}) collective-permute-start(bf16[192,512]{1,0:T(8,128)(2,1)} %get-tuple-element.273), channel_id=1, source_target_pairs={{0,6},{2,4},{4,2},{6,0},{1,7},{3,5},{5,3},{7,1},{8,14},{10,12},{12... | collective-permute-start | bytes 589832 | tf_op jit(solution)/shard_map/ppermute | solution.py:979
  398.4 17.1 %collective-permute-start.55 = (bf16[4,48,768]{2,1,0:T(8,128)(2,1)}, bf16[4,48,768]{2,1,0:T(8,128)(2,1)}, u32[]{:S(2)}, u32[]{:S(2)}) collective-permute-start(bf16[4,48,768]{2,1,0:T(8,128)(2,1)} %fusion.3), channel_id=1, source_target_pairs={{0,4},{4,0},{1,5},{5,1},{2,6},{6,2},{3,7},{7,3},{8,12},{12,8},{9,1... | collective-permute-start | bytes 884744 | tf_op jit(solution)/shard_map/ppermute | solution.py:26
  403.1 12.2 %collective-permute-start.56 = (bf16[192,896]{1,0:T(8,128)(2,1)}, bf16[192,896]{1,0:T(8,128)(2,1)S(1)}, u32[]{:S(2)}, u32[]{:S(2)}) collective-permute-start(bf16[192,896]{1,0:T(8,128)(2,1)} %reduce-scatter.4.cloned.1.call-done), channel_id=1, source_target_pairs={{0,1},{1,0},{2,3},{3,2},{4,5},{5,4},{6,7},{7,6},{8,9},{9,8},{10,11... | collective-permute-start | bytes 1032200 | tf_op jit(solution)/shard_map/ppermute | solution.py:26
  415.4 39.9 %collective-permute-start.57 = (bf16[768,1664]{1,0:T(8,128)(2,1)}, bf16[768,1664]{1,0:T(8,128)(2,1)}, u32[]{:S(2)}, u32[]{:S(2)}) collective-permute-start(bf16[768,1664]{1,0:T(8,128)(2,1)} %feed_weights.7), channel_id=1, source_target_pairs={{0,1},{1,0},{2,6},{3,7},{4,5},{5,4},{6,2},{7,3},{8,9},{9,8},{10,14... | collective-permute-start | bytes 7667720 | tf_op jit(solution)/shard_map/ppermute | solution.py:971
  455.3 17.4 %collective-permute-start.59 = (bf16[192,896]{1,0:T(8,128)(2,1)S(1)}, bf16[192,896]{1,0:T(8,128)(2,1)S(1)}, u32[]{:S(2)}, u32[]{:S(2)}) collective-permute-start(bf16[192,896]{1,0:T(8,128)(2,1)S(1)} %add_convert_fusion.5.refs_0_), channel_id=1, source_target_pairs={{0,4},{4,0},{1,5},{5,1},{2,6},{6,2},{3,7},{7,3},{8,12},{12,8},{9,1... | collective-permute-start | bytes 1032200 | tf_op jit(solution)/shard_map/ppermute | solution.py:26
  456.1 14.4 %collective-permute-start.61 = (bf16[96,1664]{1,0:T(8,128)(2,1)}, bf16[96,1664]{1,0:T(8,128)(2,1)}, u32[]{:S(2)}, u32[]{:S(2)}) collective-permute-start(bf16[96,1664]{1,0:T(8,128)(2,1)} %reduce-scatter.6.cloned.1.call-done.refs_4_), channel_id=1, source_target_pairs={{0,4},{4,0},{1,5},{5,1},{2,6},{6,2},{3,7},{7,3},{8,12},{12,8},{9,1... | collective-permute-start | bytes 958472 | tf_op jit(solution)/shard_map/ppermute | solution.py:26
  459.1 18.5 %collective-permute-start.65 = (bf16[2,512,768]{2,1,0:T(8,128)(2,1)}, bf16[2,512,768]{2,1,0:T(8,128)(2,1)S(1)}, u32[]{:S(2)}, u32[]{:S(2)}) collective-permute-start(bf16[2,512,768]{2,1,0:T(8,128)(2,1)} %get-tuple-element.309), channel_id=1, source_target_pairs={{0,2},{2,0},{1,3},{3,1},{4,6},{6,4},{5,7},{7,5},{8,10},{10,8},{9,1... | collective-permute-start | bytes 4718600 | tf_op jit(solution)/shard_map/ppermute | solution.py:26
  468.6 7.4 %collective-permute-start.58 = (bf16[192,896]{1,0:T(8,128)(2,1)S(1)}, bf16[192,896]{1,0:T(8,128)(2,1)S(1)}, u32[]{:S(2)}, u32[]{:S(2)}) collective-permute-start(bf16[192,896]{1,0:T(8,128)(2,1)S(1)} %add_convert_fusion.5.refs_0_), channel_id=1, source_target_pairs={{0,2},{2,0},{1,3},{3,1},{4,6},{6,4},{5,7},{7,5},{8,10},{10,8},{9,1... | collective-permute-start | bytes 1032200 | tf_op jit(solution)/shard_map/ppermute | solution.py:26
  477.6 16.7 %collective-permute-start.64 = (bf16[384,1664]{1,0:T(8,128)(2,1)}, bf16[384,1664]{1,0:T(8,128)(2,1)}, u32[]{:S(2)}, u32[]{:S(2)}) collective-permute-start(bf16[384,1664]{1,0:T(8,128)(2,1)} %add_convert_fusion.1), channel_id=1, source_target_pairs={{0,4},{1,5},{2,3},{3,2},{4,0},{5,1},{6,7},{7,6},{8,12},{9,13},{10,... | collective-permute-start | bytes 3833864 | tf_op jit(solution)/shard_map/ppermute | solution.py:971
  494.3 17.8 %collective-permute-start.66 = (bf16[512,768]{1,0:T(8,128)(2,1)S(1)}, bf16[512,768]{1,0:T(8,128)(2,1)S(1)}, u32[]{:S(2)}, u32[]{:S(2)}) collective-permute-start(bf16[512,768]{1,0:T(8,128)(2,1)S(1)} %fusion), channel_id=1, source_target_pairs={{0,4},{4,0},{1,5},{5,1},{2,6},{6,2},{3,7},{7,3},{8,12},{12,8},{9,1... | collective-permute-start | bytes 2359304 | tf_op jit(solution)/shard_map/ppermute | solution.py:26
  499.4 18.0 %collective-permute-start.72 = (bf16[96,1664]{1,0:T(8,128)(2,1)}, bf16[96,1664]{1,0:T(8,128)(2,1)}, u32[]{:S(2)}, u32[]{:S(2)}) collective-permute-start(bf16[96,1664]{1,0:T(8,128)(2,1)} %get-tuple-element.342), channel_id=1, source_target_pairs={{0,8},{8,16},{16,24},{24,0},{1,9},{9,17},{17,25},{25,1},{2,10},{10... | collective-permute-start | bytes 958472 | tf_op jit(solution)/shard_map/ppermute | solution.py:1069
  499.4 26.5 %collective-permute-start.73 = (bf16[96,1664]{1,0:T(8,128)(2,1)}, bf16[96,1664]{1,0:T(8,128)(2,1)}, u32[]{:S(2)}, u32[]{:S(2)}) collective-permute-start(bf16[96,1664]{1,0:T(8,128)(2,1)} %get-tuple-element.341), channel_id=1, source_target_pairs={{0,16},{8,24},{16,0},{24,8},{1,17},{9,25},{17,1},{25,9},{2,18},{10... | collective-permute-start | bytes 958472 | tf_op jit(solution)/shard_map/ppermute | solution.py:1069
  499.4 26.5 %collective-permute-start.74 = (bf16[96,1664]{1,0:T(8,128)(2,1)}, bf16[96,1664]{1,0:T(8,128)(2,1)}, u32[]{:S(2)}, u32[]{:S(2)}) collective-permute-start(bf16[96,1664]{1,0:T(8,128)(2,1)} %get-tuple-element.340), channel_id=1, source_target_pairs={{0,24},{8,0},{16,8},{24,16},{1,25},{9,1},{17,9},{25,17},{2,26},{10... | collective-permute-start | bytes 958472 | tf_op jit(solution)/shard_map/ppermute | solution.py:1069
  525.9 8.7 %collective-permute-start.68 = (bf16[192,896]{1,0:T(8,128)(2,1)}, bf16[192,896]{1,0:T(8,128)(2,1)S(1)}, u32[]{:S(2)}, u32[]{:S(2)}) collective-permute-start(bf16[192,896]{1,0:T(8,128)(2,1)} %reduce-scatter.8.cloned.1.call-done), channel_id=1, source_target_pairs={{0,1},{1,0},{2,3},{3,2},{4,5},{5,4},{6,7},{7,6},{8,9},{9,8},{10,11... | collective-permute-start | bytes 1032200 | tf_op jit(solution)/shard_map/ppermute | solution.py:26
  528.8 17.5 %collective-permute-start.75 = (bf16[96,1664]{1,0:T(8,128)(2,1)S(1)}, bf16[96,1664]{1,0:T(8,128)(2,1)}, u32[]{:S(2)}, u32[]{:S(2)}) collective-permute-start(bf16[96,1664]{1,0:T(8,128)(2,1)S(1)} %add_convert_fusion.6.refs_4_), channel_id=1, source_target_pairs={{0,4},{4,0},{1,5},{5,1},{2,6},{6,2},{3,7},{7,3},{8,12},{12,8},{9,1... | collective-permute-start | bytes 958472 | tf_op jit(solution)/shard_map/ppermute | solution.py:26
  534.7 9.7 %collective-permute-start.70 = (bf16[192,896]{1,0:T(8,128)(2,1)S(1)}, bf16[192,896]{1,0:T(8,128)(2,1)}, u32[]{:S(2)}, u32[]{:S(2)}) collective-permute-start(bf16[192,896]{1,0:T(8,128)(2,1)S(1)} %add_convert_fusion.4.refs_0_), channel_id=1, source_target_pairs={{0,4},{4,0},{1,5},{5,1},{2,6},{6,2},{3,7},{7,3},{8,12},{12,8},{9,1... | collective-permute-start | bytes 1032200 | tf_op jit(solution)/shard_map/ppermute | solution.py:26
  535.8 12.1 %collective-permute-start.67 = (bf16[256,768]{1,0:T(8,128)(2,1)S(1)}, bf16[256,768]{1,0:T(8,128)(2,1)S(1)}, u32[]{:S(2)}, u32[]{:S(2)}) collective-permute-start(bf16[256,768]{1,0:T(8,128)(2,1)S(1)} %get-tuple-element.360), channel_id=1, source_target_pairs={{0,1},{1,0},{2,3},{3,2},{4,5},{5,4},{6,7},{7,6},{8,9},{9,8},{10,11... | collective-permute-start | bytes 1179656 | tf_op jit(solution)/shard_map/ppermute | solution.py:26
  538.0 11.1 %collective-permute-start.69 = (bf16[192,896]{1,0:T(8,128)(2,1)S(1)}, bf16[192,896]{1,0:T(8,128)(2,1)S(1)}, u32[]{:S(2)}, u32[]{:S(2)}) collective-permute-start(bf16[192,896]{1,0:T(8,128)(2,1)S(1)} %add_convert_fusion.4.refs_0_), channel_id=1, source_target_pairs={{0,2},{2,0},{1,3},{3,1},{4,6},{6,4},{5,7},{7,5},{8,10},{10,8},{9,1... | collective-permute-start | bytes 1032200 | tf_op jit(solution)/shard_map/ppermute | solution.py:26
  (121 other events, 1167.4 us)
Sparse Core Ops, SparseCore 0:
  15.0 31.7 all-gather.4
  54.7 33.6 all-gather.6
  93.2 30.4 all-gather.10
  125.9 28.8 all-gather.8
  363.7 29.0 reduce-scatter.3
  395.6 29.0 reduce-scatter.5
  468.7 27.4 reduce-scatter.7

commit v6 on v5

--- a/solution.py
+++ b/solution.py
@@ -516,7 +516,7 @@
         sums_ref[...] = jnp.zeros_like(sums_ref)
 
     def rows_of(at, sums):
-        rows = pl.ds(pl.multiple_of(at * 64, 64), 64)
+        rows = pl.ds(pl.multiple_of(at * 128, 128), 128)
         found = own[rows, :] + core[0, rows, :].astype(F32) + far[rows, :].astype(F32)
         grad_in, gain_sum, bias_sum = norm_back(found, x_ref[rows, :], gain_ref[...])
         grad = mid_ref[rows, :] + grad_in
@@ -525,7 +525,7 @@
         return sums[0] + gain_sum, sums[1] + bias_sum
 
     zero = jnp.zeros((1, width), F32)
-    sums = lax.fori_loop(0, toks // 64, rows_of, (zero, zero))
+    sums = lax.fori_loop(0, toks // 128, rows_of, (zero, zero))
     sums_ref[0:1, :] += sums[0]
     sums_ref[1:2, :] += sums[1]
 
@@ -606,11 +606,11 @@
         pre = later
 
     def rows_of(at, nothing):
-        rows = pl.ds(pl.multiple_of(at * 64, 64), 64)
+        rows = pl.ds(pl.multiple_of(at * 128, 128), 128)
         a_ref[rows, :] = norm_rows(x_ref[rows, :], vec_ref[1:2, :], vec_ref[2:3, :]).astype(BF16)
         return nothing
 
-    lax.fori_loop(0, toks // 64, rows_of, 0)
+    lax.fori_loop(0, toks // 128, rows_of, 0)
     for copy in outs:
         copy.wait()
 
@@ -648,7 +648,7 @@
     loc = targets[0].shape[0]
 
     def rows_of(at, sums):
-        rows = pl.ds(pl.multiple_of(at * 64, 64), 64)
+        rows = pl.ds(pl.multiple_of(at * 128, 128), 128)
         grad_in, gain_sum, bias_sum = norm_back(dc[rows, :], mid_ref[rows, :], gain_ref[...])
         grad_mid = grad_ref[rows, :].astype(F32) + grad_in
         dmid_ref[rows, :] = grad_mid
@@ -659,7 +659,7 @@
         return sums[0] + gain_sum, sums[1] + bias_sum, sums[2] + out_sum, sums[3] + down_sum
 
     zero = jnp.zeros((1, width), F32)
-    sums = lax.fori_loop(0, toks // 64, rows_of, (zero,) * 4)
+    sums = lax.fori_loop(0, toks // 128, rows_of, (zero,) * 4)
     sums_ref[...] = jnp.zeros_like(sums_ref)
     for at in range(4):
         sums_ref[at : at + 1, :] = sums[at]

time: 575 us -> 571 us (level); the launches traced: 563 us -> 565 us
  Pallas kernels: 238 us -> 208 us
  starting transfers between devices: 61.1 us -> 80 us
  waiting for transfers between devices: 157 us -> 171 us
    pallas_call x2, Pallas kernels: 70.2 us -> 54.2 us  [attention_backward(): pl.pallas_call(partial(attention_backward_kernel, norm), name='attention_...]
    ppermute x3, starting transfers between devices: 1.47 us -> 15 us  [send_shards(): lax.ppermute(lax.dynamic_slice_in_dim(value, (index + by) % shards * coun...]
    pallas_call x2, Pallas kernels: 46.7 us -> 35.1 us  [attention_forward(): pl.pallas_call(partial(attention_forward_kernel, norm), name='attention_f...]
    ppermute x10, starting transfers between devices: 6.07 us -> 14.5 us  [turned(): return lax.ppermute(value, PLANE, pairs)]
    ppermute x10, waiting for transfers between devices: 43.8 us -> 50.1 us  [turned(): return lax.ppermute(value, PLANE, pairs)]
  transfers between devices with their start and end apart: 85 -> 85, of which waited for: 31 -> 34; matrix products, arithmetic and copies ran while one was open for 11% -> 11% of each run, Pallas kernels for 37% -> 32%
where the time goes in v6:
time: 571 us; the launch traced here: 565 us
  Pallas kernels  208 us (36%)
  waiting for transfers between devices  171 us (30%)
  starting transfers between devices  80 us (14%)
  local copies, waits for them, and re-layouts  54.5 us (10%)
  other arithmetic  30.5 us (5%)
  between operations  17.8 us (3%)
    ppermute x61, waiting for transfers between devices, swap(): return lax.ppermute(value, axis, ((0, 1), (1, 0)))  86.5 us
    pallas_call x2, Pallas kernels, attention_backward(): pl.pallas_call(partial(attention_backward_kernel, norm), name='attention_...  54.2 us
    ppermute x10, waiting for transfers between devices, turned(): return lax.ppermute(value, PLANE, pairs)  50.1 us
    ppermute x61, starting transfers between devices, swap(): return lax.ppermute(value, axis, ((0, 1), (1, 0)))  45.1 us
    pallas_call x2, Pallas kernels, attention_forward(): pl.pallas_call(partial(attention_forward_kernel, norm), name='attention_f...  35.1 us
    pallas_call x4, Pallas kernels, feed_weights(): pl.pallas_call(feed_weights_kernel, name='feed_weights', grid=(units // s...  23.5 us
    unnamed x201, local copies, waits for them, and re-layouts  23.3 us
    pallas_call x1, Pallas kernels, feed_both(): pl.pallas_call(feed_both_kernel, name='feed_both', grid_spec=pltpu.Prefet...  22.2 us
  transfers between devices with their start and end apart: 85, of which 34 were waited for; matrix products, arithmetic and copies ran while one was open for 11% of the time, Pallas kernels for 32%

profile of v6, /device:TPU:9, one launch (start us, length us, event | category | flops | bytes accessed | tf_op | source)
XLA Modules:
  0.0 565.2 jit_solution(13725344199247735197)
XLA Ops:
  7.2 2.3 dynamic-slice_bitcast_fusion
  17.6 11.6 %collective-permute-done.2 = bf16[2,256,768]{2,1,0:T(8,128)(2,1)} collective-permute-done((bf16[2,256,768]{2,1,0:T(8,128)(2,1)}, bf16[2,256,768]{2,1,0:T(8,128)(2,1)}, u32[]{:S(2)}, u32[]{:S(2)}) %collective-permute-start.2) | collective-permute-done | bytes 786464 | tf_op jit(solution)/shard_map/ppermute | solution.py:26
  29.3 1.9 slice_bitcast_fusion.3
  33.7 1.8 collective-permute-start.3
  35.6 14.4 %collective-permute-done.4.refs_2_ = bf16[512,768]{1,0:T(8,128)(2,1)S(1)} collective-permute-done((bf16[512,768]{1,0:T(8,128)(2,1)S(1)}, bf16[512,768]{1,0:T(8,128)(2,1)S(1)}, u32[]{:S(2)}, u32[]{:S(2)}) %collective-permute-start.4) | collective-permute-done | bytes 786464 | tf_op jit(solution)/shard_map/ppermute | solution.py:26
  50.0 2.5 collective-permute-start.5
  52.5 2.0 collective-permute-done.5.refs_3_
  65.5 17.2 %collective-permute-done.refs_1_ = bf16[384,1664]{1,0:T(8,128)(2,1)} collective-permute-done((bf16[384,1664]{1,0:T(8,128)(2,1)}, bf16[384,1664]{1,0:T(8,128)(2,1)}, u32[]{:S(2)}, u32[]{:S(2)}) %collective-permute-start) | collective-permute-done | bytes 1277984 | tf_op jit(solution)/shard_map/ppermute | solution.py:971
  82.7 3.2 collective-permute-done.1.refs_2_
  97.3 18.2 %attention_forward.2 = (bf16[768,2048]{1,0:T(8,128)(2,1)}, bf16[2048,576]{1,0:T(8,128)(2,1)}, bf16[4,192,512]{2,1,0:T(8,128)(2,1)S(1)}, f32[8,2048]{1,0:T(8,128)S(1)}, bf16[4,512,768]{2,1,0:T(8,128)(2,1)}) custom-call(s32[8]{0:T(128)S(1)} %stack.76.info, bf16[512,768]{1,0:T(8,128)(2,1)S(1)} %get-tuple-element.178.refs_0_, bf16[512,768]{1,0:T(8,128)(2,1)S(1)} %copy-done.34, ...), custom_call_target="tpu_custom_call" | custom-call | flops 14000000000 | bytes 12582912 | tf_op jit(solution)/shard_map/attention_forward/pallas_call | solution.py:189
  120.7 3.6 collective-permute-done.14.p2
  124.2 4.6 collective-permute-done.15.p3
  128.9 4.4 out_forward.2
  136.2 3.4 collective-permute-start.17
  140.2 14.1 %feed_forward.1 = (bf16[4,512,768]{2,1,0:T(8,128)(2,1)}, bf16[2,768,512]{2,1,0:T(8,128)(2,1)}, bf16[2,768,512]{2,1,0:T(8,128)(2,1)}, f32[512,768]{1,0:T(8,128)}, bf16[512,768]{1,0:T(8,128)(2,1)}) custom-call(bf16[512,768]{1,0:T(8,128)(2,1)} %copy-done.5, f32[512,768]{1,0:T(8,128)} %copy-done.36, f32[3,768]{1,0:T(4,128)} %pad_maximum_fusion.7.vec_ref, ...), custom_call_target="tpu_custom_call" | custom-call | flops 5000000000 | bytes 20971520 | tf_op jit(solution)/shard_map/feed_forward/pallas_call | solution.py:621
  159.2 15.3 %collective-permute-done.24.refs_2_ = bf16[512,768]{1,0:T(8,128)(2,1)S(1)} collective-permute-done((bf16[512,768]{1,0:T(8,128)(2,1)}, bf16[512,768]{1,0:T(8,128)(2,1)S(1)}, u32[]{:S(2)}, u32[]{:S(2)}) %collective-permute-start.24) | collective-permute-done | bytes 786464 | tf_op jit(solution)/shard_map/ppermute | solution.py:26
  174.7 5.2 collective-permute-done.19
  182.8 2.9 collective-permute-start.28
  185.9 17.0 %attention_forward.3 = (bf16[768,2048]{1,0:T(8,128)(2,1)}, bf16[2048,576]{1,0:T(8,128)(2,1)}, bf16[4,192,512]{2,1,0:T(8,128)(2,1)S(1)}, f32[8,2048]{1,0:T(8,128)S(1)}) custom-call(s32[8]{0:T(128)S(1)} %stack.76.info, bf16[512,768]{1,0:T(8,128)(2,1)S(1)} %copy-done.35, bf16[512,768]{1,0:T(8,128)(2,1)S(1)} %collective-permute-done.23.refs_1_, ...), custom_call_target="tpu_custom_call" | custom-call | flops 14000000000 | bytes 12582912 | tf_op jit(solution)/shard_map/attention_forward/pallas_call | solution.py:189
  203.5 9.2 %collective-permute-done.27.refs_3_ = bf16[384,1664]{1,0:T(8,128)(2,1)} collective-permute-done((bf16[384,1664]{1,0:T(8,128)(2,1)}, bf16[384,1664]{1,0:T(8,128)(2,1)}, u32[]{:S(2)}, u32[]{:S(2)}) %collective-permute-start.27) | collective-permute-done | bytes 1277984 | tf_op jit(solution)/shard_map/ppermute | solution.py:971
  212.8 2.0 collective-permute-start.30
  216.6 4.8 collective-permute-done.31.p2
  221.3 4.4 collective-permute-done.32.p3
  229.4 4.4 out_forward.3
  237.7 22.2 %feed_both.1 = (bf16[2,512,768]{2,1,0:T(8,128)(2,1)}, bf16[2,512,768]{2,1,0:T(8,128)(2,1)}, f32[512,768]{1,0:T(8,128)}, bf16[512,768]{1,0:T(8,128)(2,1)}, f32[8,...) custom-call(s32[8]{0:T(128)} %copy-done.31, ...), custom_call_target="tpu_custom_call" | custom-call | flops 10000000000 | bytes 25165824 | tf_op jit(solution)/shard_map/feed_both/pallas_call | solution.py:812
  260.9 1.9 convolution_convert_fusion.1
  263.6 2.9 collective-permute-done.35.g1
  268.5 6.4 %collective-permute-done.37.g3 = bf16[192,512]{1,0:T(8,128)(2,1)S(1)} collective-permute-done((bf16[192,512]{1,0:T(8,128)(2,1)S(1)}, bf16[192,512]{1,0:T(8,128)(2,1)S(1)}, u32[]{:S(2)}, u32[]{:S(2)}) %collective-permute-start.37) | collective-permute-done | bytes 196640 | tf_op jit(solution)/shard_map/ppermute | solution.py:979
  276.7 5.6 feed_weights.4
  284.4 25.5 %attention_backward.2 = (bf16[2048,576]{1,0:T(8,128)(2,1)}, bf16[2,512,768]{2,1,0:T(8,128)(2,1)}, f32[512,768]{1,0:T(8,128)}, f32[512,768]{1,0:T(8,128)}, f32[8,576]{1,0:T(8,128)}) custom-call(s32[8]{0:T(128)} %copy-done.31, bf16[2048,576]{1,0:T(8,128)(2,1)} %get-tuple-element.224.qkv_ref, bf16[4,192,512]{2,1,0:T(8,128)(2,1)} %copy-done.24, ...), custom_call_target="tpu_custom_call" | custom-call | flops 20000000000 | bytes 16777216 | tf_op jit(solution)/shard_map/attention_backward/pallas_call | solution.py:386
  310.0 4.6 collective-permute-done.44
  320.9 1.9 fusion.1
  325.7 5.6 feed_weights.5
  331.3 3.2 add_convert_fusion.3
  335.1 7.0 %collective-permute-done.46.far = bf16[512,768]{1,0:T(8,128)(2,1)S(1)} collective-permute-done((bf16[512,768]{1,0:T(8,128)(2,1)S(1)}, bf16[512,768]{1,0:T(8,128)(2,1)S(1)}, u32[]{:S(2)}, u32[]{:S(2)}) %collective-permute-start.46) | collective-permute-done | bytes 786464 | tf_op jit(solution)/shard_map/ppermute | solution.py:26
  346.0 4.8 norm_backward.2
  351.9 5.7 %attention_weights.2 = bf16[768,896]{1,0:T(8,128)(2,1)} custom-call(bf16[768,2048]{1,0:T(8,128)(2,1)} %get-tuple-element.260.at_ref, bf16[2048,576]{1,0:T(8,128)(2,1)S(1)} %copy-done.16, f32[16,768]{1,0:T(8,128)S(1)} %maximum_maximum_fusion.vec_ref, bf16[192,768]{1,0:T(8,128)(2,1)S(1)} %bitcast.156, bf16[192,768]{1,0:T(8,128)(2,1)S(1)} %bitcast.158, ...), custom_call_target="tpu_custom_call" | custom-call | flops 1800000000 | bytes 8388608 | tf_op jit(solution)/shard_map/attention_weights/pallas_call | solution.py:443
  357.7 2.2 collective-permute-done.48
  359.9 17.2 %feed_backward.1 = (bf16[2,512,768]{2,1,0:T(8,128)(2,1)}, bf16[2,512,768]{2,1,0:T(8,128)(2,1)}, f32[512,768]{1,0:T(8,128)}, bf16[512,768]{1,0:T(8,128)(2,1)}, f3...) custom-call(s32[8]{0:T(128)} %copy-done.31, ...), custom_call_target="tpu_custom_call" | custom-call | flops 6000000000 | bytes 25165824 | tf_op jit(solution)/shard_map/feed_backward/pallas_call | solution.py:727
  379.1 1.9 convolution_convert_fusion
  383.4 3.3 add_convert_fusion.2
  390.4 3.9 collective-permute-done.51.g3
  396.1 6.1 %feed_weights.7 = bf16[768,1664]{1,0:T(8,128)(2,1)} custom-call(bf16[2,512,768]{2,1,0:T(8,128)(2,1)S(1)} %copy-done.4, bf16[2,512,768]{2,1,0:T(8,128)(2,1)} %collective-permute-done.52.dh2, bf16[2,768,512]{2,1,0:T(8,128)(2,1)} %get-tuple-element.277.act, bf16[2,768,512]{2,1,0:T(8,128)(2,1)} %collective-permute-done.21.act2, bf16[512,768]{1,0:T(8,128)(2,1)S(1)} %copy-done.6, ...), custom_call_target="tpu_custom_call" | custom-call | flops 2400000000 | bytes 9437184 | tf_op jit(solution)/shard_map/feed_weights/pallas_call | solution.py:851
  402.2 6.2 %feed_weights.6 = bf16[768,1664]{1,0:T(8,128)(2,1)} custom-call(bf16[2,512,768]{2,1,0:T(8,128)(2,1)S(1)} %copy-done.4, bf16[2,512,768]{2,1,0:T(8,128)(2,1)} %collective-permute-done.52.dh2, bf16[2,768,512]{2,1,0:T(8,128)(2,1)} %get-tuple-element.277.act, bf16[2,768,512]{2,1,0:T(8,128)(2,1)} %collective-permute-done.21.act2, bf16[512,768]{1,0:T(8,128)(2,1)S(1)} %copy-done.6, ...), custom_call_target="tpu_custom_call" | custom-call | flops 2400000000 | bytes 9437184 | tf_op jit(solution)/shard_map/feed_weights/pallas_call | solution.py:851
  410.9 28.7 %attention_backward.3 = (bf16[2048,576]{1,0:T(8,128)(2,1)}, bf16[2,512,768]{2,1,0:T(8,128)(2,1)}, f32[512,768]{1,0:T(8,128)}, f32[512,768]{1,0:T(8,128)}, f32[8,576]{1,0:T(8,128)}, /*index=5*/f32[8,768]{1,0:T(8,128)}) custom-call(s32[8]{0:T(128)} %copy-done.31, bf16[2048,576]{1,0:T(8,128)(2,1)} %get-tuple-element.289.qkv_ref, ...), custom_call_target="tpu_custom_call" | custom-call | flops 20000000000 | bytes 16777216 | tf_op jit(solution)/shard_map/attention_backward/pallas_call | solution.py:386
  446.7 5.7 %attention_weights.3 = bf16[768,896]{1,0:T(8,128)(2,1)} custom-call(bf16[768,2048]{1,0:T(8,128)(2,1)} %get-tuple-element.288.at_ref, bf16[2048,576]{1,0:T(8,128)(2,1)S(1)} %copy-done.17, f32[16,768]{1,0:T(8,128)S(1)} %concatenate.91.vec_ref, bf16[192,768]{1,0:T(8,128)(2,1)S(1)} %bitcast.157, bf16[192,768]{1,0:T(8,128)(2,1)S(1)} %bitcast.159, ...), custom_call_target="tpu_custom_call" | custom-call | flops 1800000000 | bytes 8388608 | tf_op jit(solution)/shard_map/attention_weights/pallas_call | solution.py:443
  453.1 4.3 collective-permute-done.61.refs_5_
  457.9 3.0 add_convert_fusion.1
  462.6 3.6 collective-permute-start.64
  466.2 2.2 fusion
  468.4 13.0 %collective-permute-done.64 = bf16[384,1664]{1,0:T(8,128)(2,1)} collective-permute-done((bf16[384,1664]{1,0:T(8,128)(2,1)}, bf16[384,1664]{1,0:T(8,128)(2,1)}, u32[]{:S(2)}, u32[]{:S(2)}) %collective-permute-start.64) | collective-permute-done | bytes 1277984 | tf_op jit(solution)/shard_map/ppermute | solution.py:971
  481.6 2.2 add_convert_fusion
  485.8 12.5 %collective-permute-start.72 = (bf16[96,1664]{1,0:T(8,128)(2,1)}, bf16[96,1664]{1,0:T(8,128)(2,1)}, u32[]{:S(2)}, u32[]{:S(2)}) collective-permute-start(bf16[96,1664]{1,0:T(8,128)(2,1)} %get-tuple-element.342), channel_id=1, source_target_pairs={{0,8},{8,16},{16,24},{24,0},{1,9},{9,17},{17,25},{25,1},{2,10},{10... | collective-permute-start | bytes 958472 | tf_op jit(solution)/shard_map/ppermute | solution.py:1069
  498.2 2.6 collective-permute-start.73
  500.8 5.5 finish.2
  506.3 4.7 norm_backward.3
  511.1 8.3 %collective-permute-done.72 = bf16[96,1664]{1,0:T(8,128)(2,1)} collective-permute-done((bf16[96,1664]{1,0:T(8,128)(2,1)}, bf16[96,1664]{1,0:T(8,128)(2,1)}, u32[]{:S(2)}, u32[]{:S(2)}) %collective-permute-start.72) | collective-permute-done | bytes 319520 | tf_op jit(solution)/shard_map/ppermute | solution.py:1069
  519.4 3.7 collective-permute-done.73
  524.9 4.4 collective-permute-start.68
  531.5 5.1 collective-permute-done.68
  538.7 2.8 collective-permute-start.69
  541.5 4.7 collective-permute-done.70.refs_2_
  546.2 2.0 collective-permute-start.71
  551.9 6.0 %finish.3 = (f32[2,192,2304]{2,1,0:T(8,128)}, f32[2,192,768]{2,1,0:T(8,128)}, f32[2,768,384]{2,1,0:T(8,128)}, f32[2,384,768]{2,1,0:T(8,128)}, f32[2,192]{1,0:T(2...) custom-call(s32[8]{0:T(128)} %copy-done.31, ...), custom_call_target="tpu_custom_call", output_to_operand_aliasing={{0}: (11, {}), {1}: (12, {}), {2}: (13, {}), {3}: (14, {})} | custom-call | flops 1000000 | bytes 8388608 | tf_op jit(solution)/shard_map/finish/pallas_call | solution.py:937
  (468 shorter events, 113.8 us)
Async XLA Ops:
  7.2 45.3 %all-gather.5.cloned.1.call-start = ((), (), s32[]{:S(2)}) async-start(), calls=%async_computation.3 | async-start | bytes 1597440 | tf_op jit(solution)/shard_map/all_gather | solution.py:1062
  10.5 18.7 %collective-permute-start.2 = (bf16[2,256,768]{2,1,0:T(8,128)(2,1)}, bf16[2,256,768]{2,1,0:T(8,128)(2,1)}, u32[]{:S(2)}, u32[]{:S(2)}) collective-permute-start(bf16[2,256,768]{2,1,0:T(8,128)(2,1)} %pad_maximum_fusion), channel_id=1, source_target_pairs={{0,1},{1,0},{2,3},{3,2},{4,5},{5,4},{6,7},{7,6},{8,9},{9,8},{10,11... | collective-permute-start | bytes 2359304 | tf_op jit(solution)/shard_map/ppermute | solution.py:26
  14.9 73.5 %all-gather.7.cloned.1.call-start = ((), (), s32[]{:S(2)}) async-start(), calls=%async_computation.4 | async-start | bytes 1720320 | tf_op jit(solution)/shard_map/all_gather | solution.py:1062
  32.5 17.5 %collective-permute-start.4 = (bf16[512,768]{1,0:T(8,128)(2,1)S(1)}, bf16[512,768]{1,0:T(8,128)(2,1)S(1)}, u32[]{:S(2)}, u32[]{:S(2)}) collective-permute-start(bf16[512,768]{1,0:T(8,128)(2,1)S(1)} %get-tuple-element.178.refs_0_), channel_id=1, source_target_pairs={{0,4},{4,0},{1,5},{5,1},{2,6},{6,2},{3,7},{7,3},{8,12},{12,8},{9,1... | collective-permute-start | bytes 2359304 | tf_op jit(solution)/shard_map/ppermute | solution.py:26
  33.7 18.7 %collective-permute-start.3 = (bf16[512,768]{1,0:T(8,128)(2,1)S(1)}, bf16[512,768]{1,0:T(8,128)(2,1)S(1)}, u32[]{:S(2)}, u32[]{:S(2)}) collective-permute-start(bf16[512,768]{1,0:T(8,128)(2,1)S(1)} %get-tuple-element.178.refs_0_), channel_id=1, source_target_pairs={{0,2},{2,0},{1,3},{3,1},{4,6},{6,4},{5,7},{7,5},{8,10},{10,8},{9,1... | collective-permute-start | bytes 2359304 | tf_op jit(solution)/shard_map/ppermute | solution.py:26
  54.6 81.6 %all-gather.11.cloned.1.call-start = ((), (), s32[]{:S(2)}) async-start(), calls=%async_computation.6 | async-start | bytes 1597440 | tf_op jit(solution)/shard_map/all_gather | solution.py:1062
  54.6 28.1 %collective-permute-start = (bf16[384,1664]{1,0:T(8,128)(2,1)}, bf16[384,1664]{1,0:T(8,128)(2,1)}, u32[]{:S(2)}, u32[]{:S(2)}) collective-permute-start(bf16[384,1664]{1,0:T(8,128)(2,1)} %all-gather.5.cloned.1.call-done.refs_0_), channel_id=1, source_target_pairs={{0,4},{1,5},{2,3},{3,2},{4,0},{5,1},{6,7},{7,6},{8,12},{9,13},{10,... | collective-permute-start | bytes 3833864 | tf_op jit(solution)/shard_map/ppermute | solution.py:971
  55.9 30.0 %collective-permute-start.1 = (bf16[384,1664]{1,0:T(8,128)(2,1)}, bf16[384,1664]{1,0:T(8,128)(2,1)}, u32[]{:S(2)}, u32[]{:S(2)}) collective-permute-start(bf16[384,1664]{1,0:T(8,128)(2,1)} %all-gather.5.cloned.1.call-done.refs_0_), channel_id=1, source_target_pairs={{0,1},{1,0},{2,6},{3,7},{4,5},{5,4},{6,2},{7,3},{8,9},{9,8},{10,14... | collective-permute-start | bytes 3833864 | tf_op jit(solution)/shard_map/ppermute | solution.py:971
  64.5 52.8 %collective-permute-start.10 = (bf16[384,1664]{1,0:T(8,128)(2,1)}, bf16[384,1664]{1,0:T(8,128)(2,1)}, u32[]{:S(2)}, u32[]{:S(2)}) collective-permute-start(bf16[384,1664]{1,0:T(8,128)(2,1)} %all-gather.5.cloned.1.call-done.refs_0_), channel_id=1, source_target_pairs={{0,2},{2,0},{1,3},{3,1},{4,6},{6,4},{5,7},{7,5},{8,10},{10,8},{9,1... | collective-permute-start | bytes 3833864 | tf_op jit(solution)/shard_map/ppermute | solution.py:26
  85.9 31.4 %collective-permute-start.11 = (bf16[384,1664]{1,0:T(8,128)(2,1)}, bf16[384,1664]{1,0:T(8,128)(2,1)}, u32[]{:S(2)}, u32[]{:S(2)}) collective-permute-start(bf16[384,1664]{1,0:T(8,128)(2,1)} %collective-permute-done.refs_1_), channel_id=1, source_target_pairs={{0,2},{2,0},{1,3},{3,1},{4,6},{6,4},{5,7},{7,5},{8,10},{10,8},{9,1... | collective-permute-start | bytes 3833864 | tf_op jit(solution)/shard_map/ppermute | solution.py:26
  86.0 31.3 %collective-permute-start.9 = (bf16[384,1664]{1,0:T(8,128)(2,1)}, bf16[384,1664]{1,0:T(8,128)(2,1)}, u32[]{:S(2)}, u32[]{:S(2)}) collective-permute-start(bf16[384,1664]{1,0:T(8,128)(2,1)} %collective-permute-done.refs_1_), channel_id=1, source_target_pairs={{0,1},{1,0},{2,6},{3,7},{4,5},{5,4},{6,2},{7,3},{8,9},{9,8},{10,14... | collective-permute-start | bytes 3833864 | tf_op jit(solution)/shard_map/ppermute | solution.py:971
  87.2 30.1 %collective-permute-start.12 = (bf16[384,1664]{1,0:T(8,128)(2,1)}, bf16[384,1664]{1,0:T(8,128)(2,1)}, u32[]{:S(2)}, u32[]{:S(2)}) collective-permute-start(bf16[384,1664]{1,0:T(8,128)(2,1)} %collective-permute-done.1.refs_2_), channel_id=1, source_target_pairs={{0,2},{2,0},{1,3},{3,1},{4,6},{6,4},{5,7},{7,5},{8,10},{10,8},{9,1... | collective-permute-start | bytes 3833864 | tf_op jit(solution)/shard_map/ppermute | solution.py:26
  93.1 62.8 %all-gather.9.cloned.1.call-start = ((), (), s32[]{:S(2)}) async-start(), calls=%async_computation.5 | async-start | bytes 1474560 | tf_op jit(solution)/shard_map/all_gather | solution.py:1062
  94.9 20.7 %collective-permute-start.7 = (bf16[4,1,48,768]{3,2,0,1:T(8,128)(2,1)}, bf16[4,1,48,768]{3,2,0,1:T(8,128)(2,1)S(1)}, u32[]{:S(2)}, u32[]{:S(2)}) collective-permute-start(bf16[4,1,48,768]{3,2,0,1:T(8,128)(2,1)} %reshape.175), channel_id=1, source_target_pairs={{0,4},{4,0},{1,5},{5,1},{2,6},{6,2},{3,7},{7,3},{8,12},{12,8},{9,1... | collective-permute-start | bytes 884744 | tf_op jit(solution)/shard_map/ppermute | solution.py:26
  117.3 22.8 %collective-permute-start.16 = (bf16[384,1664]{1,0:T(8,128)(2,1)}, bf16[384,1664]{1,0:T(8,128)(2,1)}, u32[]{:S(2)}, u32[]{:S(2)}) collective-permute-start(bf16[384,1664]{1,0:T(8,128)(2,1)} %collective-permute-done.9.refs_3_), channel_id=1, source_target_pairs={{0,2},{2,0},{1,3},{3,1},{4,6},{6,4},{5,7},{7,5},{8,10},{10,8},{9,1... | collective-permute-start | bytes 3833864 | tf_op jit(solution)/shard_map/ppermute | solution.py:26
  118.3 10.6 %collective-permute-start.15 = (bf16[192,512]{1,0:T(8,128)(2,1)S(1)}, bf16[192,512]{1,0:T(8,128)(2,1)S(1)}, u32[]{:S(2)}, u32[]{:S(2)}) collective-permute-start(bf16[192,512]{1,0:T(8,128)(2,1)S(1)} %get-tuple-element.373), channel_id=1, source_target_pairs={{0,6},{2,4},{4,2},{6,0},{1,7},{3,5},{5,3},{7,1},{8,14},{10,12},{12... | collective-permute-start | bytes 589832 | tf_op jit(solution)/shard_map/ppermute | solution.py:979
  120.0 274.3 %reduce-scatter.4.cloned.1.call-start = ((), (), s32[]{:S(2)}) async-start(), calls=%async_computation.7 | async-start | bytes 1720320 | tf_op jit(solution)/shard_map/reduce_scatter | solution.py:1248
  136.2 18.6 %collective-permute-start.17 = (bf16[384,1664]{1,0:T(8,128)(2,1)}, bf16[384,1664]{1,0:T(8,128)(2,1)S(1)}, u32[]{:S(2)}, u32[]{:S(2)}) collective-permute-start(bf16[384,1664]{1,0:T(8,128)(2,1)} %all-gather.11.cloned.1.call-done.refs_0_), channel_id=1, source_target_pairs={{0,4},{1,5},{2,3},{3,2},{4,0},{5,1},{6,7},{7,6},{8,12},{9,13},{10,... | collective-permute-start | bytes 3833864 | tf_op jit(solution)/shard_map/ppermute | solution.py:971
  154.8 19.7 %collective-permute-start.24 = (bf16[512,768]{1,0:T(8,128)(2,1)}, bf16[512,768]{1,0:T(8,128)(2,1)S(1)}, u32[]{:S(2)}, u32[]{:S(2)}) collective-permute-start(bf16[512,768]{1,0:T(8,128)(2,1)} %get-tuple-element.202.refs_0_), channel_id=1, source_target_pairs={{0,4},{4,0},{1,5},{5,1},{2,6},{6,2},{3,7},{7,3},{8,12},{12,8},{9,1... | collective-permute-start | bytes 2359304 | tf_op jit(solution)/shard_map/ppermute | solution.py:26
  155.0 27.4 %collective-permute-start.21 = (bf16[2,768,512]{2,1,0:T(8,128)(2,1)}, bf16[2,768,512]{2,1,0:T(8,128)(2,1)}, u32[]{:S(2)}, u32[]{:S(2)}) collective-permute-start(bf16[2,768,512]{2,1,0:T(8,128)(2,1)} %get-tuple-element.201), channel_id=1, source_target_pairs={{0,2},{2,0},{1,3},{3,1},{4,6},{6,4},{5,7},{7,5},{8,10},{10,8},{9,1... | collective-permute-start | bytes 4718600 | tf_op jit(solution)/shard_map/ppermute | solution.py:26
  157.5 22.4 %collective-permute-start.19 = (bf16[4,1,48,768]{3,2,0,1:T(8,128)(2,1)S(1)}, bf16[4,1,48,768]{3,2,0,1:T(8,128)(2,1)S(1)}, u32[]{:S(2)}, u32[]{:S(2)}) collective-permute-start(bf16[4,1,48,768]{3,2,0,1:T(8,128)(2,1)S(1)} %reshape.177), channel_id=1, source_target_pairs={{0,4},{4,0},{1,5},{5,1},{2,6},{6,2},{3,7},{7,3},{8,12},{12,8},{9,1... | collective-permute-start | bytes 884744 | tf_op jit(solution)/shard_map/ppermute | solution.py:26
  158.6 23.0 %collective-permute-start.22 = (bf16[512,768]{1,0:T(8,128)(2,1)S(1)}, bf16[512,768]{1,0:T(8,128)(2,1)S(1)}, u32[]{:S(2)}, u32[]{:S(2)}) collective-permute-start(bf16[512,768]{1,0:T(8,128)(2,1)S(1)} %copy-done.6), channel_id=1, source_target_pairs={{0,2},{2,0},{1,3},{3,1},{4,6},{6,4},{5,7},{7,5},{8,10},{10,8},{9,1... | collective-permute-start | bytes 2359304 | tf_op jit(solution)/shard_map/ppermute | solution.py:26
  159.1 23.4 %collective-permute-start.23 = (bf16[512,768]{1,0:T(8,128)(2,1)}, bf16[512,768]{1,0:T(8,128)(2,1)S(1)}, u32[]{:S(2)}, u32[]{:S(2)}) collective-permute-start(bf16[512,768]{1,0:T(8,128)(2,1)} %get-tuple-element.202.refs_0_), channel_id=1, source_target_pairs={{0,2},{2,0},{1,3},{3,1},{4,6},{6,4},{5,7},{7,5},{8,10},{10,8},{9,1... | collective-permute-start | bytes 2359304 | tf_op jit(solution)/shard_map/ppermute | solution.py:26
  174.5 7.9 %collective-permute-start.25 = (bf16[512,768]{1,0:T(8,128)(2,1)S(1)}, bf16[512,768]{1,0:T(8,128)(2,1)S(1)}, u32[]{:S(2)}, u32[]{:S(2)}) collective-permute-start(bf16[512,768]{1,0:T(8,128)(2,1)S(1)} %collective-permute-done.24.refs_2_), channel_id=1, source_target_pairs={{0,2},{2,0},{1,3},{3,1},{4,6},{6,4},{5,7},{7,5},{8,10},{10,8},{9,1... | collective-permute-start | bytes 2359304 | tf_op jit(solution)/shard_map/ppermute | solution.py:26
  182.4 21.1 %collective-permute-start.26 = (bf16[384,1664]{1,0:T(8,128)(2,1)S(1)}, bf16[384,1664]{1,0:T(8,128)(2,1)}, u32[]{:S(2)}, u32[]{:S(2)}) collective-permute-start(bf16[384,1664]{1,0:T(8,128)(2,1)S(1)} %copy-done.92), channel_id=1, source_target_pairs={{0,1},{1,0},{2,6},{3,7},{4,5},{5,4},{6,2},{7,3},{8,9},{9,8},{10,14... | collective-permute-start | bytes 3833864 | tf_op jit(solution)/shard_map/ppermute | solution.py:971
  182.8 29.9 %collective-permute-start.28 = (bf16[384,1664]{1,0:T(8,128)(2,1)S(1)}, bf16[384,1664]{1,0:T(8,128)(2,1)S(1)}, u32[]{:S(2)}, u32[]{:S(2)}) collective-permute-start(bf16[384,1664]{1,0:T(8,128)(2,1)S(1)} %copy-done.92), channel_id=1, source_target_pairs={{0,2},{2,0},{1,3},{3,1},{4,6},{6,4},{5,7},{7,5},{8,10},{10,8},{9,1... | collective-permute-start | bytes 3833864 | tf_op jit(solution)/shard_map/ppermute | solution.py:26
  185.7 27.1 %collective-permute-start.27 = (bf16[384,1664]{1,0:T(8,128)(2,1)}, bf16[384,1664]{1,0:T(8,128)(2,1)}, u32[]{:S(2)}, u32[]{:S(2)}) collective-permute-start(bf16[384,1664]{1,0:T(8,128)(2,1)} %copy-done.93), channel_id=1, source_target_pairs={{0,1},{1,0},{2,6},{3,7},{4,5},{5,4},{6,2},{7,3},{8,9},{9,8},{10,14... | collective-permute-start | bytes 3833864 | tf_op jit(solution)/shard_map/ppermute | solution.py:971
  185.8 27.0 %collective-permute-start.29 = (bf16[384,1664]{1,0:T(8,128)(2,1)}, bf16[384,1664]{1,0:T(8,128)(2,1)S(1)}, u32[]{:S(2)}, u32[]{:S(2)}) collective-permute-start(bf16[384,1664]{1,0:T(8,128)(2,1)} %copy-done.93), channel_id=1, source_target_pairs={{0,2},{2,0},{1,3},{3,1},{4,6},{6,4},{5,7},{7,5},{8,10},{10,8},{9,1... | collective-permute-start | bytes 3833864 | tf_op jit(solution)/shard_map/ppermute | solution.py:26
  215.0 10.7 %collective-permute-start.32 = (bf16[192,512]{1,0:T(8,128)(2,1)S(1)}, bf16[192,512]{1,0:T(8,128)(2,1)S(1)}, u32[]{:S(2)}, u32[]{:S(2)}) collective-permute-start(bf16[192,512]{1,0:T(8,128)(2,1)S(1)} %get-tuple-element.367), channel_id=1, source_target_pairs={{0,6},{2,4},{4,2},{6,0},{1,7},{3,5},{5,3},{7,1},{8,14},{10,12},{12... | collective-permute-start | bytes 589832 | tf_op jit(solution)/shard_map/ppermute | solution.py:979
  225.7 12.0 %collective-permute-start.34 = (bf16[384,1664]{1,0:T(8,128)(2,1)}, bf16[384,1664]{1,0:T(8,128)(2,1)}, u32[]{:S(2)}, u32[]{:S(2)}) collective-permute-start(bf16[384,1664]{1,0:T(8,128)(2,1)} %collective-permute-done.27.refs_3_), channel_id=1, source_target_pairs={{0,2},{2,0},{1,3},{3,1},{4,6},{6,4},{5,7},{7,5},{8,10},{10,8},{9,1... | collective-permute-start | bytes 3833864 | tf_op jit(solution)/shard_map/ppermute | solution.py:26
  226.0 11.8 %collective-permute-start.33 = (bf16[384,1664]{1,0:T(8,128)(2,1)}, bf16[384,1664]{1,0:T(8,128)(2,1)}, u32[]{:S(2)}, u32[]{:S(2)}) collective-permute-start(bf16[384,1664]{1,0:T(8,128)(2,1)} %collective-permute-done.26.refs_2_), channel_id=1, source_target_pairs={{0,2},{2,0},{1,3},{3,1},{4,6},{6,4},{5,7},{7,5},{8,10},{10,8},{9,1... | collective-permute-start | bytes 3833864 | tf_op jit(solution)/shard_map/ppermute | solution.py:26
  259.9 15.1 %collective-permute-start.38 = (bf16[2,512,768]{2,1,0:T(8,128)(2,1)}, bf16[2,512,768]{2,1,0:T(8,128)(2,1)S(1)}, u32[]{:S(2)}, u32[]{:S(2)}) collective-permute-start(bf16[2,512,768]{2,1,0:T(8,128)(2,1)} %get-tuple-element.230), channel_id=1, source_target_pairs={{0,2},{2,0},{1,3},{3,1},{4,6},{6,4},{5,7},{7,5},{8,10},{10,8},{9,1... | collective-permute-start | bytes 4718600 | tf_op jit(solution)/shard_map/ppermute | solution.py:26
  260.2 14.8 %collective-permute-start.39 = (bf16[2,768,512]{2,1,0:T(8,128)(2,1)}, bf16[2,768,512]{2,1,0:T(8,128)(2,1)S(1)}, u32[]{:S(2)}, u32[]{:S(2)}) collective-permute-start(bf16[2,768,512]{2,1,0:T(8,128)(2,1)} %get-tuple-element.238), channel_id=1, source_target_pairs={{0,2},{2,0},{1,3},{3,1},{4,6},{6,4},{5,7},{7,5},{8,10},{10,8},{9,1... | collective-permute-start | bytes 4718600 | tf_op jit(solution)/shard_map/ppermute | solution.py:26
  266.4 8.6 %collective-permute-start.41 = (bf16[512,768]{1,0:T(8,128)(2,1)S(1)}, bf16[512,768]{1,0:T(8,128)(2,1)S(1)}, u32[]{:S(2)}, u32[]{:S(2)}) collective-permute-start(bf16[512,768]{1,0:T(8,128)(2,1)S(1)} %copy-done.2), channel_id=1, source_target_pairs={{0,2},{2,0},{1,3},{3,1},{4,6},{6,4},{5,7},{7,5},{8,10},{10,8},{9,1... | collective-permute-start | bytes 2359304 | tf_op jit(solution)/shard_map/ppermute | solution.py:26
  267.2 7.9 %collective-permute-start.40 = (bf16[512,768]{1,0:T(8,128)(2,1)S(1)}, bf16[512,768]{1,0:T(8,128)(2,1)S(1)}, u32[]{:S(2)}, u32[]{:S(2)}) collective-permute-start(bf16[512,768]{1,0:T(8,128)(2,1)S(1)} %copy-done.10), channel_id=1, source_target_pairs={{0,2},{2,0},{1,3},{3,1},{4,6},{6,4},{5,7},{7,5},{8,10},{10,8},{9,1... | collective-permute-start | bytes 2359304 | tf_op jit(solution)/shard_map/ppermute | solution.py:26
  274.9 8.6 %collective-permute-start.43 = (bf16[4,48,768]{2,1,0:T(8,128)(2,1)S(1)}, bf16[4,48,768]{2,1,0:T(8,128)(2,1)S(1)}, u32[]{:S(2)}, u32[]{:S(2)}) collective-permute-start(bf16[4,48,768]{2,1,0:T(8,128)(2,1)S(1)} %fusion.4), channel_id=1, source_target_pairs={{0,4},{4,0},{1,5},{5,1},{2,6},{6,2},{3,7},{7,3},{8,12},{12,8},{9,1... | collective-permute-start | bytes 884744 | tf_op jit(solution)/shard_map/ppermute | solution.py:26
  284.2 30.4 %collective-permute-start.44 = (bf16[768,1664]{1,0:T(8,128)(2,1)}, bf16[768,1664]{1,0:T(8,128)(2,1)}, u32[]{:S(2)}, u32[]{:S(2)}) collective-permute-start(bf16[768,1664]{1,0:T(8,128)(2,1)} %feed_weights.4), channel_id=1, source_target_pairs={{0,1},{1,0},{2,6},{3,7},{4,5},{5,4},{6,2},{7,3},{8,9},{9,8},{10,14... | collective-permute-start | bytes 7667720 | tf_op jit(solution)/shard_map/ppermute | solution.py:971
  322.8 19.2 %collective-permute-start.46 = (bf16[512,768]{1,0:T(8,128)(2,1)S(1)}, bf16[512,768]{1,0:T(8,128)(2,1)S(1)}, u32[]{:S(2)}, u32[]{:S(2)}) collective-permute-start(bf16[512,768]{1,0:T(8,128)(2,1)S(1)} %fusion.1), channel_id=1, source_target_pairs={{0,4},{4,0},{1,5},{5,1},{2,6},{6,2},{3,7},{7,3},{8,12},{12,8},{9,1... | collective-permute-start | bytes 2359304 | tf_op jit(solution)/shard_map/ppermute | solution.py:26
  324.0 11.1 %collective-permute-start.47 = (bf16[256,768]{1,0:T(8,128)(2,1)S(1)}, bf16[256,768]{1,0:T(8,128)(2,1)S(1)}, u32[]{:S(2)}, u32[]{:S(2)}) collective-permute-start(bf16[256,768]{1,0:T(8,128)(2,1)S(1)} %get-tuple-element.362), channel_id=1, source_target_pairs={{0,1},{1,0},{2,3},{3,2},{4,5},{5,4},{6,7},{7,6},{8,9},{9,8},{10,11... | collective-permute-start | bytes 1179656 | tf_op jit(solution)/shard_map/ppermute | solution.py:26
  342.9 17.0 %collective-permute-start.48 = (bf16[384,1664]{1,0:T(8,128)(2,1)}, bf16[384,1664]{1,0:T(8,128)(2,1)}, u32[]{:S(2)}, u32[]{:S(2)}) collective-permute-start(bf16[384,1664]{1,0:T(8,128)(2,1)} %add_convert_fusion.3), channel_id=1, source_target_pairs={{0,4},{1,5},{2,3},{3,2},{4,0},{5,1},{6,7},{7,6},{8,12},{9,13},{10,... | collective-permute-start | bytes 3833864 | tf_op jit(solution)/shard_map/ppermute | solution.py:971
  357.6 83.5 %reduce-scatter.6.cloned.1.call-start = ((), (), s32[]{:S(2)}) async-start(), calls=%async_computation.8 | async-start | bytes 1597440 | tf_op jit(solution)/shard_map/reduce_scatter | solution.py:1253
  377.1 17.2 %collective-permute-start.52 = (bf16[2,512,768]{2,1,0:T(8,128)(2,1)}, bf16[2,512,768]{2,1,0:T(8,128)(2,1)}, u32[]{:S(2)}, u32[]{:S(2)}) collective-permute-start(bf16[2,512,768]{2,1,0:T(8,128)(2,1)} %get-tuple-element.274), channel_id=1, source_target_pairs={{0,2},{2,0},{1,3},{3,1},{4,6},{6,4},{5,7},{7,5},{8,10},{10,8},{9,1... | collective-permute-start | bytes 4718600 | tf_op jit(solution)/shard_map/ppermute | solution.py:26
  378.5 17.6 %collective-permute-start.53 = (bf16[512,768]{1,0:T(8,128)(2,1)}, bf16[512,768]{1,0:T(8,128)(2,1)}, u32[]{:S(2)}, u32[]{:S(2)}) collective-permute-start(bf16[512,768]{1,0:T(8,128)(2,1)} %get-tuple-element.267.dm_ref.dm), channel_id=1, source_target_pairs={{0,2},{2,0},{1,3},{3,1},{4,6},{6,4},{5,7},{7,5},{8,10},{10,8},{9,1... | collective-permute-start | bytes 2359304 | tf_op jit(solution)/shard_map/ppermute | solution.py:26
  378.6 11.7 %collective-permute-start.49 = (bf16[192,512]{1,0:T(8,128)(2,1)}, bf16[192,512]{1,0:T(8,128)(2,1)}, u32[]{:S(2)}, u32[]{:S(2)}) collective-permute-start(bf16[192,512]{1,0:T(8,128)(2,1)} %get-tuple-element.271), channel_id=1, source_target_pairs={{0,2},{2,0},{1,3},{3,1},{4,6},{6,4},{5,7},{7,5},{8,10},{10,8},{9,1... | collective-permute-start | bytes 589832 | tf_op jit(solution)/shard_map/ppermute | solution.py:26
  379.0 11.4 %collective-permute-start.50 = (bf16[192,512]{1,0:T(8,128)(2,1)}, bf16[192,512]{1,0:T(8,128)(2,1)}, u32[]{:S(2)}, u32[]{:S(2)}) collective-permute-start(bf16[192,512]{1,0:T(8,128)(2,1)} %get-tuple-element.272), channel_id=1, source_target_pairs={{0,4},{4,0},{1,5},{5,1},{2,6},{6,2},{3,7},{7,3},{8,12},{12,8},{9,1... | collective-permute-start | bytes 589832 | tf_op jit(solution)/shard_map/ppermute | solution.py:26
  386.8 138.1 %reduce-scatter.8.cloned.1.call-start = ((), (), s32[]{:S(2)}) async-start(), calls=%async_computation.9 | async-start | bytes 1720320 | tf_op jit(solution)/shard_map/reduce_scatter | solution.py:1220
  390.3 18.3 %collective-permute-start.55 = (bf16[4,48,768]{2,1,0:T(8,128)(2,1)}, bf16[4,48,768]{2,1,0:T(8,128)(2,1)}, u32[]{:S(2)}, u32[]{:S(2)}) collective-permute-start(bf16[4,48,768]{2,1,0:T(8,128)(2,1)} %fusion.3), channel_id=1, source_target_pairs={{0,4},{4,0},{1,5},{5,1},{2,6},{6,2},{3,7},{7,3},{8,12},{12,8},{9,1... | collective-permute-start | bytes 884744 | tf_op jit(solution)/shard_map/ppermute | solution.py:26
  394.3 14.1 %collective-permute-start.56 = (bf16[192,896]{1,0:T(8,128)(2,1)}, bf16[192,896]{1,0:T(8,128)(2,1)S(1)}, u32[]{:S(2)}, u32[]{:S(2)}) collective-permute-start(bf16[192,896]{1,0:T(8,128)(2,1)} %reduce-scatter.4.cloned.1.call-done), channel_id=1, source_target_pairs={{0,1},{1,0},{2,3},{3,2},{4,5},{5,4},{6,7},{7,6},{8,9},{9,8},{10,11... | collective-permute-start | bytes 1032200 | tf_op jit(solution)/shard_map/ppermute | solution.py:26
  408.6 32.5 %collective-permute-start.57 = (bf16[768,1664]{1,0:T(8,128)(2,1)}, bf16[768,1664]{1,0:T(8,128)(2,1)}, u32[]{:S(2)}, u32[]{:S(2)}) collective-permute-start(bf16[768,1664]{1,0:T(8,128)(2,1)} %feed_weights.7), channel_id=1, source_target_pairs={{0,1},{1,0},{2,6},{3,7},{4,5},{5,4},{6,2},{7,3},{8,9},{9,8},{10,14... | collective-permute-start | bytes 7667720 | tf_op jit(solution)/shard_map/ppermute | solution.py:971
  441.1 16.7 %collective-permute-start.59 = (bf16[192,896]{1,0:T(8,128)(2,1)S(1)}, bf16[192,896]{1,0:T(8,128)(2,1)S(1)}, u32[]{:S(2)}, u32[]{:S(2)}) collective-permute-start(bf16[192,896]{1,0:T(8,128)(2,1)S(1)} %add_convert_fusion.5.refs_0_), channel_id=1, source_target_pairs={{0,4},{4,0},{1,5},{5,1},{2,6},{6,2},{3,7},{7,3},{8,12},{12,8},{9,1... | collective-permute-start | bytes 1032200 | tf_op jit(solution)/shard_map/ppermute | solution.py:26
  441.2 16.2 %collective-permute-start.61 = (bf16[96,1664]{1,0:T(8,128)(2,1)}, bf16[96,1664]{1,0:T(8,128)(2,1)}, u32[]{:S(2)}, u32[]{:S(2)}) collective-permute-start(bf16[96,1664]{1,0:T(8,128)(2,1)} %reduce-scatter.6.cloned.1.call-done.refs_4_), channel_id=1, source_target_pairs={{0,4},{4,0},{1,5},{5,1},{2,6},{6,2},{3,7},{7,3},{8,12},{12,8},{9,1... | collective-permute-start | bytes 958472 | tf_op jit(solution)/shard_map/ppermute | solution.py:26
  444.8 21.4 %collective-permute-start.65 = (bf16[2,512,768]{2,1,0:T(8,128)(2,1)}, bf16[2,512,768]{2,1,0:T(8,128)(2,1)S(1)}, u32[]{:S(2)}, u32[]{:S(2)}) collective-permute-start(bf16[2,512,768]{2,1,0:T(8,128)(2,1)} %get-tuple-element.309), channel_id=1, source_target_pairs={{0,2},{2,0},{1,3},{3,1},{4,6},{6,4},{5,7},{7,5},{8,10},{10,8},{9,1... | collective-permute-start | bytes 4718600 | tf_op jit(solution)/shard_map/ppermute | solution.py:26
  452.4 8.5 %collective-permute-start.58 = (bf16[192,896]{1,0:T(8,128)(2,1)S(1)}, bf16[192,896]{1,0:T(8,128)(2,1)S(1)}, u32[]{:S(2)}, u32[]{:S(2)}) collective-permute-start(bf16[192,896]{1,0:T(8,128)(2,1)S(1)} %add_convert_fusion.5.refs_0_), channel_id=1, source_target_pairs={{0,2},{2,0},{1,3},{3,1},{4,6},{6,4},{5,7},{7,5},{8,10},{10,8},{9,1... | collective-permute-start | bytes 1032200 | tf_op jit(solution)/shard_map/ppermute | solution.py:26
  453.0 8.0 %collective-permute-start.62 = (bf16[96,1664]{1,0:T(8,128)(2,1)}, bf16[96,1664]{1,0:T(8,128)(2,1)S(1)}, u32[]{:S(2)}, u32[]{:S(2)}) collective-permute-start(bf16[96,1664]{1,0:T(8,128)(2,1)} %reduce-scatter.6.cloned.1.call-done.refs_4_), channel_id=1, source_target_pairs={{0,2},{2,0},{1,3},{3,1},{4,6},{6,4},{5,7},{7,5},{8,10},{10,8},{9,1... | collective-permute-start | bytes 958472 | tf_op jit(solution)/shard_map/ppermute | solution.py:26
  462.6 18.9 %collective-permute-start.64 = (bf16[384,1664]{1,0:T(8,128)(2,1)}, bf16[384,1664]{1,0:T(8,128)(2,1)}, u32[]{:S(2)}, u32[]{:S(2)}) collective-permute-start(bf16[384,1664]{1,0:T(8,128)(2,1)} %add_convert_fusion.1), channel_id=1, source_target_pairs={{0,4},{1,5},{2,3},{3,2},{4,0},{5,1},{6,7},{7,6},{8,12},{9,13},{10,... | collective-permute-start | bytes 3833864 | tf_op jit(solution)/shard_map/ppermute | solution.py:971
  481.5 24.8 %collective-permute-start.66 = (bf16[512,768]{1,0:T(8,128)(2,1)S(1)}, bf16[512,768]{1,0:T(8,128)(2,1)S(1)}, u32[]{:S(2)}, u32[]{:S(2)}) collective-permute-start(bf16[512,768]{1,0:T(8,128)(2,1)S(1)} %fusion), channel_id=1, source_target_pairs={{0,4},{4,0},{1,5},{5,1},{2,6},{6,2},{3,7},{7,3},{8,12},{12,8},{9,1... | collective-permute-start | bytes 2359304 | tf_op jit(solution)/shard_map/ppermute | solution.py:26
  485.8 33.7 %collective-permute-start.72 = (bf16[96,1664]{1,0:T(8,128)(2,1)}, bf16[96,1664]{1,0:T(8,128)(2,1)}, u32[]{:S(2)}, u32[]{:S(2)}) collective-permute-start(bf16[96,1664]{1,0:T(8,128)(2,1)} %get-tuple-element.342), channel_id=1, source_target_pairs={{0,8},{8,16},{16,24},{24,0},{1,9},{9,17},{17,25},{25,1},{2,10},{10... | collective-permute-start | bytes 958472 | tf_op jit(solution)/shard_map/ppermute | solution.py:1069
  498.2 24.9 %collective-permute-start.73 = (bf16[96,1664]{1,0:T(8,128)(2,1)}, bf16[96,1664]{1,0:T(8,128)(2,1)}, u32[]{:S(2)}, u32[]{:S(2)}) collective-permute-start(bf16[96,1664]{1,0:T(8,128)(2,1)} %get-tuple-element.341), channel_id=1, source_target_pairs={{0,16},{8,24},{16,0},{24,8},{1,17},{9,25},{17,1},{25,9},{2,18},{10... | collective-permute-start | bytes 958472 | tf_op jit(solution)/shard_map/ppermute | solution.py:1069
  500.8 24.1 %collective-permute-start.74 = (bf16[96,1664]{1,0:T(8,128)(2,1)}, bf16[96,1664]{1,0:T(8,128)(2,1)}, u32[]{:S(2)}, u32[]{:S(2)}) collective-permute-start(bf16[96,1664]{1,0:T(8,128)(2,1)} %get-tuple-element.340), channel_id=1, source_target_pairs={{0,24},{8,0},{16,8},{24,16},{1,25},{9,1},{17,9},{25,17},{2,26},{10... | collective-permute-start | bytes 958472 | tf_op jit(solution)/shard_map/ppermute | solution.py:1069
  524.9 11.7 %collective-permute-start.68 = (bf16[192,896]{1,0:T(8,128)(2,1)}, bf16[192,896]{1,0:T(8,128)(2,1)S(1)}, u32[]{:S(2)}, u32[]{:S(2)}) collective-permute-start(bf16[192,896]{1,0:T(8,128)(2,1)} %reduce-scatter.8.cloned.1.call-done), channel_id=1, source_target_pairs={{0,1},{1,0},{2,3},{3,2},{4,5},{5,4},{6,7},{7,6},{8,9},{9,8},{10,11... | collective-permute-start | bytes 1032200 | tf_op jit(solution)/shard_map/ppermute | solution.py:26
  530.7 17.5 %collective-permute-start.75 = (bf16[96,1664]{1,0:T(8,128)(2,1)S(1)}, bf16[96,1664]{1,0:T(8,128)(2,1)}, u32[]{:S(2)}, u32[]{:S(2)}) collective-permute-start(bf16[96,1664]{1,0:T(8,128)(2,1)S(1)} %add_convert_fusion.6.refs_4_), channel_id=1, source_target_pairs={{0,4},{4,0},{1,5},{5,1},{2,6},{6,2},{3,7},{7,3},{8,12},{12,8},{9,1... | collective-permute-start | bytes 958472 | tf_op jit(solution)/shard_map/ppermute | solution.py:26
  536.7 9.5 %collective-permute-start.70 = (bf16[192,896]{1,0:T(8,128)(2,1)S(1)}, bf16[192,896]{1,0:T(8,128)(2,1)}, u32[]{:S(2)}, u32[]{:S(2)}) collective-permute-start(bf16[192,896]{1,0:T(8,128)(2,1)S(1)} %add_convert_fusion.4.refs_0_), channel_id=1, source_target_pairs={{0,4},{4,0},{1,5},{5,1},{2,6},{6,2},{3,7},{7,3},{8,12},{12,8},{9,1... | collective-permute-start | bytes 1032200 | tf_op jit(solution)/shard_map/ppermute | solution.py:26
  537.5 12.2 %collective-permute-start.67 = (bf16[256,768]{1,0:T(8,128)(2,1)S(1)}, bf16[256,768]{1,0:T(8,128)(2,1)S(1)}, u32[]{:S(2)}, u32[]{:S(2)}) collective-permute-start(bf16[256,768]{1,0:T(8,128)(2,1)S(1)} %get-tuple-element.360), channel_id=1, source_target_pairs={{0,1},{1,0},{2,3},{3,2},{4,5},{5,4},{6,7},{7,6},{8,9},{9,8},{10,11... | collective-permute-start | bytes 1179656 | tf_op jit(solution)/shard_map/ppermute | solution.py:26
  538.7 12.4 %collective-permute-start.69 = (bf16[192,896]{1,0:T(8,128)(2,1)S(1)}, bf16[192,896]{1,0:T(8,128)(2,1)S(1)}, u32[]{:S(2)}, u32[]{:S(2)}) collective-permute-start(bf16[192,896]{1,0:T(8,128)(2,1)S(1)} %add_convert_fusion.4.refs_0_), channel_id=1, source_target_pairs={{0,2},{2,0},{1,3},{3,1},{4,6},{6,4},{5,7},{7,5},{8,10},{10,8},{9,1... | collective-permute-start | bytes 1032200 | tf_op jit(solution)/shard_map/ppermute | solution.py:26
  (121 other events, 1161.7 us)
Sparse Core Ops, SparseCore 0:
  15.0 31.7 all-gather.4
  54.7 33.6 all-gather.6
  93.2 30.4 all-gather.10
  125.2 29.5 all-gather.8
  357.7 35.3 reduce-scatter.3
  395.4 29.5 reduce-scatter.5
  452.5 43.6 reduce-scatter.7
